TPU v7x, 32 devices: a whole 2x2x4 slice. The times are simulated.
32 devices in a mesh: row: 8 (over y, x, core), col: 4 (over z).
Axes of the slice: x: 2, y: 2, z: 4, core: 2. Of those that a mesh axis runs over, the one named last changes fastest.
Arguments:
- matrix: float32 [12288, 12288], P('row', 'col'), may hold values from -10 to 10, as said below
- panel: float32 [12288, 64], P('row'), may hold values from -1.12763724 to 1.12763724
Outputs:
- updated: float32 [12288, 12288], P('row', 'col')
- band_block: float32 [64, 64], replicated
Inputs may be any that keep to these rules, and one draw needn't show every extreme that they name: matrix is exactly symmetric.
All inputs are finite; a program needn't handle non-finite values.
Results may differ from a plain program's by a relative error of at most 0.0002.
Values sent between devices are 32-bit elements; how exact they have to be, the bound alone decides.
No kernel may reach another device: no remote copies, remote signals or barrier semaphores. Data moves between devices by JAX's collectives and lax.ppermute only.
A program may use at most 128 MiB of HBM per device.

v0:
```python
import jax
import jax.numpy as jnp
from jax import lax
from jax.sharding import PartitionSpec as P

precise = lax.Precision.HIGHEST


def upper_cholesky(gram_block):
    order_now = gram_block.shape[0]
    positions = jnp.arange(order_now)

    def one_column(column_index, lower_part):
        gram_column = lax.dynamic_slice_in_dim(gram_block, column_index, 1, 1)[:, 0]
        lower_row = lax.dynamic_slice_in_dim(lower_part, column_index, 1, 0)[0]
        earlier = jnp.where(positions < column_index, lower_row, 0.0)
        reduced = gram_column - jnp.dot(lower_part, earlier, precision=precise)
        pivot_value = jnp.sum(jnp.where(positions == column_index, reduced, 0.0))
        diagonal_value = jnp.sqrt(pivot_value)
        new_column = jnp.where(positions > column_index, reduced / diagonal_value, 0.0) + jnp.where(
            positions == column_index, diagonal_value, 0.0
        )
        return jnp.where(positions[None, :] == column_index, new_column[:, None], lower_part)

    lower_part = lax.fori_loop(
        0, order_now, one_column, jnp.zeros((order_now, order_now), jnp.float32)
    )
    return lower_part.T


def upper_inverse(upper_block):
    order_now = upper_block.shape[0]
    positions = jnp.arange(order_now)

    def one_row(step_count, inverse_part):
        row_at = order_now - 1 - step_count
        upper_row = lax.dynamic_slice_in_dim(upper_block, row_at, 1, 0)[0]
        diagonal_value = jnp.sum(jnp.where(positions == row_at, upper_row, 0.0))
        beyond = jnp.where(positions > row_at, upper_row, 0.0)
        unit_row = jnp.where(positions == row_at, 1.0, 0.0)
        new_row = (unit_row - jnp.dot(beyond, inverse_part, precision=precise)) / diagonal_value
        return jnp.where(positions[:, None] == row_at, new_row[None, :], inverse_part)

    return lax.fori_loop(0, order_now, one_row, jnp.zeros((order_now, order_now), jnp.float32))


def small_factor(block_in):
    order_now = block_in.shape[0]
    positions = jnp.arange(order_now)

    def one_pivot(pivot_index, state_pair):
        working, lower_whole = state_pair
        pivot_column = lax.dynamic_slice_in_dim(working, pivot_index, 1, 1)[:, 0]
        pivot_row = lax.dynamic_slice_in_dim(working, pivot_index, 1, 0)[0]
        pivot_value = jnp.sum(jnp.where(positions == pivot_index, pivot_column, 0.0))
        multipliers = jnp.where(positions > pivot_index, pivot_column / pivot_value, 0.0)
        lower_whole = lower_whole + multipliers[:, None] * (
            positions[None, :] == pivot_index
        ).astype(jnp.float32)
        working = working - multipliers[:, None] * pivot_row[None, :]
        return (working, lower_whole)

    working, lower_whole = lax.fori_loop(
        0, order_now, one_pivot, (block_in, jnp.eye(order_now, dtype=jnp.float32))
    )
    return (lower_whole, jnp.triu(working))


def body(matrix, panel):
    local_rows, local_columns = matrix.shape
    panel_width = panel.shape[1]
    row_index = lax.axis_index("row")
    current_column_index = lax.axis_index("col")
    local_inner = jnp.dot(panel.T, panel, precision=precise)
    head_rows = panel[:panel_width]
    masked = jnp.where(row_index == 0, head_rows, 0.0)
    total_inner, head_rows = lax.psum((local_inner, masked), "row")
    band_factor = -upper_cholesky(total_inner)
    factor_inverse = upper_inverse(band_factor)
    orthogonal_rows = jnp.dot(panel, factor_inverse, precision=precise)
    orthogonal_head = jnp.dot(head_rows, factor_inverse, precision=precise)
    identity = jnp.eye(panel_width, dtype=jnp.float32)
    lower_whole, upper_whole = small_factor(orthogonal_head - identity)
    global_rows = row_index * local_rows + jnp.arange(local_rows)
    unit_rows = (global_rows[:, None] == jnp.arange(panel_width)[None, :]).astype(jnp.float32)
    reflect_rows = jnp.dot(
        orthogonal_rows - unit_rows, upper_inverse(upper_whole), precision=precise
    )
    triangle = -jnp.dot(upper_whole, upper_inverse(lower_whole.T), precision=precise)
    gathered_reflect = lax.all_gather(reflect_rows, "row", axis=0, tiled=True)
    reflect_columns = lax.dynamic_slice_in_dim(
        gathered_reflect, current_column_index * local_columns, local_columns, 0
    )
    partial_product = lax.dot_general(
        matrix, reflect_rows, (((0,), (0,)), ((), ())), precision=precise
    )
    product = lax.psum(partial_product, "row")
    applied_cols = jnp.dot(product, triangle, precision=precise)
    inner_part = jnp.dot(reflect_columns.T, applied_cols, precision=precise)
    inner_total = lax.psum(inner_part, "col")
    coupling = jnp.dot(triangle.T, inner_total, precision=precise)
    corrected_cols = applied_cols - 0.5 * jnp.dot(reflect_columns, coupling, precision=precise)
    gathered_corrected = lax.all_gather(corrected_cols, "col", axis=0, tiled=True)
    corrected_rows = lax.dynamic_slice_in_dim(
        gathered_corrected, row_index * local_rows, local_rows, 0
    )
    left_factor = jnp.concatenate([reflect_rows, corrected_rows], 1)
    right_factor = jnp.concatenate([corrected_cols, reflect_columns], 1)
    updated = matrix - lax.dot_general(
        left_factor, right_factor, (((1,), (1,)), ((), ())), precision=precise
    )
    return (updated, band_factor)


def solution(mesh):
    return jax.shard_map(
        body,
        mesh=mesh,
        in_specs=(P("row", "col"), P("row", None)),
        out_specs=(P("row", "col"), P()),
        check_vma=False,
    )
```

profile of v0, /device:TPU:0, one launch (start us, length us, event | category | flops | bytes accessed | tf_op | source)
XLA Modules:
  0.0 656.6 jit_solution(17921866801268675758)
XLA Ops:
  7.2 1.6 fusion.69
  9.8 26.1 %all-reduce = (f32[64,64]{1,0:T(8,128)S(1)}, f32[64,64]{1,0:T(8,128)S(1)}) all-reduce(f32[64,64]{1,0:T(8,128)S(1)} %fusion.69, f32[64,64]{1,0:T(8,128)S(1)} %broadcast_select_fusion.2), channel_id=1, replica_groups=mesh['row'=8,'col'=4] {'row'}, use_global_device_ids=true, to_apply=%region_0.1 | all-reduce | flops 8192 | bytes 65536 | tf_op jit(solution)/shard_map/psum | solution.py:77
  36.0 102.3 %while.84 = (s32[]{:T(128)}, f32[64,64]{1,0:T(8,128)S(1)}, f32[64,64]{0,1:T(8,128)S(1)}, s32[]{:T(128)}, s32[]{:T(128)}) while((s32[]{:T(128)}, f32[64,64]{1,0:T(8,128)S(1)}, f32[64,64]{0,1:T(8,128)S(1)}, s32[]{:T(128)}, s32[]{:T(128)}) %tuple.192), condition=%wide.region_3.4_spmd.clone.clone, body=%wide.region_1.0_spmd.clone.clone.sunk | while | flops 62274 | bytes 102632 | solution.py:25
  36.1 0.8 select_reduce_fusion.2
  37.7 0.8 select_reduce_fusion.2
  39.2 0.8 select_reduce_fusion.2
  40.8 0.8 select_reduce_fusion.2
  42.4 0.8 select_reduce_fusion.2
  44.0 0.8 select_reduce_fusion.2
  45.6 0.8 select_reduce_fusion.2
  47.2 0.8 select_reduce_fusion.2
  48.8 0.8 select_reduce_fusion.2
  50.4 0.8 select_reduce_fusion.2
  52.0 0.8 select_reduce_fusion.2
  53.6 0.8 select_reduce_fusion.2
  55.2 0.8 select_reduce_fusion.2
  56.8 0.8 select_reduce_fusion.2
  58.4 0.8 select_reduce_fusion.2
  60.0 0.8 select_reduce_fusion.2
  61.6 0.8 select_reduce_fusion.2
  63.2 0.8 select_reduce_fusion.2
  64.8 0.8 select_reduce_fusion.2
  66.4 0.8 select_reduce_fusion.2
  68.0 0.8 select_reduce_fusion.2
  69.6 0.8 select_reduce_fusion.2
  71.2 0.8 select_reduce_fusion.2
  72.8 0.8 select_reduce_fusion.2
  74.4 0.8 select_reduce_fusion.2
  76.0 0.8 select_reduce_fusion.2
  77.6 0.8 select_reduce_fusion.2
  79.2 0.8 select_reduce_fusion.2
  80.8 0.8 select_reduce_fusion.2
  82.4 0.8 select_reduce_fusion.2
  84.0 0.8 select_reduce_fusion.2
  85.6 0.8 select_reduce_fusion.2
  87.2 0.8 select_reduce_fusion.2
  88.8 0.8 select_reduce_fusion.2
  90.4 0.8 select_reduce_fusion.2
  92.0 0.8 select_reduce_fusion.2
  93.6 0.8 select_reduce_fusion.2
  95.2 0.8 select_reduce_fusion.2
  96.8 0.8 select_reduce_fusion.2
  98.4 0.8 select_reduce_fusion.2
  100.0 0.8 select_reduce_fusion.2
  101.6 0.8 select_reduce_fusion.2
  108.0 0.8 select_reduce_fusion.2
  114.4 0.8 select_reduce_fusion.2
  119.1 0.8 select_reduce_fusion.2
  120.7 0.8 select_reduce_fusion.2
  125.5 0.8 select_reduce_fusion.2
  131.9 0.8 select_reduce_fusion.2
  138.4 95.1 %while.85 = (s32[]{:T(128)}, f32[64,64]{1,0:T(8,128)S(1)}, f32[64,64]{1,0:T(8,128)S(1)}, s32[]{:T(128)}, s32[]{:T(128)}, /*index=5*/s32[]{:T(128)}, s32[]{:T(128)}) while((s32[]{:T(128)}, f32[64,64]{1,0:T(8,128)S(1)}, f32[64,64]{1,0:T(8,128)S(1)}, s32[]{:T(128)}, s32[]{:T(128)}, /*index=5*/s32[]{:T(128)}, ...), condition=%wide.region_6.7_spmd.clone.clone, body=%wide.region_4.6_spmd.clone.clone.sunk | while | flops 62086 | bytes 69153 | solution.py:44
  233.7 100.6 %while.83 = (s32[]{:T(128)}, f32[64,64]{0,1:T(8,128)S(1)}, f32[64,64]{0,1:T(8,128)S(1)}, s32[]{:T(128)}) while((s32[]{:T(128)}, f32[64,64]{0,1:T(8,128)S(1)}, f32[64,64]{0,1:T(8,128)S(1)}, s32[]{:T(128)}) %tuple.198), condition=%wide.region_10.11_spmd.clone.clone, body=%wide.region_8.10_spmd.clone.clone.sunk | while | flops 16897 | bytes 69965 | solution.py:63
  334.5 95.1 %while.86 = (s32[]{:T(128)}, f32[64,64]{1,0:T(8,128)S(1)}, f32[64,64]{1,0:T(8,128)S(1)}, s32[]{:T(128)}, s32[]{:T(128)}, /*index=5*/s32[]{:T(128)}, s32[]{:T(128)}) while((s32[]{:T(128)}, f32[64,64]{1,0:T(8,128)S(1)}, f32[64,64]{1,0:T(8,128)S(1)}, s32[]{:T(128)}, s32[]{:T(128)}, /*index=5*/s32[]{:T(128)}, ...), condition=%wide.region_13.14_spmd.clone.clone, body=%wide.region_11.13_spmd.clone.clone.sunk | while | flops 62086 | bytes 69153 | solution.py:44
  429.6 1.5 fusion.59
  431.7 15.5 %convolution_bitcast_fusion.4 = f32[3072,64]{0,1:T(8,128)} fusion(f32[1536,64]{0,1:T(8,128)S(1)} %fusion.70, f32[1536,3072]{1,0:T(8,128)} %param.12), kind=kOutput, calls=%fused_computation.84 | convolution fusion | flops 3623878656 | bytes 20054016 | tf_op jit(solution)/shard_map/dot_general | solution.py:94
  448.0 94.6 %while.87 = (s32[]{:T(128)}, f32[64,64]{1,0:T(8,128)S(1)}, f32[64,64]{1,0:T(8,128)S(1)}, s32[]{:T(128)}, s32[]{:T(128)}, /*index=5*/s32[]{:T(128)}, s32[]{:T(128)}) while((s32[]{:T(128)}, f32[64,64]{1,0:T(8,128)S(1)}, f32[64,64]{1,0:T(8,128)S(1)}, s32[]{:T(128)}, s32[]{:T(128)}, /*index=5*/s32[]{:T(128)}, ...), condition=%wide.region_17.18_spmd.clone.clone, body=%wide.region_15.17_spmd.clone.clone.sunk | while | flops 62086 | bytes 69153 | solution.py:44
  542.8 2.0 fusion.71
  544.8 1.2 constant_dynamic-slice_fusion.8
  546.8 19.3 %psum.31 = f32[64,64]{1,0:T(8,128)S(1)} all-reduce(f32[64,64]{1,0:T(8,128)S(1)} %fusion.72), channel_id=1, replica_groups=mesh['row'=8,'col'=4] {'col'}, use_global_device_ids=true, to_apply=%region_18.19 | all-reduce | flops 4096 | bytes 32768 | tf_op jit(solution)/shard_map/psum | solution.py:100
  566.3 1.7 fusion.58
  568.0 60.0 %all-gather.5.cloned.1.call-done = f32[12288,64]{0,1:T(8,128)} async-done(((f32[3072,64]{0,1:T(8,128)}), f32[12288,64]{0,1:T(8,128)}) %all-gather.5.cloned.1.call-update) | async-done | bytes 3145744 | tf_op jit(solution)/shard_map/all_gather | solution.py:103
  628.0 1.0 constant_dynamic-slice_fusion.7
  629.0 21.1 %convolution_subtract_fusion = f32[1536,3072]{1,0:T(8,128)} fusion(f32[1536,3072]{1,0:T(8,128)} %param.12, f32[3072,64]{0,1:T(8,128)S(1)} %constant_dynamic-slice_fusion.8, f32[3072,64]{0,1:T(8,128)} %fusion.58, f32[1536,64]{0,1:T(8,128)S(1)} %constant_dynamic-slice_fusion.7, f32[1536,64]{0,1:T(8,128)} %copy-done), kind=kOutput, calls=%fused_computation.81 | convolution fusion | flops 7253065728 | bytes 40108032 | tf_op jit(solution)/shard_map/dot_general | solution.py:109
  (1394 shorter events, 404.7 us)
Async XLA Ops:
  7.2 535.6 %all-reduce.3.cloned.1.call-start = ((), (), s32[]{:S(2)}) async-start(), calls=%async_computation | async-start | bytes 1572864 | tf_op jit(solution)/shard_map/psum | solution.py:97
  233.5 416.6 %copy-start.1 = (f32[64,64]{1,0:T(8,128)}, f32[64,64]{1,0:T(8,128)S(1)}, u32[]{:S(2)}) copy-start(f32[64,64]{1,0:T(8,128)S(1)} %get-tuple-element.894) | copy-start | bytes 49156
  431.7 15.6 %copy-start = (f32[1536,64]{0,1:T(8,128)}, f32[1536,64]{0,1:T(8,128)S(1)}, u32[]{:S(2)}) copy-start(f32[1536,64]{0,1:T(8,128)S(1)} %fusion.70) | copy-start | bytes 1179652
  447.2 97.6 %all-gather.3.cloned.1.call-start = ((), (), s32[]{:S(2)}) async-start(), calls=%async_computation.1 | async-start | bytes 3538944 | tf_op jit(solution)/shard_map/all_gather | solution.py:90
  448.0 180.0 %all-gather.5.cloned.1.call-start = ((), (), s32[]{:S(2)}) async-start(), calls=%async_computation.2 | async-start | bytes 3932160 | tf_op jit(solution)/shard_map/all_gather | solution.py:103
Sparse Core Ops, SparseCore 0:
  447.3 55.3 all-reduce.2
  504.6 31.5 all-gather.2
  568.1 59.7 all-gather.4
where the time goes:
time: 660 us; the launch traced here: 657 us
  matrix products  245 us (37%)
  other arithmetic  228 us (35%)
  waiting for transfers between devices  60.7 us (9%)
  loops' own time  48.6 us (7%)
  blocking collectives  45.3 us (7%)
  local copies, waits for them, and re-layouts  14.7 us (2%)
  between operations  14 us (2%)
    dot_general x192, matrix products, one_row(): jnp.dot(beyond, inverse_part, precision=precise)  148 us
    reduce_sum x192, other arithmetic, one_row(): diagonal_value = jnp.sum(jnp.where(positions == row_at, upper_row, 0.0))  120 us
    all_gather x1, waiting for transfers between devices, body(): lax.all_gather(corrected_cols, 'col', axis=0, tiled=True)  60 us
    dot_general x64, matrix products, one_column(): reduced = gram_column - jnp.dot(lower_part, earlier, precision=precise)  51.2 us
    another operation x1, loops' own time, upper_cholesky(): lax.fori_loop(0, order_now, one_column, jnp.zeros((order_now, order_now),...  45 us
    mul x64, other arithmetic, one_pivot(): working = working - multipliers[:, None] * pivot_row[None, :]  41.9 us
    reduce_sum x64, other arithmetic, one_pivot(): jnp.sum(jnp.where(positions == pivot_index, pivot_column, 0.0))  38.8 us
    psum x1, blocking collectives, body(): total_inner, head_rows = lax.psum((local_inner, masked), 'row')  26.1 us
  transfers between devices with their start and end apart: 3, of which 1 were waited for; matrix products, arithmetic and copies ran while one was open for 15% of the time, Pallas kernels for 0%

commit v1 on v0

v1 whole, which is shorter than its diff:
```python
import jax
import jax.numpy as jnp
from jax import lax
from jax.experimental import pallas as pl
from jax.experimental.pallas import tpu as pltpu
from jax.sharding import PartitionSpec as P

precise = lax.Precision.HIGHEST
f32 = jnp.float32
bf16 = jnp.bfloat16


def params(mib):
    return pltpu.CompilerParams(vmem_limit_bytes=mib * 1024 * 1024)


def split(value):
    high = value.astype(bf16)
    return high, (value - high.astype(f32)).astype(bf16)


def block_of(size, wanted):
    while size % wanted:
        wanted //= 2
    return wanted


def down_kernel(kt_ref, a_ref, out_ref, acc_ref):
    step = pl.program_id(0)
    width = kt_ref.shape[0]
    kh, kl = split(kt_ref[...])
    left = jnp.concatenate([kh, kl], 0)
    columns = a_ref.shape[1]
    chunk = block_of(columns, 512)
    for c in range(0, columns, chunk):
        ah, al = split(a_ref[:, c : c + chunk])
        term = jnp.dot(left, ah, preferred_element_type=f32) + jnp.dot(
            left, al, preferred_element_type=f32
        )

        @pl.when(step == 0)
        def _():
            acc_ref[:, c : c + chunk] = term

        @pl.when(step > 0)
        def _():
            acc_ref[:, c : c + chunk] += term

    @pl.when(step == pl.num_programs(0) - 1)
    def _():
        out_ref[...] = acc_ref[:width] + acc_ref[width:]


def product_down(kt, a):
    rows, columns = a.shape
    width = kt.shape[0]
    br = block_of(rows, 256)
    return pl.pallas_call(
        down_kernel,
        grid=(rows // br,),
        in_specs=[
            pl.BlockSpec((width, br), lambda i: (0, i)),
            pl.BlockSpec((br, columns), lambda i: (i, 0)),
        ],
        out_specs=pl.BlockSpec((width, columns), lambda i: (0, 0)),
        out_shape=jax.ShapeDtypeStruct((width, columns), f32),
        scratch_shapes=[pltpu.VMEM((2 * width, columns), f32)],
        compiler_params=params(24),
        cost_estimate=pl.CostEstimate(
            flops=8 * rows * columns * width, bytes_accessed=4 * rows * columns, transcendentals=0
        ),
        name="product_down",
    )(kt, a)


def across_kernel(kt_ref, a_ref, out_ref):
    width = kt_ref.shape[0]
    columns = a_ref.shape[1]
    chunk = block_of(columns, 512)
    total = None
    for c in range(0, columns, chunk):
        kh, kl = split(kt_ref[:, c : c + chunk])
        left = jnp.concatenate([kh, kl], 0)
        ah, al = split(a_ref[:, c : c + chunk])
        dims = (((1,), (1,)), ((), ()))
        term = lax.dot_general(left, ah, dims, preferred_element_type=f32) + lax.dot_general(
            left, al, dims, preferred_element_type=f32
        )
        total = term if total is None else total + term
    out_ref[...] = total[:width] + total[width:]


def product_across(kt, a):
    rows, columns = a.shape
    width = kt.shape[0]
    br = block_of(rows, 256)
    return pl.pallas_call(
        across_kernel,
        grid=(rows // br,),
        in_specs=[
            pl.BlockSpec((width, columns), lambda i: (0, 0)),
            pl.BlockSpec((br, columns), lambda i: (i, 0)),
        ],
        out_specs=pl.BlockSpec((width, br), lambda i: (0, i)),
        out_shape=jax.ShapeDtypeStruct((width, rows), f32),
        compiler_params=params(24),
        cost_estimate=pl.CostEstimate(
            flops=8 * rows * columns * width, bytes_accessed=4 * rows * columns, transcendentals=0
        ),
        name="product_across",
    )(kt, a)


def eliminate_kernel(gram_ref, band_ref, inverse_ref):
    order = gram_ref.shape[0]
    lane = lax.broadcasted_iota(jnp.int32, (8, order), 1)
    sub = lax.broadcasted_iota(jnp.int32, (8, order), 0)
    tiles = [gram_ref[8 * t : 8 * t + 8, :] for t in range(order // 8)]
    for j in range(order):
        at, off = divmod(j, 8)
        row = jnp.broadcast_to(tiles[at][off : off + 1, :], (8, order))
        pivot = jnp.broadcast_to(row[:, j : j + 1], (8, order))
        scaled = row / pivot
        here = lane == j
        for t in range(at, order // 8):
            column = jnp.broadcast_to(tiles[t][:, j : j + 1], (8, order))
            new = jnp.where(here, -(column / pivot), tiles[t] - column * scaled)
            tiles[t] = jnp.where(sub > off, new, tiles[t]) if t == at else new
    for t in range(order // 8):
        row_at = sub + 8 * t
        diagonal = jnp.sum(jnp.where(lane == row_at, tiles[t], 0.0), axis=1, keepdims=True)
        length = jnp.sqrt(diagonal)
        scaled = tiles[t] / length
        band_ref[8 * t : 8 * t + 8, :] = jnp.where(
            lane > row_at, -scaled, jnp.where(lane == row_at, -length, 0.0)
        )
        inverse_ref[8 * t : 8 * t + 8, :] = jnp.where(
            lane < row_at, -scaled, jnp.where(lane == row_at, -1.0 / length, 0.0)
        )


def eliminate(gram):
    shape = jax.ShapeDtypeStruct(gram.shape, f32)
    return pl.pallas_call(
        eliminate_kernel,
        out_shape=(shape, shape),
        compiler_params=params(8),
        cost_estimate=pl.CostEstimate(flops=20_000_000, bytes_accessed=50_000_000, transcendentals=0),
        name="eliminate",
    )(gram)


def invert_kernel(head_ref, band_ref, inverse_ref, out_ref):
    order = head_ref.shape[0]
    lane = lax.broadcasted_iota(jnp.int32, (8, order), 1)
    sub = lax.broadcasted_iota(jnp.int32, (8, order), 0)
    tiles = [
        head_ref[8 * t : 8 * t + 8, :] - band_ref[8 * t : 8 * t + 8, :] for t in range(order // 8)
    ]
    for j in range(order):
        at, off = divmod(j, 8)
        here = lane == j
        row = jnp.broadcast_to(tiles[at][off : off + 1, :], (8, order))
        pivot = jnp.broadcast_to(row[:, j : j + 1], (8, order))
        scaled = jnp.where(here, 1.0, row) / pivot
        for t in range(order // 8):
            column = jnp.broadcast_to(tiles[t][:, j : j + 1], (8, order))
            new = jnp.where(here, 0.0, tiles[t]) - column * scaled
            tiles[t] = jnp.where(sub == off, scaled, new) if t == at else new
    block_inverse = jnp.concatenate(tiles, 0)
    out_ref[...] = -jnp.dot(
        block_inverse, inverse_ref[...], precision=precise, preferred_element_type=f32
    )


def invert(head, band, band_inverse):
    return pl.pallas_call(
        invert_kernel,
        out_shape=jax.ShapeDtypeStruct(head.shape, f32),
        compiler_params=params(8),
        cost_estimate=pl.CostEstimate(flops=20_000_000, bytes_accessed=50_000_000, transcendentals=0),
        name="invert",
    )(head, band, band_inverse)


def update_kernel(krt, xrt, kct, xct, st, cm, a_ref, out_ref, right_ref):
    width = krt.shape[0]

    def corrected(xt, kt):
        return jnp.dot(st[...], xt, precision=precise, preferred_element_type=f32) - 0.5 * jnp.dot(
            cm[...], kt, precision=precise, preferred_element_type=f32
        )

    @pl.when(pl.program_id(0) == 0)
    def _():
        columns = kct.shape[1]
        chunk = block_of(columns, 512)
        for c in range(0, columns, chunk):
            k = kct[:, c : c + chunk]
            wh, wl = split(corrected(xct[:, c : c + chunk], k))
            kh, kl = split(k)
            right_ref[:, c : c + chunk] = jnp.concatenate([wh, kh, wh, kh, wl, kl, wl, kl], 0)

    k = krt[...]
    lh, ll = split(jnp.concatenate([k, corrected(xrt[...], k)], 0).T)
    left = jnp.concatenate([lh, ll, lh, ll], 1)
    columns = a_ref.shape[1]
    chunk = block_of(columns, 512)
    for c in range(0, columns, chunk):
        out_ref[:, c : c + chunk] = a_ref[:, c : c + chunk] - jnp.dot(
            left, right_ref[:, c : c + chunk], preferred_element_type=f32
        )


def update(krt, xrt, kct, xct, st, cm, a):
    rows, columns = a.shape
    width = krt.shape[0]
    br = block_of(rows, 256)
    narrow = pl.BlockSpec((width, br), lambda i: (0, i))
    wide = pl.BlockSpec((width, columns), lambda i: (0, 0))
    small = pl.BlockSpec((width, width), lambda i: (0, 0))
    return pl.pallas_call(
        update_kernel,
        grid=(rows // br,),
        in_specs=[narrow, narrow, wide, wide, small, small, pl.BlockSpec((br, columns), lambda i: (i, 0))],
        out_specs=pl.BlockSpec((br, columns), lambda i: (i, 0)),
        out_shape=jax.ShapeDtypeStruct((rows, columns), f32),
        scratch_shapes=[pltpu.VMEM((8 * width, columns), bf16)],
        compiler_params=params(32),
        cost_estimate=pl.CostEstimate(
            flops=16 * rows * columns * width, bytes_accessed=8 * rows * columns, transcendentals=0
        ),
        name="update",
    )(krt, xrt, kct, xct, st, cm, a)


def flip(value, bit, size, axis="row"):
    return lax.ppermute(value, axis, [(i, i ^ bit) for i in range(size)])


def small_sum(value, row_size):
    if row_size != 8:
        return lax.psum(value, "row")
    value = value + flip(value, 1, row_size)
    a, b, c = flip(value, 2, row_size), flip(value, 4, row_size), flip(value, 6, row_size)
    return (value + a) + (b + c)


def big_sum(value, row_size, core):
    half = value.shape[1] // 2
    first, second = value[:, :half], value[:, half:]
    keep = jnp.where(core == 0, first, second)
    give = jnp.where(core == 0, second, first)
    keep = keep + flip(give, 1, row_size)
    quarter = half // 2
    a, b = keep[:, :quarter], keep[:, quarter:]
    bits = []
    bit = 2
    while bit < row_size:
        bits.append(bit)
        bit *= 2
    for forward, backward in zip(bits, bits[::-1]):
        a, b = a + flip(a, forward, row_size), b + flip(b, backward, row_size)
    keep = jnp.concatenate([a, b], 1)
    other = flip(keep, 1, row_size)
    return jnp.where(
        core == 0, jnp.concatenate([keep, other], 1), jnp.concatenate([other, keep], 1)
    )


def column_rows(value, row_size, col_size, row_index, col_index):
    if row_size != 2 * col_size:
        gathered = lax.all_gather(value, "row", axis=1, tiled=True)
        size = gathered.shape[1] // col_size
        return lax.dynamic_slice_in_dim(gathered, col_index * size, size, 1)

    def send(piece, source_flips, bit):
        pairs = []
        for c in range(col_size):
            for source in source_flips:
                for core in range(2):
                    at = (2 * c + core) ^ source
                    pairs.append((at * col_size + c, (at ^ bit) * col_size + c))
        return lax.ppermute(piece, ("row", "col"), pairs)

    core = row_index % 2
    relation = (row_index // 2) ^ col_index
    held = jnp.where(relation == 0, value, 0.0)
    if row_size == 8:
        by_x, by_y = send(held, [0], 2), send(held, [0], 4)
        held = held + by_x + by_y
        half = value.shape[1] // 2
        far_x = send(held[:, :half], [2], 4)
        far_y = send(held[:, half:], [4], 2)
        held = held + jnp.concatenate([far_x, far_y], 1)
    else:
        reached = [0]
        bit = 2
        while bit < row_size:
            held = held + send(held, reached, bit)
            reached = reached + [r ^ bit for r in reached]
            bit *= 2
    other = flip(held, 1, row_size)
    return jnp.where(
        core == 0, jnp.concatenate([held, other], 1), jnp.concatenate([other, held], 1)
    )


def line_sum(value, col_size, col_index):
    if col_size != 4:
        return lax.psum(value, "col")
    size = value.shape[1] // col_size

    def shift(piece, by):
        return lax.ppermute(piece, "col", [(i, (i + by) % col_size) for i in range(col_size)])

    def part(index):
        return lax.dynamic_slice_in_dim(value, (index % col_size) * size, size, 1)

    mine = part(col_index)
    for by in (2, 1, 3):
        mine = mine + shift(part(col_index + by), by)
    total = jnp.zeros_like(value)
    total = lax.dynamic_update_slice_in_dim(total, mine, col_index * size, 1)
    for by in (2, 1, 3):
        got = shift(mine, by)
        start = ((col_index - by) % col_size) * size
        total = lax.dynamic_update_slice_in_dim(total, got, start, 1)
    return total


def small_line_sum(value, col_size):
    bit = 1
    while bit < col_size:
        value = value + flip(value, bit, col_size, "col")
        bit *= 2
    return value


def body_of(row_size, col_size):
    def body(matrix, panel):
        width = panel.shape[1]
        row_index = lax.axis_index("row")
        col_index = lax.axis_index("col")
        core = row_index % 2
        panel_t = panel.T
        local = jnp.dot(panel_t, panel, precision=precise)
        head = jnp.where(row_index == 0, panel[:width], 0.0)
        summed = small_sum(jnp.concatenate([local, head], 1), row_size)
        gram, head = summed[:, :width], summed[:, width:]
        panel_cols = column_rows(panel_t, row_size, col_size, row_index, col_index)
        down = product_down(panel_t, matrix)
        band, band_inverse = eliminate(gram)
        top_row = jnp.where(row_index == 0, band.T, 0.0)
        top_col = jnp.where(col_index == 0, band.T, 0.0)
        down = down - jnp.dot(top_row, matrix[:width], precision=precise)
        krt = panel_t.at[:, :width].add(-top_row)
        kct = panel_cols.at[:, :width].add(-top_col)
        across = product_across(kct, matrix)
        xct = big_sum(down, row_size, core)
        xrt = line_sum(across, col_size, col_index)
        st = invert(head, band, band_inverse)
        inner = lax.dot_general(kct, xct, (((1,), (1,)), ((), ())), precision=precise)
        inner = small_line_sum(inner, col_size)
        cm = jnp.dot(jnp.dot(st, inner, precision=precise), st.T, precision=precise)
        updated = update(krt, xrt, kct, xct, st, cm, matrix)
        return updated, band

    return body


def solution(mesh):
    return jax.shard_map(
        body_of(mesh.shape["row"], mesh.shape["col"]),
        mesh=mesh,
        in_specs=(P("row", "col"), P("row", None)),
        out_specs=(P("row", "col"), P()),
        check_vma=False,
    )
```

time: 660 us -> 131 us (0.20)
  matrix products: 245 us -> 3.49 us
  other arithmetic: 228 us -> 2.55 us
  loops' own time: 48.6 us -> 0 us
  Pallas kernels: 0 us -> 46.2 us
  blocking collectives: 45.3 us -> 0 us
  waiting for transfers between devices: 60.7 us -> 24.8 us
  starting transfers between devices: 0.12 us -> 29.8 us
  between operations: 14 us -> 1.06 us
  local copies, waits for them, and re-layouts: 14.7 us -> 22.2 us
    dot_general x267 -> x5, matrix products: 245 us -> 3.49 us  [the longest x1 1.91 us: body(): down = down - jnp.dot(top_row, matrix[:width], precision=precise)]
    reduce_sum x256 -> x0, other arithmetic: 159 us -> none  [the longest x192 120 us: one_row(): diagonal_value = jnp.sum(jnp.where(positions == row_at, upper_row, 0.0))]
    all_gather x2 -> x0, waiting for transfers between devices: 60 us -> none  [the longest x1 60 us: body(): lax.all_gather(corrected_cols, 'col', axis=0, tiled=True)]
    another operation x5 -> x0, loops' own time: 48.6 us -> none  [the longest x1 45 us: upper_cholesky(): lax.fori_loop(0, order_now, one_column, jnp.zeros((order_now, order_now),...]
    pallas_call x0 -> x5, Pallas kernels: none -> 46.2 us  [the longest x1 11.5 us: update(): pl.pallas_call(update_kernel, grid=(rows // br,), in_specs=[narrow, narro...]
    psum x2 -> x0, blocking collectives: 45.3 us -> none  [the longest x1 26.1 us: body(): total_inner, head_rows = lax.psum((local_inner, masked), 'row')]
    mul x64 -> x0, other arithmetic: 41.9 us -> none  [one_pivot(): working = working - multipliers[:, None] * pivot_row[None, :]]
    ppermute x0 -> x23, starting transfers between devices: none -> 29.8 us  [the longest x13 12.1 us: flip(): return lax.ppermute(value, axis, [(i, i ^ bit) for i in range(size)])]
  transfers between devices with their start and end apart: 3 -> 23, of which waited for: 1 -> 10; matrix products, arithmetic and copies ran while one was open for 15% -> 4% of each run, Pallas kernels for 0% -> 21%
where the time goes in v1:
time: 131 us; the launch traced here: 130 us
  Pallas kernels  46.2 us (35%)
  starting transfers between devices  29.8 us (23%)
  waiting for transfers between devices  24.8 us (19%)
  local copies, waits for them, and re-layouts  22.2 us (17%)
  matrix products  3.49 us (3%)
  other arithmetic  2.55 us (2%)
    unnamed x9, local copies, waits for them, and re-layouts  20.1 us
    ppermute x13, waiting for transfers between devices, flip(): return lax.ppermute(value, axis, [(i, i ^ bit) for i in range(size)])  16.7 us
    ppermute x13, starting transfers between devices, flip(): return lax.ppermute(value, axis, [(i, i ^ bit) for i in range(size)])  12.1 us
    pallas_call x1, Pallas kernels, update(): pl.pallas_call(update_kernel, grid=(rows // br,), in_specs=[narrow, narro...  11.5 us
    ppermute x6, starting transfers between devices, shift(): lax.ppermute(piece, 'col', [(i, (i + by) % col_size) for i in range(col_s...  10.6 us
    pallas_call x1, Pallas kernels, product_down(): pl.pallas_call(down_kernel, grid=(rows // br,), in_specs=[pl.BlockSpec((w...  10 us
    pallas_call x1, Pallas kernels, eliminate(): pl.pallas_call(eliminate_kernel, out_shape=(shape, shape), compiler_param...  9 us
    pallas_call x1, Pallas kernels, invert(): pl.pallas_call(invert_kernel, out_shape=jax.ShapeDtypeStruct(head.shape,...  8.65 us
  transfers between devices with their start and end apart: 23, of which 10 were waited for; matrix products, arithmetic and copies ran while one was open for 4% of the time, Pallas kernels for 21%

profile of v1, /device:TPU:0, one launch (start us, length us, event | category | flops | bytes accessed | tf_op | source)
XLA Modules:
  0.0 130.1 jit_solution(3405314333689696918)
XLA Ops:
  0.6 1.0 copy.17
  1.6 0.5 fusion.11
  2.1 0.6 collective-permute-start
  2.7 4.5 %collective-permute-start.5 = (f32[64,1536]{1,0:T(8,128)S(1)}, f32[64,1536]{1,0:T(8,128)S(1)}, u32[]{:S(2)}, u32[]{:S(2)}) collective-permute-start(f32[64,1536]{1,0:T(8,128)S(1)} %broadcast_select_fusion), channel_id=1, source_target_pairs={{0,16},{4,20},{9,25},{13,29},{18,2},{22,6},{27,11},{31,15}} | collective-permute-start | bytes 1179656 | tf_op jit(solution)/shard_map/ppermute | solution.py:284
  7.2 1.3 %collective-permute-start.4 = (f32[64,1536]{1,0:T(8,128)S(1)}, f32[64,1536]{1,0:T(8,128)S(1)}, u32[]{:S(2)}, u32[]{:S(2)}) collective-permute-start(f32[64,1536]{1,0:T(8,128)S(1)} %broadcast_select_fusion), channel_id=1, source_target_pairs={{0,8},{4,12},{9,1},{13,5},{18,26},{22,30},{27,19},{31,23}} | collective-permute-start | bytes 1179656 | tf_op jit(solution)/shard_map/ppermute | solution.py:284
  8.5 0.0 collective-permute-done
  8.6 0.1 collective-permute-start.3
  8.6 0.2 collective-permute-start.2
  8.8 3.3 %collective-permute-start.1 = (f32[64,128]{0,1:T(8,128)S(1)}, f32[64,128]{0,1:T(8,128)S(1)}, u32[]{:S(2)}, u32[]{:S(2)}) collective-permute-start(f32[64,128]{0,1:T(8,128)S(1)} %fusion.7), channel_id=1, source_target_pairs={{0,8},{4,12},{8,0},{12,4},{16,24},{20,28},{24,16},{28,20},{1,9},{5... | collective-permute-start | bytes 98312 | tf_op jit(solution)/shard_map/ppermute | solution.py:238
  12.1 6.4 %copy-done = f32[1536,3072]{1,0:T(8,128)S(1)} copy-done((f32[1536,3072]{1,0:T(8,128)S(1)}, f32[1536,3072]{1,0:T(8,128)}, u32[]{:S(2)}) %copy-start) | copy-done | bytes 18874392
  18.5 10.0 %product_down.1 = f32[64,3072]{1,0:T(8,128)S(1)} custom-call(f32[64,1536]{1,0:T(8,128)S(1)} %bitcast.17, f32[1536,3072]{1,0:T(8,128)S(1)} %copy-done), custom_call_target="tpu_custom_call" | custom-call | flops 2415919104 | bytes 18874368 | tf_op jit(solution)/shard_map/product_down/pallas_call | solution.py:58
  28.5 0.0 collective-permute-done.3
  28.6 0.0 collective-permute-done.1
  28.6 0.1 copy.5.gram_ref
  28.7 9.0 %eliminate.1 = (f32[64,64]{1,0:T(8,128)}, f32[64,64]{1,0:T(8,128)S(1)}) custom-call(f32[64,64]{1,0:T(8,128)S(1)} %copy.5.gram_ref), custom_call_target="tpu_custom_call" | custom-call | flops 20000000 | bytes 50000000 | tf_op jit(solution)/shard_map/eliminate/pallas_call | solution.py:144
  37.7 0.9 copy.6
  38.6 1.9 %convolution_subtract_fusion = f32[64,3072]{1,0:T(8,128)S(1)} fusion(f32[64,3072]{1,0:T(8,128)S(1)} %product_down.1, f32[1536,3072]{1,0:T(8,128)} %a_ref.5, f32[64,64]{0,1:T(8,128)S(1)} %copy.6, pred[]{:T(512)S(6)} %eq.26), kind=kOutput, calls=%fused_computation | convolution fusion | flops 151195648 | bytes 2375681 | tf_op jit(solution)/shard_map/dot_general | solution.py:356
  40.6 0.1 collective-permute-start.15
  40.6 0.0 collective-permute-done.5
  40.7 0.1 add_add_fusion
  40.8 0.7 collective-permute-start.6
  41.4 0.7 collective-permute-start.7
  42.1 0.2 collective-permute-done.15
  42.3 0.1 select_add_fusion
  42.5 1.7 %collective-permute-start.16 = (f32[64,768]{1,0:T(8,128)S(1)}, f32[64,768]{1,0:T(8,128)S(1)}, u32[]{:S(2)}, u32[]{:S(2)}) collective-permute-start(f32[64,768]{1,0:T(8,128)S(1)} %get-tuple-element.34), channel_id=1, source_target_pairs={{0,8},{4,12},{8,0},{12,4},{16,24},{20,28},{24,16},{28,20},{1,9},{5... | collective-permute-start | bytes 589832 | tf_op jit(solution)/shard_map/ppermute | solution.py:238
  44.2 0.7 collective-permute-start.18
  44.9 0.1 maximum_add_fusion
  45.0 0.1 collective-permute-start.8
  45.0 4.6 %collective-permute-done.16 = f32[64,768]{1,0:T(8,128)S(1)} collective-permute-done((f32[64,768]{1,0:T(8,128)S(1)}, f32[64,768]{1,0:T(8,128)S(1)}, u32[]{:S(2)}, u32[]{:S(2)}) %collective-permute-start.16) | collective-permute-done | bytes 196640 | tf_op jit(solution)/shard_map/ppermute | solution.py:238
  49.6 1.3 %collective-permute-done.18 = f32[64,768]{1,0:T(8,128)S(1)} collective-permute-done((f32[64,768]{1,0:T(8,128)S(1)}, f32[64,768]{1,0:T(8,128)S(1)}, u32[]{:S(2)}, u32[]{:S(2)}) %collective-permute-start.18) | collective-permute-done | bytes 196640 | tf_op jit(solution)/shard_map/ppermute | solution.py:238
  51.0 2.8 %collective-permute-start.17 = (f32[64,768]{1,0:T(8,128)S(1)}, f32[64,768]{1,0:T(8,128)S(1)}, u32[]{:S(2)}, u32[]{:S(2)}) collective-permute-start(f32[64,768]{1,0:T(8,128)S(1)} %get-tuple-element.32), channel_id=1, source_target_pairs={{0,16},{4,20},{8,24},{12,28},{16,0},{20,4},{24,8},{28,12},{1,17},{... | collective-permute-start | bytes 589832 | tf_op jit(solution)/shard_map/ppermute | solution.py:238
  53.7 2.5 %collective-permute-start.19 = (f32[64,768]{1,0:T(8,128)S(1)}, f32[64,768]{1,0:T(8,128)S(1)}, u32[]{:S(2)}, u32[]{:S(2)}) collective-permute-start(f32[64,768]{1,0:T(8,128)S(1)} %get-tuple-element.33), channel_id=1, source_target_pairs={{0,8},{4,12},{8,0},{12,4},{16,24},{20,28},{24,16},{28,20},{1,9},{5... | collective-permute-start | bytes 589832 | tf_op jit(solution)/shard_map/ppermute | solution.py:238
  56.2 0.7 compare_reduce_fusion
  56.9 1.5 %collective-permute-done.17 = f32[64,768]{1,0:T(8,128)S(1)} collective-permute-done((f32[64,768]{1,0:T(8,128)S(1)}, f32[64,768]{1,0:T(8,128)S(1)}, u32[]{:S(2)}, u32[]{:S(2)}) %collective-permute-start.17) | collective-permute-done | bytes 196640 | tf_op jit(solution)/shard_map/ppermute | solution.py:238
  58.4 2.2 %collective-permute-done.19 = f32[64,768]{1,0:T(8,128)S(1)} collective-permute-done((f32[64,768]{1,0:T(8,128)S(1)}, f32[64,768]{1,0:T(8,128)S(1)}, u32[]{:S(2)}, u32[]{:S(2)}) %collective-permute-start.19) | collective-permute-done | bytes 196640 | tf_op jit(solution)/shard_map/ppermute | solution.py:238
  60.6 0.0 collective-permute-done.8
  60.7 0.1 maximum_select_fusion
  60.7 1.3 add_select_fusion
  62.0 0.4 scatter-add.9.kt_ref.kct
  62.5 0.0 copy-start.1
  62.5 6.4 %copy-done.1 = f32[1536,3072]{1,0:T(8,128)S(1)} copy-done((f32[1536,3072]{1,0:T(8,128)S(1)}, f32[1536,3072]{1,0:T(8,128)}, u32[]{:S(2)}) %copy-start.1) | copy-done | bytes 18874392
  68.8 7.0 %product_across.1 = f32[64,1536]{1,0:T(8,128)S(1)} custom-call(f32[64,3072]{1,0:T(8,128)S(1)} %scatter-add.9.kt_ref.kct, f32[1536,3072]{1,0:T(8,128)S(1)} %copy-done.1), custom_call_target="tpu_custom_call" | custom-call | flops 2415919104 | bytes 18874368 | tf_op jit(solution)/shard_map/product_across/pallas_call | solution.py:97
  75.9 1.9 %collective-permute-start.9 = (f32[64,384]{1,0:T(8,128)S(1)}, f32[64,384]{1,0:T(8,128)S(1)}, u32[]{:S(2)}, u32[]{:S(2)}) collective-permute-start(f32[64,384]{1,0:T(8,128)S(1)} %get-tuple-element.36), channel_id=1, source_target_pairs={{0,2},{1,3},{2,0},{3,1},{4,6},{5,7},{6,4},{7,5},{8,10},{9,11},{10,... | collective-permute-start | bytes 294920 | tf_op jit(solution)/shard_map/ppermute | solution.py:315
  77.8 3.4 %collective-permute-start.11 = (f32[64,384]{1,0:T(8,128)S(1)}, f32[64,384]{1,0:T(8,128)S(1)}, u32[]{:S(2)}, u32[]{:S(2)}) collective-permute-start(f32[64,384]{1,0:T(8,128)S(1)} %get-tuple-element.37), channel_id=1, source_target_pairs={{0,3},{1,0},{2,1},{3,2},{4,7},{5,4},{6,5},{7,6},{8,11},{9,8},{10,9... | collective-permute-start | bytes 294920 | tf_op jit(solution)/shard_map/ppermute | solution.py:315
  81.2 0.1 collective-permute-start.20
  81.2 4.0 %collective-permute-done.9 = f32[64,384]{1,0:T(8,128)S(1)} collective-permute-done((f32[64,384]{1,0:T(8,128)S(1)}, f32[64,384]{1,0:T(8,128)S(1)}, u32[]{:S(2)}, u32[]{:S(2)}) %collective-permute-start.9) | collective-permute-done | bytes 98336 | tf_op jit(solution)/shard_map/ppermute | solution.py:315
  85.3 2.3 %collective-permute-done.10 = f32[64,384]{1,0:T(8,128)S(1)} collective-permute-done((f32[64,384]{1,0:T(8,128)S(1)}, f32[64,384]{1,0:T(8,128)S(1)}, u32[]{:S(2)}, u32[]{:S(2)}) %collective-permute-start.10) | collective-permute-done | bytes 98336 | tf_op jit(solution)/shard_map/ppermute | solution.py:315
  87.6 1.5 %collective-permute-start.12 = (f32[64,384]{1,0:T(8,128)S(1)}, f32[64,384]{1,0:T(8,128)S(1)}, u32[]{:S(2)}, u32[]{:S(2)}) collective-permute-start(f32[64,384]{1,0:T(8,128)S(1)} %get-tuple-element.31), channel_id=1, source_target_pairs={{0,2},{1,3},{2,0},{3,1},{4,6},{5,7},{6,4},{7,5},{8,10},{9,11},{10,... | collective-permute-start | bytes 294920 | tf_op jit(solution)/shard_map/ppermute | solution.py:315
  89.1 0.1 copy.8.head_ref
  89.2 8.7 %invert.1.st = f32[64,64]{1,0:T(8,128)S(1)} custom-call(f32[64,64]{1,0:T(8,128)S(1)} %copy.8.head_ref, f32[64,64]{1,0:T(8,128)S(1)} %copy-done.3, f32[64,64]{1,0:T(8,128)S(1)} %get-tuple-element.29.inverse_ref), custom_call_target="tpu_custom_call" | custom-call | flops 20000000 | bytes 50000000 | tf_op jit(solution)/shard_map/invert/pallas_call | solution.py:177
  97.9 0.4 scatter-add.6.krt
  98.3 0.2 collective-permute-start.13
  98.5 3.7 %collective-permute-start.14 = (f32[64,384]{1,0:T(8,128)S(1)}, f32[64,384]{1,0:T(8,128)S(1)}, u32[]{:S(2)}, u32[]{:S(2)}) collective-permute-start(f32[64,384]{1,0:T(8,128)S(1)} %get-tuple-element.31), channel_id=1, source_target_pairs={{0,3},{1,0},{2,1},{3,2},{4,7},{5,4},{6,5},{7,6},{8,11},{9,8},{10,9... | collective-permute-start | bytes 294920 | tf_op jit(solution)/shard_map/ppermute | solution.py:315
  102.2 0.1 maximum_select_fusion.1.xct
  102.3 0.8 fusion.12
  103.1 0.1 collective-permute-start.21
  103.2 1.8 %collective-permute-done.13 = f32[64,384]{1,0:T(8,128)S(1)} collective-permute-done((f32[64,384]{1,0:T(8,128)S(1)}, f32[64,384]{1,0:T(8,128)S(1)}, u32[]{:S(2)}, u32[]{:S(2)}) %collective-permute-start.13) | collective-permute-done | bytes 98336 | tf_op jit(solution)/shard_map/ppermute | solution.py:315
  105.0 2.1 %collective-permute-done.21 = f32[64,64]{1,0:T(8,128)S(1)} collective-permute-done((f32[64,64]{1,0:T(8,128)S(1)}, f32[64,64]{1,0:T(8,128)S(1)}, u32[]{:S(2)}, u32[]{:S(2)}) %collective-permute-start.21) | collective-permute-done | bytes 16416 | tf_op jit(solution)/shard_map/ppermute | solution.py:238
  107.1 4.8 %collective-permute-done.22 = f32[64,64]{1,0:T(8,128)S(1)} collective-permute-done((f32[64,64]{1,0:T(8,128)S(1)}, f32[64,64]{1,0:T(8,128)S(1)}, u32[]{:S(2)}, u32[]{:S(2)}) %collective-permute-start.22) | collective-permute-done | bytes 16416 | tf_op jit(solution)/shard_map/ppermute | solution.py:238
  111.9 0.2 fusion.1
  112.1 0.2 fusion.13.cm
  112.3 0.0 copy-start.2
  112.3 6.4 %copy-done.2 = f32[1536,3072]{1,0:T(8,128)S(1)} copy-done((f32[1536,3072]{1,0:T(8,128)S(1)}, f32[1536,3072]{1,0:T(8,128)}, u32[]{:S(2)}) %copy-start.2) | copy-done | bytes 18874392
  118.6 11.5 %update.1 = f32[1536,3072]{1,0:T(8,128)} custom-call(f32[64,1536]{1,0:T(8,128)S(1)} %scatter-add.6.krt, f32[64,1536]{1,0:T(8,128)S(1)} %constant_dynamic-update-slice_fusion.xrt, f32[64,3072]{1,0:T(8,128)S(1)} %scatter-add.9.kt_ref.kct, f32[64,3072]{1,0:T(8,128)S(1)} %maximum_select_fusion.1.xct, f32[64,64]{1,0:T(8,128)S(1)} %invert.1.st, ...), custom_call_target="tpu_custom_call" | custom-call | flops 4831838208 | bytes 37748736 | tf_op jit(solution)/shard_map/update/pallas_call | solution.py:222
  (33 shorter events, 0.5 us)
Async XLA Ops:
  2.1 6.4 %collective-permute-start = (f32[64,128]{0,1:T(8,128)S(1)}, f32[64,128]{0,1:T(8,128)S(1)}, u32[]{:S(2)}, u32[]{:S(2)}) collective-permute-start(f32[64,128]{0,1:T(8,128)S(1)} %pad_maximum_fusion.1), channel_id=1, source_target_pairs={{0,4},{4,0},{8,12},{12,8},{16,20},{20,16},{24,28},{28,24},{1,5},{5... | collective-permute-start | bytes 98312 | tf_op jit(solution)/shard_map/ppermute | solution.py:238
  2.7 37.9 %collective-permute-start.5 = (f32[64,1536]{1,0:T(8,128)S(1)}, f32[64,1536]{1,0:T(8,128)S(1)}, u32[]{:S(2)}, u32[]{:S(2)}) collective-permute-start(f32[64,1536]{1,0:T(8,128)S(1)} %broadcast_select_fusion), channel_id=1, source_target_pairs={{0,16},{4,20},{9,25},{13,29},{18,2},{22,6},{27,11},{31,15}} | collective-permute-start | bytes 1179656 | tf_op jit(solution)/shard_map/ppermute | solution.py:284
  7.2 33.5 %collective-permute-start.4 = (f32[64,1536]{1,0:T(8,128)S(1)}, f32[64,1536]{1,0:T(8,128)S(1)}, u32[]{:S(2)}, u32[]{:S(2)}) collective-permute-start(f32[64,1536]{1,0:T(8,128)S(1)} %broadcast_select_fusion), channel_id=1, source_target_pairs={{0,8},{4,12},{9,1},{13,5},{18,26},{22,30},{27,19},{31,23}} | collective-permute-start | bytes 1179656 | tf_op jit(solution)/shard_map/ppermute | solution.py:284
  8.6 20.0 %collective-permute-start.3 = (f32[64,128]{0,1:T(8,128)S(1)}, f32[64,128]{0,1:T(8,128)S(1)}, u32[]{:S(2)}, u32[]{:S(2)}) collective-permute-start(f32[64,128]{0,1:T(8,128)S(1)} %fusion.7), channel_id=1, source_target_pairs={{0,24},{4,28},{8,16},{12,20},{16,8},{20,12},{24,0},{28,4},{1,25},{... | collective-permute-start | bytes 98312 | tf_op jit(solution)/shard_map/ppermute | solution.py:238
  8.6 19.9 %collective-permute-start.2 = (f32[64,128]{0,1:T(8,128)S(1)}, f32[64,128]{0,1:T(8,128)S(1)}, u32[]{:S(2)}, u32[]{:S(2)}) collective-permute-start(f32[64,128]{0,1:T(8,128)S(1)} %fusion.7), channel_id=1, source_target_pairs={{0,16},{4,20},{8,24},{12,28},{16,0},{20,4},{24,8},{28,12},{1,17},{... | collective-permute-start | bytes 98312 | tf_op jit(solution)/shard_map/ppermute | solution.py:238
  8.8 19.8 %collective-permute-start.1 = (f32[64,128]{0,1:T(8,128)S(1)}, f32[64,128]{0,1:T(8,128)S(1)}, u32[]{:S(2)}, u32[]{:S(2)}) collective-permute-start(f32[64,128]{0,1:T(8,128)S(1)} %fusion.7), channel_id=1, source_target_pairs={{0,8},{4,12},{8,0},{12,4},{16,24},{20,28},{24,16},{28,20},{1,9},{5... | collective-permute-start | bytes 98312 | tf_op jit(solution)/shard_map/ppermute | solution.py:238
  12.1 6.4 %copy-start = (f32[1536,3072]{1,0:T(8,128)S(1)}, f32[1536,3072]{1,0:T(8,128)}, u32[]{:S(2)}) copy-start(f32[1536,3072]{1,0:T(8,128)} %a_ref.5) | copy-start | bytes 56623108
  37.7 51.5 %copy-start.3 = (f32[64,64]{1,0:T(8,128)S(1)}, f32[64,64]{1,0:T(8,128)}, u32[]{:S(2)}) copy-start(f32[64,64]{1,0:T(8,128)} %get-tuple-element.27.band_ref) | copy-start | bytes 49156
  40.6 1.8 %collective-permute-start.15 = (f32[64,1536]{1,0:T(8,128)S(1)}, f32[64,1536]{1,0:T(8,128)S(1)}, u32[]{:S(2)}, u32[]{:S(2)}) collective-permute-start(f32[64,1536]{1,0:T(8,128)S(1)} %slice_select_fusion), channel_id=1, source_target_pairs={{0,4},{4,0},{8,12},{12,8},{16,20},{20,16},{24,28},{28,24},{1,5},{5... | collective-permute-start | bytes 1179656 | tf_op jit(solution)/shard_map/ppermute | solution.py:238
  40.8 4.1 %collective-permute-start.6 = (f32[64,768]{1,0:T(8,128)S(1)}, f32[64,768]{1,0:T(8,128)S(1)}, u32[]{:S(2)}, u32[]{:S(2)}) collective-permute-start(f32[64,768]{1,0:T(8,128)S(1)} %get-tuple-element.39), channel_id=1, source_target_pairs={{8,24},{12,28},{1,17},{5,21},{26,10},{30,14},{19,3},{23,7}} | collective-permute-start | bytes 589832 | tf_op jit(solution)/shard_map/ppermute | solution.py:284
  41.4 3.5 %collective-permute-start.7 = (f32[64,768]{1,0:T(8,128)S(1)}, f32[64,768]{1,0:T(8,128)S(1)}, u32[]{:S(2)}, u32[]{:S(2)}) collective-permute-start(f32[64,768]{1,0:T(8,128)S(1)} %get-tuple-element.40), channel_id=1, source_target_pairs={{16,24},{20,28},{25,17},{29,21},{2,10},{6,14},{11,3},{15,7}} | collective-permute-start | bytes 589832 | tf_op jit(solution)/shard_map/ppermute | solution.py:284
  42.5 7.1 %collective-permute-start.16 = (f32[64,768]{1,0:T(8,128)S(1)}, f32[64,768]{1,0:T(8,128)S(1)}, u32[]{:S(2)}, u32[]{:S(2)}) collective-permute-start(f32[64,768]{1,0:T(8,128)S(1)} %get-tuple-element.34), channel_id=1, source_target_pairs={{0,8},{4,12},{8,0},{12,4},{16,24},{20,28},{24,16},{28,20},{1,9},{5... | collective-permute-start | bytes 589832 | tf_op jit(solution)/shard_map/ppermute | solution.py:238
  44.2 6.7 %collective-permute-start.18 = (f32[64,768]{1,0:T(8,128)S(1)}, f32[64,768]{1,0:T(8,128)S(1)}, u32[]{:S(2)}, u32[]{:S(2)}) collective-permute-start(f32[64,768]{1,0:T(8,128)S(1)} %get-tuple-element.35), channel_id=1, source_target_pairs={{0,16},{4,20},{8,24},{12,28},{16,0},{20,4},{24,8},{28,12},{1,17},{... | collective-permute-start | bytes 589832 | tf_op jit(solution)/shard_map/ppermute | solution.py:238
  45.0 15.7 %collective-permute-start.8 = (f32[64,1536]{1,0:T(8,128)S(1)}, f32[64,1536]{1,0:T(8,128)S(1)}, u32[]{:S(2)}, u32[]{:S(2)}) collective-permute-start(f32[64,1536]{1,0:T(8,128)S(1)} %maximum_add_fusion), channel_id=1, source_target_pairs={{0,4},{4,0},{8,12},{12,8},{16,20},{20,16},{24,28},{28,24},{1,5},{5... | collective-permute-start | bytes 1179656 | tf_op jit(solution)/shard_map/ppermute | solution.py:238
  51.0 7.4 %collective-permute-start.17 = (f32[64,768]{1,0:T(8,128)S(1)}, f32[64,768]{1,0:T(8,128)S(1)}, u32[]{:S(2)}, u32[]{:S(2)}) collective-permute-start(f32[64,768]{1,0:T(8,128)S(1)} %get-tuple-element.32), channel_id=1, source_target_pairs={{0,16},{4,20},{8,24},{12,28},{16,0},{20,4},{24,8},{28,12},{1,17},{... | collective-permute-start | bytes 589832 | tf_op jit(solution)/shard_map/ppermute | solution.py:238
  53.7 6.9 %collective-permute-start.19 = (f32[64,768]{1,0:T(8,128)S(1)}, f32[64,768]{1,0:T(8,128)S(1)}, u32[]{:S(2)}, u32[]{:S(2)}) collective-permute-start(f32[64,768]{1,0:T(8,128)S(1)} %get-tuple-element.33), channel_id=1, source_target_pairs={{0,8},{4,12},{8,0},{12,4},{16,24},{20,28},{24,16},{28,20},{1,9},{5... | collective-permute-start | bytes 589832 | tf_op jit(solution)/shard_map/ppermute | solution.py:238
  62.5 6.4 %copy-start.1 = (f32[1536,3072]{1,0:T(8,128)S(1)}, f32[1536,3072]{1,0:T(8,128)}, u32[]{:S(2)}) copy-start(f32[1536,3072]{1,0:T(8,128)} %a_ref.5) | copy-start | bytes 56623108
  75.9 9.3 %collective-permute-start.9 = (f32[64,384]{1,0:T(8,128)S(1)}, f32[64,384]{1,0:T(8,128)S(1)}, u32[]{:S(2)}, u32[]{:S(2)}) collective-permute-start(f32[64,384]{1,0:T(8,128)S(1)} %get-tuple-element.36), channel_id=1, source_target_pairs={{0,2},{1,3},{2,0},{3,1},{4,6},{5,7},{6,4},{7,5},{8,10},{9,11},{10,... | collective-permute-start | bytes 294920 | tf_op jit(solution)/shard_map/ppermute | solution.py:315
  77.8 7.5 %collective-permute-start.11 = (f32[64,384]{1,0:T(8,128)S(1)}, f32[64,384]{1,0:T(8,128)S(1)}, u32[]{:S(2)}, u32[]{:S(2)}) collective-permute-start(f32[64,384]{1,0:T(8,128)S(1)} %get-tuple-element.37), channel_id=1, source_target_pairs={{0,3},{1,0},{2,1},{3,2},{4,7},{5,4},{6,5},{7,6},{8,11},{9,8},{10,9... | collective-permute-start | bytes 294920 | tf_op jit(solution)/shard_map/ppermute | solution.py:315
  81.1 6.4 %collective-permute-start.10 = (f32[64,384]{1,0:T(8,128)S(1)}, f32[64,384]{1,0:T(8,128)S(1)}, u32[]{:S(2)}, u32[]{:S(2)}) collective-permute-start(f32[64,384]{1,0:T(8,128)S(1)} %get-tuple-element.38), channel_id=1, source_target_pairs={{0,1},{1,2},{2,3},{3,0},{4,5},{5,6},{6,7},{7,4},{8,9},{9,10},{10,1... | collective-permute-start | bytes 294920 | tf_op jit(solution)/shard_map/ppermute | solution.py:315
  81.2 21.1 %collective-permute-start.20 = (f32[64,1536]{1,0:T(8,128)S(1)}, f32[64,1536]{1,0:T(8,128)S(1)}, u32[]{:S(2)}, u32[]{:S(2)}) collective-permute-start(f32[64,1536]{1,0:T(8,128)S(1)} %pad_maximum_fusion), channel_id=1, source_target_pairs={{0,4},{4,0},{8,12},{12,8},{16,20},{20,16},{24,28},{28,24},{1,5},{5... | collective-permute-start | bytes 1179656 | tf_op jit(solution)/shard_map/ppermute | solution.py:238
  87.6 14.6 %collective-permute-start.12 = (f32[64,384]{1,0:T(8,128)S(1)}, f32[64,384]{1,0:T(8,128)S(1)}, u32[]{:S(2)}, u32[]{:S(2)}) collective-permute-start(f32[64,384]{1,0:T(8,128)S(1)} %get-tuple-element.31), channel_id=1, source_target_pairs={{0,2},{1,3},{2,0},{3,1},{4,6},{5,7},{6,4},{7,5},{8,10},{9,11},{10,... | collective-permute-start | bytes 294920 | tf_op jit(solution)/shard_map/ppermute | solution.py:315
  98.3 6.6 %collective-permute-start.13 = (f32[64,384]{1,0:T(8,128)S(1)}, f32[64,384]{1,0:T(8,128)S(1)}, u32[]{:S(2)}, u32[]{:S(2)}) collective-permute-start(f32[64,384]{1,0:T(8,128)S(1)} %get-tuple-element.31), channel_id=1, source_target_pairs={{0,1},{1,2},{2,3},{3,0},{4,5},{5,6},{6,7},{7,4},{8,9},{9,10},{10,1... | collective-permute-start | bytes 294920 | tf_op jit(solution)/shard_map/ppermute | solution.py:315
  98.5 8.6 %collective-permute-start.14 = (f32[64,384]{1,0:T(8,128)S(1)}, f32[64,384]{1,0:T(8,128)S(1)}, u32[]{:S(2)}, u32[]{:S(2)}) collective-permute-start(f32[64,384]{1,0:T(8,128)S(1)} %get-tuple-element.31), channel_id=1, source_target_pairs={{0,3},{1,0},{2,1},{3,2},{4,7},{5,4},{6,5},{7,6},{8,11},{9,8},{10,9... | collective-permute-start | bytes 294920 | tf_op jit(solution)/shard_map/ppermute | solution.py:315
  103.1 4.0 %collective-permute-start.21 = (f32[64,64]{1,0:T(8,128)S(1)}, f32[64,64]{1,0:T(8,128)S(1)}, u32[]{:S(2)}, u32[]{:S(2)}) collective-permute-start(f32[64,64]{1,0:T(8,128)S(1)} %fusion.12), channel_id=1, source_target_pairs={{0,1},{1,0},{2,3},{3,2},{4,5},{5,4},{6,7},{7,6},{8,9},{9,8},{10,11... | collective-permute-start | bytes 49160 | tf_op jit(solution)/shard_map/ppermute | solution.py:238
  107.1 4.8 %collective-permute-start.22 = (f32[64,64]{1,0:T(8,128)S(1)}, f32[64,64]{1,0:T(8,128)S(1)}, u32[]{:S(2)}, u32[]{:S(2)}) collective-permute-start(f32[64,64]{1,0:T(8,128)S(1)} %add.164), channel_id=1, source_target_pairs={{0,2},{1,3},{2,0},{3,1},{4,6},{5,7},{6,4},{7,5},{8,10},{9,11},{10,... | collective-permute-start | bytes 49160 | tf_op jit(solution)/shard_map/ppermute | solution.py:238
  112.3 6.4 %copy-start.2 = (f32[1536,3072]{1,0:T(8,128)S(1)}, f32[1536,3072]{1,0:T(8,128)}, u32[]{:S(2)}) copy-start(f32[1536,3072]{1,0:T(8,128)} %a_ref.5) | copy-start | bytes 56623108

commit v2 on v0

v2 whole, which is shorter than its diff:
```python
import jax
import jax.numpy as jnp
from jax import lax
from jax.experimental import pallas as pl
from jax.experimental.pallas import tpu as pltpu
from jax.sharding import PartitionSpec as P

precise = lax.Precision.HIGHEST
f32 = jnp.float32
bf16 = jnp.bfloat16


def shape(*dims, dtype=f32):
    return jax.ShapeDtypeStruct(dims, dtype)


def params(mib):
    return pltpu.CompilerParams(vmem_limit_bytes=mib * 1024 * 1024)


def cost(flops, moved):
    return pl.CostEstimate(flops=flops, bytes_accessed=moved, transcendentals=0)


def dot(a, b):
    return jnp.dot(a, b, precision=precise, preferred_element_type=f32)


def fast(a, b):
    return jnp.dot(a, b, preferred_element_type=f32)


def split(value):
    high = value.astype(bf16)
    return high, (value - high.astype(f32)).astype(bf16)


def block_of(size, wanted):
    while size % wanted:
        wanted //= 2
    return wanted


def small_call(kernel, out, *operands, name, carry=None, flops=1_000_000, moved=1_000_000, mib=8):
    extra = {}
    body = kernel
    if carry is not None:
        outs = out if isinstance(out, tuple) else (out,)
        count = len(operands)
        anywhere = pl.BlockSpec(memory_space=pl.ANY)
        whole = pl.BlockSpec(memory_space=pltpu.VMEM)
        extra = dict(
            in_specs=[whole] * count + [anywhere],
            out_specs=(whole,) * len(outs) + (anywhere,),
            input_output_aliases={count: len(outs)},
        )
        operands = operands + (carry,)
        out = outs + (shape(*carry.shape),)

        def body(*refs):
            kernel(*refs[:count], *refs[count + 1 : -1])

    return pl.pallas_call(
        body,
        out_shape=out,
        compiler_params=params(mib),
        cost_estimate=cost(flops, moved),
        name=name,
        **extra,
    )(*operands)


def open_kernel(turned_ref, first_ref, second_ref, packed_ref):
    width = turned_ref.shape[0]
    half = first_ref.shape[1]
    turned = turned_ref[...]
    first_ref[...] = turned[:, :half]
    second_ref[...] = turned[:, half:]
    gram = lax.dot_general(
        turned, turned, (((1,), (1,)), ((), ())), precision=precise, preferred_element_type=f32
    )
    head = jnp.where(lax.axis_index("row") == 0, turned[:, : 2 * width].T[:width], 0.0)
    packed_ref[...] = jnp.concatenate([gram, head], 1)


def add_kernel(*refs):
    total = refs[0][...]
    for ref in refs[1:-1]:
        total = total + ref[...]
    refs[-1][...] = total


def spread(tile, at):
    return jnp.broadcast_to(tile[at : at + 1, :], tile.shape)


def pick(tile, at):
    return jnp.broadcast_to(tile[:, at : at + 1], tile.shape)


def sweep(tiles, order, full):
    lane = lax.broadcasted_iota(jnp.int32, (8, order), 1)
    sub = lax.broadcasted_iota(jnp.int32, (8, order), 0)
    tiles = list(tiles)
    for at in range(order // 8):
        base = 8 * at
        inside = (lane >= base) & (lane < base + 8)
        tile = tiles[at]
        others = [t for t in range(order // 8) if (t != at if full else t > at)]
        picked = {t: [pick(tiles[t], base + q) for q in range(8)] for t in others}
        columns = [pick(tile, base + q) for q in range(8)]
        rows = jnp.where(inside, jnp.where(lane - base == sub, 1.0, 0.0), tile)
        lower, upper = rows, tile
        for q in range(8):
            here = sub == q
            inverse = 1.0 / spread(columns[q], q)
            scaled = spread(rows, q) * inverse
            if not full:
                lower = jnp.where(here, rows, lower)
                upper = jnp.where(
                    sub > q, upper - columns[q] * (spread(upper, q) * inverse), upper
                )
            rows = jnp.where(here, scaled, rows - columns[q] * scaled)
            for p in range(q + 1, 8):
                part = spread(columns[p], q) * inverse
                columns[p] = jnp.where(here, part, columns[p] - columns[q] * part)
        finals = [spread(rows, q) for q in range(8)]
        for t in others:
            value = jnp.where(inside, 0.0, tiles[t])
            for q in range(8):
                value = value - picked[t][q] * finals[q]
            tiles[t] = value
        tiles[at] = rows if full else jnp.where(inside & (lane - base >= sub), upper, lower)
    return tiles


def eliminate_kernel(a_ref, b_ref, c_ref, d_ref, band_ref, inverse_ref, head_ref):
    order = band_ref.shape[0]
    lane = lax.broadcasted_iota(jnp.int32, (8, order), 1)
    sub = lax.broadcasted_iota(jnp.int32, (8, order), 0)
    total = (a_ref[...] + b_ref[...]) + (c_ref[...] + d_ref[...])
    head_ref[...] = total[:, order:]
    gram = total[:, :order]
    tiles = sweep([gram[8 * t : 8 * t + 8, :] for t in range(order // 8)], order, False)
    for t in range(order // 8):
        row_at = sub + 8 * t
        diagonal = jnp.sum(jnp.where(lane == row_at, tiles[t], 0.0), axis=1, keepdims=True)
        length = jnp.sqrt(diagonal)
        scaled = tiles[t] / length
        band_ref[8 * t : 8 * t + 8, :] = jnp.where(
            lane > row_at, -scaled, jnp.where(lane == row_at, -length, 0.0)
        )
        inverse_ref[8 * t : 8 * t + 8, :] = jnp.where(
            lane < row_at, -scaled, jnp.where(lane == row_at, -1.0 / length, 0.0)
        )


def invert_kernel(head_ref, band_ref, inverse_ref, out_ref):
    order = head_ref.shape[0]
    tiles = [
        head_ref[8 * t : 8 * t + 8, :] - band_ref[8 * t : 8 * t + 8, :] for t in range(order // 8)
    ]
    tiles = sweep(tiles, order, True)
    out_ref[...] = -dot(jnp.concatenate(tiles, 0), inverse_ref[...])


def down_kernel(first_ref, second_ref, a_ref, out_ref, kept_ref):
    width = first_ref.shape[0]
    kh, kl = split(jnp.concatenate([first_ref[...], second_ref[...]], 1))
    left = jnp.concatenate([kh, kl], 0)
    value = a_ref[...]
    kept_ref[...] = value
    ah, al = split(value)
    term = fast(left, ah) + fast(left, al)
    out_ref[...] = term[:width] + term[width:]


def product_down(first, second, a):
    rows, columns = a.shape
    width, half = first.shape
    bc = block_of(columns, 512)
    part = pl.BlockSpec((width, half), lambda i: (0, 0))
    block = pl.BlockSpec((rows, bc), lambda i: (0, i))
    return pl.pallas_call(
        down_kernel,
        grid=(columns // bc,),
        in_specs=[part, part, block],
        out_specs=(pl.BlockSpec((width, bc), lambda i: (0, i)), block),
        out_shape=(shape(width, columns), shape(rows, columns)),
        compiler_params=params(22),
        cost_estimate=cost(8 * rows * columns * width, 4 * rows * columns),
        name="product_down",
    )(first, second, pltpu.with_memory_space_constraint(a, pltpu.HBM))


def fix_kernel(raw_ref, band_ref, top_ref, keep_ref, give_ref, _):
    half = keep_ref.shape[1]
    row = lax.axis_index("row")
    core = lax.rem(row, 2)
    first, second = raw_ref[:, :half], raw_ref[:, half:]

    @pl.when(row == 0)
    def _():
        turned = band_ref[...].T
        keep_ref[...] = first - dot(turned, top_ref[:, :half])
        give_ref[...] = second - dot(turned, top_ref[:, half:])

    @pl.when((row != 0) & (core == 0))
    def _():
        keep_ref[...] = first
        give_ref[...] = second

    @pl.when(core == 1)
    def _():
        keep_ref[...] = second
        give_ref[...] = first


def fix_down(raw, band, a):
    width, columns = raw.shape
    half = shape(width, columns // 2)
    whole = pl.BlockSpec((width, columns), lambda i: (0, 0))
    halves = pl.BlockSpec((width, columns // 2), lambda i: (0, 0))
    return pl.pallas_call(
        fix_kernel,
        grid=(1,),
        in_specs=[whole, pl.BlockSpec((width, width), lambda i: (0, 0)), whole],
        out_specs=(halves, halves, pl.BlockSpec(memory_space=pl.ANY)),
        out_shape=(half, half, shape(*a.shape)),
        input_output_aliases={2: 2},
        compiler_params=params(12),
        cost_estimate=cost(12 * width * width * columns, 16 * width * columns),
        name="fix_down",
    )(raw, band, a)


def across_kernel(held_ref, other_ref, band_ref, a_ref, *refs):
    kct_ref, outs, right_ref = refs[0], refs[1:-2], refs[-1]
    width, half = held_ref.shape
    columns = a_ref.shape[1]
    step = pl.program_id(0)
    chunk = block_of(columns, 512)

    @pl.when(step == 0)
    def _():
        core = lax.rem(lax.axis_index("row"), 2)

        @pl.when(core == 0)
        def _():
            kct_ref[:, :half] = held_ref[...]
            kct_ref[:, half:] = other_ref[...]

        @pl.when(core == 1)
        def _():
            kct_ref[:, :half] = other_ref[...]
            kct_ref[:, half:] = held_ref[...]

        @pl.when(lax.axis_index("col") == 0)
        def _():
            kct_ref[:, :width] = kct_ref[:, :width] - band_ref[...].T

        for c in range(0, columns, chunk):
            right_ref[c : c + chunk, :] = jnp.concatenate(split(kct_ref[:, c : c + chunk].T), 1)

    total = None
    for c in range(0, columns, chunk):
        ah, al = split(a_ref[:, c : c + chunk])
        right = right_ref[c : c + chunk, :]
        term = fast(ah, right) + fast(al, right)
        total = term if total is None else total + term
    result = (total[:, :width] + total[:, width:]).T
    for at, out_ref in enumerate(outs):

        @pl.when(step == at)
        def _():
            out_ref[...] = result


def product_across(held, other, band, a, pieces):
    rows, columns = a.shape
    width, half = held.shape
    size = rows // pieces

    def turn(i):
        return (lax.rem(i + lax.axis_index("col"), pieces), 0)

    part = pl.BlockSpec((width, half), lambda i: (0, 0))
    one = pl.BlockSpec((width, size), lambda i: (0, 0))
    return pl.pallas_call(
        across_kernel,
        grid=(pieces,),
        in_specs=[
            part,
            part,
            pl.BlockSpec((width, width), lambda i: (0, 0)),
            pl.BlockSpec((size, columns), turn),
        ],
        out_specs=(pl.BlockSpec((width, columns), lambda i: (0, 0)),)
        + (one,) * pieces
        + (pl.BlockSpec(memory_space=pl.ANY),),
        out_shape=(shape(width, columns),)
        + (shape(width, size),) * pieces
        + (shape(rows, columns),),
        input_output_aliases={3: pieces + 1},
        scratch_shapes=[pltpu.VMEM((columns, 2 * width), bf16)],
        compiler_params=params(22),
        cost_estimate=cost(8 * rows * columns * width, 4 * rows * columns),
        name="product_across",
    )(held, other, band, a)


def merge_first_kernel(first_ref, second_ref, by_x_ref, by_y_ref, a_ref, b_ref):
    source = lax.div(lax.axis_index("row"), 2) == lax.axis_index("col")
    a_ref[...] = jnp.where(source, first_ref[...], by_x_ref[...])
    b_ref[...] = jnp.where(source, second_ref[...], by_y_ref[...])


def join_kernel(a_ref, b_ref, c_ref, d_ref, out_ref):
    half = a_ref.shape[1]
    out_ref[:, :half] = a_ref[...] + b_ref[...]
    out_ref[:, half:] = c_ref[...] + d_ref[...]


def halve_kernel(keep_ref, other_ref, a_ref, b_ref):
    half = a_ref.shape[1]
    a_ref[...] = keep_ref[:, :half] + other_ref[:, :half]
    b_ref[...] = keep_ref[:, half:] + other_ref[:, half:]


def pair_kernel(a_ref, b_ref, c_ref, d_ref, e_ref, f_ref):
    e_ref[...] = a_ref[...] + b_ref[...]
    f_ref[...] = c_ref[...] + d_ref[...]


def inner_kernel(kct_ref, held_ref, other_ref, xct_ref, inner_ref):
    half = held_ref.shape[1]
    core = lax.rem(lax.axis_index("row"), 2)

    @pl.when(core == 0)
    def _():
        xct_ref[:, :half] = held_ref[...]
        xct_ref[:, half:] = other_ref[...]

    @pl.when(core == 1)
    def _():
        xct_ref[:, :half] = other_ref[...]
        xct_ref[:, half:] = held_ref[...]

    inner_ref[...] = lax.dot_general(
        kct_ref[...],
        xct_ref[...],
        (((1,), (1,)), ((), ())),
        precision=precise,
        preferred_element_type=f32,
    )


def corrected(st, cm, xt, kt):
    return dot(st, xt) - 0.5 * dot(cm, kt)


def right_kernel(part_ref, more_ref, st_ref, xct_ref, kct_ref, cm_ref, right_ref):
    width, columns = kct_ref.shape
    st = st_ref[...]
    cm = dot(dot(st, part_ref[...] + more_ref[...]), st.T)
    cm_ref[...] = cm
    chunk = block_of(columns, 512)
    for c in range(0, columns, chunk):
        k = kct_ref[:, c : c + chunk]
        wh, wl = split(corrected(st, cm, xct_ref[:, c : c + chunk], k))
        kh, kl = split(k)
        right_ref[:, c : c + chunk] = jnp.concatenate([wh, kh, wl, kl], 0)


def left_kernel(first_ref, second_ref, band_ref, st_ref, cm_ref, *refs):
    chunks, left_ref, krt_ref = refs[:-2], refs[-2], refs[-1]
    width, half = first_ref.shape
    pieces = len(chunks)
    size = chunks[0].shape[1]
    krt_ref[:, :half] = first_ref[...]
    krt_ref[:, half:] = second_ref[...]

    @pl.when(lax.axis_index("row") == 0)
    def _():
        krt_ref[:, :width] = krt_ref[:, :width] - band_ref[...].T

    st, cm = st_ref[...], cm_ref[...]
    col = lax.axis_index("col")
    for at, ref in enumerate(chunks):
        start = pl.multiple_of(lax.rem(col + pieces - at, pieces) * size, size)
        k = krt_ref[:, pl.ds(start, size)]
        both = jnp.concatenate([k, corrected(st, cm, ref[...], k)], 0)
        left_ref[pl.ds(start, size), :] = jnp.concatenate(split(both.T), 1)


def subtract_kernel(left_ref, right_ref, a_ref, out_ref):
    width = left_ref.shape[1] // 2
    left = left_ref[...]
    left = jnp.concatenate([left, left], 1)
    columns = a_ref.shape[1]
    chunk = block_of(columns, 512)
    for c in range(0, columns, chunk):
        high = right_ref[:width, c : c + chunk]
        low = right_ref[width:, c : c + chunk]
        both = jnp.concatenate([high, high, low, low], 0)
        out_ref[:, c : c + chunk] = a_ref[:, c : c + chunk] - fast(left, both)


def subtract(left, right, a):
    rows, columns = a.shape
    deep = left.shape[1]
    br = block_of(rows, 256)
    return pl.pallas_call(
        subtract_kernel,
        grid=(rows // br,),
        in_specs=[
            pl.BlockSpec((br, deep), lambda i: (i, 0)),
            pl.BlockSpec((deep, columns), lambda i: (0, 0)),
            pl.BlockSpec((br, columns), lambda i: (i, 0)),
        ],
        out_specs=pl.BlockSpec((br, columns), lambda i: (i, 0)),
        out_shape=shape(rows, columns),
        compiler_params=params(22),
        cost_estimate=cost(4 * rows * columns * deep, 8 * rows * columns),
        name="subtract",
    )(left, right, a)


def flip(value, bit, size, axis="row"):
    return lax.ppermute(value, axis, [(i, i ^ bit) for i in range(size)])


def from_sources(piece, col_size, source_flips, bit):
    pairs = []
    for c in range(col_size):
        for source in source_flips:
            for core in range(2):
                at = (2 * c + core) ^ source
                pairs.append((at * col_size + c, (at ^ bit) * col_size + c))
    return lax.ppermute(piece, ("row", "col"), pairs)


def shift(piece, by, size):
    return lax.ppermute(piece, "col", [(i, (i + by) % size) for i in range(size)])


def body_of(row_size, col_size):
    assert row_size == 2 * col_size

    def body(matrix, panel):
        rows, width = panel.shape
        columns = matrix.shape[1]
        small = shape(width, width)
        packed = shape(width, 2 * width)
        half = shape(width, rows // 2)
        first, second, partial = small_call(
            open_kernel, (half, half, packed), panel.T, name="open", flops=100_000_000, mib=12
        )
        partial = small_call(add_kernel, packed, partial, flip(partial, 1, row_size), name="add_cores")
        if row_size == 8:
            terms = [partial] + [flip(partial, bit, row_size) for bit in (2, 4, 6)]
        else:
            bit = 2
            total = partial
            while bit < row_size // 2:
                total = total + flip(total, bit, row_size)
                bit *= 2
            zero = jnp.zeros_like(total)
            terms = [total, flip(total, row_size // 2, row_size), zero, zero]
        first, second, partial = lax.optimization_barrier((first, second, partial))
        raw, resident = product_down(first, second, matrix)
        if row_size == 8:
            by_x = from_sources(first, col_size, [0], 2)
            by_y = from_sources(second, col_size, [0], 4)
            one, two, resident = small_call(
                merge_first_kernel,
                (half, half),
                first,
                second,
                by_x,
                by_y,
                name="merge_first",
                carry=resident,
            )
            more_x = from_sources(two, col_size, [0, 4], 2)
            more_y = from_sources(one, col_size, [0, 2], 4)
        else:
            relation = (lax.axis_index("row") // 2) ^ lax.axis_index("col")
            held = jnp.where(relation == 0, jnp.concatenate([first, second], 1), 0.0)
            reached = [0]
            bit = 2
            while bit < row_size:
                held = held + from_sources(held, col_size, reached, bit)
                reached = reached + [r ^ bit for r in reached]
                bit *= 2
        band, band_inverse, head, resident = small_call(
            eliminate_kernel,
            (small, small, small),
            *terms,
            name="eliminate",
            flops=50_000_000,
            carry=resident,
        )
        keep, give, resident = fix_down(raw, band, resident)
        if row_size == 8:
            held, resident = small_call(
                join_kernel,
                shape(width, rows),
                one,
                more_y,
                two,
                more_x,
                name="merge_second",
                carry=resident,
            )
        other = flip(held, 1, row_size)
        quarter = shape(width, columns // 4)
        a, b, resident = small_call(
            halve_kernel,
            (quarter, quarter),
            keep,
            flip(give, 1, row_size),
            name="add_halves",
            carry=resident,
        )
        bits = []
        bit = 2
        while bit < row_size:
            bits.append(bit)
            bit *= 2
        for forward, backward in list(zip(bits, bits[::-1]))[:-1]:
            ra, rb = flip(a, forward, row_size), flip(b, backward, row_size)
            if bits[0] == forward:
                pieces = 1 if (rows // col_size) % 128 else col_size
                kct, *chunks, resident = product_across(held, other, band, resident, pieces)
            a, b, resident = small_call(
                pair_kernel, (quarter, quarter), a, ra, b, rb, name="add_chips", carry=resident
            )
        ra, rb = flip(a, bits[-1], row_size), flip(b, bits[0], row_size)
        st, resident = small_call(
            invert_kernel,
            small,
            head,
            band,
            band_inverse,
            name="invert",
            flops=50_000_000,
            carry=resident,
        )
        if pieces == 1:
            whole = [lax.psum(chunks[0], "col")]
        else:
            received = [shift(chunks[by], by, col_size) for by in range(1, col_size)]
            mine, resident = small_call(
                add_kernel,
                shape(width, rows // col_size),
                chunks[0],
                *received,
                name="add_line",
                carry=resident,
            )
            whole = [mine] + [shift(mine, by, col_size) for by in range(1, col_size)]
        summed, resident = small_call(
            join_kernel,
            shape(width, columns // 2),
            a,
            ra,
            b,
            rb,
            name="add_last",
            carry=resident,
        )
        xct, inner, resident = small_call(
            inner_kernel,
            (shape(width, columns), small),
            kct,
            summed,
            flip(summed, 1, row_size),
            name="inner",
            carry=resident,
        )
        bit = 1
        while bit < col_size // 2:
            inner, resident = small_call(
                add_kernel,
                small,
                inner,
                flip(inner, bit, col_size, "col"),
                name="add_inner",
                carry=resident,
            )
            bit *= 2
        more = flip(inner, bit, col_size, "col")
        cm, right, resident = small_call(
            right_kernel,
            (small, shape(4 * width, columns, dtype=bf16)),
            inner,
            more,
            st,
            xct,
            kct,
            name="right",
            mib=12,
            carry=resident,
        )
        left, _, resident = small_call(
            left_kernel,
            (shape(rows, 4 * width, dtype=bf16), shape(width, rows)),
            first,
            second,
            band,
            st,
            cm,
            *whole,
            name="left",
            mib=12,
            carry=resident,
        )
        return subtract(left, right, resident), band

    return body


def solution(mesh):
    return jax.shard_map(
        body_of(mesh.shape["row"], mesh.shape["col"]),
        mesh=mesh,
        in_specs=(P("row", "col"), P("row", None)),
        out_specs=(P("row", "col"), P()),
        check_vma=False,
    )
```

time: 660 us -> 87.4 us (0.13)
  matrix products: 245 us -> 0 us
  other arithmetic: 228 us -> 0 us
  loops' own time: 48.6 us -> 0 us
  blocking collectives: 45.3 us -> 0 us
  waiting for transfers between devices: 60.7 us -> 17.9 us
  Pallas kernels: 0 us -> 36.5 us
  starting transfers between devices: 0.12 us -> 30.1 us
  between operations: 14 us -> 0.89 us
  local copies, waits for them, and re-layouts: 14.7 us -> 1.75 us
    dot_general x267 -> x0, matrix products: 245 us -> none  [the longest x192 148 us: one_row(): jnp.dot(beyond, inverse_part, precision=precise)]
    reduce_sum x256 -> x0, other arithmetic: 159 us -> none  [the longest x192 120 us: one_row(): diagonal_value = jnp.sum(jnp.where(positions == row_at, upper_row, 0.0))]
    all_gather x2 -> x0, waiting for transfers between devices: 60 us -> none  [the longest x1 60 us: body(): lax.all_gather(corrected_cols, 'col', axis=0, tiled=True)]
    another operation x5 -> x0, loops' own time: 48.6 us -> none  [the longest x1 45 us: upper_cholesky(): lax.fori_loop(0, order_now, one_column, jnp.zeros((order_now, order_now),...]
    psum x2 -> x0, blocking collectives: 45.3 us -> none  [the longest x1 26.1 us: body(): total_inner, head_rows = lax.psum((local_inner, masked), 'row')]
    mul x64 -> x0, other arithmetic: 41.9 us -> none  [one_pivot(): working = working - multipliers[:, None] * pivot_row[None, :]]
    pallas_call x0 -> x18, Pallas kernels: none -> 36.5 us  [the longest x1 10.1 us: product_down(): pl.pallas_call(down_kernel, grid=(columns // bc,), in_specs=[part, part,...]
    ppermute x0 -> x23, starting transfers between devices: none -> 30.1 us  [the longest x13 10.4 us: flip(): return lax.ppermute(value, axis, [(i, i ^ bit) for i in range(size)])]
  transfers between devices with their start and end apart: 3 -> 23, of which waited for: 1 -> 9; matrix products, arithmetic and copies ran while one was open for 15% -> 0% of each run, Pallas kernels for 0% -> 29%
where the time goes in v2:
time: 87.4 us; the launch traced here: 87.1 us
  Pallas kernels  36.5 us (42%)
  starting transfers between devices  30.1 us (34%)
  waiting for transfers between devices  17.9 us (20%)
  local copies, waits for them, and re-layouts  1.75 us (2%)
  between operations  0.89 us (1%)
    ppermute x13, waiting for transfers between devices, flip(): return lax.ppermute(value, axis, [(i, i ^ bit) for i in range(size)])  14 us
    ppermute x13, starting transfers between devices, flip(): return lax.ppermute(value, axis, [(i, i ^ bit) for i in range(size)])  10.4 us
    ppermute x6, starting transfers between devices, shift(): lax.ppermute(piece, 'col', [(i, (i + by) % size) for i in range(size)])  10.1 us
    pallas_call x1, Pallas kernels, product_down(): pl.pallas_call(down_kernel, grid=(columns // bc,), in_specs=[part, part,...  10.1 us
    ppermute x4, starting transfers between devices, from_sources(): return lax.ppermute(piece, ('row', 'col'), pairs)  9.5 us
    pallas_call x14, Pallas kernels, small_call(): pl.pallas_call(body, out_shape=out, compiler_params=params(mib), cost_est...  9.48 us
    pallas_call x1, Pallas kernels, subtract(): pl.pallas_call(subtract_kernel, grid=(rows // br,), in_specs=[pl.BlockSpe...  8.98 us
    pallas_call x1, Pallas kernels, product_across(): pl.pallas_call(across_kernel, grid=(pieces,), in_specs=[part, part, pl.Bl...  7 us
  transfers between devices with their start and end apart: 23, of which 9 were waited for; matrix products, arithmetic and copies ran while one was open for 0% of the time, Pallas kernels for 29%

profile of v2, /device:TPU:0, one launch (start us, length us, event | category | flops | bytes accessed | tf_op | source)
XLA Modules:
  0.0 87.1 jit_solution(11684253757210057440)
XLA Ops:
  0.6 0.0 copy-start.1
  0.6 1.0 %copy-done.1 = f32[1536,64]{0,1:T(8,128)S(1)} copy-done((f32[1536,64]{0,1:T(8,128)S(1)}, f32[1536,64]{0,1:T(8,128)}, u32[]{:S(2)}) %copy-start.1) | copy-done | bytes 393240
  1.6 0.5 open.1
  2.1 0.6 collective-permute-start
  2.7 0.9 collective-permute-done.refs_1_
  3.5 4.7 %collective-permute-start.4 = (f32[64,768]{1,0:T(8,128)S(1)}, f32[64,768]{1,0:T(8,128)S(1)}, u32[]{:S(2)}, u32[]{:S(2)}) collective-permute-start(f32[64,768]{1,0:T(8,128)S(1)} %get-tuple-element.52.first_ref.refs_0_), channel_id=1, source_target_pairs={{0,8},{4,12},{9,1},{13,5},{18,26},{22,30},{27,19},{31,23}} | collective-permute-start | bytes 589832 | tf_op jit(solution)/shard_map/ppermute | solution.py:440
  8.3 1.3 %collective-permute-start.5 = (f32[64,768]{1,0:T(8,128)S(1)}, f32[64,768]{1,0:T(8,128)S(1)}, u32[]{:S(2)}, u32[]{:S(2)}) collective-permute-start(f32[64,768]{1,0:T(8,128)S(1)} %get-tuple-element.53.second_ref.refs_1_), channel_id=1, source_target_pairs={{0,16},{4,20},{9,25},{13,29},{18,2},{22,6},{27,11},{31,15}} | collective-permute-start | bytes 589832 | tf_op jit(solution)/shard_map/ppermute | solution.py:440
  9.6 10.1 %product_down.1 = (f32[64,3072]{1,0:T(8,128)S(1)}, f32[1536,3072]{1,0:T(8,128)S(1)}) custom-call(f32[64,768]{1,0:T(8,128)S(1)} %get-tuple-element.52.first_ref.refs_0_, f32[64,768]{1,0:T(8,128)S(1)} %get-tuple-element.53.second_ref.refs_1_, f32[1536,3072]{1,0:T(8,128)} %a_ref.1), custom_call_target="tpu_custom_call" | custom-call | flops 2415919104 | bytes 18874368 | tf_op jit(solution)/shard_map/product_down/pallas_call | solution.py:184
  19.7 0.0 collective-permute-done.4.refs_2_
  19.7 0.0 collective-permute-done.5.refs_3_
  19.8 1.3 %collective-permute-start.7 = (f32[64,768]{1,0:T(8,128)S(1)}, f32[64,768]{1,0:T(8,128)S(1)}, u32[]{:S(2)}, u32[]{:S(2)}) collective-permute-start(f32[64,768]{1,0:T(8,128)S(1)} %get-tuple-element.63.refs_0_), channel_id=1, source_target_pairs={{0,16},{4,20},{8,24},{12,28},{9,25},{13,29},{1,17},{5,21},{18,2},{... | collective-permute-start | bytes 589832 | tf_op jit(solution)/shard_map/ppermute | solution.py:440
  21.1 2.2 %collective-permute-start.8 = (f32[64,768]{1,0:T(8,128)S(1)}, f32[64,768]{1,0:T(8,128)S(1)}, u32[]{:S(2)}, u32[]{:S(2)}) collective-permute-start(f32[64,768]{1,0:T(8,128)S(1)} %get-tuple-element.64.refs_2_), channel_id=1, source_target_pairs={{0,8},{4,12},{16,24},{20,28},{9,1},{13,5},{25,17},{29,21},{18,26},... | collective-permute-start | bytes 589832 | tf_op jit(solution)/shard_map/ppermute | solution.py:440
  23.3 0.1 collective-permute-start.1
  23.4 0.1 collective-permute-start.2
  23.4 3.4 %collective-permute-start.3 = (f32[64,128]{1,0:T(8,128)S(1)}, f32[64,128]{1,0:T(8,128)S(1)}, u32[]{:S(2)}, u32[]{:S(2)}) collective-permute-start(f32[64,128]{1,0:T(8,128)S(1)} %add_cores.1.refs_0_), channel_id=1, source_target_pairs={{0,24},{4,28},{8,16},{12,20},{16,8},{20,12},{24,0},{28,4},{1,25},{... | collective-permute-start | bytes 98312 | tf_op jit(solution)/shard_map/ppermute | solution.py:430
  26.8 1.7 %collective-permute-done.1.refs_1_ = f32[64,128]{1,0:T(8,128)S(1)} collective-permute-done((f32[64,128]{1,0:T(8,128)S(1)}, f32[64,128]{1,0:T(8,128)S(1)}, u32[]{:S(2)}, u32[]{:S(2)}) %collective-permute-start.1) | collective-permute-done | bytes 32800 | tf_op jit(solution)/shard_map/ppermute | solution.py:430
  28.5 0.0 collective-permute-done.2.refs_2_
  28.5 0.3 collective-permute-done.3.refs_3_
  28.9 2.7 %eliminate.1 = (f32[64,64]{1,0:T(8,128)}, f32[64,64]{1,0:T(8,128)S(1)}, f32[64,64]{1,0:T(8,128)S(1)}, f32[1536,3072]{1,0:T(8,128)S(1)}) custom-call(f32[64,128]{1,0:T(8,128)S(1)} %add_cores.1.refs_0_, f32[64,128]{1,0:T(8,128)S(1)} %collective-permute-done.1.refs_1_, f32[64,128]{1,0:T(8,128)S(1)} %collective-permute-done.2.refs_2_, ...), custom_call_target="tpu_custom_call", output_to_operand_aliasing={{3}: (4, {})} | custom-call | flops 50000000 | bytes 1000000 | tf_op jit(solution)/shard_map/eliminate/pallas_call | solution.py:63
  31.5 0.0 copy-start
  31.5 0.8 copy-done
  32.3 0.9 %fix_down.1 = (f32[64,1536]{1,0:T(8,128)S(1)}, f32[64,1536]{1,0:T(8,128)S(1)}, f32[1536,3072]{1,0:T(8,128)S(1)}) custom-call(f32[64,3072]{1,0:T(8,128)S(1)} %get-tuple-element.59.raw_ref, f32[64,64]{1,0:T(8,128)S(1)} %copy-done, f32[1536,3072]{1,0:T(8,128)S(1)} %get-tuple-element.60.top_ref), custom_call_target="tpu_custom_call", output_to_operand_aliasing={{2}: (2, {})} | custom-call | flops 150994944 | bytes 3145728 | tf_op jit(solution)/shard_map/fix_down/pallas_call | solution.py:224
  33.2 0.1 collective-permute-start.6
  33.3 0.0 collective-permute-done.7.refs_1_
  33.3 0.0 collective-permute-done.8.refs_3_
  33.4 0.5 collective-permute-start.11
  33.9 1.1 %collective-permute-done.6.refs_1_ = f32[64,1536]{1,0:T(8,128)S(1)} collective-permute-done((f32[64,1536]{1,0:T(8,128)S(1)}, f32[64,1536]{1,0:T(8,128)S(1)}, u32[]{:S(2)}, u32[]{:S(2)}) %collective-permute-start.6) | collective-permute-done | bytes 393248 | tf_op jit(solution)/shard_map/ppermute | solution.py:430
  35.0 0.7 collective-permute-start.10
  35.7 2.5 %collective-permute-start.9 = (f32[64,768]{1,0:T(8,128)S(1)}, f32[64,768]{1,0:T(8,128)S(1)}, u32[]{:S(2)}, u32[]{:S(2)}) collective-permute-start(f32[64,768]{1,0:T(8,128)S(1)} %get-tuple-element.67.refs_0_), channel_id=1, source_target_pairs={{0,8},{4,12},{8,0},{12,4},{16,24},{20,28},{24,16},{28,20},{1,9},{5... | collective-permute-start | bytes 589832 | tf_op jit(solution)/shard_map/ppermute | solution.py:430
  38.3 0.0 collective-permute-done.11.other_ref
  38.3 7.0 %product_across.1 = (f32[64,3072]{1,0:T(8,128)S(1)}, f32[64,384]{1,0:T(8,128)S(1)}, f32[64,384]{1,0:T(8,128)S(1)}, f32[64,384]{1,0:T(8,128)S(1)}, f32[64,384]{1,0:T(8,128)S(1)}, /*index=5*/f32[1536,3072]{1,0:T(8,128)S(1)}) custom-call(f32[64,1536]{1,0:T(8,128)S(1)} %get-tuple-element.69.held_ref, ...), custom_call_target="tpu_custom_call", output_to_operand_aliasing={{5}: (3, {})} | custom-call | flops 2415919104 | bytes 18874368 | tf_op jit(solution)/shard_map/product_across/pallas_call | solution.py:289
  45.3 0.0 collective-permute-done.10.refs_3_
  45.3 0.0 collective-permute-done.9.refs_1_
  45.3 0.3 collective-permute-start.12
  45.6 0.7 collective-permute-start.13
  46.3 2.1 %collective-permute-start.14 = (f32[64,384]{1,0:T(8,128)S(1)}, f32[64,384]{1,0:T(8,128)S(1)}, u32[]{:S(2)}, u32[]{:S(2)}) collective-permute-start(f32[64,384]{1,0:T(8,128)S(1)} %get-tuple-element.78), channel_id=1, source_target_pairs={{0,1},{1,2},{2,3},{3,0},{4,5},{5,6},{6,7},{7,4},{8,9},{9,10},{10,1... | collective-permute-start | bytes 294920 | tf_op jit(solution)/shard_map/ppermute | solution.py:444
  48.4 3.3 %collective-permute-start.15 = (f32[64,384]{1,0:T(8,128)S(1)}, f32[64,384]{1,0:T(8,128)S(1)}, u32[]{:S(2)}, u32[]{:S(2)}) collective-permute-start(f32[64,384]{1,0:T(8,128)S(1)} %get-tuple-element.79), channel_id=1, source_target_pairs={{0,2},{1,3},{2,0},{3,1},{4,6},{5,7},{6,4},{7,5},{8,10},{9,11},{10,... | collective-permute-start | bytes 294920 | tf_op jit(solution)/shard_map/ppermute | solution.py:444
  51.7 0.1 collective-permute-start.16
  51.8 2.3 %invert.1 = (f32[64,64]{1,0:T(8,128)S(1)}, f32[1536,3072]{1,0:T(8,128)S(1)}) custom-call(f32[64,64]{1,0:T(8,128)S(1)} %get-tuple-element.57.refs_0_, f32[64,64]{1,0:T(8,128)S(1)} %copy-done, f32[64,64]{1,0:T(8,128)S(1)} %get-tuple-element.58.refs_2_, f32[1536,3072]{1,0:T(8,128)S(1)} %get-tuple-element.72.refs_3_), custom_call_target="tpu_custom_call", output_to_operand_aliasing={{1}: (3, {})} | custom-call | flops 50000000 | bytes 1000000 | tf_op jit(solution)/shard_map/invert/pallas_call | solution.py:63
  54.1 0.8 collective-permute-done.14.refs_1_
  54.9 2.6 %collective-permute-done.15.refs_2_ = f32[64,384]{1,0:T(8,128)S(1)} collective-permute-done((f32[64,384]{1,0:T(8,128)S(1)}, f32[64,384]{1,0:T(8,128)S(1)}, u32[]{:S(2)}, u32[]{:S(2)}) %collective-permute-start.15) | collective-permute-done | bytes 98336 | tf_op jit(solution)/shard_map/ppermute | solution.py:444
  57.5 0.4 collective-permute-done.16.refs_3_
  58.0 0.0 collective-permute-done.12.refs_1_
  58.0 0.0 collective-permute-done.13.refs_3_
  58.1 0.1 collective-permute-start.17
  58.1 2.2 %collective-permute-start.20 = (f32[64,384]{1,0:T(8,128)S(1)}, f32[64,384]{1,0:T(8,128)S(1)}, u32[]{:S(2)}, u32[]{:S(2)}) collective-permute-start(f32[64,384]{1,0:T(8,128)S(1)} %get-tuple-element.91.refs_5_), channel_id=1, source_target_pairs={{0,1},{1,2},{2,3},{3,0},{4,5},{5,6},{6,7},{7,4},{8,9},{9,10},{10,1... | collective-permute-start | bytes 294920 | tf_op jit(solution)/shard_map/ppermute | solution.py:444
  60.3 1.2 %collective-permute-start.21 = (f32[64,384]{1,0:T(8,128)S(1)}, f32[64,384]{1,0:T(8,128)S(1)}, u32[]{:S(2)}, u32[]{:S(2)}) collective-permute-start(f32[64,384]{1,0:T(8,128)S(1)} %get-tuple-element.91.refs_5_), channel_id=1, source_target_pairs={{0,2},{1,3},{2,0},{3,1},{4,6},{5,7},{6,4},{7,5},{8,10},{9,11},{10,... | collective-permute-start | bytes 294920 | tf_op jit(solution)/shard_map/ppermute | solution.py:444
  61.5 1.3 %collective-permute-start.22 = (f32[64,384]{1,0:T(8,128)S(1)}, f32[64,384]{1,0:T(8,128)S(1)}, u32[]{:S(2)}, u32[]{:S(2)}) collective-permute-start(f32[64,384]{1,0:T(8,128)S(1)} %get-tuple-element.91.refs_5_), channel_id=1, source_target_pairs={{0,3},{1,0},{2,1},{3,2},{4,7},{5,4},{6,5},{7,6},{8,11},{9,8},{10,9... | collective-permute-start | bytes 294920 | tf_op jit(solution)/shard_map/ppermute | solution.py:444
  62.8 0.0 collective-permute-done.17.refs_2_
  62.8 0.8 inner.1
  63.6 0.8 collective-permute-start.18
  64.4 5.6 %collective-permute-done.18.refs_1_ = f32[64,64]{1,0:T(8,128)S(1)} collective-permute-done((f32[64,64]{1,0:T(8,128)S(1)}, f32[64,64]{1,0:T(8,128)S(1)}, u32[]{:S(2)}, u32[]{:S(2)}) %collective-permute-start.18) | collective-permute-done | bytes 16416 | tf_op jit(solution)/shard_map/ppermute | solution.py:430
  70.0 0.6 collective-permute-start.19
  70.7 4.4 %collective-permute-done.19.refs_1_ = f32[64,64]{1,0:T(8,128)S(1)} collective-permute-done((f32[64,64]{1,0:T(8,128)S(1)}, f32[64,64]{1,0:T(8,128)S(1)}, u32[]{:S(2)}, u32[]{:S(2)}) %collective-permute-start.19) | collective-permute-done | bytes 16416 | tf_op jit(solution)/shard_map/ppermute | solution.py:430
  75.1 1.6 %right.1 = (f32[64,64]{1,0:T(8,128)S(1)}, bf16[256,3072]{1,0:T(8,128)(2,1)S(1)}, f32[1536,3072]{1,0:T(8,128)S(1)}) custom-call(f32[64,64]{1,0:T(8,128)S(1)} %get-tuple-element.87.refs_0_, f32[64,64]{1,0:T(8,128)S(1)} %collective-permute-done.19.refs_1_, f32[64,64]{1,0:T(8,128)S(1)} %get-tuple-element.73.refs_2_.refs_3_, ...), custom_call_target="tpu_custom_call", output_to_operand_aliasing={{2}: (5, {})} | custom-call | flops 1000000 | bytes 1000000 | tf_op jit(solution)/shard_map/right/pallas_call | solution.py:63
  76.7 0.0 collective-permute-done.20.refs_6_
  76.7 0.0 collective-permute-done.21.refs_7_
  76.7 0.0 collective-permute-done.22.refs_8_
  76.7 1.3 %left.1 = (bf16[1536,256]{1,0:T(8,128)(2,1)S(1)}, f32[64,1536]{1,0:T(8,128)}, f32[1536,3072]{1,0:T(8,128)S(1)}) custom-call(f32[64,768]{1,0:T(8,128)S(1)} %get-tuple-element.52.first_ref.refs_0_, f32[64,768]{1,0:T(8,128)S(1)} %get-tuple-element.53.second_ref.refs_1_, f32[64,64]{1,0:T(8,128)S(1)} %copy-done, ...), custom_call_target="tpu_custom_call", output_to_operand_aliasing={{2}: (9, {})} | custom-call | flops 1000000 | bytes 1000000 | tf_op jit(solution)/shard_map/left/pallas_call | solution.py:63
  78.1 9.0 %subtract.1 = f32[1536,3072]{1,0:T(8,128)} custom-call(bf16[1536,256]{1,0:T(8,128)(2,1)S(1)} %get-tuple-element.93.left_ref, bf16[256,3072]{1,0:T(8,128)(2,1)S(1)} %get-tuple-element.94.right_ref, f32[1536,3072]{1,0:T(8,128)S(1)} %get-tuple-element.95.a_ref), custom_call_target="tpu_custom_call" | custom-call | flops 4831838208 | bytes 37748736 | tf_op jit(solution)/shard_map/subtract/pallas_call | solution.py:413
  (8 shorter events, 0.3 us)
Async XLA Ops:
  0.6 1.0 %copy-start.1 = (f32[1536,64]{0,1:T(8,128)S(1)}, f32[1536,64]{0,1:T(8,128)}, u32[]{:S(2)}) copy-start(f32[1536,64]{0,1:T(8,128)} %param.3) | copy-start | bytes 1179652
  2.1 1.4 %collective-permute-start = (f32[64,128]{1,0:T(8,128)S(1)}, f32[64,128]{1,0:T(8,128)S(1)}, u32[]{:S(2)}, u32[]{:S(2)}) collective-permute-start(f32[64,128]{1,0:T(8,128)S(1)} %get-tuple-element.51.refs_0_), channel_id=1, source_target_pairs={{0,4},{4,0},{8,12},{12,8},{16,20},{20,16},{24,28},{28,24},{1,5},{5... | collective-permute-start | bytes 98312 | tf_op jit(solution)/shard_map/ppermute | solution.py:430
  3.5 16.2 %collective-permute-start.4 = (f32[64,768]{1,0:T(8,128)S(1)}, f32[64,768]{1,0:T(8,128)S(1)}, u32[]{:S(2)}, u32[]{:S(2)}) collective-permute-start(f32[64,768]{1,0:T(8,128)S(1)} %get-tuple-element.52.first_ref.refs_0_), channel_id=1, source_target_pairs={{0,8},{4,12},{9,1},{13,5},{18,26},{22,30},{27,19},{31,23}} | collective-permute-start | bytes 589832 | tf_op jit(solution)/shard_map/ppermute | solution.py:440
  8.3 11.5 %collective-permute-start.5 = (f32[64,768]{1,0:T(8,128)S(1)}, f32[64,768]{1,0:T(8,128)S(1)}, u32[]{:S(2)}, u32[]{:S(2)}) collective-permute-start(f32[64,768]{1,0:T(8,128)S(1)} %get-tuple-element.53.second_ref.refs_1_), channel_id=1, source_target_pairs={{0,16},{4,20},{9,25},{13,29},{18,2},{22,6},{27,11},{31,15}} | collective-permute-start | bytes 589832 | tf_op jit(solution)/shard_map/ppermute | solution.py:440
  19.8 13.5 %collective-permute-start.7 = (f32[64,768]{1,0:T(8,128)S(1)}, f32[64,768]{1,0:T(8,128)S(1)}, u32[]{:S(2)}, u32[]{:S(2)}) collective-permute-start(f32[64,768]{1,0:T(8,128)S(1)} %get-tuple-element.63.refs_0_), channel_id=1, source_target_pairs={{0,16},{4,20},{8,24},{12,28},{9,25},{13,29},{1,17},{5,21},{18,2},{... | collective-permute-start | bytes 589832 | tf_op jit(solution)/shard_map/ppermute | solution.py:440
  21.1 12.2 %collective-permute-start.8 = (f32[64,768]{1,0:T(8,128)S(1)}, f32[64,768]{1,0:T(8,128)S(1)}, u32[]{:S(2)}, u32[]{:S(2)}) collective-permute-start(f32[64,768]{1,0:T(8,128)S(1)} %get-tuple-element.64.refs_2_), channel_id=1, source_target_pairs={{0,8},{4,12},{16,24},{20,28},{9,1},{13,5},{25,17},{29,21},{18,26},... | collective-permute-start | bytes 589832 | tf_op jit(solution)/shard_map/ppermute | solution.py:440
  23.3 5.2 %collective-permute-start.1 = (f32[64,128]{1,0:T(8,128)S(1)}, f32[64,128]{1,0:T(8,128)S(1)}, u32[]{:S(2)}, u32[]{:S(2)}) collective-permute-start(f32[64,128]{1,0:T(8,128)S(1)} %add_cores.1.refs_0_), channel_id=1, source_target_pairs={{0,8},{4,12},{8,0},{12,4},{16,24},{20,28},{24,16},{28,20},{1,9},{5... | collective-permute-start | bytes 98312 | tf_op jit(solution)/shard_map/ppermute | solution.py:430
  23.4 5.2 %collective-permute-start.2 = (f32[64,128]{1,0:T(8,128)S(1)}, f32[64,128]{1,0:T(8,128)S(1)}, u32[]{:S(2)}, u32[]{:S(2)}) collective-permute-start(f32[64,128]{1,0:T(8,128)S(1)} %add_cores.1.refs_0_), channel_id=1, source_target_pairs={{0,16},{4,20},{8,24},{12,28},{16,0},{20,4},{24,8},{28,12},{1,17},{... | collective-permute-start | bytes 98312 | tf_op jit(solution)/shard_map/ppermute | solution.py:430
  23.4 5.4 %collective-permute-start.3 = (f32[64,128]{1,0:T(8,128)S(1)}, f32[64,128]{1,0:T(8,128)S(1)}, u32[]{:S(2)}, u32[]{:S(2)}) collective-permute-start(f32[64,128]{1,0:T(8,128)S(1)} %add_cores.1.refs_0_), channel_id=1, source_target_pairs={{0,24},{4,28},{8,16},{12,20},{16,8},{20,12},{24,0},{28,4},{1,25},{... | collective-permute-start | bytes 98312 | tf_op jit(solution)/shard_map/ppermute | solution.py:430
  31.5 0.8 copy-start
  33.2 1.8 %collective-permute-start.6 = (f32[64,1536]{1,0:T(8,128)S(1)}, f32[64,1536]{1,0:T(8,128)S(1)}, u32[]{:S(2)}, u32[]{:S(2)}) collective-permute-start(f32[64,1536]{1,0:T(8,128)S(1)} %get-tuple-element.62), channel_id=1, source_target_pairs={{0,4},{4,0},{8,12},{12,8},{16,20},{20,16},{24,28},{28,24},{1,5},{5... | collective-permute-start | bytes 1179656 | tf_op jit(solution)/shard_map/ppermute | solution.py:430
  33.4 4.9 %collective-permute-start.11 = (f32[64,1536]{1,0:T(8,128)S(1)}, f32[64,1536]{1,0:T(8,128)S(1)}, u32[]{:S(2)}, u32[]{:S(2)}) collective-permute-start(f32[64,1536]{1,0:T(8,128)S(1)} %get-tuple-element.69.held_ref), channel_id=1, source_target_pairs={{0,4},{4,0},{8,12},{12,8},{16,20},{20,16},{24,28},{28,24},{1,5},{5... | collective-permute-start | bytes 1179656 | tf_op jit(solution)/shard_map/ppermute | solution.py:430
  35.0 10.2 %collective-permute-start.10 = (f32[64,768]{1,0:T(8,128)S(1)}, f32[64,768]{1,0:T(8,128)S(1)}, u32[]{:S(2)}, u32[]{:S(2)}) collective-permute-start(f32[64,768]{1,0:T(8,128)S(1)} %get-tuple-element.68.refs_2_), channel_id=1, source_target_pairs={{0,16},{4,20},{8,24},{12,28},{16,0},{20,4},{24,8},{28,12},{1,17},{... | collective-permute-start | bytes 589832 | tf_op jit(solution)/shard_map/ppermute | solution.py:430
  35.7 9.6 %collective-permute-start.9 = (f32[64,768]{1,0:T(8,128)S(1)}, f32[64,768]{1,0:T(8,128)S(1)}, u32[]{:S(2)}, u32[]{:S(2)}) collective-permute-start(f32[64,768]{1,0:T(8,128)S(1)} %get-tuple-element.67.refs_0_), channel_id=1, source_target_pairs={{0,8},{4,12},{8,0},{12,4},{16,24},{20,28},{24,16},{28,20},{1,9},{5... | collective-permute-start | bytes 589832 | tf_op jit(solution)/shard_map/ppermute | solution.py:430
  45.3 12.6 %collective-permute-start.12 = (f32[64,768]{1,0:T(8,128)S(1)}, f32[64,768]{1,0:T(8,128)S(1)}, u32[]{:S(2)}, u32[]{:S(2)}) collective-permute-start(f32[64,768]{1,0:T(8,128)S(1)} %get-tuple-element.75.refs_0_), channel_id=1, source_target_pairs={{0,16},{4,20},{8,24},{12,28},{16,0},{20,4},{24,8},{28,12},{1,17},{... | collective-permute-start | bytes 589832 | tf_op jit(solution)/shard_map/ppermute | solution.py:430
  45.6 12.4 %collective-permute-start.13 = (f32[64,768]{1,0:T(8,128)S(1)}, f32[64,768]{1,0:T(8,128)S(1)}, u32[]{:S(2)}, u32[]{:S(2)}) collective-permute-start(f32[64,768]{1,0:T(8,128)S(1)} %get-tuple-element.76.refs_2_), channel_id=1, source_target_pairs={{0,8},{4,12},{8,0},{12,4},{16,24},{20,28},{24,16},{28,20},{1,9},{5... | collective-permute-start | bytes 589832 | tf_op jit(solution)/shard_map/ppermute | solution.py:430
  46.3 8.6 %collective-permute-start.14 = (f32[64,384]{1,0:T(8,128)S(1)}, f32[64,384]{1,0:T(8,128)S(1)}, u32[]{:S(2)}, u32[]{:S(2)}) collective-permute-start(f32[64,384]{1,0:T(8,128)S(1)} %get-tuple-element.78), channel_id=1, source_target_pairs={{0,1},{1,2},{2,3},{3,0},{4,5},{5,6},{6,7},{7,4},{8,9},{9,10},{10,1... | collective-permute-start | bytes 294920 | tf_op jit(solution)/shard_map/ppermute | solution.py:444
  48.4 9.1 %collective-permute-start.15 = (f32[64,384]{1,0:T(8,128)S(1)}, f32[64,384]{1,0:T(8,128)S(1)}, u32[]{:S(2)}, u32[]{:S(2)}) collective-permute-start(f32[64,384]{1,0:T(8,128)S(1)} %get-tuple-element.79), channel_id=1, source_target_pairs={{0,2},{1,3},{2,0},{3,1},{4,6},{5,7},{6,4},{7,5},{8,10},{9,11},{10,... | collective-permute-start | bytes 294920 | tf_op jit(solution)/shard_map/ppermute | solution.py:444
  51.7 6.2 %collective-permute-start.16 = (f32[64,384]{1,0:T(8,128)S(1)}, f32[64,384]{1,0:T(8,128)S(1)}, u32[]{:S(2)}, u32[]{:S(2)}) collective-permute-start(f32[64,384]{1,0:T(8,128)S(1)} %get-tuple-element.80), channel_id=1, source_target_pairs={{0,3},{1,0},{2,1},{3,2},{4,7},{5,4},{6,5},{7,6},{8,11},{9,8},{10,9... | collective-permute-start | bytes 294920 | tf_op jit(solution)/shard_map/ppermute | solution.py:444
  58.1 4.7 %collective-permute-start.17 = (f32[64,1536]{1,0:T(8,128)S(1)}, f32[64,1536]{1,0:T(8,128)S(1)}, u32[]{:S(2)}, u32[]{:S(2)}) collective-permute-start(f32[64,1536]{1,0:T(8,128)S(1)} %get-tuple-element.83.refs_1_), channel_id=1, source_target_pairs={{0,4},{4,0},{8,12},{12,8},{16,20},{20,16},{24,28},{28,24},{1,5},{5... | collective-permute-start | bytes 1179656 | tf_op jit(solution)/shard_map/ppermute | solution.py:430
  58.1 18.6 %collective-permute-start.20 = (f32[64,384]{1,0:T(8,128)S(1)}, f32[64,384]{1,0:T(8,128)S(1)}, u32[]{:S(2)}, u32[]{:S(2)}) collective-permute-start(f32[64,384]{1,0:T(8,128)S(1)} %get-tuple-element.91.refs_5_), channel_id=1, source_target_pairs={{0,1},{1,2},{2,3},{3,0},{4,5},{5,6},{6,7},{7,4},{8,9},{9,10},{10,1... | collective-permute-start | bytes 294920 | tf_op jit(solution)/shard_map/ppermute | solution.py:444
  60.3 16.4 %collective-permute-start.21 = (f32[64,384]{1,0:T(8,128)S(1)}, f32[64,384]{1,0:T(8,128)S(1)}, u32[]{:S(2)}, u32[]{:S(2)}) collective-permute-start(f32[64,384]{1,0:T(8,128)S(1)} %get-tuple-element.91.refs_5_), channel_id=1, source_target_pairs={{0,2},{1,3},{2,0},{3,1},{4,6},{5,7},{6,4},{7,5},{8,10},{9,11},{10,... | collective-permute-start | bytes 294920 | tf_op jit(solution)/shard_map/ppermute | solution.py:444
  61.5 15.2 %collective-permute-start.22 = (f32[64,384]{1,0:T(8,128)S(1)}, f32[64,384]{1,0:T(8,128)S(1)}, u32[]{:S(2)}, u32[]{:S(2)}) collective-permute-start(f32[64,384]{1,0:T(8,128)S(1)} %get-tuple-element.91.refs_5_), channel_id=1, source_target_pairs={{0,3},{1,0},{2,1},{3,2},{4,7},{5,4},{6,5},{7,6},{8,11},{9,8},{10,9... | collective-permute-start | bytes 294920 | tf_op jit(solution)/shard_map/ppermute | solution.py:444
  63.6 6.4 %collective-permute-start.18 = (f32[64,64]{1,0:T(8,128)S(1)}, f32[64,64]{1,0:T(8,128)S(1)}, u32[]{:S(2)}, u32[]{:S(2)}) collective-permute-start(f32[64,64]{1,0:T(8,128)S(1)} %get-tuple-element.85.refs_0_), channel_id=1, source_target_pairs={{0,1},{1,0},{2,3},{3,2},{4,5},{5,4},{6,7},{7,6},{8,9},{9,8},{10,11... | collective-permute-start | bytes 49160 | tf_op jit(solution)/shard_map/ppermute | solution.py:430
  70.0 5.0 %collective-permute-start.19 = (f32[64,64]{1,0:T(8,128)S(1)}, f32[64,64]{1,0:T(8,128)S(1)}, u32[]{:S(2)}, u32[]{:S(2)}) collective-permute-start(f32[64,64]{1,0:T(8,128)S(1)} %get-tuple-element.87.refs_0_), channel_id=1, source_target_pairs={{0,2},{1,3},{2,0},{3,1},{4,6},{5,7},{6,4},{7,5},{8,10},{9,11},{10,... | collective-permute-start | bytes 49160 | tf_op jit(solution)/shard_map/ppermute | solution.py:430

commit v3 on v2

--- a/solution.py
+++ b/solution.py
@@ -5,6 +5,7 @@
 from jax.experimental.pallas import tpu as pltpu
 from jax.sharding import PartitionSpec as P
 
+
 precise = lax.Precision.HIGHEST
 f32 = jnp.float32
 bf16 = jnp.bfloat16
@@ -41,7 +42,7 @@
     return wanted
 
 
-def small_call(kernel, out, *operands, name, carry=None, flops=1_000_000, moved=1_000_000, mib=8):
+def small_call(kernel, out, *operands, carry=None, flops=1_000_000, moved=1_000_000, mib=8):
     extra = {}
     body = kernel
     if carry is not None:
@@ -61,12 +62,7 @@
             kernel(*refs[:count], *refs[count + 1 : -1])
 
     return pl.pallas_call(
-        body,
-        out_shape=out,
-        compiler_params=params(mib),
-        cost_estimate=cost(flops, moved),
-        name=name,
-        **extra,
+        body, out_shape=out, compiler_params=params(mib), cost_estimate=cost(flops, moved), **extra
     )(*operands)
 
 
@@ -134,7 +130,7 @@
     return tiles
 
 
-def eliminate_kernel(a_ref, b_ref, c_ref, d_ref, band_ref, inverse_ref, head_ref):
+def eliminate_kernel(a_ref, b_ref, c_ref, d_ref, band_ref, again_ref, inverse_ref, head_ref):
     order = band_ref.shape[0]
     lane = lax.broadcasted_iota(jnp.int32, (8, order), 1)
     sub = lax.broadcasted_iota(jnp.int32, (8, order), 0)
@@ -147,9 +143,9 @@
         diagonal = jnp.sum(jnp.where(lane == row_at, tiles[t], 0.0), axis=1, keepdims=True)
         length = jnp.sqrt(diagonal)
         scaled = tiles[t] / length
-        band_ref[8 * t : 8 * t + 8, :] = jnp.where(
-            lane > row_at, -scaled, jnp.where(lane == row_at, -length, 0.0)
-        )
+        band = jnp.where(lane > row_at, -scaled, jnp.where(lane == row_at, -length, 0.0))
+        band_ref[8 * t : 8 * t + 8, :] = band
+        again_ref[8 * t : 8 * t + 8, :] = band
         inverse_ref[8 * t : 8 * t + 8, :] = jnp.where(
             lane < row_at, -scaled, jnp.where(lane == row_at, -1.0 / length, 0.0)
         )
@@ -164,30 +160,42 @@
     out_ref[...] = -dot(jnp.concatenate(tiles, 0), inverse_ref[...])
 
 
-def down_kernel(first_ref, second_ref, a_ref, out_ref, kept_ref):
+def down_kernel(first_ref, second_ref, a_ref, out_ref, kept_ref, sems):
     width = first_ref.shape[0]
+    columns = a_ref.shape[1]
+    count = sems.shape[0]
+    size = columns // count
+
+    def load(i):
+        part = pl.ds(pl.multiple_of(i * size, size), size)
+        return pltpu.make_async_copy(a_ref.at[:, part], kept_ref.at[:, part], sems.at[i])
+
+    for i in range(count):
+        load(i).start()
     kh, kl = split(jnp.concatenate([first_ref[...], second_ref[...]], 1))
     left = jnp.concatenate([kh, kl], 0)
-    value = a_ref[...]
-    kept_ref[...] = value
-    ah, al = split(value)
-    term = fast(left, ah) + fast(left, al)
-    out_ref[...] = term[:width] + term[width:]
+
+    @pl.loop(0, count)
+    def _(i):
+        load(i).wait()
+        part = pl.ds(pl.multiple_of(i * size, size), size)
+        ah, al = split(kept_ref[:, part])
+        term = fast(left, ah) + fast(left, al)
+        out_ref[:, part] = term[:width] + term[width:]
 
 
 def product_down(first, second, a):
     rows, columns = a.shape
-    width, half = first.shape
-    bc = block_of(columns, 512)
-    part = pl.BlockSpec((width, half), lambda i: (0, 0))
-    block = pl.BlockSpec((rows, bc), lambda i: (0, i))
+    width = first.shape[0]
+    size = block_of(columns, 256)
+    whole = pl.BlockSpec(memory_space=pltpu.VMEM)
     return pl.pallas_call(
         down_kernel,
-        grid=(columns // bc,),
-        in_specs=[part, part, block],
-        out_specs=(pl.BlockSpec((width, bc), lambda i: (0, i)), block),
+        in_specs=[whole, whole, pl.BlockSpec(memory_space=pltpu.HBM)],
+        out_specs=(whole, whole),
         out_shape=(shape(width, columns), shape(rows, columns)),
-        compiler_params=params(22),
+        scratch_shapes=[pltpu.SemaphoreType.DMA((columns // size,))],
+        compiler_params=params(12),
         cost_estimate=cost(8 * rows * columns * width, 4 * rows * columns),
         name="product_down",
     )(first, second, pltpu.with_memory_space_constraint(a, pltpu.HBM))
@@ -355,63 +363,101 @@
     )
 
 
-def corrected(st, cm, xt, kt):
-    return dot(st, xt) - 0.5 * dot(cm, kt)
-
-
-def right_kernel(part_ref, more_ref, st_ref, xct_ref, kct_ref, cm_ref, right_ref):
+def wide_kernel(st_ref, xct_ref, kct_ref, first_ref, second_ref, band_ref, x_ref, k_ref, rows_ref):
     width, columns = kct_ref.shape
     st = st_ref[...]
-    cm = dot(dot(st, part_ref[...] + more_ref[...]), st.T)
-    cm_ref[...] = cm
     chunk = block_of(columns, 512)
     for c in range(0, columns, chunk):
-        k = kct_ref[:, c : c + chunk]
-        wh, wl = split(corrected(st, cm, xct_ref[:, c : c + chunk], k))
-        kh, kl = split(k)
-        right_ref[:, c : c + chunk] = jnp.concatenate([wh, kh, wl, kl], 0)
-
-
-def left_kernel(first_ref, second_ref, band_ref, st_ref, cm_ref, *refs):
-    chunks, left_ref, krt_ref = refs[:-2], refs[-2], refs[-1]
-    width, half = first_ref.shape
+        for ref, value in (
+            (x_ref, dot(st, xct_ref[:, c : c + chunk])),
+            (k_ref, kct_ref[:, c : c + chunk]),
+        ):
+            ref[:, c : c + chunk] = jnp.concatenate(split(value), 0)
+    half = first_ref.shape[1]
+    rows_ref[:, :half] = first_ref[...]
+    rows_ref[:, half:] = second_ref[...]
+
+    @pl.when(lax.axis_index("row") == 0)
+    def _():
+        rows_ref[:, :width] = rows_ref[:, :width] - band_ref[...].T
+
+
+def four_products(left, right_ref, start, size):
+    width = left.shape[1] // 2
+    high = right_ref[:width, pl.ds(start, size)]
+    low = right_ref[width:, pl.ds(start, size)]
+    return fast(
+        jnp.concatenate([left, left], 1), jnp.concatenate([high, high, low, low], 0)
+    )
+
+
+def near_kernel(rows_ref, right_ref, a_ref, out_ref, left_ref):
+    rows, columns = a_ref.shape
+    deep = block_of(rows, 512)
+    for r in range(0, rows, deep):
+        left_ref[r : r + deep, :] = jnp.concatenate(split(rows_ref[:, r : r + deep].T), 1)
+    chunk = block_of(columns, 512)
+
+    @pl.loop(0, columns // chunk)
+    def _(i):
+        c = pl.multiple_of(i * chunk, chunk)
+        for r in range(0, rows, deep):
+            out_ref[r : r + deep, pl.ds(c, chunk)] = a_ref[r : r + deep, pl.ds(c, chunk)] - (
+                four_products(left_ref[r : r + deep, :], right_ref, c, chunk)
+            )
+
+
+def subtract_near(krt, right, a):
+    rows, columns = a.shape
+    width = krt.shape[0]
+    whole = pl.BlockSpec(memory_space=pltpu.VMEM)
+    return pl.pallas_call(
+        near_kernel,
+        in_specs=[whole] * 3,
+        out_specs=whole,
+        out_shape=shape(rows, columns),
+        input_output_aliases={2: 0},
+        scratch_shapes=[pltpu.VMEM((rows, 2 * width), bf16)],
+        compiler_params=params(12),
+        cost_estimate=cost(8 * rows * columns * width, 8 * rows * columns),
+        name="subtract_near",
+    )(krt, right, a)
+
+
+def core_kernel(part_ref, more_ref, st_ref, krt_ref, out_ref):
+    st = st_ref[...]
+    cm = dot(dot(st, part_ref[...] + more_ref[...]), st.T)
+    out_ref[...] = dot(cm, krt_ref[...])
+
+
+def left_kernel(st_ref, core_ref, *refs):
+    chunks, left_ref = refs[:-1], refs[-1]
     pieces = len(chunks)
     size = chunks[0].shape[1]
-    krt_ref[:, :half] = first_ref[...]
-    krt_ref[:, half:] = second_ref[...]
-
-    @pl.when(lax.axis_index("row") == 0)
-    def _():
-        krt_ref[:, :width] = krt_ref[:, :width] - band_ref[...].T
-
-    st, cm = st_ref[...], cm_ref[...]
+    st = st_ref[...]
     col = lax.axis_index("col")
     for at, ref in enumerate(chunks):
         start = pl.multiple_of(lax.rem(col + pieces - at, pieces) * size, size)
-        k = krt_ref[:, pl.ds(start, size)]
-        both = jnp.concatenate([k, corrected(st, cm, ref[...], k)], 0)
-        left_ref[pl.ds(start, size), :] = jnp.concatenate(split(both.T), 1)
-
-
-def subtract_kernel(left_ref, right_ref, a_ref, out_ref):
-    width = left_ref.shape[1] // 2
-    left = left_ref[...]
-    left = jnp.concatenate([left, left], 1)
+        value = dot(st, ref[...]) - core_ref[:, pl.ds(start, size)]
+        left_ref[pl.ds(start, size), :] = jnp.concatenate(split(value.T), 1)
+
+
+def far_kernel(left_ref, right_ref, a_ref, out_ref):
     columns = a_ref.shape[1]
     chunk = block_of(columns, 512)
+    left = left_ref[...]
     for c in range(0, columns, chunk):
-        high = right_ref[:width, c : c + chunk]
-        low = right_ref[width:, c : c + chunk]
-        both = jnp.concatenate([high, high, low, low], 0)
-        out_ref[:, c : c + chunk] = a_ref[:, c : c + chunk] - fast(left, both)
-
-
-def subtract(left, right, a):
+        out_ref[:, c : c + chunk] = a_ref[:, c : c + chunk] - four_products(
+            left, right_ref, c, chunk
+        )
+
+
+def subtract_far(left, right, a):
     rows, columns = a.shape
     deep = left.shape[1]
     br = block_of(rows, 256)
     return pl.pallas_call(
-        subtract_kernel,
+        far_kernel,
         grid=(rows // br,),
         in_specs=[
             pl.BlockSpec((br, deep), lambda i: (i, 0)),
@@ -422,7 +468,7 @@
         out_shape=shape(rows, columns),
         compiler_params=params(22),
         cost_estimate=cost(4 * rows * columns * deep, 8 * rows * columns),
-        name="subtract",
+        name="subtract_far",
     )(left, right, a)
 
 
@@ -454,9 +500,9 @@
         packed = shape(width, 2 * width)
         half = shape(width, rows // 2)
         first, second, partial = small_call(
-            open_kernel, (half, half, packed), panel.T, name="open", flops=100_000_000, mib=12
-        )
-        partial = small_call(add_kernel, packed, partial, flip(partial, 1, row_size), name="add_cores")
+            open_kernel, (half, half, packed), panel.T, flops=100_000_000, mib=12
+        )
+        partial = small_call(add_kernel, packed, partial, flip(partial, 1, row_size))
         if row_size == 8:
             terms = [partial] + [flip(partial, bit, row_size) for bit in (2, 4, 6)]
         else:
@@ -473,14 +519,7 @@
             by_x = from_sources(first, col_size, [0], 2)
             by_y = from_sources(second, col_size, [0], 4)
             one, two, resident = small_call(
-                merge_first_kernel,
-                (half, half),
-                first,
-                second,
-                by_x,
-                by_y,
-                name="merge_first",
-                carry=resident,
+                merge_first_kernel, (half, half), first, second, by_x, by_y, carry=resident
             )
             more_x = from_sources(two, col_size, [0, 4], 2)
             more_y = from_sources(one, col_size, [0, 2], 4)
@@ -493,35 +532,18 @@
                 held = held + from_sources(held, col_size, reached, bit)
                 reached = reached + [r ^ bit for r in reached]
                 bit *= 2
-        band, band_inverse, head, resident = small_call(
-            eliminate_kernel,
-            (small, small, small),
-            *terms,
-            name="eliminate",
-            flops=50_000_000,
-            carry=resident,
-        )
-        keep, give, resident = fix_down(raw, band, resident)
+        band, again, band_inverse, head, resident = small_call(
+            eliminate_kernel, (small, small, small, small), *terms, flops=50_000_000, carry=resident
+        )
+        keep, give, resident = fix_down(raw, again, resident)
         if row_size == 8:
             held, resident = small_call(
-                join_kernel,
-                shape(width, rows),
-                one,
-                more_y,
-                two,
-                more_x,
-                name="merge_second",
-                carry=resident,
+                join_kernel, shape(width, rows), one, more_y, two, more_x, carry=resident
             )
         other = flip(held, 1, row_size)
         quarter = shape(width, columns // 4)
         a, b, resident = small_call(
-            halve_kernel,
-            (quarter, quarter),
-            keep,
-            flip(give, 1, row_size),
-            name="add_halves",
-            carry=resident,
+            halve_kernel, (quarter, quarter), keep, flip(give, 1, row_size), carry=resident
         )
         bits = []
         bit = 2
@@ -529,46 +551,20 @@
             bits.append(bit)
             bit *= 2
         for forward, backward in list(zip(bits, bits[::-1]))[:-1]:
-            ra, rb = flip(a, forward, row_size), flip(b, backward, row_size)
+            ra = flip(a, forward, row_size)
+            rb = flip(b, backward, row_size)
             if bits[0] == forward:
                 pieces = 1 if (rows // col_size) % 128 else col_size
-                kct, *chunks, resident = product_across(held, other, band, resident, pieces)
+                kct, *chunks, resident = product_across(held, other, again, resident, pieces)
             a, b, resident = small_call(
-                pair_kernel, (quarter, quarter), a, ra, b, rb, name="add_chips", carry=resident
+                pair_kernel, (quarter, quarter), a, ra, b, rb, carry=resident
             )
         ra, rb = flip(a, bits[-1], row_size), flip(b, bits[0], row_size)
         st, resident = small_call(
-            invert_kernel,
-            small,
-            head,
-            band,
-            band_inverse,
-            name="invert",
-            flops=50_000_000,
-            carry=resident,
-        )
-        if pieces == 1:
-            whole = [lax.psum(chunks[0], "col")]
-        else:
-            received = [shift(chunks[by], by, col_size) for by in range(1, col_size)]
-            mine, resident = small_call(
-                add_kernel,
-                shape(width, rows // col_size),
-                chunks[0],
-                *received,
-                name="add_line",
-                carry=resident,
-            )
-            whole = [mine] + [shift(mine, by, col_size) for by in range(1, col_size)]
+            invert_kernel, small, head, again, band_inverse, flops=50_000_000, carry=resident
+        )
         summed, resident = small_call(
-            join_kernel,
-            shape(width, columns // 2),
-            a,
-            ra,
-            b,
-            rb,
-            name="add_last",
-            carry=resident,
+            join_kernel, shape(width, columns // 2), a, ra, b, rb, carry=resident
         )
         xct, inner, resident = small_call(
             inner_kernel,
@@ -576,54 +572,65 @@
             kct,
             summed,
             flip(summed, 1, row_size),
-            name="inner",
             carry=resident,
         )
         bit = 1
+        others = []
         while bit < col_size // 2:
-            inner, resident = small_call(
-                add_kernel,
-                small,
-                inner,
-                flip(inner, bit, col_size, "col"),
-                name="add_inner",
-                carry=resident,
+            others.append(bit)
+            bit *= 2
+        first_inner = flip(inner, 1, col_size, "col")
+        if pieces == 1:
+            whole = [lax.psum(chunks[0], "col")]
+        else:
+            received = [shift(chunks[by], by, col_size) for by in range(1, col_size)]
+            mine, resident = small_call(
+                add_kernel, shape(width, rows // col_size), chunks[0], *received, carry=resident
             )
-            bit *= 2
+            whole = [mine] + [shift(mine, by, col_size) for by in range(1, col_size)]
+        for at in others:
+            got = first_inner if at == 1 else flip(inner, at, col_size, "col")
+            inner, resident = small_call(add_kernel, small, inner, got, carry=resident)
         more = flip(inner, bit, col_size, "col")
-        cm, right, resident = small_call(
-            right_kernel,
-            (small, shape(4 * width, columns, dtype=bf16)),
-            inner,
-            more,
+        xparts, kparts, krt, resident = small_call(
+            wide_kernel,
+            (
+                shape(2 * width, columns, dtype=bf16),
+                shape(2 * width, columns, dtype=bf16),
+                shape(width, rows),
+            ),
             st,
             xct,
             kct,
-            name="right",
+            first,
+            second,
+            again,
             mib=12,
             carry=resident,
         )
-        left, _, resident = small_call(
+        resident = subtract_near(krt, xparts, resident)
+        core, resident = small_call(
+            core_kernel, shape(width, rows), inner, more, st, krt, carry=resident
+        )
+        left, resident = small_call(
             left_kernel,
-            (shape(rows, 4 * width, dtype=bf16), shape(width, rows)),
-            first,
-            second,
-            band,
+            shape(rows, 2 * width, dtype=bf16),
             st,
-            cm,
+            core,
             *whole,
-            name="left",
             mib=12,
             carry=resident,
         )
-        return subtract(left, right, resident), band
+        return subtract_far(left, kparts, resident), band
 
     return body
 
 
 def solution(mesh):
+    body = body_of(mesh.shape["row"], mesh.shape["col"])
+
     return jax.shard_map(
-        body_of(mesh.shape["row"], mesh.shape["col"]),
+        body,
         mesh=mesh,
         in_specs=(P("row", "col"), P("row", None)),
         out_specs=(P("row", "col"), P()),

time: 87.4 us -> 83.8 us (0.959)
  waiting for transfers between devices: 17.9 us -> 14.2 us
    ppermute x13, waiting for transfers between devices: 14 us -> 9.41 us  [flip(): return lax.ppermute(value, axis, [(i, i ^ bit) for i in range(size)])]
    ppermute x13, starting transfers between devices: 10.4 us -> 11.7 us  [flip(): return lax.ppermute(value, axis, [(i, i ^ bit) for i in range(size)])]
    ppermute x6, waiting for transfers between devices: 3.87 us -> 4.82 us  [shift(): lax.ppermute(piece, 'col', [(i, (i + by) % size) for i in range(size)])]
    pallas_call x2 -> x3, Pallas kernels: 19.1 us -> 19.6 us  [the longest x1 7.78 us: subtract_far(): pl.pallas_call(far_kernel, grid=(rows // br,), in_specs=[pl.BlockSpec((br...]
    pallas_call x14 -> x15, Pallas kernels: 9.48 us -> 9.15 us  [small_call(): pl.pallas_call(body, out_shape=out, compiler_params=params(mib), cost_est...]
  transfers between devices with their start and end apart: 23 -> 23, of which waited for: 9 -> 10; matrix products, arithmetic and copies ran while one was open for 0% -> 0% of each run, Pallas kernels for 29% -> 33%
where the time goes in v3:
time: 83.8 us; the launch traced here: 83.6 us
  Pallas kernels  36.7 us (44%)
  starting transfers between devices  30.8 us (37%)
  waiting for transfers between devices  14.2 us (17%)
  local copies, waits for them, and re-layouts  0.99 us (1%)
  between operations  0.89 us (1%)
    ppermute x13, starting transfers between devices, flip(): return lax.ppermute(value, axis, [(i, i ^ bit) for i in range(size)])  11.7 us
    ppermute x6, starting transfers between devices, shift(): lax.ppermute(piece, 'col', [(i, (i + by) % size) for i in range(size)])  9.6 us
    ppermute x4, starting transfers between devices, from_sources(): return lax.ppermute(piece, ('row', 'col'), pairs)  9.51 us
    ppermute x13, waiting for transfers between devices, flip(): return lax.ppermute(value, axis, [(i, i ^ bit) for i in range(size)])  9.41 us
    pallas_call x15, Pallas kernels, small_call(): pl.pallas_call(body, out_shape=out, compiler_params=params(mib), cost_est...  9.15 us
    pallas_call x1, Pallas kernels, subtract_far(): pl.pallas_call(far_kernel, grid=(rows // br,), in_specs=[pl.BlockSpec((br...  7.78 us
    pallas_call x1, Pallas kernels, product_down(): pl.pallas_call(down_kernel, in_specs=[whole, whole, pl.BlockSpec(memory_s...  7.06 us
    pallas_call x1, Pallas kernels, product_across(): pl.pallas_call(across_kernel, grid=(pieces,), in_specs=[part, part, pl.Bl...  7 us
  transfers between devices with their start and end apart: 23, of which 10 were waited for; matrix products, arithmetic and copies ran while one was open for 0% of the time, Pallas kernels for 33%

profile of v3, /device:TPU:0, one launch (start us, length us, event | category | flops | bytes accessed | tf_op | source)
XLA Modules:
  0.0 83.6 jit_solution(982915811684059191)
XLA Ops:
  0.6 0.0 copy-start
  0.6 1.0 %copy-done = f32[1536,64]{0,1:T(8,128)S(1)} copy-done((f32[1536,64]{0,1:T(8,128)S(1)}, f32[1536,64]{0,1:T(8,128)}, u32[]{:S(2)}) %copy-start) | copy-done | bytes 393240
  1.6 0.5 shard_map.41
  2.1 0.6 collective-permute-start
  2.7 0.9 %collective-permute-done.refs_1_ = f32[64,128]{1,0:T(8,128)S(1)} collective-permute-done((f32[64,128]{1,0:T(8,128)S(1)}, f32[64,128]{1,0:T(8,128)S(1)}, u32[]{:S(2)}, u32[]{:S(2)}) %collective-permute-start) | collective-permute-done | bytes 32800 | tf_op jit(solution)/shard_map/ppermute | solution.py:476
  3.5 4.7 %collective-permute-start.4 = (f32[64,768]{1,0:T(8,128)S(1)}, f32[64,768]{1,0:T(8,128)S(1)}, u32[]{:S(2)}, u32[]{:S(2)}) collective-permute-start(f32[64,768]{1,0:T(8,128)S(1)} %get-tuple-element.56.first_ref.refs_0_.refs_3_), channel_id=1, source_target_pairs={{0,8},{4,12},{9,1},{13,5},{18,26},{22,30},{27,19},{31,23}} | collective-permute-start | bytes 589832 | tf_op jit(solution)/shard_map/ppermute | solution.py:486
  8.3 1.3 %collective-permute-start.5 = (f32[64,768]{1,0:T(8,128)S(1)}, f32[64,768]{1,0:T(8,128)S(1)}, u32[]{:S(2)}, u32[]{:S(2)}) collective-permute-start(f32[64,768]{1,0:T(8,128)S(1)} %get-tuple-element.57.second_ref.refs_1_.refs_4_), channel_id=1, source_target_pairs={{0,16},{4,20},{9,25},{13,29},{18,2},{22,6},{27,11},{31,15}} | collective-permute-start | bytes 589832 | tf_op jit(solution)/shard_map/ppermute | solution.py:486
  9.6 7.1 %product_down.1 = (f32[64,3072]{1,0:T(8,128)S(1)}, f32[1536,3072]{1,0:T(8,128)S(1)}) custom-call(f32[64,768]{1,0:T(8,128)S(1)} %get-tuple-element.56.first_ref.refs_0_.refs_3_, f32[64,768]{1,0:T(8,128)S(1)} %get-tuple-element.57.second_ref.refs_1_.refs_4_, f32[1536,3072]{1,0:T(8,128)} %a_ref.1), custom_call_target="tpu_custom_call" | custom-call | flops 2415919104 | bytes 18874368 | tf_op jit(solution)/shard_map/product_down/pallas_call | solution.py:192
  16.6 0.0 collective-permute-done.4.refs_2_
  16.6 0.0 collective-permute-done.5.refs_3_
  16.7 1.8 %collective-permute-start.7 = (f32[64,768]{1,0:T(8,128)S(1)}, f32[64,768]{1,0:T(8,128)S(1)}, u32[]{:S(2)}, u32[]{:S(2)}) collective-permute-start(f32[64,768]{1,0:T(8,128)S(1)} %get-tuple-element.67.refs_0_), channel_id=1, source_target_pairs={{0,16},{4,20},{8,24},{12,28},{9,25},{13,29},{1,17},{5,21},{18,2},{... | collective-permute-start | bytes 589832 | tf_op jit(solution)/shard_map/ppermute | solution.py:486
  18.5 1.7 %collective-permute-start.8 = (f32[64,768]{1,0:T(8,128)S(1)}, f32[64,768]{1,0:T(8,128)S(1)}, u32[]{:S(2)}, u32[]{:S(2)}) collective-permute-start(f32[64,768]{1,0:T(8,128)S(1)} %get-tuple-element.68.refs_2_), channel_id=1, source_target_pairs={{0,8},{4,12},{16,24},{20,28},{9,1},{13,5},{25,17},{29,21},{18,26},... | collective-permute-start | bytes 589832 | tf_op jit(solution)/shard_map/ppermute | solution.py:486
  20.2 0.1 collective-permute-start.3
  20.3 0.8 collective-permute-start.2
  21.1 2.6 %collective-permute-start.1 = (f32[64,128]{1,0:T(8,128)S(1)}, f32[64,128]{1,0:T(8,128)S(1)}, u32[]{:S(2)}, u32[]{:S(2)}) collective-permute-start(f32[64,128]{1,0:T(8,128)S(1)} %shard_map.42.refs_0_), channel_id=1, source_target_pairs={{0,8},{4,12},{8,0},{12,4},{16,24},{20,28},{24,16},{28,20},{1,9},{5... | collective-permute-start | bytes 98312 | tf_op jit(solution)/shard_map/ppermute | solution.py:476
  23.8 1.7 %collective-permute-done.3.refs_3_ = f32[64,128]{1,0:T(8,128)S(1)} collective-permute-done((f32[64,128]{1,0:T(8,128)S(1)}, f32[64,128]{1,0:T(8,128)S(1)}, u32[]{:S(2)}, u32[]{:S(2)}) %collective-permute-start.3) | collective-permute-done | bytes 32800 | tf_op jit(solution)/shard_map/ppermute | solution.py:476
  25.4 0.0 collective-permute-done.2.refs_2_
  25.4 0.3 collective-permute-done.1.refs_1_
  25.8 2.7 %shard_map.44 = (f32[64,64]{1,0:T(8,128)}, f32[64,64]{1,0:T(8,128)S(1)}, f32[64,64]{1,0:T(8,128)S(1)}, f32[64,64]{1,0:T(8,128)S(1)}, f32[1536,3072]{1,0:T(8,128)S(1)}) custom-call(f32[64,128]{1,0:T(8,128)S(1)} %shard_map.42.refs_0_, f32[64,128]{1,0:T(8,128)S(1)} %collective-permute-done.1.refs_1_, ...), custom_call_target="tpu_custom_call", output_to_operand_aliasing={{4}: (4, {})} | custom-call | flops 50000000 | bytes 1000000 | tf_op jit(solution)/shard_map/pallas_call | solution.py:64
  28.5 0.9 %fix_down.1 = (f32[64,1536]{1,0:T(8,128)S(1)}, f32[64,1536]{1,0:T(8,128)S(1)}, f32[1536,3072]{1,0:T(8,128)S(1)}) custom-call(f32[64,3072]{1,0:T(8,128)S(1)} %get-tuple-element.63.raw_ref, f32[64,64]{1,0:T(8,128)S(1)} %get-tuple-element.61.band_ref.refs_1_.refs_5_, f32[1536,3072]{1,0:T(8,128)S(1)} %get-tuple-element.64.top_ref), custom_call_target="tpu_custom_call", output_to_operand_aliasing={{2}: (2, {})} | custom-call | flops 150994944 | bytes 3145728 | tf_op jit(solution)/shard_map/fix_down/pallas_call | solution.py:232
  29.4 0.1 collective-permute-start.6
  29.4 0.0 collective-permute-done.7.refs_1_
  29.5 0.0 collective-permute-done.8.refs_3_
  29.5 0.5 collective-permute-start.11
  30.1 1.1 %collective-permute-done.6.refs_1_ = f32[64,1536]{1,0:T(8,128)S(1)} collective-permute-done((f32[64,1536]{1,0:T(8,128)S(1)}, f32[64,1536]{1,0:T(8,128)S(1)}, u32[]{:S(2)}, u32[]{:S(2)}) %collective-permute-start.6) | collective-permute-done | bytes 393248 | tf_op jit(solution)/shard_map/ppermute | solution.py:476
  31.2 1.8 %collective-permute-start.9 = (f32[64,768]{1,0:T(8,128)S(1)}, f32[64,768]{1,0:T(8,128)S(1)}, u32[]{:S(2)}, u32[]{:S(2)}) collective-permute-start(f32[64,768]{1,0:T(8,128)S(1)} %get-tuple-element.71.refs_0_), channel_id=1, source_target_pairs={{0,8},{4,12},{8,0},{12,4},{16,24},{20,28},{24,16},{28,20},{1,9},{5... | collective-permute-start | bytes 589832 | tf_op jit(solution)/shard_map/ppermute | solution.py:476
  33.0 1.1 %collective-permute-start.10 = (f32[64,768]{1,0:T(8,128)S(1)}, f32[64,768]{1,0:T(8,128)S(1)}, u32[]{:S(2)}, u32[]{:S(2)}) collective-permute-start(f32[64,768]{1,0:T(8,128)S(1)} %get-tuple-element.72.refs_2_), channel_id=1, source_target_pairs={{0,16},{4,20},{8,24},{12,28},{16,0},{20,4},{24,8},{28,12},{1,17},{... | collective-permute-start | bytes 589832 | tf_op jit(solution)/shard_map/ppermute | solution.py:476
  34.1 0.0 collective-permute-done.11.other_ref
  34.1 7.0 %product_across.1 = (f32[64,3072]{1,0:T(8,128)S(1)}, f32[64,384]{1,0:T(8,128)S(1)}, f32[64,384]{1,0:T(8,128)S(1)}, f32[64,384]{1,0:T(8,128)S(1)}, f32[64,384]{1,0:T(8,128)S(1)}, /*index=5*/f32[1536,3072]{1,0:T(8,128)S(1)}) custom-call(f32[64,1536]{1,0:T(8,128)S(1)} %get-tuple-element.73.held_ref, ...), custom_call_target="tpu_custom_call", output_to_operand_aliasing={{5}: (3, {})} | custom-call | flops 2415919104 | bytes 18874368 | tf_op jit(solution)/shard_map/product_across/pallas_call | solution.py:297
  41.1 0.0 collective-permute-done.9.refs_1_
  41.1 0.0 collective-permute-done.10.refs_3_
  41.2 1.0 %collective-permute-start.12 = (f32[64,768]{1,0:T(8,128)S(1)}, f32[64,768]{1,0:T(8,128)S(1)}, u32[]{:S(2)}, u32[]{:S(2)}) collective-permute-start(f32[64,768]{1,0:T(8,128)S(1)} %get-tuple-element.79.refs_0_), channel_id=1, source_target_pairs={{0,16},{4,20},{8,24},{12,28},{16,0},{20,4},{24,8},{28,12},{1,17},{... | collective-permute-start | bytes 589832 | tf_op jit(solution)/shard_map/ppermute | solution.py:476
  42.1 0.3 collective-permute-start.13
  42.5 2.3 %shard_map.48 = (f32[64,64]{1,0:T(8,128)S(1)}, f32[1536,3072]{1,0:T(8,128)S(1)}) custom-call(f32[64,64]{1,0:T(8,128)S(1)} %get-tuple-element.60.refs_0_, f32[64,64]{1,0:T(8,128)S(1)} %get-tuple-element.61.band_ref.refs_1_.refs_5_, f32[64,64]{1,0:T(8,128)S(1)} %get-tuple-element.62.refs_2_, ...), custom_call_target="tpu_custom_call", output_to_operand_aliasing={{1}: (3, {})} | custom-call | flops 50000000 | bytes 1000000 | tf_op jit(solution)/shard_map/pallas_call | solution.py:64
  44.7 2.9 %collective-permute-done.12.refs_1_ = f32[64,768]{1,0:T(8,128)S(1)} collective-permute-done((f32[64,768]{1,0:T(8,128)S(1)}, f32[64,768]{1,0:T(8,128)S(1)}, u32[]{:S(2)}, u32[]{:S(2)}) %collective-permute-start.12) | collective-permute-done | bytes 196640 | tf_op jit(solution)/shard_map/ppermute | solution.py:476
  47.6 0.6 collective-permute-done.13.refs_3_
  48.3 0.1 collective-permute-start.14
  48.4 1.2 %collective-permute-start.16 = (f32[64,384]{1,0:T(8,128)S(1)}, f32[64,384]{1,0:T(8,128)S(1)}, u32[]{:S(2)}, u32[]{:S(2)}) collective-permute-start(f32[64,384]{1,0:T(8,128)S(1)} %get-tuple-element.86), channel_id=1, source_target_pairs={{0,1},{1,2},{2,3},{3,0},{4,5},{5,6},{6,7},{7,4},{8,9},{9,10},{10,1... | collective-permute-start | bytes 294920 | tf_op jit(solution)/shard_map/ppermute | solution.py:490
  49.6 2.6 %collective-permute-start.17 = (f32[64,384]{1,0:T(8,128)S(1)}, f32[64,384]{1,0:T(8,128)S(1)}, u32[]{:S(2)}, u32[]{:S(2)}) collective-permute-start(f32[64,384]{1,0:T(8,128)S(1)} %get-tuple-element.87), channel_id=1, source_target_pairs={{0,2},{1,3},{2,0},{3,1},{4,6},{5,7},{6,4},{7,5},{8,10},{9,11},{10,... | collective-permute-start | bytes 294920 | tf_op jit(solution)/shard_map/ppermute | solution.py:490
  52.1 1.7 %collective-permute-start.18 = (f32[64,384]{1,0:T(8,128)S(1)}, f32[64,384]{1,0:T(8,128)S(1)}, u32[]{:S(2)}, u32[]{:S(2)}) collective-permute-start(f32[64,384]{1,0:T(8,128)S(1)} %get-tuple-element.88), channel_id=1, source_target_pairs={{0,3},{1,0},{2,1},{3,2},{4,7},{5,4},{6,5},{7,6},{8,11},{9,8},{10,9... | collective-permute-start | bytes 294920 | tf_op jit(solution)/shard_map/ppermute | solution.py:490
  53.9 0.0 collective-permute-done.14.refs_2_
  53.9 0.8 shard_map.50
  54.7 0.4 collective-permute-start.15
  55.1 0.9 %collective-permute-done.16.refs_1_ = f32[64,384]{1,0:T(8,128)S(1)} collective-permute-done((f32[64,384]{1,0:T(8,128)S(1)}, f32[64,384]{1,0:T(8,128)S(1)}, u32[]{:S(2)}, u32[]{:S(2)}) %collective-permute-start.16) | collective-permute-done | bytes 98336 | tf_op jit(solution)/shard_map/ppermute | solution.py:490
  56.0 3.7 %collective-permute-done.17.refs_2_ = f32[64,384]{1,0:T(8,128)S(1)} collective-permute-done((f32[64,384]{1,0:T(8,128)S(1)}, f32[64,384]{1,0:T(8,128)S(1)}, u32[]{:S(2)}, u32[]{:S(2)}) %collective-permute-start.17) | collective-permute-done | bytes 98336 | tf_op jit(solution)/shard_map/ppermute | solution.py:490
  59.7 0.2 collective-permute-done.18.refs_3_
  59.9 3.5 %collective-permute-start.22 = (f32[64,384]{1,0:T(8,128)S(1)}, f32[64,384]{1,0:T(8,128)S(1)}, u32[]{:S(2)}, u32[]{:S(2)}) collective-permute-start(f32[64,384]{1,0:T(8,128)S(1)} %get-tuple-element.98.refs_2_), channel_id=1, source_target_pairs={{0,3},{1,0},{2,1},{3,2},{4,7},{5,4},{6,5},{7,6},{8,11},{9,8},{10,9... | collective-permute-start | bytes 294920 | tf_op jit(solution)/shard_map/ppermute | solution.py:490
  63.4 0.4 collective-permute-start.21
  63.8 0.2 collective-permute-start.20
  64.0 0.0 collective-permute-done.15.refs_1_
  64.0 2.4 %collective-permute-start.19 = (f32[64,64]{1,0:T(8,128)S(1)}, f32[64,64]{1,0:T(8,128)S(1)}, u32[]{:S(2)}, u32[]{:S(2)}) collective-permute-start(f32[64,64]{1,0:T(8,128)S(1)} %get-tuple-element.91.refs_0_), channel_id=1, source_target_pairs={{0,2},{1,3},{2,0},{3,1},{4,6},{5,7},{6,4},{7,5},{8,10},{9,11},{10,... | collective-permute-start | bytes 49160 | tf_op jit(solution)/shard_map/ppermute | solution.py:476
  66.4 1.0 %shard_map.53 = (bf16[128,3072]{1,0:T(8,128)(2,1)S(1)}, bf16[128,3072]{1,0:T(8,128)(2,1)S(1)}, f32[64,1536]{1,0:T(8,128)S(1)}, f32[1536,3072]{1,0:T(8,128)S(1)}) custom-call(f32[64,64]{1,0:T(8,128)S(1)} %get-tuple-element.77.refs_0_.refs_2_, f32[64,3072]{1,0:T(8,128)S(1)} %get-tuple-element.92.refs_1_, ...), custom_call_target="tpu_custom_call", output_to_operand_aliasing={{3}: (6, {})} | custom-call | flops 1000000 | bytes 1000000 | tf_op jit(solution)/shard_map/pallas_call | solution.py:64
  67.4 4.8 %subtract_near.1.refs_4_ = f32[1536,3072]{1,0:T(8,128)S(1)} custom-call(f32[64,1536]{1,0:T(8,128)S(1)} %get-tuple-element.94.rows_ref.refs_3_, bf16[128,3072]{1,0:T(8,128)(2,1)S(1)} %get-tuple-element.95.right_ref, f32[1536,3072]{1,0:T(8,128)S(1)} %get-tuple-element.96.a_ref), custom_call_target="tpu_custom_call", output_to_operand_aliasing={{}: (2, {})} | custom-call | flops 2415919104 | bytes 37748736 | tf_op jit(solution)/shard_map/subtract_near/pallas_call | solution.py:414
  72.2 1.9 %collective-permute-done.19.refs_1_ = f32[64,64]{1,0:T(8,128)S(1)} collective-permute-done((f32[64,64]{1,0:T(8,128)S(1)}, f32[64,64]{1,0:T(8,128)S(1)}, u32[]{:S(2)}, u32[]{:S(2)}) %collective-permute-start.19) | collective-permute-done | bytes 16416 | tf_op jit(solution)/shard_map/ppermute | solution.py:476
  74.2 0.8 shard_map.54
  75.0 0.0 collective-permute-done.22.refs_5_
  75.0 0.0 collective-permute-done.21.refs_4_
  75.0 0.0 collective-permute-done.20.refs_3_
  75.0 0.8 shard_map.55
  75.8 7.8 %subtract_far.1 = f32[1536,3072]{1,0:T(8,128)} custom-call(bf16[1536,128]{1,0:T(8,128)(2,1)S(1)} %get-tuple-element.100.left_ref, bf16[128,3072]{1,0:T(8,128)(2,1)S(1)} %get-tuple-element.101.right_ref, f32[1536,3072]{1,0:T(8,128)S(1)} %get-tuple-element.102.a_ref), custom_call_target="tpu_custom_call" | custom-call | flops 2415919104 | bytes 37748736 | tf_op jit(solution)/shard_map/subtract_far/pallas_call | solution.py:459
  (8 shorter events, 0.3 us)
Async XLA Ops:
  0.6 1.0 %copy-start = (f32[1536,64]{0,1:T(8,128)S(1)}, f32[1536,64]{0,1:T(8,128)}, u32[]{:S(2)}) copy-start(f32[1536,64]{0,1:T(8,128)} %param.3) | copy-start | bytes 1179652
  2.1 1.4 %collective-permute-start = (f32[64,128]{1,0:T(8,128)S(1)}, f32[64,128]{1,0:T(8,128)S(1)}, u32[]{:S(2)}, u32[]{:S(2)}) collective-permute-start(f32[64,128]{1,0:T(8,128)S(1)} %get-tuple-element.53.refs_0_), channel_id=1, source_target_pairs={{0,4},{4,0},{8,12},{12,8},{16,20},{20,16},{24,28},{28,24},{1,5},{5... | collective-permute-start | bytes 98312 | tf_op jit(solution)/shard_map/ppermute | solution.py:476
  3.5 13.1 %collective-permute-start.4 = (f32[64,768]{1,0:T(8,128)S(1)}, f32[64,768]{1,0:T(8,128)S(1)}, u32[]{:S(2)}, u32[]{:S(2)}) collective-permute-start(f32[64,768]{1,0:T(8,128)S(1)} %get-tuple-element.56.first_ref.refs_0_.refs_3_), channel_id=1, source_target_pairs={{0,8},{4,12},{9,1},{13,5},{18,26},{22,30},{27,19},{31,23}} | collective-permute-start | bytes 589832 | tf_op jit(solution)/shard_map/ppermute | solution.py:486
  8.3 8.4 %collective-permute-start.5 = (f32[64,768]{1,0:T(8,128)S(1)}, f32[64,768]{1,0:T(8,128)S(1)}, u32[]{:S(2)}, u32[]{:S(2)}) collective-permute-start(f32[64,768]{1,0:T(8,128)S(1)} %get-tuple-element.57.second_ref.refs_1_.refs_4_), channel_id=1, source_target_pairs={{0,16},{4,20},{9,25},{13,29},{18,2},{22,6},{27,11},{31,15}} | collective-permute-start | bytes 589832 | tf_op jit(solution)/shard_map/ppermute | solution.py:486
  16.7 12.7 %collective-permute-start.7 = (f32[64,768]{1,0:T(8,128)S(1)}, f32[64,768]{1,0:T(8,128)S(1)}, u32[]{:S(2)}, u32[]{:S(2)}) collective-permute-start(f32[64,768]{1,0:T(8,128)S(1)} %get-tuple-element.67.refs_0_), channel_id=1, source_target_pairs={{0,16},{4,20},{8,24},{12,28},{9,25},{13,29},{1,17},{5,21},{18,2},{... | collective-permute-start | bytes 589832 | tf_op jit(solution)/shard_map/ppermute | solution.py:486
  18.5 11.0 %collective-permute-start.8 = (f32[64,768]{1,0:T(8,128)S(1)}, f32[64,768]{1,0:T(8,128)S(1)}, u32[]{:S(2)}, u32[]{:S(2)}) collective-permute-start(f32[64,768]{1,0:T(8,128)S(1)} %get-tuple-element.68.refs_2_), channel_id=1, source_target_pairs={{0,8},{4,12},{16,24},{20,28},{9,1},{13,5},{25,17},{29,21},{18,26},... | collective-permute-start | bytes 589832 | tf_op jit(solution)/shard_map/ppermute | solution.py:486
  20.2 5.2 %collective-permute-start.3 = (f32[64,128]{1,0:T(8,128)S(1)}, f32[64,128]{1,0:T(8,128)S(1)}, u32[]{:S(2)}, u32[]{:S(2)}) collective-permute-start(f32[64,128]{1,0:T(8,128)S(1)} %shard_map.42.refs_0_), channel_id=1, source_target_pairs={{0,24},{4,28},{8,16},{12,20},{16,8},{20,12},{24,0},{28,4},{1,25},{... | collective-permute-start | bytes 98312 | tf_op jit(solution)/shard_map/ppermute | solution.py:476
  20.3 5.2 %collective-permute-start.2 = (f32[64,128]{1,0:T(8,128)S(1)}, f32[64,128]{1,0:T(8,128)S(1)}, u32[]{:S(2)}, u32[]{:S(2)}) collective-permute-start(f32[64,128]{1,0:T(8,128)S(1)} %shard_map.42.refs_0_), channel_id=1, source_target_pairs={{0,16},{4,20},{8,24},{12,28},{16,0},{20,4},{24,8},{28,12},{1,17},{... | collective-permute-start | bytes 98312 | tf_op jit(solution)/shard_map/ppermute | solution.py:476
  21.1 4.7 %collective-permute-start.1 = (f32[64,128]{1,0:T(8,128)S(1)}, f32[64,128]{1,0:T(8,128)S(1)}, u32[]{:S(2)}, u32[]{:S(2)}) collective-permute-start(f32[64,128]{1,0:T(8,128)S(1)} %shard_map.42.refs_0_), channel_id=1, source_target_pairs={{0,8},{4,12},{8,0},{12,4},{16,24},{20,28},{24,16},{28,20},{1,9},{5... | collective-permute-start | bytes 98312 | tf_op jit(solution)/shard_map/ppermute | solution.py:476
  29.4 1.8 %collective-permute-start.6 = (f32[64,1536]{1,0:T(8,128)S(1)}, f32[64,1536]{1,0:T(8,128)S(1)}, u32[]{:S(2)}, u32[]{:S(2)}) collective-permute-start(f32[64,1536]{1,0:T(8,128)S(1)} %get-tuple-element.66), channel_id=1, source_target_pairs={{0,4},{4,0},{8,12},{12,8},{16,20},{20,16},{24,28},{28,24},{1,5},{5... | collective-permute-start | bytes 1179656 | tf_op jit(solution)/shard_map/ppermute | solution.py:476
  29.5 4.6 %collective-permute-start.11 = (f32[64,1536]{1,0:T(8,128)S(1)}, f32[64,1536]{1,0:T(8,128)S(1)}, u32[]{:S(2)}, u32[]{:S(2)}) collective-permute-start(f32[64,1536]{1,0:T(8,128)S(1)} %get-tuple-element.73.held_ref), channel_id=1, source_target_pairs={{0,4},{4,0},{8,12},{12,8},{16,20},{20,16},{24,28},{28,24},{1,5},{5... | collective-permute-start | bytes 1179656 | tf_op jit(solution)/shard_map/ppermute | solution.py:476
  31.2 9.9 %collective-permute-start.9 = (f32[64,768]{1,0:T(8,128)S(1)}, f32[64,768]{1,0:T(8,128)S(1)}, u32[]{:S(2)}, u32[]{:S(2)}) collective-permute-start(f32[64,768]{1,0:T(8,128)S(1)} %get-tuple-element.71.refs_0_), channel_id=1, source_target_pairs={{0,8},{4,12},{8,0},{12,4},{16,24},{20,28},{24,16},{28,20},{1,9},{5... | collective-permute-start | bytes 589832 | tf_op jit(solution)/shard_map/ppermute | solution.py:476
  33.0 8.1 %collective-permute-start.10 = (f32[64,768]{1,0:T(8,128)S(1)}, f32[64,768]{1,0:T(8,128)S(1)}, u32[]{:S(2)}, u32[]{:S(2)}) collective-permute-start(f32[64,768]{1,0:T(8,128)S(1)} %get-tuple-element.72.refs_2_), channel_id=1, source_target_pairs={{0,16},{4,20},{8,24},{12,28},{16,0},{20,4},{24,8},{28,12},{1,17},{... | collective-permute-start | bytes 589832 | tf_op jit(solution)/shard_map/ppermute | solution.py:476
  41.2 6.4 %collective-permute-start.12 = (f32[64,768]{1,0:T(8,128)S(1)}, f32[64,768]{1,0:T(8,128)S(1)}, u32[]{:S(2)}, u32[]{:S(2)}) collective-permute-start(f32[64,768]{1,0:T(8,128)S(1)} %get-tuple-element.79.refs_0_), channel_id=1, source_target_pairs={{0,16},{4,20},{8,24},{12,28},{16,0},{20,4},{24,8},{28,12},{1,17},{... | collective-permute-start | bytes 589832 | tf_op jit(solution)/shard_map/ppermute | solution.py:476
  42.1 6.1 %collective-permute-start.13 = (f32[64,768]{1,0:T(8,128)S(1)}, f32[64,768]{1,0:T(8,128)S(1)}, u32[]{:S(2)}, u32[]{:S(2)}) collective-permute-start(f32[64,768]{1,0:T(8,128)S(1)} %get-tuple-element.80.refs_2_), channel_id=1, source_target_pairs={{0,8},{4,12},{8,0},{12,4},{16,24},{20,28},{24,16},{28,20},{1,9},{5... | collective-permute-start | bytes 589832 | tf_op jit(solution)/shard_map/ppermute | solution.py:476
  48.3 5.6 %collective-permute-start.14 = (f32[64,1536]{1,0:T(8,128)S(1)}, f32[64,1536]{1,0:T(8,128)S(1)}, u32[]{:S(2)}, u32[]{:S(2)}) collective-permute-start(f32[64,1536]{1,0:T(8,128)S(1)} %get-tuple-element.82.refs_1_), channel_id=1, source_target_pairs={{0,4},{4,0},{8,12},{12,8},{16,20},{20,16},{24,28},{28,24},{1,5},{5... | collective-permute-start | bytes 1179656 | tf_op jit(solution)/shard_map/ppermute | solution.py:476
  48.4 7.6 %collective-permute-start.16 = (f32[64,384]{1,0:T(8,128)S(1)}, f32[64,384]{1,0:T(8,128)S(1)}, u32[]{:S(2)}, u32[]{:S(2)}) collective-permute-start(f32[64,384]{1,0:T(8,128)S(1)} %get-tuple-element.86), channel_id=1, source_target_pairs={{0,1},{1,2},{2,3},{3,0},{4,5},{5,6},{6,7},{7,4},{8,9},{9,10},{10,1... | collective-permute-start | bytes 294920 | tf_op jit(solution)/shard_map/ppermute | solution.py:490
  49.6 10.2 %collective-permute-start.17 = (f32[64,384]{1,0:T(8,128)S(1)}, f32[64,384]{1,0:T(8,128)S(1)}, u32[]{:S(2)}, u32[]{:S(2)}) collective-permute-start(f32[64,384]{1,0:T(8,128)S(1)} %get-tuple-element.87), channel_id=1, source_target_pairs={{0,2},{1,3},{2,0},{3,1},{4,6},{5,7},{6,4},{7,5},{8,10},{9,11},{10,... | collective-permute-start | bytes 294920 | tf_op jit(solution)/shard_map/ppermute | solution.py:490
  52.1 7.7 %collective-permute-start.18 = (f32[64,384]{1,0:T(8,128)S(1)}, f32[64,384]{1,0:T(8,128)S(1)}, u32[]{:S(2)}, u32[]{:S(2)}) collective-permute-start(f32[64,384]{1,0:T(8,128)S(1)} %get-tuple-element.88), channel_id=1, source_target_pairs={{0,3},{1,0},{2,1},{3,2},{4,7},{5,4},{6,5},{7,6},{8,11},{9,8},{10,9... | collective-permute-start | bytes 294920 | tf_op jit(solution)/shard_map/ppermute | solution.py:490
  54.7 9.3 %collective-permute-start.15 = (f32[64,64]{1,0:T(8,128)S(1)}, f32[64,64]{1,0:T(8,128)S(1)}, u32[]{:S(2)}, u32[]{:S(2)}) collective-permute-start(f32[64,64]{1,0:T(8,128)S(1)} %get-tuple-element.84.refs_0_), channel_id=1, source_target_pairs={{0,1},{1,0},{2,3},{3,2},{4,5},{5,4},{6,7},{7,6},{8,9},{9,8},{10,11... | collective-permute-start | bytes 49160 | tf_op jit(solution)/shard_map/ppermute | solution.py:476
  59.9 15.1 %collective-permute-start.22 = (f32[64,384]{1,0:T(8,128)S(1)}, f32[64,384]{1,0:T(8,128)S(1)}, u32[]{:S(2)}, u32[]{:S(2)}) collective-permute-start(f32[64,384]{1,0:T(8,128)S(1)} %get-tuple-element.98.refs_2_), channel_id=1, source_target_pairs={{0,3},{1,0},{2,1},{3,2},{4,7},{5,4},{6,5},{7,6},{8,11},{9,8},{10,9... | collective-permute-start | bytes 294920 | tf_op jit(solution)/shard_map/ppermute | solution.py:490
  63.4 11.6 %collective-permute-start.21 = (f32[64,384]{1,0:T(8,128)S(1)}, f32[64,384]{1,0:T(8,128)S(1)}, u32[]{:S(2)}, u32[]{:S(2)}) collective-permute-start(f32[64,384]{1,0:T(8,128)S(1)} %get-tuple-element.98.refs_2_), channel_id=1, source_target_pairs={{0,2},{1,3},{2,0},{3,1},{4,6},{5,7},{6,4},{7,5},{8,10},{9,11},{10,... | collective-permute-start | bytes 294920 | tf_op jit(solution)/shard_map/ppermute | solution.py:490
  63.8 11.2 %collective-permute-start.20 = (f32[64,384]{1,0:T(8,128)S(1)}, f32[64,384]{1,0:T(8,128)S(1)}, u32[]{:S(2)}, u32[]{:S(2)}) collective-permute-start(f32[64,384]{1,0:T(8,128)S(1)} %get-tuple-element.98.refs_2_), channel_id=1, source_target_pairs={{0,1},{1,2},{2,3},{3,0},{4,5},{5,6},{6,7},{7,4},{8,9},{9,10},{10,1... | collective-permute-start | bytes 294920 | tf_op jit(solution)/shard_map/ppermute | solution.py:490
  64.0 10.1 %collective-permute-start.19 = (f32[64,64]{1,0:T(8,128)S(1)}, f32[64,64]{1,0:T(8,128)S(1)}, u32[]{:S(2)}, u32[]{:S(2)}) collective-permute-start(f32[64,64]{1,0:T(8,128)S(1)} %get-tuple-element.91.refs_0_), channel_id=1, source_target_pairs={{0,2},{1,3},{2,0},{3,1},{4,6},{5,7},{6,4},{7,5},{8,10},{9,11},{10,... | collective-permute-start | bytes 49160 | tf_op jit(solution)/shard_map/ppermute | solution.py:476

commit v4 on v3

--- a/solution.py
+++ b/solution.py
@@ -77,6 +77,15 @@
     )
     head = jnp.where(lax.axis_index("row") == 0, turned[:, : 2 * width].T[:width], 0.0)
     packed_ref[...] = jnp.concatenate([gram, head], 1)
+
+
+def add_cores_kernel(first_ref, second_ref, a_ref, b_ref, x_ref, y_ref, sum_ref):
+    half = first_ref.shape[1]
+    total = a_ref[...] + b_ref[...]
+    sum_ref[...] = total
+    for source, target in ((first_ref, x_ref), (second_ref, y_ref)):
+        target[:, :half] = source[...]
+        target[:, half:] = total
 
 
 def add_kernel(*refs):
@@ -134,7 +143,8 @@
     order = band_ref.shape[0]
     lane = lax.broadcasted_iota(jnp.int32, (8, order), 1)
     sub = lax.broadcasted_iota(jnp.int32, (8, order), 0)
-    total = (a_ref[...] + b_ref[...]) + (c_ref[...] + d_ref[...])
+    skip = b_ref.shape[1] - a_ref.shape[1]
+    total = (a_ref[...] + b_ref[:, skip:]) + (c_ref[:, skip:] + d_ref[...])
     head_ref[...] = total[:, order:]
     gram = total[:, :order]
     tiles = sweep([gram[8 * t : 8 * t + 8, :] for t in range(order // 8)], order, False)
@@ -242,34 +252,10 @@
     )(raw, band, a)
 
 
-def across_kernel(held_ref, other_ref, band_ref, a_ref, *refs):
-    kct_ref, outs, right_ref = refs[0], refs[1:-2], refs[-1]
-    width, half = held_ref.shape
+def rows_product(right_ref, a_ref, outs):
     columns = a_ref.shape[1]
-    step = pl.program_id(0)
+    width = right_ref.shape[1] // 2
     chunk = block_of(columns, 512)
-
-    @pl.when(step == 0)
-    def _():
-        core = lax.rem(lax.axis_index("row"), 2)
-
-        @pl.when(core == 0)
-        def _():
-            kct_ref[:, :half] = held_ref[...]
-            kct_ref[:, half:] = other_ref[...]
-
-        @pl.when(core == 1)
-        def _():
-            kct_ref[:, :half] = other_ref[...]
-            kct_ref[:, half:] = held_ref[...]
-
-        @pl.when(lax.axis_index("col") == 0)
-        def _():
-            kct_ref[:, :width] = kct_ref[:, :width] - band_ref[...].T
-
-        for c in range(0, columns, chunk):
-            right_ref[c : c + chunk, :] = jnp.concatenate(split(kct_ref[:, c : c + chunk].T), 1)
-
     total = None
     for c in range(0, columns, chunk):
         ah, al = split(a_ref[:, c : c + chunk])
@@ -279,48 +265,78 @@
     result = (total[:, :width] + total[:, width:]).T
     for at, out_ref in enumerate(outs):
 
-        @pl.when(step == at)
+        @pl.when(pl.program_id(0) == at)
         def _():
             out_ref[...] = result
 
 
-def product_across(held, other, band, a, pieces):
+def across_kernel(held_ref, other_ref, band_ref, a_ref, kct_ref, right_ref, *refs):
+    width, half = held_ref.shape
+    columns = a_ref.shape[1]
+    chunk = block_of(columns, 512)
+
+    @pl.when(pl.program_id(0) == 0)
+    def _():
+        core = lax.rem(lax.axis_index("row"), 2)
+
+        @pl.when(core == 0)
+        def _():
+            kct_ref[:, :half] = held_ref[...]
+            kct_ref[:, half:] = other_ref[...]
+
+        @pl.when(core == 1)
+        def _():
+            kct_ref[:, :half] = other_ref[...]
+            kct_ref[:, half:] = held_ref[...]
+
+        @pl.when(lax.axis_index("col") == 0)
+        def _():
+            kct_ref[:, :width] = kct_ref[:, :width] - band_ref[...].T
+
+        for c in range(0, columns, chunk):
+            right_ref[c : c + chunk, :] = jnp.concatenate(split(kct_ref[:, c : c + chunk].T), 1)
+
+    rows_product(right_ref, a_ref, refs[:-1])
+
+
+def more_kernel(right_ref, a_ref, *refs):
+    rows_product(right_ref, a_ref, refs[:-1])
+
+
+def across_call(kernel, operands, extra, a, pieces, start, count, width):
     rows, columns = a.shape
-    width, half = held.shape
     size = rows // pieces
 
     def turn(i):
-        return (lax.rem(i + lax.axis_index("col"), pieces), 0)
-
-    part = pl.BlockSpec((width, half), lambda i: (0, 0))
-    one = pl.BlockSpec((width, size), lambda i: (0, 0))
+        return (lax.rem(i + start + lax.axis_index("col"), pieces), 0)
+
+    def fixed(array):
+        return pl.BlockSpec(array.shape, lambda i: (0, 0))
+
+    one = shape(width, size)
+    outs = tuple(extra) + (one,) * count
     return pl.pallas_call(
-        across_kernel,
-        grid=(pieces,),
-        in_specs=[
-            part,
-            part,
-            pl.BlockSpec((width, width), lambda i: (0, 0)),
-            pl.BlockSpec((size, columns), turn),
-        ],
-        out_specs=(pl.BlockSpec((width, columns), lambda i: (0, 0)),)
-        + (one,) * pieces
-        + (pl.BlockSpec(memory_space=pl.ANY),),
-        out_shape=(shape(width, columns),)
-        + (shape(width, size),) * pieces
-        + (shape(rows, columns),),
-        input_output_aliases={3: pieces + 1},
-        scratch_shapes=[pltpu.VMEM((columns, 2 * width), bf16)],
+        kernel,
+        grid=(count,),
+        in_specs=[fixed(x) for x in operands] + [pl.BlockSpec((size, columns), turn)],
+        out_specs=tuple(fixed(x) for x in outs) + (pl.BlockSpec(memory_space=pl.ANY),),
+        out_shape=outs + (shape(rows, columns),),
+        input_output_aliases={len(operands): len(outs)},
         compiler_params=params(22),
-        cost_estimate=cost(8 * rows * columns * width, 4 * rows * columns),
-        name="product_across",
-    )(held, other, band, a)
+        cost_estimate=cost(8 * size * count * columns * width, 4 * size * count * columns),
+    )(*operands, a)
 
 
 def merge_first_kernel(first_ref, second_ref, by_x_ref, by_y_ref, a_ref, b_ref):
-    source = lax.div(lax.axis_index("row"), 2) == lax.axis_index("col")
-    a_ref[...] = jnp.where(source, first_ref[...], by_x_ref[...])
-    b_ref[...] = jnp.where(source, second_ref[...], by_y_ref[...])
+    half = a_ref.shape[1]
+    relation = lax.div(lax.axis_index("row"), 2) ^ lax.axis_index("col")
+    for at, own, got, out in (
+        (1, first_ref, by_x_ref, a_ref),
+        (2, second_ref, by_y_ref, b_ref),
+    ):
+        out[...] = jnp.where(
+            relation == 0, own[...], jnp.where(relation == at, got[:, :half], 0.0)
+        )
 
 
 def join_kernel(a_ref, b_ref, c_ref, d_ref, out_ref):
@@ -442,31 +458,55 @@
         left_ref[pl.ds(start, size), :] = jnp.concatenate(split(value.T), 1)
 
 
-def far_kernel(left_ref, right_ref, a_ref, out_ref):
-    columns = a_ref.shape[1]
-    chunk = block_of(columns, 512)
-    left = left_ref[...]
-    for c in range(0, columns, chunk):
-        out_ref[:, c : c + chunk] = a_ref[:, c : c + chunk] - four_products(
-            left, right_ref, c, chunk
-        )
+def far_kernel(left_ref, right_ref, a_ref, out_ref, buffer, sems):
+    rows, columns = a_ref.shape
+    slots, deep, wide = buffer.shape
+    down, along = rows // deep, columns // wide
+    count = down * along
+
+    def place(i):
+        return (
+            pl.multiple_of(lax.rem(i, down) * deep, deep),
+            pl.multiple_of(lax.div(i, down) * wide, wide),
+        )
+
+    def store(i, slot):
+        r, c = place(i)
+        return pltpu.make_async_copy(
+            buffer.at[slot], out_ref.at[pl.ds(r, deep), pl.ds(c, wide)], sems.at[slot]
+        )
+
+    @pl.loop(0, count)
+    def _(i):
+        slot = lax.rem(i, slots)
+
+        @pl.when(i >= slots)
+        def _():
+            store(i - slots, slot).wait()
+
+        r, c = place(i)
+        buffer[slot] = a_ref[pl.ds(r, deep), pl.ds(c, wide)] - four_products(
+            left_ref[pl.ds(r, deep), :], right_ref, c, wide
+        )
+        store(i, slot).start()
+
+    for back in range(slots, 0, -1):
+        store(count - back, (count - back) % slots).wait()
 
 
 def subtract_far(left, right, a):
     rows, columns = a.shape
     deep = left.shape[1]
-    br = block_of(rows, 256)
+    whole = pl.BlockSpec(memory_space=pltpu.VMEM)
+    wide = columns if (columns // 4) % 128 else columns // 4
+    piece = (block_of(rows, 512), wide)
     return pl.pallas_call(
         far_kernel,
-        grid=(rows // br,),
-        in_specs=[
-            pl.BlockSpec((br, deep), lambda i: (i, 0)),
-            pl.BlockSpec((deep, columns), lambda i: (0, 0)),
-            pl.BlockSpec((br, columns), lambda i: (i, 0)),
-        ],
-        out_specs=pl.BlockSpec((br, columns), lambda i: (i, 0)),
+        in_specs=[whole] * 3,
+        out_specs=pl.BlockSpec(memory_space=pltpu.HBM),
         out_shape=shape(rows, columns),
-        compiler_params=params(22),
+        scratch_shapes=[pltpu.VMEM((3,) + piece, f32), pltpu.SemaphoreType.DMA((3,))],
+        compiler_params=params(12),
         cost_estimate=cost(4 * rows * columns * deep, 8 * rows * columns),
         name="subtract_far",
     )(left, right, a)
@@ -502,10 +542,17 @@
         first, second, partial = small_call(
             open_kernel, (half, half, packed), panel.T, flops=100_000_000, mib=12
         )
-        partial = small_call(add_kernel, packed, partial, flip(partial, 1, row_size))
+        apart = flip(partial, 1, row_size)
         if row_size == 8:
-            terms = [partial] + [flip(partial, bit, row_size) for bit in (2, 4, 6)]
+            wide_half = shape(width, rows // 2 + 2 * width)
+            send_x, send_y, partial = small_call(
+                add_cores_kernel, (wide_half, wide_half, packed), first, second, partial, apart
+            )
+            by_x = flip(send_x, 2, row_size)
+            by_y = flip(send_y, 4, row_size)
+            terms = [partial, by_x, by_y, flip(partial, 6, row_size)]
         else:
+            partial = small_call(add_kernel, packed, partial, apart)
             bit = 2
             total = partial
             while bit < row_size // 2:
@@ -516,8 +563,6 @@
         first, second, partial = lax.optimization_barrier((first, second, partial))
         raw, resident = product_down(first, second, matrix)
         if row_size == 8:
-            by_x = from_sources(first, col_size, [0], 2)
-            by_y = from_sources(second, col_size, [0], 4)
             one, two, resident = small_call(
                 merge_first_kernel, (half, half), first, second, by_x, by_y, carry=resident
             )
@@ -536,33 +581,47 @@
             eliminate_kernel, (small, small, small, small), *terms, flops=50_000_000, carry=resident
         )
         keep, give, resident = fix_down(raw, again, resident)
+        quarter = shape(width, columns // 4)
+        a, b, resident = small_call(
+            halve_kernel, (quarter, quarter), keep, flip(give, 1, row_size), carry=resident
+        )
         if row_size == 8:
             held, resident = small_call(
                 join_kernel, shape(width, rows), one, more_y, two, more_x, carry=resident
             )
         other = flip(held, 1, row_size)
-        quarter = shape(width, columns // 4)
-        a, b, resident = small_call(
-            halve_kernel, (quarter, quarter), keep, flip(give, 1, row_size), carry=resident
-        )
         bits = []
         bit = 2
         while bit < row_size:
             bits.append(bit)
             bit *= 2
+        pieces = 1 if (rows // col_size) % 128 else col_size
+        late = pieces // 2
         for forward, backward in list(zip(bits, bits[::-1]))[:-1]:
             ra = flip(a, forward, row_size)
             rb = flip(b, backward, row_size)
             if bits[0] == forward:
-                pieces = 1 if (rows // col_size) % 128 else col_size
-                kct, *chunks, resident = product_across(held, other, again, resident, pieces)
+                kct, right, *chunks, resident = across_call(
+                    across_kernel,
+                    (held, other, again),
+                    (shape(width, columns), shape(columns, 2 * width, dtype=bf16)),
+                    resident,
+                    pieces,
+                    late,
+                    pieces - late,
+                    width,
+                )
             a, b, resident = small_call(
                 pair_kernel, (quarter, quarter), a, ra, b, rb, carry=resident
             )
-        ra, rb = flip(a, bits[-1], row_size), flip(b, bits[0], row_size)
-        st, resident = small_call(
-            invert_kernel, small, head, again, band_inverse, flops=50_000_000, carry=resident
-        )
+        ra = flip(a, bits[-1], row_size)
+        rb = flip(b, bits[0], row_size)
+        if late:
+            received = [shift(chunks[at], late + at, col_size) for at in range(pieces - late)]
+            *chunks, resident = across_call(
+                more_kernel, (right,), (), resident, pieces, 0, late, width
+            )
+            received += [shift(chunks[by], by, col_size) for by in range(1, late)]
         summed, resident = small_call(
             join_kernel, shape(width, columns // 2), a, ra, b, rb, carry=resident
         )
@@ -583,7 +642,6 @@
         if pieces == 1:
             whole = [lax.psum(chunks[0], "col")]
         else:
-            received = [shift(chunks[by], by, col_size) for by in range(1, col_size)]
             mine, resident = small_call(
                 add_kernel, shape(width, rows // col_size), chunks[0], *received, carry=resident
             )
@@ -592,6 +650,9 @@
             got = first_inner if at == 1 else flip(inner, at, col_size, "col")
             inner, resident = small_call(add_kernel, small, inner, got, carry=resident)
         more = flip(inner, bit, col_size, "col")
+        st, resident = small_call(
+            invert_kernel, small, head, again, band_inverse, flops=50_000_000, carry=resident
+        )
         xparts, kparts, krt, resident = small_call(
             wide_kernel,
             (

time: 83.8 us -> 81.4 us (0.971)
  starting transfers between devices: 30.8 us -> 27.4 us
  waiting for transfers between devices: 14.2 us -> 15.7 us
    ppermute x4 -> x2, waiting for transfers between devices: 0.01 us -> 4.44 us  [from_sources(): return lax.ppermute(piece, ('row', 'col'), pairs)]
    ppermute x4 -> x2, starting transfers between devices: 9.51 us -> 6.52 us  [from_sources(): return lax.ppermute(piece, ('row', 'col'), pairs)]
    ppermute x13, waiting for transfers between devices: 9.41 us -> 6.68 us  [flip(): return lax.ppermute(value, axis, [(i, i ^ bit) for i in range(size)])]
    pallas_call x2 -> x3, Pallas kernels: 14.8 us -> 14.1 us  [the longest x1 7.14 us: subtract_far(): pl.pallas_call(far_kernel, in_specs=[whole] * 3, out_specs=pl.BlockSpec(m...]
  transfers between devices with their start and end apart: 23 -> 21, of which waited for: 10 -> 10; matrix products, arithmetic and copies ran while one was open for 0% -> 0% of each run, Pallas kernels for 33% -> 29%
where the time goes in v4:
time: 81.4 us; the launch traced here: 81.2 us
  Pallas kernels  36 us (44%)
  starting transfers between devices  27.4 us (34%)
  waiting for transfers between devices  15.7 us (19%)
  between operations  1.03 us (1%)
  local copies, waits for them, and re-layouts  0.99 us (1%)
    ppermute x13, starting transfers between devices, flip(): return lax.ppermute(value, axis, [(i, i ^ bit) for i in range(size)])  11.3 us
    ppermute x6, starting transfers between devices, shift(): lax.ppermute(piece, 'col', [(i, (i + by) % size) for i in range(size)])  9.59 us
    pallas_call x15, Pallas kernels, small_call(): pl.pallas_call(body, out_shape=out, compiler_params=params(mib), cost_est...  9.21 us
    pallas_call x1, Pallas kernels, subtract_far(): pl.pallas_call(far_kernel, in_specs=[whole] * 3, out_specs=pl.BlockSpec(m...  7.14 us
    pallas_call x1, Pallas kernels, product_down(): pl.pallas_call(down_kernel, in_specs=[whole, whole, pl.BlockSpec(memory_s...  7.05 us
    pallas_call x2, Pallas kernels, across_call(): pl.pallas_call(kernel, grid=(count,), in_specs=[fixed(x) for x in operand...  6.95 us
    ppermute x13, waiting for transfers between devices, flip(): return lax.ppermute(value, axis, [(i, i ^ bit) for i in range(size)])  6.68 us
    ppermute x2, starting transfers between devices, from_sources(): return lax.ppermute(piece, ('row', 'col'), pairs)  6.52 us
  transfers between devices with their start and end apart: 21, of which 10 were waited for; matrix products, arithmetic and copies ran while one was open for 0% of the time, Pallas kernels for 29%

profile of v4, /device:TPU:0, one launch (start us, length us, event | category | flops | bytes accessed | tf_op | source)
XLA Modules:
  0.0 81.2 jit_solution(11746325382590829810)
XLA Ops:
  0.6 0.0 copy-start
  0.6 1.0 %copy-done = f32[1536,64]{0,1:T(8,128)S(1)} copy-done((f32[1536,64]{0,1:T(8,128)S(1)}, f32[1536,64]{0,1:T(8,128)}, u32[]{:S(2)}) %copy-start) | copy-done | bytes 393240
  1.6 0.5 shard_map.41
  2.1 0.6 collective-permute-start
  2.7 0.9 %collective-permute-done.b_ref = f32[64,128]{1,0:T(8,128)S(1)} collective-permute-done((f32[64,128]{1,0:T(8,128)S(1)}, f32[64,128]{1,0:T(8,128)S(1)}, u32[]{:S(2)}, u32[]{:S(2)}) %collective-permute-start) | collective-permute-done | bytes 32800 | tf_op jit(solution)/shard_map/ppermute | solution.py:516
  3.6 2.9 %collective-permute-start.1 = (f32[64,896]{1,0:T(8,128)S(1)}, f32[64,896]{1,0:T(8,128)S(1)}, u32[]{:S(2)}, u32[]{:S(2)}) collective-permute-start(f32[64,896]{1,0:T(8,128)S(1)} %get-tuple-element.62), channel_id=1, source_target_pairs={{0,8},{4,12},{8,0},{12,4},{16,24},{20,28},{24,16},{28,20},{1,9},{5... | collective-permute-start | bytes 688136 | tf_op jit(solution)/shard_map/ppermute | solution.py:516
  6.4 1.5 %collective-permute-start.2 = (f32[64,896]{1,0:T(8,128)S(1)}, f32[64,896]{1,0:T(8,128)S(1)}, u32[]{:S(2)}, u32[]{:S(2)}) collective-permute-start(f32[64,896]{1,0:T(8,128)S(1)} %get-tuple-element.63), channel_id=1, source_target_pairs={{0,16},{4,20},{8,24},{12,28},{16,0},{20,4},{24,8},{28,12},{1,17},{... | collective-permute-start | bytes 688136 | tf_op jit(solution)/shard_map/ppermute | solution.py:516
  8.0 0.0 collective-permute-start.3
  8.0 7.1 %product_down.1 = (f32[64,3072]{1,0:T(8,128)S(1)}, f32[1536,3072]{1,0:T(8,128)S(1)}) custom-call(f32[64,768]{1,0:T(8,128)S(1)} %get-tuple-element.64.first_ref.refs_0_.refs_3_, f32[64,768]{1,0:T(8,128)S(1)} %get-tuple-element.65.second_ref.refs_1_.refs_4_, f32[1536,3072]{1,0:T(8,128)} %a_ref.1), custom_call_target="tpu_custom_call" | custom-call | flops 2415919104 | bytes 18874368 | tf_op jit(solution)/shard_map/product_down/pallas_call | solution.py:202
  15.0 0.0 collective-permute-done.1.refs_2_.refs_1_
  15.1 0.0 collective-permute-done.2.refs_3_.refs_2_
  15.1 0.1 shard_map.43
  15.1 0.0 collective-permute-done.3.refs_3_
  15.2 2.7 %shard_map.44 = (f32[64,64]{1,0:T(8,128)}, f32[64,64]{1,0:T(8,128)S(1)}, f32[64,64]{1,0:T(8,128)S(1)}, f32[64,64]{1,0:T(8,128)S(1)}, f32[1536,3072]{1,0:T(8,128)S(1)}) custom-call(f32[64,128]{1,0:T(8,128)S(1)} %get-tuple-element.61.refs_0_, f32[64,896]{1,0:T(8,128)S(1)} %collective-permute-done.1.refs_2_.refs_1_, ...), custom_call_target="tpu_custom_call", output_to_operand_aliasing={{4}: (4, {})} | custom-call | flops 50000000 | bytes 1000000 | tf_op jit(solution)/shard_map/pallas_call | solution.py:64
  17.8 0.9 %fix_down.1 = (f32[64,1536]{1,0:T(8,128)S(1)}, f32[64,1536]{1,0:T(8,128)S(1)}, f32[1536,3072]{1,0:T(8,128)S(1)}) custom-call(f32[64,3072]{1,0:T(8,128)S(1)} %get-tuple-element.73.raw_ref, f32[64,64]{1,0:T(8,128)S(1)} %get-tuple-element.69.band_ref.refs_1_.refs_5_, f32[1536,3072]{1,0:T(8,128)S(1)} %get-tuple-element.74.top_ref), custom_call_target="tpu_custom_call", output_to_operand_aliasing={{2}: (2, {})} | custom-call | flops 150994944 | bytes 3145728 | tf_op jit(solution)/shard_map/fix_down/pallas_call | solution.py:242
  18.7 0.1 collective-permute-start.6
  18.8 3.1 %collective-permute-start.4 = (f32[64,768]{1,0:T(8,128)S(1)}, f32[64,768]{1,0:T(8,128)S(1)}, u32[]{:S(2)}, u32[]{:S(2)}) collective-permute-start(f32[64,768]{1,0:T(8,128)S(1)} %get-tuple-element.71.refs_0_), channel_id=1, source_target_pairs={{0,16},{4,20},{8,24},{12,28},{9,25},{13,29},{1,17},{5,21},{18,2},{... | collective-permute-start | bytes 589832 | tf_op jit(solution)/shard_map/ppermute | solution.py:526
  21.9 3.4 %collective-permute-start.5 = (f32[64,768]{1,0:T(8,128)S(1)}, f32[64,768]{1,0:T(8,128)S(1)}, u32[]{:S(2)}, u32[]{:S(2)}) collective-permute-start(f32[64,768]{1,0:T(8,128)S(1)} %get-tuple-element.72.refs_2_), channel_id=1, source_target_pairs={{0,8},{4,12},{16,24},{20,28},{9,1},{13,5},{25,17},{29,21},{18,26},... | collective-permute-start | bytes 589832 | tf_op jit(solution)/shard_map/ppermute | solution.py:526
  25.3 0.0 collective-permute-done.6.refs_1_
  25.4 1.3 %collective-permute-done.4.refs_1_ = f32[64,768]{1,0:T(8,128)S(1)} collective-permute-done((f32[64,768]{1,0:T(8,128)S(1)}, f32[64,768]{1,0:T(8,128)S(1)}, u32[]{:S(2)}, u32[]{:S(2)}) %collective-permute-start.4) | collective-permute-done | bytes 196640 | tf_op jit(solution)/shard_map/ppermute | solution.py:526
  26.7 3.1 %collective-permute-done.5.refs_3_ = f32[64,768]{1,0:T(8,128)S(1)} collective-permute-done((f32[64,768]{1,0:T(8,128)S(1)}, f32[64,768]{1,0:T(8,128)S(1)}, u32[]{:S(2)}, u32[]{:S(2)}) %collective-permute-start.5) | collective-permute-done | bytes 196640 | tf_op jit(solution)/shard_map/ppermute | solution.py:526
  29.9 0.1 collective-permute-start.7
  30.0 2.5 %collective-permute-start.8 = (f32[64,768]{1,0:T(8,128)S(1)}, f32[64,768]{1,0:T(8,128)S(1)}, u32[]{:S(2)}, u32[]{:S(2)}) collective-permute-start(f32[64,768]{1,0:T(8,128)S(1)} %get-tuple-element.82.refs_0_), channel_id=1, source_target_pairs={{0,8},{4,12},{8,0},{12,4},{16,24},{20,28},{24,16},{28,20},{1,9},{5... | collective-permute-start | bytes 589832 | tf_op jit(solution)/shard_map/ppermute | solution.py:516
  32.5 0.0 collective-permute-start.9
  32.5 0.0 collective-permute-done.7.other_ref
  32.5 3.9 %shard_map.47 = (f32[64,3072]{1,0:T(8,128)S(1)}, bf16[3072,128]{1,0:T(8,128)(2,1)S(1)}, f32[64,384]{1,0:T(8,128)S(1)}, f32[64,384]{1,0:T(8,128)S(1)}, f32[1536,3072]{1,0:T(8,128)S(1)}) custom-call(f32[64,1536]{1,0:T(8,128)S(1)} %get-tuple-element.79.held_ref, f32[64,1536]{1,0:T(8,128)S(1)} %collective-permute-done.7.other_ref, ...), custom_call_target="tpu_custom_call", output_to_operand_aliasing={{4}: (3, {})} | custom-call | flops 1207959552 | bytes 9437184 | tf_op jit(solution)/shard_map/pallas_call | solution.py:318
  36.4 1.6 %collective-permute-done.8.refs_1_ = f32[64,768]{1,0:T(8,128)S(1)} collective-permute-done((f32[64,768]{1,0:T(8,128)S(1)}, f32[64,768]{1,0:T(8,128)S(1)}, u32[]{:S(2)}, u32[]{:S(2)}) %collective-permute-start.8) | collective-permute-done | bytes 196640 | tf_op jit(solution)/shard_map/ppermute | solution.py:516
  38.0 1.5 %collective-permute-done.9.refs_3_ = f32[64,768]{1,0:T(8,128)S(1)} collective-permute-done((f32[64,768]{1,0:T(8,128)S(1)}, f32[64,768]{1,0:T(8,128)S(1)}, u32[]{:S(2)}, u32[]{:S(2)}) %collective-permute-start.9) | collective-permute-done | bytes 196640 | tf_op jit(solution)/shard_map/ppermute | solution.py:516
  39.5 0.3 collective-permute-start.10
  39.9 0.3 collective-permute-start.11
  40.1 3.1 %shard_map.49 = (f32[64,384]{1,0:T(8,128)S(1)}, f32[64,384]{1,0:T(8,128)S(1)}, f32[1536,3072]{1,0:T(8,128)S(1)}) custom-call(bf16[3072,128]{1,0:T(8,128)(2,1)S(1)} %get-tuple-element.87.right_ref, f32[1536,3072]{1,0:T(8,128)S(1)} %get-tuple-element.88.a_ref), custom_call_target="tpu_custom_call", output_to_operand_aliasing={{2}: (1, {})} | custom-call | flops 1207959552 | bytes 9437184 | tf_op jit(solution)/shard_map/pallas_call | solution.py:318
  43.2 2.5 %collective-permute-done.10.refs_1_ = f32[64,768]{1,0:T(8,128)S(1)} collective-permute-done((f32[64,768]{1,0:T(8,128)S(1)}, f32[64,768]{1,0:T(8,128)S(1)}, u32[]{:S(2)}, u32[]{:S(2)}) %collective-permute-start.10) | collective-permute-done | bytes 196640 | tf_op jit(solution)/shard_map/ppermute | solution.py:516
  45.7 0.3 collective-permute-done.11.refs_3_
  46.0 0.1 collective-permute-start.12
  46.1 0.6 collective-permute-start.16
  46.7 3.4 %collective-permute-start.14 = (f32[64,384]{1,0:T(8,128)S(1)}, f32[64,384]{1,0:T(8,128)S(1)}, u32[]{:S(2)}, u32[]{:S(2)}) collective-permute-start(f32[64,384]{1,0:T(8,128)S(1)} %get-tuple-element.94), channel_id=1, source_target_pairs={{0,2},{1,3},{2,0},{3,1},{4,6},{5,7},{6,4},{7,5},{8,10},{9,11},{10,... | collective-permute-start | bytes 294920 | tf_op jit(solution)/shard_map/ppermute | solution.py:530
  50.1 1.5 %collective-permute-start.15 = (f32[64,384]{1,0:T(8,128)S(1)}, f32[64,384]{1,0:T(8,128)S(1)}, u32[]{:S(2)}, u32[]{:S(2)}) collective-permute-start(f32[64,384]{1,0:T(8,128)S(1)} %get-tuple-element.95), channel_id=1, source_target_pairs={{0,3},{1,0},{2,1},{3,2},{4,7},{5,4},{6,5},{7,6},{8,11},{9,8},{10,9... | collective-permute-start | bytes 294920 | tf_op jit(solution)/shard_map/ppermute | solution.py:530
  51.6 0.0 collective-permute-done.12.refs_2_
  51.6 0.8 %shard_map.51 = (f32[64,3072]{1,0:T(8,128)S(1)}, f32[64,64]{1,0:T(8,128)S(1)}, f32[1536,3072]{1,0:T(8,128)S(1)}) custom-call(f32[64,3072]{1,0:T(8,128)S(1)} %get-tuple-element.81.refs_0_.refs_2_, f32[64,1536]{1,0:T(8,128)S(1)} %get-tuple-element.90.refs_1_, f32[64,1536]{1,0:T(8,128)S(1)} %collective-permute-done.12.refs_2_, ...), custom_call_target="tpu_custom_call", output_to_operand_aliasing={{2}: (3, {})} | custom-call | flops 1000000 | bytes 1000000 | tf_op jit(solution)/shard_map/pallas_call | solution.py:64
  52.4 0.6 collective-permute-start.13
  53.0 0.7 collective-permute-done.16.refs_3_
  53.7 3.7 %collective-permute-done.14.refs_1_ = f32[64,384]{1,0:T(8,128)S(1)} collective-permute-done((f32[64,384]{1,0:T(8,128)S(1)}, f32[64,384]{1,0:T(8,128)S(1)}, u32[]{:S(2)}, u32[]{:S(2)}) %collective-permute-start.14) | collective-permute-done | bytes 98336 | tf_op jit(solution)/shard_map/ppermute | solution.py:530
  57.4 0.3 collective-permute-done.15.refs_2_
  57.7 3.4 %collective-permute-start.20 = (f32[64,384]{1,0:T(8,128)S(1)}, f32[64,384]{1,0:T(8,128)S(1)}, u32[]{:S(2)}, u32[]{:S(2)}) collective-permute-start(f32[64,384]{1,0:T(8,128)S(1)} %get-tuple-element.108.refs_2_), channel_id=1, source_target_pairs={{0,3},{1,0},{2,1},{3,2},{4,7},{5,4},{6,5},{7,6},{8,11},{9,8},{10,9... | collective-permute-start | bytes 294920 | tf_op jit(solution)/shard_map/ppermute | solution.py:530
  61.1 0.4 collective-permute-start.19
  61.5 0.2 collective-permute-start.18
  61.8 0.0 collective-permute-done.13.refs_1_
  61.8 2.4 %collective-permute-start.17 = (f32[64,64]{1,0:T(8,128)S(1)}, f32[64,64]{1,0:T(8,128)S(1)}, u32[]{:S(2)}, u32[]{:S(2)}) collective-permute-start(f32[64,64]{1,0:T(8,128)S(1)} %get-tuple-element.101.refs_0_), channel_id=1, source_target_pairs={{0,2},{1,3},{2,0},{3,1},{4,6},{5,7},{6,4},{7,5},{8,10},{9,11},{10,... | collective-permute-start | bytes 49160 | tf_op jit(solution)/shard_map/ppermute | solution.py:516
  64.1 2.3 %shard_map.54 = (f32[64,64]{1,0:T(8,128)S(1)}, f32[1536,3072]{1,0:T(8,128)S(1)}) custom-call(f32[64,64]{1,0:T(8,128)S(1)} %get-tuple-element.68.refs_0_, f32[64,64]{1,0:T(8,128)S(1)} %get-tuple-element.69.band_ref.refs_1_.refs_5_, f32[64,64]{1,0:T(8,128)S(1)} %get-tuple-element.70.refs_2_, ...), custom_call_target="tpu_custom_call", output_to_operand_aliasing={{1}: (3, {})} | custom-call | flops 50000000 | bytes 1000000 | tf_op jit(solution)/shard_map/pallas_call | solution.py:64
  66.4 1.0 %shard_map.55 = (bf16[128,3072]{1,0:T(8,128)(2,1)S(1)}, bf16[128,3072]{1,0:T(8,128)(2,1)S(1)}, f32[64,1536]{1,0:T(8,128)S(1)}, f32[1536,3072]{1,0:T(8,128)S(1)}) custom-call(f32[64,64]{1,0:T(8,128)S(1)} %get-tuple-element.100.refs_0_.refs_2_, f32[64,3072]{1,0:T(8,128)S(1)} %get-tuple-element.102.refs_1_, ...), custom_call_target="tpu_custom_call", output_to_operand_aliasing={{3}: (6, {})} | custom-call | flops 1000000 | bytes 1000000 | tf_op jit(solution)/shard_map/pallas_call | solution.py:64
  67.4 4.8 %subtract_near.1.refs_4_ = f32[1536,3072]{1,0:T(8,128)S(1)} custom-call(f32[64,1536]{1,0:T(8,128)S(1)} %get-tuple-element.104.rows_ref.refs_3_, bf16[128,3072]{1,0:T(8,128)(2,1)S(1)} %get-tuple-element.105.right_ref, f32[1536,3072]{1,0:T(8,128)S(1)} %get-tuple-element.106.a_ref), custom_call_target="tpu_custom_call", output_to_operand_aliasing={{}: (2, {})} | custom-call | flops 2415919104 | bytes 37748736 | tf_op jit(solution)/shard_map/subtract_near/pallas_call | solution.py:430
  72.3 0.0 collective-permute-done.17.refs_1_
  72.3 0.8 %shard_map.56 = (f32[64,1536]{1,0:T(8,128)S(1)}, f32[1536,3072]{1,0:T(8,128)S(1)}) custom-call(f32[64,64]{1,0:T(8,128)S(1)} %get-tuple-element.101.refs_0_, f32[64,64]{1,0:T(8,128)S(1)} %collective-permute-done.17.refs_1_, f32[64,64]{1,0:T(8,128)S(1)} %get-tuple-element.100.refs_0_.refs_2_, ...), custom_call_target="tpu_custom_call", output_to_operand_aliasing={{1}: (4, {})} | custom-call | flops 1000000 | bytes 1000000 | tf_op jit(solution)/shard_map/pallas_call | solution.py:64
  73.1 0.0 collective-permute-done.20.refs_5_
  73.1 0.0 collective-permute-done.19.refs_4_
  73.1 0.0 collective-permute-done.18.refs_3_
  73.1 0.8 shard_map.57
  73.9 7.1 %subtract_far.1 = f32[1536,3072]{1,0:T(8,128)} custom-call(bf16[1536,128]{1,0:T(8,128)(2,1)S(1)} %get-tuple-element.110.left_ref, bf16[128,3072]{1,0:T(8,128)(2,1)S(1)} %get-tuple-element.111.right_ref, f32[1536,3072]{1,0:T(8,128)S(1)} %get-tuple-element.112.a_ref), custom_call_target="tpu_custom_call" | custom-call | flops 2415919104 | bytes 37748736 | tf_op jit(solution)/shard_map/subtract_far/pallas_call | solution.py:503
  (7 shorter events, 0.2 us)
Async XLA Ops:
  0.6 1.0 %copy-start = (f32[1536,64]{0,1:T(8,128)S(1)}, f32[1536,64]{0,1:T(8,128)}, u32[]{:S(2)}) copy-start(f32[1536,64]{0,1:T(8,128)} %param.3) | copy-start | bytes 1179652
  2.1 1.4 %collective-permute-start = (f32[64,128]{1,0:T(8,128)S(1)}, f32[64,128]{1,0:T(8,128)S(1)}, u32[]{:S(2)}, u32[]{:S(2)}) collective-permute-start(f32[64,128]{1,0:T(8,128)S(1)} %get-tuple-element.60.a_ref), channel_id=1, source_target_pairs={{0,4},{4,0},{8,12},{12,8},{16,20},{20,16},{24,28},{28,24},{1,5},{5... | collective-permute-start | bytes 98312 | tf_op jit(solution)/shard_map/ppermute | solution.py:516
  3.6 11.5 %collective-permute-start.1 = (f32[64,896]{1,0:T(8,128)S(1)}, f32[64,896]{1,0:T(8,128)S(1)}, u32[]{:S(2)}, u32[]{:S(2)}) collective-permute-start(f32[64,896]{1,0:T(8,128)S(1)} %get-tuple-element.62), channel_id=1, source_target_pairs={{0,8},{4,12},{8,0},{12,4},{16,24},{20,28},{24,16},{28,20},{1,9},{5... | collective-permute-start | bytes 688136 | tf_op jit(solution)/shard_map/ppermute | solution.py:516
  6.4 8.6 %collective-permute-start.2 = (f32[64,896]{1,0:T(8,128)S(1)}, f32[64,896]{1,0:T(8,128)S(1)}, u32[]{:S(2)}, u32[]{:S(2)}) collective-permute-start(f32[64,896]{1,0:T(8,128)S(1)} %get-tuple-element.63), channel_id=1, source_target_pairs={{0,16},{4,20},{8,24},{12,28},{16,0},{20,4},{24,8},{28,12},{1,17},{... | collective-permute-start | bytes 688136 | tf_op jit(solution)/shard_map/ppermute | solution.py:516
  8.0 7.2 %collective-permute-start.3 = (f32[64,128]{1,0:T(8,128)S(1)}, f32[64,128]{1,0:T(8,128)S(1)}, u32[]{:S(2)}, u32[]{:S(2)}) collective-permute-start(f32[64,128]{1,0:T(8,128)S(1)} %get-tuple-element.61.refs_0_), channel_id=1, source_target_pairs={{0,24},{4,28},{8,16},{12,20},{16,8},{20,12},{24,0},{28,4},{1,25},{... | collective-permute-start | bytes 98312 | tf_op jit(solution)/shard_map/ppermute | solution.py:516
  18.7 6.6 %collective-permute-start.6 = (f32[64,1536]{1,0:T(8,128)S(1)}, f32[64,1536]{1,0:T(8,128)S(1)}, u32[]{:S(2)}, u32[]{:S(2)}) collective-permute-start(f32[64,1536]{1,0:T(8,128)S(1)} %get-tuple-element.76), channel_id=1, source_target_pairs={{0,4},{4,0},{8,12},{12,8},{16,20},{20,16},{24,28},{28,24},{1,5},{5... | collective-permute-start | bytes 1179656 | tf_op jit(solution)/shard_map/ppermute | solution.py:516
  18.8 7.9 %collective-permute-start.4 = (f32[64,768]{1,0:T(8,128)S(1)}, f32[64,768]{1,0:T(8,128)S(1)}, u32[]{:S(2)}, u32[]{:S(2)}) collective-permute-start(f32[64,768]{1,0:T(8,128)S(1)} %get-tuple-element.71.refs_0_), channel_id=1, source_target_pairs={{0,16},{4,20},{8,24},{12,28},{9,25},{13,29},{1,17},{5,21},{18,2},{... | collective-permute-start | bytes 589832 | tf_op jit(solution)/shard_map/ppermute | solution.py:526
  21.9 7.9 %collective-permute-start.5 = (f32[64,768]{1,0:T(8,128)S(1)}, f32[64,768]{1,0:T(8,128)S(1)}, u32[]{:S(2)}, u32[]{:S(2)}) collective-permute-start(f32[64,768]{1,0:T(8,128)S(1)} %get-tuple-element.72.refs_2_), channel_id=1, source_target_pairs={{0,8},{4,12},{16,24},{20,28},{9,1},{13,5},{25,17},{29,21},{18,26},... | collective-permute-start | bytes 589832 | tf_op jit(solution)/shard_map/ppermute | solution.py:526
  29.9 2.6 %collective-permute-start.7 = (f32[64,1536]{1,0:T(8,128)S(1)}, f32[64,1536]{1,0:T(8,128)S(1)}, u32[]{:S(2)}, u32[]{:S(2)}) collective-permute-start(f32[64,1536]{1,0:T(8,128)S(1)} %get-tuple-element.79.held_ref), channel_id=1, source_target_pairs={{0,4},{4,0},{8,12},{12,8},{16,20},{20,16},{24,28},{28,24},{1,5},{5... | collective-permute-start | bytes 1179656 | tf_op jit(solution)/shard_map/ppermute | solution.py:516
  30.0 8.0 %collective-permute-start.8 = (f32[64,768]{1,0:T(8,128)S(1)}, f32[64,768]{1,0:T(8,128)S(1)}, u32[]{:S(2)}, u32[]{:S(2)}) collective-permute-start(f32[64,768]{1,0:T(8,128)S(1)} %get-tuple-element.82.refs_0_), channel_id=1, source_target_pairs={{0,8},{4,12},{8,0},{12,4},{16,24},{20,28},{24,16},{28,20},{1,9},{5... | collective-permute-start | bytes 589832 | tf_op jit(solution)/shard_map/ppermute | solution.py:516
  32.5 7.0 %collective-permute-start.9 = (f32[64,768]{1,0:T(8,128)S(1)}, f32[64,768]{1,0:T(8,128)S(1)}, u32[]{:S(2)}, u32[]{:S(2)}) collective-permute-start(f32[64,768]{1,0:T(8,128)S(1)} %get-tuple-element.83.refs_2_), channel_id=1, source_target_pairs={{0,16},{4,20},{8,24},{12,28},{16,0},{20,4},{24,8},{28,12},{1,17},{... | collective-permute-start | bytes 589832 | tf_op jit(solution)/shard_map/ppermute | solution.py:516
  39.5 6.2 %collective-permute-start.10 = (f32[64,768]{1,0:T(8,128)S(1)}, f32[64,768]{1,0:T(8,128)S(1)}, u32[]{:S(2)}, u32[]{:S(2)}) collective-permute-start(f32[64,768]{1,0:T(8,128)S(1)} %get-tuple-element.85.refs_0_), channel_id=1, source_target_pairs={{0,16},{4,20},{8,24},{12,28},{16,0},{20,4},{24,8},{28,12},{1,17},{... | collective-permute-start | bytes 589832 | tf_op jit(solution)/shard_map/ppermute | solution.py:516
  39.9 6.1 %collective-permute-start.11 = (f32[64,768]{1,0:T(8,128)S(1)}, f32[64,768]{1,0:T(8,128)S(1)}, u32[]{:S(2)}, u32[]{:S(2)}) collective-permute-start(f32[64,768]{1,0:T(8,128)S(1)} %get-tuple-element.86.refs_2_), channel_id=1, source_target_pairs={{0,8},{4,12},{8,0},{12,4},{16,24},{20,28},{24,16},{28,20},{1,9},{5... | collective-permute-start | bytes 589832 | tf_op jit(solution)/shard_map/ppermute | solution.py:516
  46.0 5.6 %collective-permute-start.12 = (f32[64,1536]{1,0:T(8,128)S(1)}, f32[64,1536]{1,0:T(8,128)S(1)}, u32[]{:S(2)}, u32[]{:S(2)}) collective-permute-start(f32[64,1536]{1,0:T(8,128)S(1)} %get-tuple-element.90.refs_1_), channel_id=1, source_target_pairs={{0,4},{4,0},{8,12},{12,8},{16,20},{20,16},{24,28},{28,24},{1,5},{5... | collective-permute-start | bytes 1179656 | tf_op jit(solution)/shard_map/ppermute | solution.py:516
  46.1 7.6 %collective-permute-start.16 = (f32[64,384]{1,0:T(8,128)S(1)}, f32[64,384]{1,0:T(8,128)S(1)}, u32[]{:S(2)}, u32[]{:S(2)}) collective-permute-start(f32[64,384]{1,0:T(8,128)S(1)} %get-tuple-element.96), channel_id=1, source_target_pairs={{0,1},{1,2},{2,3},{3,0},{4,5},{5,6},{6,7},{7,4},{8,9},{9,10},{10,1... | collective-permute-start | bytes 294920 | tf_op jit(solution)/shard_map/ppermute | solution.py:530
  46.7 10.7 %collective-permute-start.14 = (f32[64,384]{1,0:T(8,128)S(1)}, f32[64,384]{1,0:T(8,128)S(1)}, u32[]{:S(2)}, u32[]{:S(2)}) collective-permute-start(f32[64,384]{1,0:T(8,128)S(1)} %get-tuple-element.94), channel_id=1, source_target_pairs={{0,2},{1,3},{2,0},{3,1},{4,6},{5,7},{6,4},{7,5},{8,10},{9,11},{10,... | collective-permute-start | bytes 294920 | tf_op jit(solution)/shard_map/ppermute | solution.py:530
  50.1 7.5 %collective-permute-start.15 = (f32[64,384]{1,0:T(8,128)S(1)}, f32[64,384]{1,0:T(8,128)S(1)}, u32[]{:S(2)}, u32[]{:S(2)}) collective-permute-start(f32[64,384]{1,0:T(8,128)S(1)} %get-tuple-element.95), channel_id=1, source_target_pairs={{0,3},{1,0},{2,1},{3,2},{4,7},{5,4},{6,5},{7,6},{8,11},{9,8},{10,9... | collective-permute-start | bytes 294920 | tf_op jit(solution)/shard_map/ppermute | solution.py:530
  52.4 9.3 %collective-permute-start.13 = (f32[64,64]{1,0:T(8,128)S(1)}, f32[64,64]{1,0:T(8,128)S(1)}, u32[]{:S(2)}, u32[]{:S(2)}) collective-permute-start(f32[64,64]{1,0:T(8,128)S(1)} %get-tuple-element.92.refs_0_), channel_id=1, source_target_pairs={{0,1},{1,0},{2,3},{3,2},{4,5},{5,4},{6,7},{7,6},{8,9},{9,8},{10,11... | collective-permute-start | bytes 49160 | tf_op jit(solution)/shard_map/ppermute | solution.py:516
  57.7 15.4 %collective-permute-start.20 = (f32[64,384]{1,0:T(8,128)S(1)}, f32[64,384]{1,0:T(8,128)S(1)}, u32[]{:S(2)}, u32[]{:S(2)}) collective-permute-start(f32[64,384]{1,0:T(8,128)S(1)} %get-tuple-element.108.refs_2_), channel_id=1, source_target_pairs={{0,3},{1,0},{2,1},{3,2},{4,7},{5,4},{6,5},{7,6},{8,11},{9,8},{10,9... | collective-permute-start | bytes 294920 | tf_op jit(solution)/shard_map/ppermute | solution.py:530
  61.1 12.0 %collective-permute-start.19 = (f32[64,384]{1,0:T(8,128)S(1)}, f32[64,384]{1,0:T(8,128)S(1)}, u32[]{:S(2)}, u32[]{:S(2)}) collective-permute-start(f32[64,384]{1,0:T(8,128)S(1)} %get-tuple-element.108.refs_2_), channel_id=1, source_target_pairs={{0,2},{1,3},{2,0},{3,1},{4,6},{5,7},{6,4},{7,5},{8,10},{9,11},{10,... | collective-permute-start | bytes 294920 | tf_op jit(solution)/shard_map/ppermute | solution.py:530
  61.5 11.6 %collective-permute-start.18 = (f32[64,384]{1,0:T(8,128)S(1)}, f32[64,384]{1,0:T(8,128)S(1)}, u32[]{:S(2)}, u32[]{:S(2)}) collective-permute-start(f32[64,384]{1,0:T(8,128)S(1)} %get-tuple-element.108.refs_2_), channel_id=1, source_target_pairs={{0,1},{1,2},{2,3},{3,0},{4,5},{5,6},{6,7},{7,4},{8,9},{9,10},{10,1... | collective-permute-start | bytes 294920 | tf_op jit(solution)/shard_map/ppermute | solution.py:530
  61.8 10.5 %collective-permute-start.17 = (f32[64,64]{1,0:T(8,128)S(1)}, f32[64,64]{1,0:T(8,128)S(1)}, u32[]{:S(2)}, u32[]{:S(2)}) collective-permute-start(f32[64,64]{1,0:T(8,128)S(1)} %get-tuple-element.101.refs_0_), channel_id=1, source_target_pairs={{0,2},{1,3},{2,0},{3,1},{4,6},{5,7},{6,4},{7,5},{8,10},{9,11},{10,... | collective-permute-start | bytes 49160 | tf_op jit(solution)/shard_map/ppermute | solution.py:516

commit v5 on v4

--- a/solution.py
+++ b/solution.py
@@ -42,28 +42,31 @@
     return wanted
 
 
-def small_call(kernel, out, *operands, carry=None, flops=1_000_000, moved=1_000_000, mib=8):
+def small_call(kernel, out, *operands, carry=(), flops=1_000_000, moved=1_000_000, mib=8):
     extra = {}
     body = kernel
-    if carry is not None:
+    if carry:
         outs = out if isinstance(out, tuple) else (out,)
-        count = len(operands)
+        count, more = len(operands), len(carry)
         anywhere = pl.BlockSpec(memory_space=pl.ANY)
         whole = pl.BlockSpec(memory_space=pltpu.VMEM)
         extra = dict(
-            in_specs=[whole] * count + [anywhere],
-            out_specs=(whole,) * len(outs) + (anywhere,),
-            input_output_aliases={count: len(outs)},
-        )
-        operands = operands + (carry,)
-        out = outs + (shape(*carry.shape),)
+            in_specs=[whole] * count + [anywhere] * more,
+            out_specs=(whole,) * len(outs) + (anywhere,) * more,
+            input_output_aliases={count + k: len(outs) + k for k in range(more)},
+        )
+        operands = operands + tuple(carry)
+        out = outs + tuple(shape(*x.shape) for x in carry)
 
         def body(*refs):
-            kernel(*refs[:count], *refs[count + 1 : -1])
-
-    return pl.pallas_call(
+            kernel(*refs[:count], *refs[count + more : -more])
+
+    result = pl.pallas_call(
         body, out_shape=out, compiler_params=params(mib), cost_estimate=cost(flops, moved), **extra
     )(*operands)
+    if carry:
+        return tuple(result[: -len(carry)]) + (tuple(result[-len(carry) :]),)
+    return result
 
 
 def open_kernel(turned_ref, first_ref, second_ref, packed_ref):
@@ -170,15 +173,15 @@
     out_ref[...] = -dot(jnp.concatenate(tiles, 0), inverse_ref[...])
 
 
-def down_kernel(first_ref, second_ref, a_ref, out_ref, kept_ref, sems):
+def down_kernel(base, first_ref, second_ref, a_ref, out_ref, kept_ref, sems):
     width = first_ref.shape[0]
-    columns = a_ref.shape[1]
     count = sems.shape[0]
-    size = columns // count
+    size = out_ref.shape[1] // count
 
     def load(i):
-        part = pl.ds(pl.multiple_of(i * size, size), size)
-        return pltpu.make_async_copy(a_ref.at[:, part], kept_ref.at[:, part], sems.at[i])
+        start = pl.multiple_of(i * size, size)
+        source = a_ref.at[:, pl.ds(pl.multiple_of(base + start, size), size)]
+        return pltpu.make_async_copy(source, kept_ref.at[:, pl.ds(start, size)], sems.at[i])
 
     for i in range(count):
         load(i).start()
@@ -194,34 +197,42 @@
         out_ref[:, part] = term[:width] + term[width:]
 
 
-def product_down(first, second, a):
+def product_down(first, second, a, at, carry=()):
     rows, columns = a.shape
     width = first.shape[0]
-    size = block_of(columns, 256)
+    span = columns // 2
+    size = block_of(span, 256)
     whole = pl.BlockSpec(memory_space=pltpu.VMEM)
-    return pl.pallas_call(
-        down_kernel,
-        in_specs=[whole, whole, pl.BlockSpec(memory_space=pltpu.HBM)],
-        out_specs=(whole, whole),
-        out_shape=(shape(width, columns), shape(rows, columns)),
-        scratch_shapes=[pltpu.SemaphoreType.DMA((columns // size,))],
+    anywhere = pl.BlockSpec(memory_space=pl.ANY)
+    more = len(carry)
+
+    def kernel(first_ref, second_ref, a_ref, *refs):
+        out_ref, kept_ref = refs[more : more + 2]
+        down_kernel(at * span, first_ref, second_ref, a_ref, out_ref, kept_ref, refs[-1])
+
+    out, kept, *carried = pl.pallas_call(
+        kernel,
+        in_specs=[whole, whole, pl.BlockSpec(memory_space=pltpu.HBM)] + [anywhere] * more,
+        out_specs=(whole, whole) + (anywhere,) * more,
+        out_shape=(shape(width, span), shape(rows, span)) + tuple(shape(*x.shape) for x in carry),
+        input_output_aliases={3 + k: 2 + k for k in range(more)},
+        scratch_shapes=[pltpu.SemaphoreType.DMA((span // size,))],
         compiler_params=params(12),
-        cost_estimate=cost(8 * rows * columns * width, 4 * rows * columns),
-        name="product_down",
-    )(first, second, pltpu.with_memory_space_constraint(a, pltpu.HBM))
-
-
-def fix_kernel(raw_ref, band_ref, top_ref, keep_ref, give_ref, _):
-    half = keep_ref.shape[1]
+        cost_estimate=cost(8 * rows * span * width, 4 * rows * span),
+    )(first, second, pltpu.with_memory_space_constraint(a, pltpu.HBM), *carry)
+    return out, tuple(carried) + (kept,)
+
+
+def fix_kernel(low_ref, high_ref, band_ref, top_ref, over_ref, keep_ref, give_ref, *_):
     row = lax.axis_index("row")
     core = lax.rem(row, 2)
-    first, second = raw_ref[:, :half], raw_ref[:, half:]
+    first, second = low_ref[...], high_ref[...]
 
     @pl.when(row == 0)
     def _():
         turned = band_ref[...].T
-        keep_ref[...] = first - dot(turned, top_ref[:, :half])
-        give_ref[...] = second - dot(turned, top_ref[:, half:])
+        keep_ref[...] = first - dot(turned, top_ref[...])
+        give_ref[...] = second - dot(turned, over_ref[...])
 
     @pl.when((row != 0) & (core == 0))
     def _():
@@ -234,34 +245,35 @@
         give_ref[...] = first
 
 
-def fix_down(raw, band, a):
-    width, columns = raw.shape
-    half = shape(width, columns // 2)
-    whole = pl.BlockSpec((width, columns), lambda i: (0, 0))
-    halves = pl.BlockSpec((width, columns // 2), lambda i: (0, 0))
-    return pl.pallas_call(
+def fix_down(low, high, band, halves):
+    width, span = low.shape
+    part = pl.BlockSpec((width, span), lambda i: (0, 0))
+    anywhere = pl.BlockSpec(memory_space=pl.ANY)
+    keep, give, *halves = pl.pallas_call(
         fix_kernel,
         grid=(1,),
-        in_specs=[whole, pl.BlockSpec((width, width), lambda i: (0, 0)), whole],
-        out_specs=(halves, halves, pl.BlockSpec(memory_space=pl.ANY)),
-        out_shape=(half, half, shape(*a.shape)),
-        input_output_aliases={2: 2},
+        in_specs=[part, part, pl.BlockSpec((width, width), lambda i: (0, 0)), part, part],
+        out_specs=(part, part, anywhere, anywhere),
+        out_shape=(shape(width, span),) * 2 + tuple(shape(*x.shape) for x in halves),
+        input_output_aliases={3: 2, 4: 3},
         compiler_params=params(12),
-        cost_estimate=cost(12 * width * width * columns, 16 * width * columns),
+        cost_estimate=cost(24 * width * width * span, 32 * width * span),
         name="fix_down",
-    )(raw, band, a)
-
-
-def rows_product(right_ref, a_ref, outs):
-    columns = a_ref.shape[1]
+    )(low, high, band, *halves)
+    return keep, give, tuple(halves)
+
+
+def rows_product(right_ref, halves, outs):
+    span = halves[0].shape[1]
     width = right_ref.shape[1] // 2
-    chunk = block_of(columns, 512)
+    chunk = block_of(span, 512)
     total = None
-    for c in range(0, columns, chunk):
-        ah, al = split(a_ref[:, c : c + chunk])
-        right = right_ref[c : c + chunk, :]
-        term = fast(ah, right) + fast(al, right)
-        total = term if total is None else total + term
+    for at, a_ref in enumerate(halves):
+        for c in range(0, span, chunk):
+            ah, al = split(a_ref[:, c : c + chunk])
+            right = right_ref[at * span + c : at * span + c + chunk, :]
+            term = fast(ah, right) + fast(al, right)
+            total = term if total is None else total + term
     result = (total[:, :width] + total[:, width:]).T
     for at, out_ref in enumerate(outs):
 
@@ -270,9 +282,9 @@
             out_ref[...] = result
 
 
-def across_kernel(held_ref, other_ref, band_ref, a_ref, kct_ref, right_ref, *refs):
+def across_kernel(held_ref, other_ref, band_ref, low_ref, high_ref, kct_ref, right_ref, *refs):
     width, half = held_ref.shape
-    columns = a_ref.shape[1]
+    columns = 2 * half
     chunk = block_of(columns, 512)
 
     @pl.when(pl.program_id(0) == 0)
@@ -296,15 +308,15 @@
         for c in range(0, columns, chunk):
             right_ref[c : c + chunk, :] = jnp.concatenate(split(kct_ref[:, c : c + chunk].T), 1)
 
-    rows_product(right_ref, a_ref, refs[:-1])
-
-
-def more_kernel(right_ref, a_ref, *refs):
-    rows_product(right_ref, a_ref, refs[:-1])
-
-
-def across_call(kernel, operands, extra, a, pieces, start, count, width):
-    rows, columns = a.shape
+    rows_product(right_ref, (low_ref, high_ref), refs[:-2])
+
+
+def more_kernel(right_ref, low_ref, high_ref, *refs):
+    rows_product(right_ref, (low_ref, high_ref), refs[:-2])
+
+
+def across_call(kernel, operands, extra, halves, pieces, start, count, width):
+    rows, span = halves[0].shape
     size = rows // pieces
 
     def turn(i):
@@ -313,18 +325,19 @@
     def fixed(array):
         return pl.BlockSpec(array.shape, lambda i: (0, 0))
 
-    one = shape(width, size)
-    outs = tuple(extra) + (one,) * count
-    return pl.pallas_call(
+    outs = tuple(extra) + (shape(width, size),) * count
+    at, to = len(operands), len(outs)
+    *results, low, high = pl.pallas_call(
         kernel,
         grid=(count,),
-        in_specs=[fixed(x) for x in operands] + [pl.BlockSpec((size, columns), turn)],
-        out_specs=tuple(fixed(x) for x in outs) + (pl.BlockSpec(memory_space=pl.ANY),),
-        out_shape=outs + (shape(rows, columns),),
-        input_output_aliases={len(operands): len(outs)},
+        in_specs=[fixed(x) for x in operands] + [pl.BlockSpec((size, span), turn)] * 2,
+        out_specs=tuple(fixed(x) for x in outs) + (pl.BlockSpec(memory_space=pl.ANY),) * 2,
+        out_shape=outs + (shape(rows, span),) * 2,
+        input_output_aliases={at: to, at + 1: to + 1},
         compiler_params=params(22),
-        cost_estimate=cost(8 * size * count * columns * width, 4 * size * count * columns),
-    )(*operands, a)
+        cost_estimate=cost(16 * size * count * span * width, 8 * size * count * span),
+    )(*operands, *halves)
+    return (*results, (low, high))
 
 
 def merge_first_kernel(first_ref, second_ref, by_x_ref, by_y_ref, a_ref, b_ref):
@@ -379,7 +392,9 @@
     )
 
 
-def wide_kernel(st_ref, xct_ref, kct_ref, first_ref, second_ref, band_ref, x_ref, k_ref, rows_ref):
+def wide_kernel(
+    st_ref, xct_ref, kct_ref, first_ref, second_ref, band_ref, x_ref, k_ref, rows_ref, left_ref
+):
     width, columns = kct_ref.shape
     st = st_ref[...]
     chunk = block_of(columns, 512)
@@ -397,47 +412,55 @@
     def _():
         rows_ref[:, :width] = rows_ref[:, :width] - band_ref[...].T
 
-
-def four_products(left, right_ref, start, size):
-    width = left.shape[1] // 2
-    high = right_ref[:width, pl.ds(start, size)]
-    low = right_ref[width:, pl.ds(start, size)]
-    return fast(
-        jnp.concatenate([left, left], 1), jnp.concatenate([high, high, low, low], 0)
-    )
-
-
-def near_kernel(rows_ref, right_ref, a_ref, out_ref, left_ref):
-    rows, columns = a_ref.shape
+    rows = rows_ref.shape[1]
     deep = block_of(rows, 512)
     for r in range(0, rows, deep):
         left_ref[r : r + deep, :] = jnp.concatenate(split(rows_ref[:, r : r + deep].T), 1)
-    chunk = block_of(columns, 512)
-
-    @pl.loop(0, columns // chunk)
+
+
+def both_parts(left):
+    return jnp.concatenate([left, left], 1)
+
+
+def four_parts(right_ref, start, size):
+    width = right_ref.shape[0] // 2
+    high = right_ref[:width, pl.ds(start, size)]
+    low = right_ref[width:, pl.ds(start, size)]
+    return jnp.concatenate([high, high, low, low], 0)
+
+
+def near_kernel(left_ref, right_ref, a_ref, _, out_ref, __):
+    rows, span = a_ref.shape
+    deep = block_of(rows, 512)
+    chunk = block_of(span, 512)
+
+    @pl.loop(0, span // chunk)
     def _(i):
         c = pl.multiple_of(i * chunk, chunk)
+        right = four_parts(right_ref, c, chunk)
         for r in range(0, rows, deep):
-            out_ref[r : r + deep, pl.ds(c, chunk)] = a_ref[r : r + deep, pl.ds(c, chunk)] - (
-                four_products(left_ref[r : r + deep, :], right_ref, c, chunk)
+            out_ref[r : r + deep, pl.ds(c, chunk)] = a_ref[r : r + deep, pl.ds(c, chunk)] - fast(
+                both_parts(left_ref[r : r + deep, :]), right
             )
 
 
-def subtract_near(krt, right, a):
-    rows, columns = a.shape
-    width = krt.shape[0]
+def subtract_near(left, right, low, high):
+    rows, span = low.shape
+    deep = left.shape[1]
     whole = pl.BlockSpec(memory_space=pltpu.VMEM)
-    return pl.pallas_call(
-        near_kernel,
-        in_specs=[whole] * 3,
-        out_specs=whole,
-        out_shape=shape(rows, columns),
-        input_output_aliases={2: 0},
-        scratch_shapes=[pltpu.VMEM((rows, 2 * width), bf16)],
-        compiler_params=params(12),
-        cost_estimate=cost(8 * rows * columns * width, 8 * rows * columns),
-        name="subtract_near",
-    )(krt, right, a)
+    anywhere = pl.BlockSpec(memory_space=pl.ANY)
+    return tuple(
+        pl.pallas_call(
+            near_kernel,
+            in_specs=[whole] * 3 + [anywhere],
+            out_specs=(whole, anywhere),
+            out_shape=(shape(rows, span),) * 2,
+            input_output_aliases={2: 0, 3: 1},
+            compiler_params=params(12),
+            cost_estimate=cost(4 * rows * span * deep, 8 * rows * span),
+            name="subtract_near",
+        )(left, right, low, high)
+    )
 
 
 def core_kernel(part_ref, more_ref, st_ref, krt_ref, out_ref):
@@ -458,58 +481,63 @@
         left_ref[pl.ds(start, size), :] = jnp.concatenate(split(value.T), 1)
 
 
-def far_kernel(left_ref, right_ref, a_ref, out_ref, buffer, sems):
-    rows, columns = a_ref.shape
+def far_kernel(
+    left_ref, right_ref, near_left_ref, near_right_ref, low_ref, high_ref, out_ref, buffer, sems
+):
+    rows, span = low_ref.shape
     slots, deep, wide = buffer.shape
-    down, along = rows // deep, columns // wide
-    count = down * along
-
-    def place(i):
-        return (
-            pl.multiple_of(lax.rem(i, down) * deep, deep),
-            pl.multiple_of(lax.div(i, down) * wide, wide),
-        )
+    down = rows // deep
+    pairs = down * (span // wide)
 
     def store(i, slot):
-        r, c = place(i)
+        turn, pair = lax.rem(i, 2), lax.div(i, 2)
+        r = pl.multiple_of(lax.rem(pair, down) * deep, deep)
+        c = pl.multiple_of(turn * span + lax.div(pair, down) * wide, wide)
         return pltpu.make_async_copy(
             buffer.at[slot], out_ref.at[pl.ds(r, deep), pl.ds(c, wide)], sems.at[slot]
         )
 
-    @pl.loop(0, count)
-    def _(i):
-        slot = lax.rem(i, slots)
-
-        @pl.when(i >= slots)
-        def _():
-            store(i - slots, slot).wait()
-
-        r, c = place(i)
-        buffer[slot] = a_ref[pl.ds(r, deep), pl.ds(c, wide)] - four_products(
-            left_ref[pl.ds(r, deep), :], right_ref, c, wide
-        )
-        store(i, slot).start()
+    @pl.loop(0, pairs)
+    def _(pair):
+        r = pl.multiple_of(lax.rem(pair, down) * deep, deep)
+        local = pl.multiple_of(lax.div(pair, down) * wide, wide)
+        for turn, a_ref in enumerate((low_ref, high_ref)):
+            i = pair * 2 + turn
+            slot = lax.rem(i, slots)
+
+            @pl.when(i >= slots)
+            def _():
+                store(i - slots, slot).wait()
+
+            c = pl.multiple_of(turn * span + local, wide)
+            left = both_parts(left_ref[pl.ds(r, deep), :])
+            right = four_parts(right_ref, c, wide)
+            if turn:
+                left = jnp.concatenate([left, both_parts(near_left_ref[pl.ds(r, deep), :])], 1)
+                right = jnp.concatenate([right, four_parts(near_right_ref, c, wide)], 0)
+            buffer[slot] = a_ref[pl.ds(r, deep), pl.ds(local, wide)] - fast(left, right)
+            store(i, slot).start()
 
     for back in range(slots, 0, -1):
-        store(count - back, (count - back) % slots).wait()
-
-
-def subtract_far(left, right, a):
-    rows, columns = a.shape
+        store(2 * pairs - back, (2 * pairs - back) % slots).wait()
+
+
+def subtract_far(left, right, near_left, near_right, low, high):
+    rows, span = low.shape
     deep = left.shape[1]
     whole = pl.BlockSpec(memory_space=pltpu.VMEM)
-    wide = columns if (columns // 4) % 128 else columns // 4
+    wide = span if (span // 2) % 128 else span // 2
     piece = (block_of(rows, 512), wide)
     return pl.pallas_call(
         far_kernel,
-        in_specs=[whole] * 3,
+        in_specs=[whole] * 6,
         out_specs=pl.BlockSpec(memory_space=pltpu.HBM),
-        out_shape=shape(rows, columns),
+        out_shape=shape(rows, 2 * span),
         scratch_shapes=[pltpu.VMEM((3,) + piece, f32), pltpu.SemaphoreType.DMA((3,))],
         compiler_params=params(12),
-        cost_estimate=cost(4 * rows * columns * deep, 8 * rows * columns),
+        cost_estimate=cost(12 * rows * span * deep, 16 * rows * span),
         name="subtract_far",
-    )(left, right, a)
+    )(left, right, near_left, near_right, low, high)
 
 
 def flip(value, bit, size, axis="row"):
@@ -561,7 +589,7 @@
             zero = jnp.zeros_like(total)
             terms = [total, flip(total, row_size // 2, row_size), zero, zero]
         first, second, partial = lax.optimization_barrier((first, second, partial))
-        raw, resident = product_down(first, second, matrix)
+        low, resident = product_down(first, second, matrix, 0)
         if row_size == 8:
             one, two, resident = small_call(
                 merge_first_kernel, (half, half), first, second, by_x, by_y, carry=resident
@@ -577,19 +605,20 @@
                 held = held + from_sources(held, col_size, reached, bit)
                 reached = reached + [r ^ bit for r in reached]
                 bit *= 2
+        high, resident = product_down(first, second, matrix, 1, resident)
         band, again, band_inverse, head, resident = small_call(
             eliminate_kernel, (small, small, small, small), *terms, flops=50_000_000, carry=resident
         )
-        keep, give, resident = fix_down(raw, again, resident)
-        quarter = shape(width, columns // 4)
-        a, b, resident = small_call(
-            halve_kernel, (quarter, quarter), keep, flip(give, 1, row_size), carry=resident
-        )
+        keep, give, resident = fix_down(low, high, again, resident)
         if row_size == 8:
             held, resident = small_call(
                 join_kernel, shape(width, rows), one, more_y, two, more_x, carry=resident
             )
         other = flip(held, 1, row_size)
+        quarter = shape(width, columns // 4)
+        a, b, resident = small_call(
+            halve_kernel, (quarter, quarter), keep, flip(give, 1, row_size), carry=resident
+        )
         bits = []
         bit = 2
         while bit < row_size:
@@ -653,12 +682,13 @@
         st, resident = small_call(
             invert_kernel, small, head, again, band_inverse, flops=50_000_000, carry=resident
         )
-        xparts, kparts, krt, resident = small_call(
+        xparts, kparts, krt, near_left, resident = small_call(
             wide_kernel,
             (
                 shape(2 * width, columns, dtype=bf16),
                 shape(2 * width, columns, dtype=bf16),
                 shape(width, rows),
+                shape(rows, 2 * width, dtype=bf16),
             ),
             st,
             xct,
@@ -669,7 +699,7 @@
             mib=12,
             carry=resident,
         )
-        resident = subtract_near(krt, xparts, resident)
+        resident = subtract_near(near_left, xparts, *resident)
         core, resident = small_call(
             core_kernel, shape(width, rows), inner, more, st, krt, carry=resident
         )
@@ -682,7 +712,7 @@
             mib=12,
             carry=resident,
         )
-        return subtract_far(left, kparts, resident), band
+        return subtract_far(left, kparts, near_left, xparts, *resident), band
 
     return body
 

time: 81.4 us -> 80.4 us (0.988)
  starting transfers between devices: 27.4 us -> 26.1 us
    ppermute x2, waiting for transfers between devices: 4.44 us -> 0.01 us  [from_sources(): return lax.ppermute(piece, ('row', 'col'), pairs)]
    ppermute x13, waiting for transfers between devices: 6.68 us -> 11 us  [flip(): return lax.ppermute(value, axis, [(i, i ^ bit) for i in range(size)])]
    pallas_call x4 -> x5, Pallas kernels: 19.9 us -> 20 us  [the longest x1 8.52 us: subtract_far(): pl.pallas_call(far_kernel, in_specs=[whole] * 6, out_specs=pl.BlockSpec(m...]
  transfers between devices with their start and end apart: 21 -> 21, of which waited for: 10 -> 13; matrix products, arithmetic and copies ran while one was open for 0% -> 0% of each run, Pallas kernels for 29% -> 33%
where the time goes in v5:
time: 80.4 us; the launch traced here: 80.2 us
  Pallas kernels  36.5 us (45%)
  starting transfers between devices  26.1 us (32%)
  waiting for transfers between devices  15.5 us (19%)
  between operations  1.03 us (1%)
  local copies, waits for them, and re-layouts  0.99 us (1%)
    ppermute x13, starting transfers between devices, flip(): return lax.ppermute(value, axis, [(i, i ^ bit) for i in range(size)])  11 us
    ppermute x13, waiting for transfers between devices, flip(): return lax.ppermute(value, axis, [(i, i ^ bit) for i in range(size)])  11 us
    pallas_call x15, Pallas kernels, small_call(): pl.pallas_call(body, out_shape=out, compiler_params=params(mib), cost_est...  9.58 us
    ppermute x6, starting transfers between devices, shift(): lax.ppermute(piece, 'col', [(i, (i + by) % size) for i in range(size)])  9.22 us
    pallas_call x1, Pallas kernels, subtract_far(): pl.pallas_call(far_kernel, in_specs=[whole] * 6, out_specs=pl.BlockSpec(m...  8.52 us
    pallas_call x2, Pallas kernels, product_down(): pl.pallas_call(kernel, in_specs=[whole, whole, pl.BlockSpec(memory_space=...  8.48 us
    pallas_call x2, Pallas kernels, across_call(): pl.pallas_call(kernel, grid=(count,), in_specs=[fixed(x) for x in operand...  6.96 us
    ppermute x2, starting transfers between devices, from_sources(): return lax.ppermute(piece, ('row', 'col'), pairs)  5.88 us
  transfers between devices with their start and end apart: 21, of which 13 were waited for; matrix products, arithmetic and copies ran while one was open for 0% of the time, Pallas kernels for 33%

profile of v5, /device:TPU:0, one launch (start us, length us, event | category | flops | bytes accessed | tf_op | source)
XLA Modules:
  0.0 80.2 jit_solution(11997868537603145253)
XLA Ops:
  0.6 0.0 copy-start
  0.6 1.0 %copy-done = f32[1536,64]{0,1:T(8,128)S(1)} copy-done((f32[1536,64]{0,1:T(8,128)S(1)}, f32[1536,64]{0,1:T(8,128)}, u32[]{:S(2)}) %copy-start) | copy-done | bytes 393240
  1.6 0.5 shard_map.41
  2.1 0.6 collective-permute-start
  2.7 0.9 %collective-permute-done.b_ref = f32[64,128]{1,0:T(8,128)S(1)} collective-permute-done((f32[64,128]{1,0:T(8,128)S(1)}, f32[64,128]{1,0:T(8,128)S(1)}, u32[]{:S(2)}, u32[]{:S(2)}) %collective-permute-start) | collective-permute-done | bytes 32800 | tf_op jit(solution)/shard_map/ppermute | solution.py:544
  3.6 2.9 %collective-permute-start.1 = (f32[64,896]{1,0:T(8,128)S(1)}, f32[64,896]{1,0:T(8,128)S(1)}, u32[]{:S(2)}, u32[]{:S(2)}) collective-permute-start(f32[64,896]{1,0:T(8,128)S(1)} %get-tuple-element.83), channel_id=1, source_target_pairs={{0,8},{4,12},{8,0},{12,4},{16,24},{20,28},{24,16},{28,20},{1,9},{5... | collective-permute-start | bytes 688136 | tf_op jit(solution)/shard_map/ppermute | solution.py:544
  6.4 1.5 %collective-permute-start.2 = (f32[64,896]{1,0:T(8,128)S(1)}, f32[64,896]{1,0:T(8,128)S(1)}, u32[]{:S(2)}, u32[]{:S(2)}) collective-permute-start(f32[64,896]{1,0:T(8,128)S(1)} %get-tuple-element.84), channel_id=1, source_target_pairs={{0,16},{4,20},{8,24},{12,28},{16,0},{20,4},{24,8},{28,12},{1,17},{... | collective-permute-start | bytes 688136 | tf_op jit(solution)/shard_map/ppermute | solution.py:544
  8.0 0.0 collective-permute-start.3
  8.0 4.2 %shard_map.43 = (f32[64,1536]{1,0:T(8,128)S(1)}, f32[1536,1536]{1,0:T(8,128)S(1)}) custom-call(f32[64,768]{1,0:T(8,128)S(1)} %get-tuple-element.85.first_ref.refs_0_.refs_3_, f32[64,768]{1,0:T(8,128)S(1)} %get-tuple-element.86.second_ref.refs_1_.refs_4_, f32[1536,3072]{1,0:T(8,128)} %a_ref.3), custom_call_target="tpu_custom_call" | custom-call | flops 1207959552 | bytes 9437184 | tf_op jit(solution)/shard_map/pallas_call | solution.py:213
  12.2 0.5 collective-permute-done.1.refs_2_.refs_1_
  12.7 1.8 %collective-permute-done.2.refs_3_.refs_2_ = f32[64,896]{1,0:T(8,128)S(1)} collective-permute-done((f32[64,896]{1,0:T(8,128)S(1)}, f32[64,896]{1,0:T(8,128)S(1)}, u32[]{:S(2)}, u32[]{:S(2)}) %collective-permute-start.2) | collective-permute-done | bytes 229408 | tf_op jit(solution)/shard_map/ppermute | solution.py:544
  14.5 0.1 shard_map.44
  14.6 3.4 %collective-permute-start.4 = (f32[64,768]{1,0:T(8,128)S(1)}, f32[64,768]{1,0:T(8,128)S(1)}, u32[]{:S(2)}, u32[]{:S(2)}) collective-permute-start(f32[64,768]{1,0:T(8,128)S(1)} %get-tuple-element.94.refs_0_), channel_id=1, source_target_pairs={{0,16},{4,20},{8,24},{12,28},{9,25},{13,29},{1,17},{5,21},{18,2},{... | collective-permute-start | bytes 589832 | tf_op jit(solution)/shard_map/ppermute | solution.py:554
  18.0 2.4 %collective-permute-start.5 = (f32[64,768]{1,0:T(8,128)S(1)}, f32[64,768]{1,0:T(8,128)S(1)}, u32[]{:S(2)}, u32[]{:S(2)}) collective-permute-start(f32[64,768]{1,0:T(8,128)S(1)} %get-tuple-element.95.refs_2_), channel_id=1, source_target_pairs={{0,8},{4,12},{16,24},{20,28},{9,1},{13,5},{25,17},{29,21},{18,26},... | collective-permute-start | bytes 589832 | tf_op jit(solution)/shard_map/ppermute | solution.py:554
  20.5 4.2 %shard_map.45 = (f32[64,1536]{1,0:T(8,128)S(1)}, f32[1536,1536]{1,0:T(8,128)S(1)}, f32[1536,1536]{1,0:T(8,128)S(1)}) custom-call(f32[64,768]{1,0:T(8,128)S(1)} %get-tuple-element.85.first_ref.refs_0_.refs_3_, f32[64,768]{1,0:T(8,128)S(1)} %get-tuple-element.86.second_ref.refs_1_.refs_4_, f32[1536,3072]{1,0:T(8,128)} %a_ref.3, ...), custom_call_target="tpu_custom_call", output_to_operand_aliasing={{2}: (3, {})} | custom-call | flops 1207959552 | bytes 9437184 | tf_op jit(solution)/shard_map/pallas_call | solution.py:213
  24.7 0.0 collective-permute-done.3.refs_3_
  24.8 2.7 %shard_map.46 = (f32[64,64]{1,0:T(8,128)}, f32[64,64]{1,0:T(8,128)S(1)}, f32[64,64]{1,0:T(8,128)S(1)}, f32[64,64]{1,0:T(8,128)S(1)}, f32[1536,1536]{1,0:T(8,128)S(1)}, /*index=5*/f32[1536,1536]{1,0:T(8,128)S(1)}) custom-call(f32[64,128]{1,0:T(8,128)S(1)} %get-tuple-element.82.refs_0_, ...), custom_call_target="tpu_custom_call", output_to_operand_aliasing={{4}: (4, {}), {5}: (5, {})} | custom-call | flops 50000000 | bytes 1000000 | tf_op jit(solution)/shard_map/pallas_call | solution.py:64
  27.4 0.9 %fix_down.1 = (f32[64,1536]{1,0:T(8,128)S(1)}, f32[64,1536]{1,0:T(8,128)S(1)}, f32[1536,1536]{1,0:T(8,128)S(1)}, f32[1536,1536]{1,0:T(8,128)S(1)}) custom-call(f32[64,1536]{1,0:T(8,128)S(1)} %get-tuple-element.96.low_ref, f32[64,1536]{1,0:T(8,128)S(1)} %get-tuple-element.97.high_ref, ...), custom_call_target="tpu_custom_call", output_to_operand_aliasing={{2}: (3, {}), {3}: (4, {})} | custom-call | flops 150994944 | bytes 3145728 | tf_op jit(solution)/shard_map/fix_down/pallas_call | solution.py:252
  28.3 0.1 collective-permute-start.7
  28.4 0.0 collective-permute-done.4.refs_1_
  28.4 0.0 collective-permute-done.5.refs_3_
  28.5 0.5 collective-permute-start.6
  29.0 1.1 %collective-permute-done.7.refs_1_ = f32[64,1536]{1,0:T(8,128)S(1)} collective-permute-done((f32[64,1536]{1,0:T(8,128)S(1)}, f32[64,1536]{1,0:T(8,128)S(1)}, u32[]{:S(2)}, u32[]{:S(2)}) %collective-permute-start.7) | collective-permute-done | bytes 393248 | tf_op jit(solution)/shard_map/ppermute | solution.py:544
  30.2 0.1 collective-permute-start.8
  30.2 0.1 collective-permute-start.9
  30.3 0.4 collective-permute-done.6.other_ref
  30.7 3.9 %shard_map.49 = (f32[64,3072]{1,0:T(8,128)S(1)}, bf16[3072,128]{1,0:T(8,128)(2,1)S(1)}, f32[64,384]{1,0:T(8,128)S(1)}, f32[64,384]{1,0:T(8,128)S(1)}, f32[1536,1...) custom-call(f32[64,1536]{1,0:T(8,128)S(1)} %get-tuple-element.102.held_ref, ...), custom_call_target="tpu_custom_call", output_to_operand_aliasing={{4}: (3, {}), {5}: (4, {})} | custom-call | flops 1207959552 | bytes 9437184 | tf_op jit(solution)/shard_map/pallas_call | solution.py:330
  34.6 2.6 %collective-permute-done.8.refs_1_ = f32[64,768]{1,0:T(8,128)S(1)} collective-permute-done((f32[64,768]{1,0:T(8,128)S(1)}, f32[64,768]{1,0:T(8,128)S(1)}, u32[]{:S(2)}, u32[]{:S(2)}) %collective-permute-start.8) | collective-permute-done | bytes 196640 | tf_op jit(solution)/shard_map/ppermute | solution.py:544
  37.2 0.1 collective-permute-done.9.refs_3_
  37.3 0.4 collective-permute-start.10
  37.7 1.7 %collective-permute-start.11 = (f32[64,768]{1,0:T(8,128)S(1)}, f32[64,768]{1,0:T(8,128)S(1)}, u32[]{:S(2)}, u32[]{:S(2)}) collective-permute-start(f32[64,768]{1,0:T(8,128)S(1)} %get-tuple-element.115.refs_2_), channel_id=1, source_target_pairs={{0,8},{4,12},{8,0},{12,4},{16,24},{20,28},{24,16},{28,20},{1,9},{5... | collective-permute-start | bytes 589832 | tf_op jit(solution)/shard_map/ppermute | solution.py:544
  39.3 3.1 %shard_map.51 = (f32[64,384]{1,0:T(8,128)S(1)}, f32[64,384]{1,0:T(8,128)S(1)}, f32[1536,1536]{1,0:T(8,128)S(1)}, f32[1536,1536]{1,0:T(8,128)S(1)}) custom-call(bf16[3072,128]{1,0:T(8,128)(2,1)S(1)} %get-tuple-element.116.right_ref, f32[1536,1536]{1,0:T(8,128)S(1)} %get-tuple-element.117.low_ref, ...), custom_call_target="tpu_custom_call", output_to_operand_aliasing={{2}: (1, {}), {3}: (2, {})} | custom-call | flops 1207959552 | bytes 9437184 | tf_op jit(solution)/shard_map/pallas_call | solution.py:330
  42.4 1.1 %collective-permute-done.10.refs_1_ = f32[64,768]{1,0:T(8,128)S(1)} collective-permute-done((f32[64,768]{1,0:T(8,128)S(1)}, f32[64,768]{1,0:T(8,128)S(1)}, u32[]{:S(2)}, u32[]{:S(2)}) %collective-permute-start.10) | collective-permute-done | bytes 196640 | tf_op jit(solution)/shard_map/ppermute | solution.py:544
  43.5 0.3 collective-permute-done.11.refs_3_
  43.8 0.1 collective-permute-start.12
  43.9 1.7 %collective-permute-start.16 = (f32[64,384]{1,0:T(8,128)S(1)}, f32[64,384]{1,0:T(8,128)S(1)}, u32[]{:S(2)}, u32[]{:S(2)}) collective-permute-start(f32[64,384]{1,0:T(8,128)S(1)} %get-tuple-element.128), channel_id=1, source_target_pairs={{0,1},{1,2},{2,3},{3,0},{4,5},{5,6},{6,7},{7,4},{8,9},{9,10},{10,1... | collective-permute-start | bytes 294920 | tf_op jit(solution)/shard_map/ppermute | solution.py:558
  45.6 2.7 %collective-permute-start.14 = (f32[64,384]{1,0:T(8,128)S(1)}, f32[64,384]{1,0:T(8,128)S(1)}, u32[]{:S(2)}, u32[]{:S(2)}) collective-permute-start(f32[64,384]{1,0:T(8,128)S(1)} %get-tuple-element.126), channel_id=1, source_target_pairs={{0,2},{1,3},{2,0},{3,1},{4,6},{5,7},{6,4},{7,5},{8,10},{9,11},{10,... | collective-permute-start | bytes 294920 | tf_op jit(solution)/shard_map/ppermute | solution.py:558
  48.2 0.0 collective-permute-start.15
  48.2 0.0 collective-permute-done.12.refs_2_
  48.2 0.8 %shard_map.53 = (f32[64,3072]{1,0:T(8,128)S(1)}, f32[64,64]{1,0:T(8,128)S(1)}, f32[1536,1536]{1,0:T(8,128)S(1)}, f32[1536,1536]{1,0:T(8,128)S(1)}) custom-call(f32[64,3072]{1,0:T(8,128)S(1)} %get-tuple-element.109.refs_0_.refs_2_, f32[64,1536]{1,0:T(8,128)S(1)} %get-tuple-element.121.refs_1_, ...), custom_call_target="tpu_custom_call", output_to_operand_aliasing={{2}: (3, {}), {3}: (4, {})} | custom-call | flops 1000000 | bytes 1000000 | tf_op jit(solution)/shard_map/pallas_call | solution.py:64
  49.1 2.1 %collective-permute-start.13 = (f32[64,64]{1,0:T(8,128)S(1)}, f32[64,64]{1,0:T(8,128)S(1)}, u32[]{:S(2)}, u32[]{:S(2)}) collective-permute-start(f32[64,64]{1,0:T(8,128)S(1)} %get-tuple-element.124.refs_0_), channel_id=1, source_target_pairs={{0,1},{1,0},{2,3},{3,2},{4,5},{5,4},{6,7},{7,6},{8,9},{9,8},{10,11... | collective-permute-start | bytes 49160 | tf_op jit(solution)/shard_map/ppermute | solution.py:544
  51.2 0.3 collective-permute-done.16.refs_3_
  51.5 3.9 %collective-permute-done.14.refs_1_ = f32[64,384]{1,0:T(8,128)S(1)} collective-permute-done((f32[64,384]{1,0:T(8,128)S(1)}, f32[64,384]{1,0:T(8,128)S(1)}, u32[]{:S(2)}, u32[]{:S(2)}) %collective-permute-start.14) | collective-permute-done | bytes 98336 | tf_op jit(solution)/shard_map/ppermute | solution.py:558
  55.4 0.2 collective-permute-done.15.refs_2_
  55.7 2.4 %collective-permute-start.18 = (f32[64,384]{1,0:T(8,128)S(1)}, f32[64,384]{1,0:T(8,128)S(1)}, u32[]{:S(2)}, u32[]{:S(2)}) collective-permute-start(f32[64,384]{1,0:T(8,128)S(1)} %get-tuple-element.148.refs_2_), channel_id=1, source_target_pairs={{0,1},{1,2},{2,3},{3,0},{4,5},{5,6},{6,7},{7,4},{8,9},{9,10},{10,1... | collective-permute-start | bytes 294920 | tf_op jit(solution)/shard_map/ppermute | solution.py:558
  58.1 0.5 collective-permute-start.19
  58.6 1.9 %collective-permute-start.20 = (f32[64,384]{1,0:T(8,128)S(1)}, f32[64,384]{1,0:T(8,128)S(1)}, u32[]{:S(2)}, u32[]{:S(2)}) collective-permute-start(f32[64,384]{1,0:T(8,128)S(1)} %get-tuple-element.148.refs_2_), channel_id=1, source_target_pairs={{0,3},{1,0},{2,1},{3,2},{4,7},{5,4},{6,5},{7,6},{8,11},{9,8},{10,9... | collective-permute-start | bytes 294920 | tf_op jit(solution)/shard_map/ppermute | solution.py:558
  60.5 0.0 collective-permute-done.13.refs_1_
  60.5 1.1 %collective-permute-start.17 = (f32[64,64]{1,0:T(8,128)S(1)}, f32[64,64]{1,0:T(8,128)S(1)}, u32[]{:S(2)}, u32[]{:S(2)}) collective-permute-start(f32[64,64]{1,0:T(8,128)S(1)} %get-tuple-element.136.refs_0_), channel_id=1, source_target_pairs={{0,2},{1,3},{2,0},{3,1},{4,6},{5,7},{6,4},{7,5},{8,10},{9,11},{10,... | collective-permute-start | bytes 49160 | tf_op jit(solution)/shard_map/ppermute | solution.py:544
  61.6 2.3 %shard_map.56 = (f32[64,64]{1,0:T(8,128)S(1)}, f32[1536,1536]{1,0:T(8,128)S(1)}, f32[1536,1536]{1,0:T(8,128)S(1)}) custom-call(f32[64,64]{1,0:T(8,128)S(1)} %get-tuple-element.91.refs_0_, f32[64,64]{1,0:T(8,128)S(1)} %get-tuple-element.92.band_ref.refs_1_.refs_5_, ...), custom_call_target="tpu_custom_call", output_to_operand_aliasing={{1}: (3, {}), {2}: (4, {})} | custom-call | flops 50000000 | bytes 1000000 | tf_op jit(solution)/shard_map/pallas_call | solution.py:64
  63.9 1.4 %shard_map.57 = (bf16[128,3072]{1,0:T(8,128)(2,1)S(1)}, bf16[128,3072]{1,0:T(8,128)(2,1)S(1)}, f32[64,1536]{1,0:T(8,128)S(1)}, bf16[1536,128]{1,0:T(8,128)(2,1)S...) custom-call(f32[64,64]{1,0:T(8,128)S(1)} %get-tuple-element.135.refs_0_.ref, ...), custom_call_target="tpu_custom_call", output_to_operand_aliasing={{4}: (6, {}), {5}: (7, {})} | custom-call | flops 1000000 | bytes 1000000 | tf_op jit(solution)/shard_map/pallas_call | solution.py:64
  65.4 2.1 %subtract_near.1 = (f32[1536,1536]{1,0:T(8,128)S(1)}, f32[1536,1536]{1,0:T(8,128)S(1)}) custom-call(bf16[1536,128]{1,0:T(8,128)(2,1)S(1)} %get-tuple-element.141.left_ref.near_left_ref, bf16[128,3072]{1,0:T(8,128)(2,1)S(1)} %get-tuple-element.142.right_ref.near_right_ref, ...), custom_call_target="tpu_custom_call", output_to_operand_aliasing={{0}: (2, {}), {1}: (3, {})} | custom-call | flops 1207959552 | bytes 18874368 | tf_op jit(solution)/shard_map/subtract_near/pallas_call | solution.py:453
  67.5 2.4 %collective-permute-done.17.refs_1_ = f32[64,64]{1,0:T(8,128)S(1)} collective-permute-done((f32[64,64]{1,0:T(8,128)S(1)}, f32[64,64]{1,0:T(8,128)S(1)}, u32[]{:S(2)}, u32[]{:S(2)}) %collective-permute-start.17) | collective-permute-done | bytes 16416 | tf_op jit(solution)/shard_map/ppermute | solution.py:544
  69.8 0.8 %shard_map.58 = (f32[64,1536]{1,0:T(8,128)S(1)}, f32[1536,1536]{1,0:T(8,128)S(1)}, f32[1536,1536]{1,0:T(8,128)S(1)}) custom-call(f32[64,64]{1,0:T(8,128)S(1)} %get-tuple-element.136.refs_0_, f32[64,64]{1,0:T(8,128)S(1)} %collective-permute-done.17.refs_1_, ...), custom_call_target="tpu_custom_call", output_to_operand_aliasing={{1}: (4, {}), {2}: (5, {})} | custom-call | flops 1000000 | bytes 1000000 | tf_op jit(solution)/shard_map/pallas_call | solution.py:64
  70.7 0.0 collective-permute-done.18.refs_3_
  70.7 0.0 collective-permute-done.19.refs_4_
  70.7 0.0 collective-permute-done.20.refs_5_
  70.7 0.8 %shard_map.59 = (bf16[1536,128]{1,0:T(8,128)(2,1)S(1)}, f32[1536,1536]{1,0:T(8,128)S(1)}, f32[1536,1536]{1,0:T(8,128)S(1)}) custom-call(f32[64,64]{1,0:T(8,128)S(1)} %get-tuple-element.135.refs_0_.refs_2_, f32[64,1536]{1,0:T(8,128)S(1)} %get-tuple-element.147.refs_1_, ...), custom_call_target="tpu_custom_call", output_to_operand_aliasing={{1}: (6, {}), {2}: (7, {})} | custom-call | flops 1000000 | bytes 1000000 | tf_op jit(solution)/shard_map/pallas_call | solution.py:64
  71.5 8.5 %subtract_far.1 = f32[1536,3072]{1,0:T(8,128)} custom-call(bf16[1536,128]{1,0:T(8,128)(2,1)S(1)} %get-tuple-element.151.left_ref, bf16[128,3072]{1,0:T(8,128)(2,1)S(1)} %get-tuple-element.152.right_ref, bf16[1536,128]{1,0:T(8,128)(2,1)S(1)} %get-tuple-element.141.left_ref.near_left_ref, bf16[128,3072]{1,0:T(8,128)(2,1)S(1)} %get-tuple-element.142.right_ref.near_right_ref, ...), custom_call_target="tpu_custom_call" | custom-call | flops 3623878656 | bytes 37748736 | tf_op jit(solution)/shard_map/subtract_far/pallas_call | solution.py:531
  (7 shorter events, 0.2 us)
Async XLA Ops:
  0.6 1.0 %copy-start = (f32[1536,64]{0,1:T(8,128)S(1)}, f32[1536,64]{0,1:T(8,128)}, u32[]{:S(2)}) copy-start(f32[1536,64]{0,1:T(8,128)} %param.3) | copy-start | bytes 1179652
  2.1 1.4 %collective-permute-start = (f32[64,128]{1,0:T(8,128)S(1)}, f32[64,128]{1,0:T(8,128)S(1)}, u32[]{:S(2)}, u32[]{:S(2)}) collective-permute-start(f32[64,128]{1,0:T(8,128)S(1)} %get-tuple-element.81.a_ref), channel_id=1, source_target_pairs={{0,4},{4,0},{8,12},{12,8},{16,20},{20,16},{24,28},{28,24},{1,5},{5... | collective-permute-start | bytes 98312 | tf_op jit(solution)/shard_map/ppermute | solution.py:544
  3.6 9.2 %collective-permute-start.1 = (f32[64,896]{1,0:T(8,128)S(1)}, f32[64,896]{1,0:T(8,128)S(1)}, u32[]{:S(2)}, u32[]{:S(2)}) collective-permute-start(f32[64,896]{1,0:T(8,128)S(1)} %get-tuple-element.83), channel_id=1, source_target_pairs={{0,8},{4,12},{8,0},{12,4},{16,24},{20,28},{24,16},{28,20},{1,9},{5... | collective-permute-start | bytes 688136 | tf_op jit(solution)/shard_map/ppermute | solution.py:544
  6.4 8.1 %collective-permute-start.2 = (f32[64,896]{1,0:T(8,128)S(1)}, f32[64,896]{1,0:T(8,128)S(1)}, u32[]{:S(2)}, u32[]{:S(2)}) collective-permute-start(f32[64,896]{1,0:T(8,128)S(1)} %get-tuple-element.84), channel_id=1, source_target_pairs={{0,16},{4,20},{8,24},{12,28},{16,0},{20,4},{24,8},{28,12},{1,17},{... | collective-permute-start | bytes 688136 | tf_op jit(solution)/shard_map/ppermute | solution.py:544
  8.0 16.8 %collective-permute-start.3 = (f32[64,128]{1,0:T(8,128)S(1)}, f32[64,128]{1,0:T(8,128)S(1)}, u32[]{:S(2)}, u32[]{:S(2)}) collective-permute-start(f32[64,128]{1,0:T(8,128)S(1)} %get-tuple-element.82.refs_0_), channel_id=1, source_target_pairs={{0,24},{4,28},{8,16},{12,20},{16,8},{20,12},{24,0},{28,4},{1,25},{... | collective-permute-start | bytes 98312 | tf_op jit(solution)/shard_map/ppermute | solution.py:544
  14.6 13.8 %collective-permute-start.4 = (f32[64,768]{1,0:T(8,128)S(1)}, f32[64,768]{1,0:T(8,128)S(1)}, u32[]{:S(2)}, u32[]{:S(2)}) collective-permute-start(f32[64,768]{1,0:T(8,128)S(1)} %get-tuple-element.94.refs_0_), channel_id=1, source_target_pairs={{0,16},{4,20},{8,24},{12,28},{9,25},{13,29},{1,17},{5,21},{18,2},{... | collective-permute-start | bytes 589832 | tf_op jit(solution)/shard_map/ppermute | solution.py:554
  18.0 10.4 %collective-permute-start.5 = (f32[64,768]{1,0:T(8,128)S(1)}, f32[64,768]{1,0:T(8,128)S(1)}, u32[]{:S(2)}, u32[]{:S(2)}) collective-permute-start(f32[64,768]{1,0:T(8,128)S(1)} %get-tuple-element.95.refs_2_), channel_id=1, source_target_pairs={{0,8},{4,12},{16,24},{20,28},{9,1},{13,5},{25,17},{29,21},{18,26},... | collective-permute-start | bytes 589832 | tf_op jit(solution)/shard_map/ppermute | solution.py:554
  28.3 1.8 %collective-permute-start.7 = (f32[64,1536]{1,0:T(8,128)S(1)}, f32[64,1536]{1,0:T(8,128)S(1)}, u32[]{:S(2)}, u32[]{:S(2)}) collective-permute-start(f32[64,1536]{1,0:T(8,128)S(1)} %get-tuple-element.104), channel_id=1, source_target_pairs={{0,4},{4,0},{8,12},{12,8},{16,20},{20,16},{24,28},{28,24},{1,5},{5... | collective-permute-start | bytes 1179656 | tf_op jit(solution)/shard_map/ppermute | solution.py:544
  28.5 2.2 %collective-permute-start.6 = (f32[64,1536]{1,0:T(8,128)S(1)}, f32[64,1536]{1,0:T(8,128)S(1)}, u32[]{:S(2)}, u32[]{:S(2)}) collective-permute-start(f32[64,1536]{1,0:T(8,128)S(1)} %get-tuple-element.102.held_ref), channel_id=1, source_target_pairs={{0,4},{4,0},{8,12},{12,8},{16,20},{20,16},{24,28},{28,24},{1,5},{5... | collective-permute-start | bytes 1179656 | tf_op jit(solution)/shard_map/ppermute | solution.py:544
  30.2 7.0 %collective-permute-start.8 = (f32[64,768]{1,0:T(8,128)S(1)}, f32[64,768]{1,0:T(8,128)S(1)}, u32[]{:S(2)}, u32[]{:S(2)}) collective-permute-start(f32[64,768]{1,0:T(8,128)S(1)} %get-tuple-element.110.refs_0_), channel_id=1, source_target_pairs={{0,8},{4,12},{8,0},{12,4},{16,24},{20,28},{24,16},{28,20},{1,9},{5... | collective-permute-start | bytes 589832 | tf_op jit(solution)/shard_map/ppermute | solution.py:544
  30.2 7.0 %collective-permute-start.9 = (f32[64,768]{1,0:T(8,128)S(1)}, f32[64,768]{1,0:T(8,128)S(1)}, u32[]{:S(2)}, u32[]{:S(2)}) collective-permute-start(f32[64,768]{1,0:T(8,128)S(1)} %get-tuple-element.111.refs_2_), channel_id=1, source_target_pairs={{0,16},{4,20},{8,24},{12,28},{16,0},{20,4},{24,8},{28,12},{1,17},{... | collective-permute-start | bytes 589832 | tf_op jit(solution)/shard_map/ppermute | solution.py:544
  37.3 6.2 %collective-permute-start.10 = (f32[64,768]{1,0:T(8,128)S(1)}, f32[64,768]{1,0:T(8,128)S(1)}, u32[]{:S(2)}, u32[]{:S(2)}) collective-permute-start(f32[64,768]{1,0:T(8,128)S(1)} %get-tuple-element.114.refs_0_), channel_id=1, source_target_pairs={{0,16},{4,20},{8,24},{12,28},{16,0},{20,4},{24,8},{28,12},{1,17},{... | collective-permute-start | bytes 589832 | tf_op jit(solution)/shard_map/ppermute | solution.py:544
  37.7 6.1 %collective-permute-start.11 = (f32[64,768]{1,0:T(8,128)S(1)}, f32[64,768]{1,0:T(8,128)S(1)}, u32[]{:S(2)}, u32[]{:S(2)}) collective-permute-start(f32[64,768]{1,0:T(8,128)S(1)} %get-tuple-element.115.refs_2_), channel_id=1, source_target_pairs={{0,8},{4,12},{8,0},{12,4},{16,24},{20,28},{24,16},{28,20},{1,9},{5... | collective-permute-start | bytes 589832 | tf_op jit(solution)/shard_map/ppermute | solution.py:544
  43.8 4.5 %collective-permute-start.12 = (f32[64,1536]{1,0:T(8,128)S(1)}, f32[64,1536]{1,0:T(8,128)S(1)}, u32[]{:S(2)}, u32[]{:S(2)}) collective-permute-start(f32[64,1536]{1,0:T(8,128)S(1)} %get-tuple-element.121.refs_1_), channel_id=1, source_target_pairs={{0,4},{4,0},{8,12},{12,8},{16,20},{20,16},{24,28},{28,24},{1,5},{5... | collective-permute-start | bytes 1179656 | tf_op jit(solution)/shard_map/ppermute | solution.py:544
  43.9 7.6 %collective-permute-start.16 = (f32[64,384]{1,0:T(8,128)S(1)}, f32[64,384]{1,0:T(8,128)S(1)}, u32[]{:S(2)}, u32[]{:S(2)}) collective-permute-start(f32[64,384]{1,0:T(8,128)S(1)} %get-tuple-element.128), channel_id=1, source_target_pairs={{0,1},{1,2},{2,3},{3,0},{4,5},{5,6},{6,7},{7,4},{8,9},{9,10},{10,1... | collective-permute-start | bytes 294920 | tf_op jit(solution)/shard_map/ppermute | solution.py:558
  45.6 9.8 %collective-permute-start.14 = (f32[64,384]{1,0:T(8,128)S(1)}, f32[64,384]{1,0:T(8,128)S(1)}, u32[]{:S(2)}, u32[]{:S(2)}) collective-permute-start(f32[64,384]{1,0:T(8,128)S(1)} %get-tuple-element.126), channel_id=1, source_target_pairs={{0,2},{1,3},{2,0},{3,1},{4,6},{5,7},{6,4},{7,5},{8,10},{9,11},{10,... | collective-permute-start | bytes 294920 | tf_op jit(solution)/shard_map/ppermute | solution.py:558
  48.2 7.4 %collective-permute-start.15 = (f32[64,384]{1,0:T(8,128)S(1)}, f32[64,384]{1,0:T(8,128)S(1)}, u32[]{:S(2)}, u32[]{:S(2)}) collective-permute-start(f32[64,384]{1,0:T(8,128)S(1)} %get-tuple-element.127), channel_id=1, source_target_pairs={{0,3},{1,0},{2,1},{3,2},{4,7},{5,4},{6,5},{7,6},{8,11},{9,8},{10,9... | collective-permute-start | bytes 294920 | tf_op jit(solution)/shard_map/ppermute | solution.py:558
  49.1 11.4 %collective-permute-start.13 = (f32[64,64]{1,0:T(8,128)S(1)}, f32[64,64]{1,0:T(8,128)S(1)}, u32[]{:S(2)}, u32[]{:S(2)}) collective-permute-start(f32[64,64]{1,0:T(8,128)S(1)} %get-tuple-element.124.refs_0_), channel_id=1, source_target_pairs={{0,1},{1,0},{2,3},{3,2},{4,5},{5,4},{6,7},{7,6},{8,9},{9,8},{10,11... | collective-permute-start | bytes 49160 | tf_op jit(solution)/shard_map/ppermute | solution.py:544
  55.7 15.0 %collective-permute-start.18 = (f32[64,384]{1,0:T(8,128)S(1)}, f32[64,384]{1,0:T(8,128)S(1)}, u32[]{:S(2)}, u32[]{:S(2)}) collective-permute-start(f32[64,384]{1,0:T(8,128)S(1)} %get-tuple-element.148.refs_2_), channel_id=1, source_target_pairs={{0,1},{1,2},{2,3},{3,0},{4,5},{5,6},{6,7},{7,4},{8,9},{9,10},{10,1... | collective-permute-start | bytes 294920 | tf_op jit(solution)/shard_map/ppermute | solution.py:558
  58.1 12.6 %collective-permute-start.19 = (f32[64,384]{1,0:T(8,128)S(1)}, f32[64,384]{1,0:T(8,128)S(1)}, u32[]{:S(2)}, u32[]{:S(2)}) collective-permute-start(f32[64,384]{1,0:T(8,128)S(1)} %get-tuple-element.148.refs_2_), channel_id=1, source_target_pairs={{0,2},{1,3},{2,0},{3,1},{4,6},{5,7},{6,4},{7,5},{8,10},{9,11},{10,... | collective-permute-start | bytes 294920 | tf_op jit(solution)/shard_map/ppermute | solution.py:558
  58.6 12.1 %collective-permute-start.20 = (f32[64,384]{1,0:T(8,128)S(1)}, f32[64,384]{1,0:T(8,128)S(1)}, u32[]{:S(2)}, u32[]{:S(2)}) collective-permute-start(f32[64,384]{1,0:T(8,128)S(1)} %get-tuple-element.148.refs_2_), channel_id=1, source_target_pairs={{0,3},{1,0},{2,1},{3,2},{4,7},{5,4},{6,5},{7,6},{8,11},{9,8},{10,9... | collective-permute-start | bytes 294920 | tf_op jit(solution)/shard_map/ppermute | solution.py:558
  60.5 9.3 %collective-permute-start.17 = (f32[64,64]{1,0:T(8,128)S(1)}, f32[64,64]{1,0:T(8,128)S(1)}, u32[]{:S(2)}, u32[]{:S(2)}) collective-permute-start(f32[64,64]{1,0:T(8,128)S(1)} %get-tuple-element.136.refs_0_), channel_id=1, source_target_pairs={{0,2},{1,3},{2,0},{3,1},{4,6},{5,7},{6,4},{7,5},{8,10},{9,11},{10,... | collective-permute-start | bytes 49160 | tf_op jit(solution)/shard_map/ppermute | solution.py:544

commit v6 on v5

--- a/solution.py
+++ b/solution.py
@@ -173,54 +173,52 @@
     out_ref[...] = -dot(jnp.concatenate(tiles, 0), inverse_ref[...])
 
 
-def down_kernel(base, first_ref, second_ref, a_ref, out_ref, kept_ref, sems):
-    width = first_ref.shape[0]
-    count = sems.shape[0]
-    size = out_ref.shape[1] // count
-
-    def load(i):
+def down_kernel(first_ref, second_ref, a_ref, low_ref, high_ref, kept_ref, over_ref, sems):
+    width, span = low_ref.shape
+    count = sems.shape[0] // 2
+    size = span // count
+    halves = ((0, low_ref, kept_ref), (1, high_ref, over_ref))
+
+    def load(at, ref, i):
         start = pl.multiple_of(i * size, size)
-        source = a_ref.at[:, pl.ds(pl.multiple_of(base + start, size), size)]
-        return pltpu.make_async_copy(source, kept_ref.at[:, pl.ds(start, size)], sems.at[i])
-
-    for i in range(count):
-        load(i).start()
+        source = a_ref.at[:, pl.ds(pl.multiple_of(at * span + start, size), size)]
+        return pltpu.make_async_copy(
+            source, ref.at[:, pl.ds(start, size)], sems.at[at * count + i]
+        )
+
+    for at, _, kept in halves:
+        for i in range(count):
+            load(at, kept, i).start()
     kh, kl = split(jnp.concatenate([first_ref[...], second_ref[...]], 1))
     left = jnp.concatenate([kh, kl], 0)
-
-    @pl.loop(0, count)
-    def _(i):
-        load(i).wait()
-        part = pl.ds(pl.multiple_of(i * size, size), size)
-        ah, al = split(kept_ref[:, part])
-        term = fast(left, ah) + fast(left, al)
-        out_ref[:, part] = term[:width] + term[width:]
-
-
-def product_down(first, second, a, at, carry=()):
+    for at, out, kept in halves:
+
+        @pl.loop(0, count)
+        def _(i):
+            load(at, kept, i).wait()
+            part = pl.ds(pl.multiple_of(i * size, size), size)
+            ah, al = split(kept[:, part])
+            term = fast(left, ah) + fast(left, al)
+            out[:, part] = term[:width] + term[width:]
+
+
+def product_down(first, second, a):
     rows, columns = a.shape
     width = first.shape[0]
     span = columns // 2
     size = block_of(span, 256)
     whole = pl.BlockSpec(memory_space=pltpu.VMEM)
-    anywhere = pl.BlockSpec(memory_space=pl.ANY)
-    more = len(carry)
-
-    def kernel(first_ref, second_ref, a_ref, *refs):
-        out_ref, kept_ref = refs[more : more + 2]
-        down_kernel(at * span, first_ref, second_ref, a_ref, out_ref, kept_ref, refs[-1])
-
-    out, kept, *carried = pl.pallas_call(
-        kernel,
-        in_specs=[whole, whole, pl.BlockSpec(memory_space=pltpu.HBM)] + [anywhere] * more,
-        out_specs=(whole, whole) + (anywhere,) * more,
-        out_shape=(shape(width, span), shape(rows, span)) + tuple(shape(*x.shape) for x in carry),
-        input_output_aliases={3 + k: 2 + k for k in range(more)},
-        scratch_shapes=[pltpu.SemaphoreType.DMA((span // size,))],
+    low, high, *halves = pl.pallas_call(
+        down_kernel,
+        in_specs=[whole, whole, pl.BlockSpec(memory_space=pltpu.HBM)],
+        out_specs=(whole,) * 4,
+        out_shape=(shape(width, span),) * 2 + (shape(rows, span),) * 2,
+        scratch_shapes=[pltpu.SemaphoreType.DMA((columns // size,))],
         compiler_params=params(12),
-        cost_estimate=cost(8 * rows * span * width, 4 * rows * span),
-    )(first, second, pltpu.with_memory_space_constraint(a, pltpu.HBM), *carry)
-    return out, tuple(carried) + (kept,)
+        cost_estimate=cost(8 * rows * columns * width, 4 * rows * columns),
+        name="product_down",
+    )(first, second, pltpu.with_memory_space_constraint(a, pltpu.HBM))
+    return low, high, tuple(halves)
 
 
 def fix_kernel(low_ref, high_ref, band_ref, top_ref, over_ref, keep_ref, give_ref, *_):
@@ -230,9 +228,11 @@
 
     @pl.when(row == 0)
     def _():
-        turned = band_ref[...].T
-        keep_ref[...] = first - dot(turned, top_ref[...])
-        give_ref[...] = second - dot(turned, over_ref[...])
+        rh, rl = split(band_ref[...].T)
+        left = jnp.concatenate([rh, rl, rh, rl], 1)
+        for value, top, out in ((first, top_ref, keep_ref), (second, over_ref, give_ref)):
+            ah, al = split(top[...])
+            out[...] = value - fast(left, jnp.concatenate([ah, ah, al, al], 0))
 
     @pl.when((row != 0) & (core == 0))
     def _():
@@ -463,9 +463,36 @@
     )
 
 
-def core_kernel(part_ref, more_ref, st_ref, krt_ref, out_ref):
+def packing(width, size):
+    beside = 1
+    while 2 * beside <= min(size // width, 8):
+        beside *= 2
+    return beside, width // beside
+
+
+def line_kernel(*refs):
+    *chunks, inner_ref, out_ref = refs
+    width, size = chunks[0].shape
+    beside, tall = packing(width, size)
+    total = chunks[0][...]
+    for ref in chunks[1:]:
+        total = total + ref[...]
+    out_ref[:width, :] = total
+    out_ref[width:, :] = jnp.zeros((tall, size), f32)
+    for k in range(beside):
+        out_ref[width:, k * width : (k + 1) * width] = inner_ref[k * tall : (k + 1) * tall, :]
+
+
+def core_kernel(st_ref, krt_ref, *refs):
+    chunks, out_ref = refs[:-1], refs[-1]
+    width = st_ref.shape[0]
+    beside, _ = packing(width, chunks[0].shape[1])
+    packed = chunks[0][width:, :]
+    for ref in chunks[1:]:
+        packed = packed + ref[width:, :]
+    inner = jnp.concatenate([packed[:, k * width : (k + 1) * width] for k in range(beside)], 0)
     st = st_ref[...]
-    cm = dot(dot(st, part_ref[...] + more_ref[...]), st.T)
+    cm = dot(dot(st, inner), st.T)
     out_ref[...] = dot(cm, krt_ref[...])
 
 
@@ -477,7 +504,7 @@
     col = lax.axis_index("col")
     for at, ref in enumerate(chunks):
         start = pl.multiple_of(lax.rem(col + pieces - at, pieces) * size, size)
-        value = dot(st, ref[...]) - core_ref[:, pl.ds(start, size)]
+        value = dot(st, ref[: st.shape[0], :]) - core_ref[:, pl.ds(start, size)]
         left_ref[pl.ds(start, size), :] = jnp.concatenate(split(value.T), 1)
 
 
@@ -589,13 +616,13 @@
             zero = jnp.zeros_like(total)
             terms = [total, flip(total, row_size // 2, row_size), zero, zero]
         first, second, partial = lax.optimization_barrier((first, second, partial))
-        low, resident = product_down(first, second, matrix, 0)
+        low, high, resident = product_down(first, second, matrix)
         if row_size == 8:
             one, two, resident = small_call(
                 merge_first_kernel, (half, half), first, second, by_x, by_y, carry=resident
             )
-            more_x = from_sources(two, col_size, [0, 4], 2)
-            more_y = from_sources(one, col_size, [0, 2], 4)
+            more_x = flip(two, 2, row_size)
+            more_y = flip(one, 4, row_size)
         else:
             relation = (lax.axis_index("row") // 2) ^ lax.axis_index("col")
             held = jnp.where(relation == 0, jnp.concatenate([first, second], 1), 0.0)
@@ -605,20 +632,19 @@
                 held = held + from_sources(held, col_size, reached, bit)
                 reached = reached + [r ^ bit for r in reached]
                 bit *= 2
-        high, resident = product_down(first, second, matrix, 1, resident)
         band, again, band_inverse, head, resident = small_call(
             eliminate_kernel, (small, small, small, small), *terms, flops=50_000_000, carry=resident
         )
         keep, give, resident = fix_down(low, high, again, resident)
+        quarter = shape(width, columns // 4)
+        a, b, resident = small_call(
+            halve_kernel, (quarter, quarter), keep, flip(give, 1, row_size), carry=resident
+        )
         if row_size == 8:
             held, resident = small_call(
                 join_kernel, shape(width, rows), one, more_y, two, more_x, carry=resident
             )
         other = flip(held, 1, row_size)
-        quarter = shape(width, columns // 4)
-        a, b, resident = small_call(
-            halve_kernel, (quarter, quarter), keep, flip(give, 1, row_size), carry=resident
-        )
         bits = []
         bit = 2
         while bit < row_size:
@@ -645,6 +671,7 @@
             )
         ra = flip(a, bits[-1], row_size)
         rb = flip(b, bits[0], row_size)
+        received = []
         if late:
             received = [shift(chunks[at], late + at, col_size) for at in range(pieces - late)]
             *chunks, resident = across_call(
@@ -662,23 +689,19 @@
             flip(summed, 1, row_size),
             carry=resident,
         )
-        bit = 1
-        others = []
-        while bit < col_size // 2:
-            others.append(bit)
-            bit *= 2
-        first_inner = flip(inner, 1, col_size, "col")
+        tall = packing(width, rows // pieces)[1]
+        mine, resident = small_call(
+            line_kernel,
+            shape(width + tall, rows // pieces),
+            chunks[0],
+            *received,
+            inner,
+            carry=resident,
+        )
         if pieces == 1:
-            whole = [lax.psum(chunks[0], "col")]
+            whole = [lax.psum(mine, "col")]
         else:
-            mine, resident = small_call(
-                add_kernel, shape(width, rows // col_size), chunks[0], *received, carry=resident
-            )
             whole = [mine] + [shift(mine, by, col_size) for by in range(1, col_size)]
-        for at in others:
-            got = first_inner if at == 1 else flip(inner, at, col_size, "col")
-            inner, resident = small_call(add_kernel, small, inner, got, carry=resident)
-        more = flip(inner, bit, col_size, "col")
         st, resident = small_call(
             invert_kernel, small, head, again, band_inverse, flops=50_000_000, carry=resident
         )
@@ -701,7 +724,7 @@
         )
         resident = subtract_near(near_left, xparts, *resident)
         core, resident = small_call(
-            core_kernel, shape(width, rows), inner, more, st, krt, carry=resident
+            core_kernel, shape(width, rows), st, krt, *whole, carry=resident
         )
         left, resident = small_call(
             left_kernel,

time: 80.4 us -> 76.8 us (0.955)
  starting transfers between devices: 26.1 us -> 22.1 us
  waiting for transfers between devices: 15.5 us -> 17.5 us
  Pallas kernels: 36.5 us -> 34.9 us
    ppermute x2 -> x0, starting transfers between devices: 5.88 us -> none  [from_sources(): return lax.ppermute(piece, ('row', 'col'), pairs)]
    ppermute x6, waiting for transfers between devices: 4.47 us -> 6.42 us  [shift(): lax.ppermute(piece, 'col', [(i, (i + by) % size) for i in range(size)])]
    pallas_call x2 -> x1, Pallas kernels: 8.48 us -> 7.05 us  [product_down(): pl.pallas_call(down_kernel, in_specs=[whole, whole, pl.BlockSpec(memory_s...]
    ppermute x6, starting transfers between devices: 9.22 us -> 10.6 us  [shift(): lax.ppermute(piece, 'col', [(i, (i + by) % size) for i in range(size)])]
    pallas_call x15 -> x14, Pallas kernels: 9.58 us -> 9.71 us  [small_call(): pl.pallas_call(body, out_shape=out, compiler_params=params(mib), cost_est...]
  transfers between devices with their start and end apart: 21 -> 19, of which waited for: 13 -> 10; matrix products, arithmetic and copies ran while one was open for 0% -> 0% of each run, Pallas kernels for 33% -> 27%
where the time goes in v6:
time: 76.8 us; the launch traced here: 76.4 us
  Pallas kernels  34.9 us (45%)
  starting transfers between devices  22.1 us (29%)
  waiting for transfers between devices  17.5 us (23%)
  local copies, waits for them, and re-layouts  0.99 us (1%)
  between operations  0.98 us (1%)
    ppermute x13, starting transfers between devices, flip(): return lax.ppermute(value, axis, [(i, i ^ bit) for i in range(size)])  11.4 us
    ppermute x13, waiting for transfers between devices, flip(): return lax.ppermute(value, axis, [(i, i ^ bit) for i in range(size)])  11.1 us
    ppermute x6, starting transfers between devices, shift(): lax.ppermute(piece, 'col', [(i, (i + by) % size) for i in range(size)])  10.6 us
    pallas_call x14, Pallas kernels, small_call(): pl.pallas_call(body, out_shape=out, compiler_params=params(mib), cost_est...  9.71 us
    pallas_call x1, Pallas kernels, subtract_far(): pl.pallas_call(far_kernel, in_specs=[whole] * 6, out_specs=pl.BlockSpec(m...  8.54 us
    pallas_call x1, Pallas kernels, product_down(): pl.pallas_call(down_kernel, in_specs=[whole, whole, pl.BlockSpec(memory_s...  7.05 us
    pallas_call x2, Pallas kernels, across_call(): pl.pallas_call(kernel, grid=(count,), in_specs=[fixed(x) for x in operand...  6.96 us
    ppermute x6, waiting for transfers between devices, shift(): lax.ppermute(piece, 'col', [(i, (i + by) % size) for i in range(size)])  6.42 us
  transfers between devices with their start and end apart: 19, of which 10 were waited for; matrix products, arithmetic and copies ran while one was open for 0% of the time, Pallas kernels for 27%

profile of v6, /device:TPU:0, one launch (start us, length us, event | category | flops | bytes accessed | tf_op | source)
XLA Modules:
  0.0 76.4 jit_solution(8567034262681891469)
XLA Ops:
  0.6 0.0 copy-start
  0.6 1.0 %copy-done = f32[1536,64]{0,1:T(8,128)S(1)} copy-done((f32[1536,64]{0,1:T(8,128)S(1)}, f32[1536,64]{0,1:T(8,128)}, u32[]{:S(2)}) %copy-start) | copy-done | bytes 393240
  1.6 0.5 shard_map.41
  2.1 0.6 collective-permute-start
  2.7 0.9 %collective-permute-done.b_ref = f32[64,128]{1,0:T(8,128)S(1)} collective-permute-done((f32[64,128]{1,0:T(8,128)S(1)}, f32[64,128]{1,0:T(8,128)S(1)}, u32[]{:S(2)}, u32[]{:S(2)}) %collective-permute-start) | collective-permute-done | bytes 32800 | tf_op jit(solution)/shard_map/ppermute | solution.py:571
  3.6 2.9 %collective-permute-start.1 = (f32[64,896]{1,0:T(8,128)S(1)}, f32[64,896]{1,0:T(8,128)S(1)}, u32[]{:S(2)}, u32[]{:S(2)}) collective-permute-start(f32[64,896]{1,0:T(8,128)S(1)} %get-tuple-element.80), channel_id=1, source_target_pairs={{0,8},{4,12},{8,0},{12,4},{16,24},{20,28},{24,16},{28,20},{1,9},{5... | collective-permute-start | bytes 688136 | tf_op jit(solution)/shard_map/ppermute | solution.py:571
  6.4 1.5 %collective-permute-start.2 = (f32[64,896]{1,0:T(8,128)S(1)}, f32[64,896]{1,0:T(8,128)S(1)}, u32[]{:S(2)}, u32[]{:S(2)}) collective-permute-start(f32[64,896]{1,0:T(8,128)S(1)} %get-tuple-element.81), channel_id=1, source_target_pairs={{0,16},{4,20},{8,24},{12,28},{16,0},{20,4},{24,8},{28,12},{1,17},{... | collective-permute-start | bytes 688136 | tf_op jit(solution)/shard_map/ppermute | solution.py:571
  8.0 0.0 collective-permute-start.3
  8.0 7.1 %product_down.1 = (f32[64,1536]{1,0:T(8,128)S(1)}, f32[64,1536]{1,0:T(8,128)S(1)}, f32[1536,1536]{1,0:T(8,128)S(1)}, f32[1536,1536]{1,0:T(8,128)S(1)}) custom-call(f32[64,768]{1,0:T(8,128)S(1)} %get-tuple-element.82.first_ref.refs_0_.refs_3_, f32[64,768]{1,0:T(8,128)S(1)} %get-tuple-element.83.second_ref.refs_1_.refs_4_, f32[1536,3072]{1,0:T(8,128)} %a_ref.1), custom_call_target="tpu_custom_call" | custom-call | flops 2415919104 | bytes 18874368 | tf_op jit(solution)/shard_map/product_down/pallas_call | solution.py:211
  15.0 0.0 collective-permute-done.1.refs_2_.refs_1_
  15.1 0.0 collective-permute-done.2.refs_3_.refs_2_
  15.1 0.1 shard_map.43
  15.1 0.0 collective-permute-done.3.refs_3_
  15.2 2.7 %shard_map.44 = (f32[64,64]{1,0:T(8,128)}, f32[64,64]{1,0:T(8,128)S(1)}, f32[64,64]{1,0:T(8,128)S(1)}, f32[64,64]{1,0:T(8,128)S(1)}, f32[1536,1536]{1,0:T(8,128)S(1)}, /*index=5*/f32[1536,1536]{1,0:T(8,128)S(1)}) custom-call(f32[64,128]{1,0:T(8,128)S(1)} %get-tuple-element.79.refs_0_, ...), custom_call_target="tpu_custom_call", output_to_operand_aliasing={{4}: (4, {}), {5}: (5, {})} | custom-call | flops 50000000 | bytes 1000000 | tf_op jit(solution)/shard_map/pallas_call | solution.py:64
  17.8 0.6 fix_down.1
  18.4 0.1 collective-permute-start.6
  18.5 1.6 %collective-permute-start.4 = (f32[64,768]{1,0:T(8,128)S(1)}, f32[64,768]{1,0:T(8,128)S(1)}, u32[]{:S(2)}, u32[]{:S(2)}) collective-permute-start(f32[64,768]{1,0:T(8,128)S(1)} %get-tuple-element.91.refs_0_), channel_id=1, source_target_pairs={{0,16},{4,20},{8,24},{12,28},{16,0},{20,4},{24,8},{28,12},{1,17},{... | collective-permute-start | bytes 589832 | tf_op jit(solution)/shard_map/ppermute | solution.py:571
  20.1 1.5 %collective-permute-start.5 = (f32[64,768]{1,0:T(8,128)S(1)}, f32[64,768]{1,0:T(8,128)S(1)}, u32[]{:S(2)}, u32[]{:S(2)}) collective-permute-start(f32[64,768]{1,0:T(8,128)S(1)} %get-tuple-element.92.refs_2_), channel_id=1, source_target_pairs={{0,8},{4,12},{8,0},{12,4},{16,24},{20,28},{24,16},{28,20},{1,9},{5... | collective-permute-start | bytes 589832 | tf_op jit(solution)/shard_map/ppermute | solution.py:571
  21.6 0.0 collective-permute-done.6.refs_1_
  21.6 4.2 %collective-permute-done.4.refs_1_ = f32[64,768]{1,0:T(8,128)S(1)} collective-permute-done((f32[64,768]{1,0:T(8,128)S(1)}, f32[64,768]{1,0:T(8,128)S(1)}, u32[]{:S(2)}, u32[]{:S(2)}) %collective-permute-start.4) | collective-permute-done | bytes 196640 | tf_op jit(solution)/shard_map/ppermute | solution.py:571
  25.8 1.2 %collective-permute-done.5.refs_3_ = f32[64,768]{1,0:T(8,128)S(1)} collective-permute-done((f32[64,768]{1,0:T(8,128)S(1)}, f32[64,768]{1,0:T(8,128)S(1)}, u32[]{:S(2)}, u32[]{:S(2)}) %collective-permute-start.5) | collective-permute-done | bytes 196640 | tf_op jit(solution)/shard_map/ppermute | solution.py:571
  27.1 0.1 collective-permute-start.7
  27.1 1.6 %collective-permute-start.8 = (f32[64,768]{1,0:T(8,128)S(1)}, f32[64,768]{1,0:T(8,128)S(1)}, u32[]{:S(2)}, u32[]{:S(2)}) collective-permute-start(f32[64,768]{1,0:T(8,128)S(1)} %get-tuple-element.107.refs_0_), channel_id=1, source_target_pairs={{0,8},{4,12},{8,0},{12,4},{16,24},{20,28},{24,16},{28,20},{1,9},{5... | collective-permute-start | bytes 589832 | tf_op jit(solution)/shard_map/ppermute | solution.py:571
  28.7 0.5 collective-permute-start.9
  29.2 0.0 collective-permute-done.7.other_ref
  29.2 3.9 %shard_map.47 = (f32[64,3072]{1,0:T(8,128)S(1)}, bf16[3072,128]{1,0:T(8,128)(2,1)S(1)}, f32[64,384]{1,0:T(8,128)S(1)}, f32[64,384]{1,0:T(8,128)S(1)}, f32[1536,1...) custom-call(f32[64,1536]{1,0:T(8,128)S(1)} %get-tuple-element.103.held_ref, ...), custom_call_target="tpu_custom_call", output_to_operand_aliasing={{4}: (3, {}), {5}: (4, {})} | custom-call | flops 1207959552 | bytes 9437184 | tf_op jit(solution)/shard_map/pallas_call | solution.py:330
  33.1 1.3 %collective-permute-done.8.refs_1_ = f32[64,768]{1,0:T(8,128)S(1)} collective-permute-done((f32[64,768]{1,0:T(8,128)S(1)}, f32[64,768]{1,0:T(8,128)S(1)}, u32[]{:S(2)}, u32[]{:S(2)}) %collective-permute-start.8) | collective-permute-done | bytes 196640 | tf_op jit(solution)/shard_map/ppermute | solution.py:571
  34.5 1.2 %collective-permute-done.9.refs_3_ = f32[64,768]{1,0:T(8,128)S(1)} collective-permute-done((f32[64,768]{1,0:T(8,128)S(1)}, f32[64,768]{1,0:T(8,128)S(1)}, u32[]{:S(2)}, u32[]{:S(2)}) %collective-permute-start.9) | collective-permute-done | bytes 196640 | tf_op jit(solution)/shard_map/ppermute | solution.py:571
  35.7 0.6 collective-permute-start.13
  36.3 0.5 collective-permute-start.14
  36.8 3.1 %shard_map.49 = (f32[64,384]{1,0:T(8,128)S(1)}, f32[64,384]{1,0:T(8,128)S(1)}, f32[1536,1536]{1,0:T(8,128)S(1)}, f32[1536,1536]{1,0:T(8,128)S(1)}) custom-call(bf16[3072,128]{1,0:T(8,128)(2,1)S(1)} %get-tuple-element.106.right_ref, f32[1536,1536]{1,0:T(8,128)S(1)} %get-tuple-element.111.low_ref, ...), custom_call_target="tpu_custom_call", output_to_operand_aliasing={{2}: (1, {}), {3}: (2, {})} | custom-call | flops 1207959552 | bytes 9437184 | tf_op jit(solution)/shard_map/pallas_call | solution.py:330
  39.9 2.0 %collective-permute-done.13.refs_1_ = f32[64,768]{1,0:T(8,128)S(1)} collective-permute-done((f32[64,768]{1,0:T(8,128)S(1)}, f32[64,768]{1,0:T(8,128)S(1)}, u32[]{:S(2)}, u32[]{:S(2)}) %collective-permute-start.13) | collective-permute-done | bytes 196640 | tf_op jit(solution)/shard_map/ppermute | solution.py:571
  41.9 0.2 collective-permute-done.14.refs_3_
  42.1 0.1 collective-permute-start.15
  42.2 1.6 %collective-permute-start.12 = (f32[64,384]{1,0:T(8,128)S(1)}, f32[64,384]{1,0:T(8,128)S(1)}, u32[]{:S(2)}, u32[]{:S(2)}) collective-permute-start(f32[64,384]{1,0:T(8,128)S(1)} %get-tuple-element.116), channel_id=1, source_target_pairs={{0,1},{1,2},{2,3},{3,0},{4,5},{5,6},{6,7},{7,4},{8,9},{9,10},{10,1... | collective-permute-start | bytes 294920 | tf_op jit(solution)/shard_map/ppermute | solution.py:585
  43.9 2.6 %collective-permute-start.10 = (f32[64,384]{1,0:T(8,128)S(1)}, f32[64,384]{1,0:T(8,128)S(1)}, u32[]{:S(2)}, u32[]{:S(2)}) collective-permute-start(f32[64,384]{1,0:T(8,128)S(1)} %get-tuple-element.114), channel_id=1, source_target_pairs={{0,2},{1,3},{2,0},{3,1},{4,6},{5,7},{6,4},{7,5},{8,10},{9,11},{10,... | collective-permute-start | bytes 294920 | tf_op jit(solution)/shard_map/ppermute | solution.py:585
  46.4 1.3 %collective-permute-start.11 = (f32[64,384]{1,0:T(8,128)S(1)}, f32[64,384]{1,0:T(8,128)S(1)}, u32[]{:S(2)}, u32[]{:S(2)}) collective-permute-start(f32[64,384]{1,0:T(8,128)S(1)} %get-tuple-element.115), channel_id=1, source_target_pairs={{0,3},{1,0},{2,1},{3,2},{4,7},{5,4},{6,5},{7,6},{8,11},{9,8},{10,9... | collective-permute-start | bytes 294920 | tf_op jit(solution)/shard_map/ppermute | solution.py:585
  47.8 0.0 collective-permute-done.15.refs_2_
  47.8 0.8 %shard_map.51 = (f32[64,3072]{1,0:T(8,128)S(1)}, f32[64,64]{1,0:T(8,128)S(1)}, f32[1536,1536]{1,0:T(8,128)S(1)}, f32[1536,1536]{1,0:T(8,128)S(1)}) custom-call(f32[64,3072]{1,0:T(8,128)S(1)} %get-tuple-element.117.refs_0_.refs_2_, f32[64,1536]{1,0:T(8,128)S(1)} %get-tuple-element.122.refs_1_, ...), custom_call_target="tpu_custom_call", output_to_operand_aliasing={{2}: (3, {}), {3}: (4, {})} | custom-call | flops 1000000 | bytes 1000000 | tf_op jit(solution)/shard_map/pallas_call | solution.py:64
  48.6 1.2 %collective-permute-done.12.refs_3_ = f32[64,384]{1,0:T(8,128)S(1)} collective-permute-done((f32[64,384]{1,0:T(8,128)S(1)}, f32[64,384]{1,0:T(8,128)S(1)}, u32[]{:S(2)}, u32[]{:S(2)}) %collective-permute-start.12) | collective-permute-done | bytes 98336 | tf_op jit(solution)/shard_map/ppermute | solution.py:585
  49.8 3.7 %collective-permute-done.10.refs_1_ = f32[64,384]{1,0:T(8,128)S(1)} collective-permute-done((f32[64,384]{1,0:T(8,128)S(1)}, f32[64,384]{1,0:T(8,128)S(1)}, u32[]{:S(2)}, u32[]{:S(2)}) %collective-permute-start.10) | collective-permute-done | bytes 98336 | tf_op jit(solution)/shard_map/ppermute | solution.py:585
  53.6 0.0 collective-permute-done.11.refs_2_
  53.6 0.1 shard_map.52
  53.6 2.6 %collective-permute-start.16 = (f32[80,384]{1,0:T(8,128)S(1)}, f32[80,384]{1,0:T(8,128)S(1)}, u32[]{:S(2)}, u32[]{:S(2)}) collective-permute-start(f32[80,384]{1,0:T(8,128)S(1)} %get-tuple-element.135.refs_2_), channel_id=1, source_target_pairs={{0,1},{1,2},{2,3},{3,0},{4,5},{5,6},{6,7},{7,4},{8,9},{9,10},{10,1... | collective-permute-start | bytes 368648 | tf_op jit(solution)/shard_map/ppermute | solution.py:585
  56.2 1.6 %collective-permute-start.17 = (f32[80,384]{1,0:T(8,128)S(1)}, f32[80,384]{1,0:T(8,128)S(1)}, u32[]{:S(2)}, u32[]{:S(2)}) collective-permute-start(f32[80,384]{1,0:T(8,128)S(1)} %get-tuple-element.135.refs_2_), channel_id=1, source_target_pairs={{0,2},{1,3},{2,0},{3,1},{4,6},{5,7},{6,4},{7,5},{8,10},{9,11},{10,... | collective-permute-start | bytes 368648 | tf_op jit(solution)/shard_map/ppermute | solution.py:585
  57.9 0.8 %collective-permute-start.18 = (f32[80,384]{1,0:T(8,128)S(1)}, f32[80,384]{1,0:T(8,128)S(1)}, u32[]{:S(2)}, u32[]{:S(2)}) collective-permute-start(f32[80,384]{1,0:T(8,128)S(1)} %get-tuple-element.135.refs_2_), channel_id=1, source_target_pairs={{0,3},{1,0},{2,1},{3,2},{4,7},{5,4},{6,5},{7,6},{8,11},{9,8},{10,9... | collective-permute-start | bytes 368648 | tf_op jit(solution)/shard_map/ppermute | solution.py:585
  58.7 2.3 %shard_map.53 = (f32[64,64]{1,0:T(8,128)S(1)}, f32[1536,1536]{1,0:T(8,128)S(1)}, f32[1536,1536]{1,0:T(8,128)S(1)}) custom-call(f32[64,64]{1,0:T(8,128)S(1)} %get-tuple-element.88.refs_0_, f32[64,64]{1,0:T(8,128)S(1)} %get-tuple-element.89.band_ref.refs_1_.refs_5_, ...), custom_call_target="tpu_custom_call", output_to_operand_aliasing={{1}: (3, {}), {2}: (4, {})} | custom-call | flops 50000000 | bytes 1000000 | tf_op jit(solution)/shard_map/pallas_call | solution.py:64
  61.0 1.4 %shard_map.54 = (bf16[128,3072]{1,0:T(8,128)(2,1)S(1)}, bf16[128,3072]{1,0:T(8,128)(2,1)S(1)}, f32[64,1536]{1,0:T(8,128)S(1)}, bf16[1536,128]{1,0:T(8,128)(2,1)S...) custom-call(f32[64,64]{1,0:T(8,128)S(1)} %get-tuple-element.130.refs_0_, ...), custom_call_target="tpu_custom_call", output_to_operand_aliasing={{4}: (6, {}), {5}: (7, {})} | custom-call | flops 1000000 | bytes 1000000 | tf_op jit(solution)/shard_map/pallas_call | solution.py:64
  62.4 2.1 %subtract_near.1 = (f32[1536,1536]{1,0:T(8,128)S(1)}, f32[1536,1536]{1,0:T(8,128)S(1)}) custom-call(bf16[1536,128]{1,0:T(8,128)(2,1)S(1)} %get-tuple-element.136.left_ref.near_left_ref, bf16[128,3072]{1,0:T(8,128)(2,1)S(1)} %get-tuple-element.137.right_ref.near_right_ref, ...), custom_call_target="tpu_custom_call", output_to_operand_aliasing={{0}: (2, {}), {1}: (3, {})} | custom-call | flops 1207959552 | bytes 18874368 | tf_op jit(solution)/shard_map/subtract_near/pallas_call | solution.py:453
  64.5 0.0 collective-permute-done.16.refs_3_
  64.5 1.5 %collective-permute-done.17.refs_4_ = f32[80,384]{1,0:T(8,128)S(1)} collective-permute-done((f32[80,384]{1,0:T(8,128)S(1)}, f32[80,384]{1,0:T(8,128)S(1)}, u32[]{:S(2)}, u32[]{:S(2)}) %collective-permute-start.17) | collective-permute-done | bytes 122912 | tf_op jit(solution)/shard_map/ppermute | solution.py:585
  66.0 0.0 collective-permute-done.18.refs_5_
  66.0 0.9 %shard_map.55 = (f32[64,1536]{1,0:T(8,128)S(1)}, f32[1536,1536]{1,0:T(8,128)S(1)}, f32[1536,1536]{1,0:T(8,128)S(1)}) custom-call(f32[64,64]{1,0:T(8,128)S(1)} %get-tuple-element.130.refs_0_, f32[64,1536]{1,0:T(8,128)S(1)} %get-tuple-element.134.refs_1_, f32[80,384]{1,0:T(8,128)S(1)} %get-tuple-element.135.refs_2_, ...), custom_call_target="tpu_custom_call", output_to_operand_aliasing={{1}: (6, {}), {2}: (7, {})} | custom-call | flops 1000000 | bytes 1000000 | tf_op jit(solution)/shard_map/pallas_call | solution.py:64
  66.9 0.8 %shard_map.56 = (bf16[1536,128]{1,0:T(8,128)(2,1)S(1)}, f32[1536,1536]{1,0:T(8,128)S(1)}, f32[1536,1536]{1,0:T(8,128)S(1)}) custom-call(f32[64,64]{1,0:T(8,128)S(1)} %get-tuple-element.130.refs_0_, f32[64,1536]{1,0:T(8,128)S(1)} %get-tuple-element.142.refs_1_, ...), custom_call_target="tpu_custom_call", output_to_operand_aliasing={{1}: (6, {}), {2}: (7, {})} | custom-call | flops 1000000 | bytes 1000000 | tf_op jit(solution)/shard_map/pallas_call | solution.py:64
  67.7 8.5 %subtract_far.1 = f32[1536,3072]{1,0:T(8,128)} custom-call(bf16[1536,128]{1,0:T(8,128)(2,1)S(1)} %get-tuple-element.145.left_ref, bf16[128,3072]{1,0:T(8,128)(2,1)S(1)} %get-tuple-element.146.right_ref, bf16[1536,128]{1,0:T(8,128)(2,1)S(1)} %get-tuple-element.136.left_ref.near_left_ref, bf16[128,3072]{1,0:T(8,128)(2,1)S(1)} %get-tuple-element.137.right_ref.near_right_ref, ...), custom_call_target="tpu_custom_call" | custom-call | flops 3623878656 | bytes 37748736 | tf_op jit(solution)/shard_map/subtract_far/pallas_call | solution.py:558
  (5 shorter events, 0.2 us)
Async XLA Ops:
  0.6 1.0 %copy-start = (f32[1536,64]{0,1:T(8,128)S(1)}, f32[1536,64]{0,1:T(8,128)}, u32[]{:S(2)}) copy-start(f32[1536,64]{0,1:T(8,128)} %param.3) | copy-start | bytes 1179652
  2.1 1.4 %collective-permute-start = (f32[64,128]{1,0:T(8,128)S(1)}, f32[64,128]{1,0:T(8,128)S(1)}, u32[]{:S(2)}, u32[]{:S(2)}) collective-permute-start(f32[64,128]{1,0:T(8,128)S(1)} %get-tuple-element.78.a_ref), channel_id=1, source_target_pairs={{0,4},{4,0},{8,12},{12,8},{16,20},{20,16},{24,28},{28,24},{1,5},{5... | collective-permute-start | bytes 98312 | tf_op jit(solution)/shard_map/ppermute | solution.py:571
  3.6 11.5 %collective-permute-start.1 = (f32[64,896]{1,0:T(8,128)S(1)}, f32[64,896]{1,0:T(8,128)S(1)}, u32[]{:S(2)}, u32[]{:S(2)}) collective-permute-start(f32[64,896]{1,0:T(8,128)S(1)} %get-tuple-element.80), channel_id=1, source_target_pairs={{0,8},{4,12},{8,0},{12,4},{16,24},{20,28},{24,16},{28,20},{1,9},{5... | collective-permute-start | bytes 688136 | tf_op jit(solution)/shard_map/ppermute | solution.py:571
  6.4 8.6 %collective-permute-start.2 = (f32[64,896]{1,0:T(8,128)S(1)}, f32[64,896]{1,0:T(8,128)S(1)}, u32[]{:S(2)}, u32[]{:S(2)}) collective-permute-start(f32[64,896]{1,0:T(8,128)S(1)} %get-tuple-element.81), channel_id=1, source_target_pairs={{0,16},{4,20},{8,24},{12,28},{16,0},{20,4},{24,8},{28,12},{1,17},{... | collective-permute-start | bytes 688136 | tf_op jit(solution)/shard_map/ppermute | solution.py:571
  8.0 7.2 %collective-permute-start.3 = (f32[64,128]{1,0:T(8,128)S(1)}, f32[64,128]{1,0:T(8,128)S(1)}, u32[]{:S(2)}, u32[]{:S(2)}) collective-permute-start(f32[64,128]{1,0:T(8,128)S(1)} %get-tuple-element.79.refs_0_), channel_id=1, source_target_pairs={{0,24},{4,28},{8,16},{12,20},{16,8},{20,12},{24,0},{28,4},{1,25},{... | collective-permute-start | bytes 98312 | tf_op jit(solution)/shard_map/ppermute | solution.py:571
  18.4 3.2 %collective-permute-start.6 = (f32[64,1536]{1,0:T(8,128)S(1)}, f32[64,1536]{1,0:T(8,128)S(1)}, u32[]{:S(2)}, u32[]{:S(2)}) collective-permute-start(f32[64,1536]{1,0:T(8,128)S(1)} %get-tuple-element.98), channel_id=1, source_target_pairs={{0,4},{4,0},{8,12},{12,8},{16,20},{20,16},{24,28},{28,24},{1,5},{5... | collective-permute-start | bytes 1179656 | tf_op jit(solution)/shard_map/ppermute | solution.py:571
  18.5 7.3 %collective-permute-start.4 = (f32[64,768]{1,0:T(8,128)S(1)}, f32[64,768]{1,0:T(8,128)S(1)}, u32[]{:S(2)}, u32[]{:S(2)}) collective-permute-start(f32[64,768]{1,0:T(8,128)S(1)} %get-tuple-element.91.refs_0_), channel_id=1, source_target_pairs={{0,16},{4,20},{8,24},{12,28},{16,0},{20,4},{24,8},{28,12},{1,17},{... | collective-permute-start | bytes 589832 | tf_op jit(solution)/shard_map/ppermute | solution.py:571
  20.1 7.0 %collective-permute-start.5 = (f32[64,768]{1,0:T(8,128)S(1)}, f32[64,768]{1,0:T(8,128)S(1)}, u32[]{:S(2)}, u32[]{:S(2)}) collective-permute-start(f32[64,768]{1,0:T(8,128)S(1)} %get-tuple-element.92.refs_2_), channel_id=1, source_target_pairs={{0,8},{4,12},{8,0},{12,4},{16,24},{20,28},{24,16},{28,20},{1,9},{5... | collective-permute-start | bytes 589832 | tf_op jit(solution)/shard_map/ppermute | solution.py:571
  27.1 2.1 %collective-permute-start.7 = (f32[64,1536]{1,0:T(8,128)S(1)}, f32[64,1536]{1,0:T(8,128)S(1)}, u32[]{:S(2)}, u32[]{:S(2)}) collective-permute-start(f32[64,1536]{1,0:T(8,128)S(1)} %get-tuple-element.103.held_ref), channel_id=1, source_target_pairs={{0,4},{4,0},{8,12},{12,8},{16,20},{20,16},{24,28},{28,24},{1,5},{5... | collective-permute-start | bytes 1179656 | tf_op jit(solution)/shard_map/ppermute | solution.py:571
  27.1 7.3 %collective-permute-start.8 = (f32[64,768]{1,0:T(8,128)S(1)}, f32[64,768]{1,0:T(8,128)S(1)}, u32[]{:S(2)}, u32[]{:S(2)}) collective-permute-start(f32[64,768]{1,0:T(8,128)S(1)} %get-tuple-element.107.refs_0_), channel_id=1, source_target_pairs={{0,8},{4,12},{8,0},{12,4},{16,24},{20,28},{24,16},{28,20},{1,9},{5... | collective-permute-start | bytes 589832 | tf_op jit(solution)/shard_map/ppermute | solution.py:571
  28.7 7.0 %collective-permute-start.9 = (f32[64,768]{1,0:T(8,128)S(1)}, f32[64,768]{1,0:T(8,128)S(1)}, u32[]{:S(2)}, u32[]{:S(2)}) collective-permute-start(f32[64,768]{1,0:T(8,128)S(1)} %get-tuple-element.108.refs_2_), channel_id=1, source_target_pairs={{0,16},{4,20},{8,24},{12,28},{16,0},{20,4},{24,8},{28,12},{1,17},{... | collective-permute-start | bytes 589832 | tf_op jit(solution)/shard_map/ppermute | solution.py:571
  35.7 6.2 %collective-permute-start.13 = (f32[64,768]{1,0:T(8,128)S(1)}, f32[64,768]{1,0:T(8,128)S(1)}, u32[]{:S(2)}, u32[]{:S(2)}) collective-permute-start(f32[64,768]{1,0:T(8,128)S(1)} %get-tuple-element.118.refs_0_), channel_id=1, source_target_pairs={{0,16},{4,20},{8,24},{12,28},{16,0},{20,4},{24,8},{28,12},{1,17},{... | collective-permute-start | bytes 589832 | tf_op jit(solution)/shard_map/ppermute | solution.py:571
  36.3 5.8 %collective-permute-start.14 = (f32[64,768]{1,0:T(8,128)S(1)}, f32[64,768]{1,0:T(8,128)S(1)}, u32[]{:S(2)}, u32[]{:S(2)}) collective-permute-start(f32[64,768]{1,0:T(8,128)S(1)} %get-tuple-element.119.refs_2_), channel_id=1, source_target_pairs={{0,8},{4,12},{8,0},{12,4},{16,24},{20,28},{24,16},{28,20},{1,9},{5... | collective-permute-start | bytes 589832 | tf_op jit(solution)/shard_map/ppermute | solution.py:571
  42.1 5.6 %collective-permute-start.15 = (f32[64,1536]{1,0:T(8,128)S(1)}, f32[64,1536]{1,0:T(8,128)S(1)}, u32[]{:S(2)}, u32[]{:S(2)}) collective-permute-start(f32[64,1536]{1,0:T(8,128)S(1)} %get-tuple-element.122.refs_1_), channel_id=1, source_target_pairs={{0,4},{4,0},{8,12},{12,8},{16,20},{20,16},{24,28},{28,24},{1,5},{5... | collective-permute-start | bytes 1179656 | tf_op jit(solution)/shard_map/ppermute | solution.py:571
  42.2 7.6 %collective-permute-start.12 = (f32[64,384]{1,0:T(8,128)S(1)}, f32[64,384]{1,0:T(8,128)S(1)}, u32[]{:S(2)}, u32[]{:S(2)}) collective-permute-start(f32[64,384]{1,0:T(8,128)S(1)} %get-tuple-element.116), channel_id=1, source_target_pairs={{0,1},{1,2},{2,3},{3,0},{4,5},{5,6},{6,7},{7,4},{8,9},{9,10},{10,1... | collective-permute-start | bytes 294920 | tf_op jit(solution)/shard_map/ppermute | solution.py:585
  43.9 9.7 %collective-permute-start.10 = (f32[64,384]{1,0:T(8,128)S(1)}, f32[64,384]{1,0:T(8,128)S(1)}, u32[]{:S(2)}, u32[]{:S(2)}) collective-permute-start(f32[64,384]{1,0:T(8,128)S(1)} %get-tuple-element.114), channel_id=1, source_target_pairs={{0,2},{1,3},{2,0},{3,1},{4,6},{5,7},{6,4},{7,5},{8,10},{9,11},{10,... | collective-permute-start | bytes 294920 | tf_op jit(solution)/shard_map/ppermute | solution.py:585
  46.4 7.1 %collective-permute-start.11 = (f32[64,384]{1,0:T(8,128)S(1)}, f32[64,384]{1,0:T(8,128)S(1)}, u32[]{:S(2)}, u32[]{:S(2)}) collective-permute-start(f32[64,384]{1,0:T(8,128)S(1)} %get-tuple-element.115), channel_id=1, source_target_pairs={{0,3},{1,0},{2,1},{3,2},{4,7},{5,4},{6,5},{7,6},{8,11},{9,8},{10,9... | collective-permute-start | bytes 294920 | tf_op jit(solution)/shard_map/ppermute | solution.py:585
  53.6 10.9 %collective-permute-start.16 = (f32[80,384]{1,0:T(8,128)S(1)}, f32[80,384]{1,0:T(8,128)S(1)}, u32[]{:S(2)}, u32[]{:S(2)}) collective-permute-start(f32[80,384]{1,0:T(8,128)S(1)} %get-tuple-element.135.refs_2_), channel_id=1, source_target_pairs={{0,1},{1,2},{2,3},{3,0},{4,5},{5,6},{6,7},{7,4},{8,9},{9,10},{10,1... | collective-permute-start | bytes 368648 | tf_op jit(solution)/shard_map/ppermute | solution.py:585
  56.2 9.8 %collective-permute-start.17 = (f32[80,384]{1,0:T(8,128)S(1)}, f32[80,384]{1,0:T(8,128)S(1)}, u32[]{:S(2)}, u32[]{:S(2)}) collective-permute-start(f32[80,384]{1,0:T(8,128)S(1)} %get-tuple-element.135.refs_2_), channel_id=1, source_target_pairs={{0,2},{1,3},{2,0},{3,1},{4,6},{5,7},{6,4},{7,5},{8,10},{9,11},{10,... | collective-permute-start | bytes 368648 | tf_op jit(solution)/shard_map/ppermute | solution.py:585
  57.9 8.1 %collective-permute-start.18 = (f32[80,384]{1,0:T(8,128)S(1)}, f32[80,384]{1,0:T(8,128)S(1)}, u32[]{:S(2)}, u32[]{:S(2)}) collective-permute-start(f32[80,384]{1,0:T(8,128)S(1)} %get-tuple-element.135.refs_2_), channel_id=1, source_target_pairs={{0,3},{1,0},{2,1},{3,2},{4,7},{5,4},{6,5},{7,6},{8,11},{9,8},{10,9... | collective-permute-start | bytes 368648 | tf_op jit(solution)/shard_map/ppermute | solution.py:585

commit v7 on v6

--- a/solution.py
+++ b/solution.py
@@ -173,66 +173,80 @@
     out_ref[...] = -dot(jnp.concatenate(tiles, 0), inverse_ref[...])
 
 
-def down_kernel(first_ref, second_ref, a_ref, low_ref, high_ref, kept_ref, over_ref, sems):
-    width, span = low_ref.shape
-    count = sems.shape[0] // 2
+def parts_of(columns):
+    return 2 if columns % 512 else 4
+
+
+def down_kernel(first_ref, second_ref, a_ref, low_ref, high_ref, *refs):
+    kept, sems = refs[:-1], refs[-1]
+    width = low_ref.shape[0]
+    span = kept[0].shape[1]
+    count = sems.shape[0] // len(kept)
     size = span // count
-    halves = ((0, low_ref, kept_ref), (1, high_ref, over_ref))
-
-    def load(at, ref, i):
+
+    def load(at, i):
         start = pl.multiple_of(i * size, size)
         source = a_ref.at[:, pl.ds(pl.multiple_of(at * span + start, size), size)]
-        return pltpu.make_async_copy(
-            source, ref.at[:, pl.ds(start, size)], sems.at[at * count + i]
-        )
-
-    for at, _, kept in halves:
+        target = kept[at].at[:, pl.ds(start, size)]
+        return pltpu.make_async_copy(source, target, sems.at[at * count + i])
+
+    for at in range(len(kept)):
         for i in range(count):
-            load(at, kept, i).start()
+            load(at, i).start()
     kh, kl = split(jnp.concatenate([first_ref[...], second_ref[...]], 1))
     left = jnp.concatenate([kh, kl], 0)
-    for at, out, kept in halves:
+    for at, ref in enumerate(kept):
+        half, place = divmod(at, len(kept) // 2)
+        out = (low_ref, high_ref)[half]
 
         @pl.loop(0, count)
         def _(i):
-            load(at, kept, i).wait()
-            part = pl.ds(pl.multiple_of(i * size, size), size)
-            ah, al = split(kept[:, part])
+            load(at, i).wait()
+            start = pl.multiple_of(i * size, size)
+            ah, al = split(ref[:, pl.ds(start, size)])
             term = fast(left, ah) + fast(left, al)
-            out[:, part] = term[:width] + term[width:]
+            into = pl.ds(pl.multiple_of(place * span + start, size), size)
+            out[:, into] = term[:width] + term[width:]
 
 
 def product_down(first, second, a):
     rows, columns = a.shape
     width = first.shape[0]
-    span = columns // 2
+    parts = parts_of(columns)
+    span = columns // parts
     size = block_of(span, 256)
     whole = pl.BlockSpec(memory_space=pltpu.VMEM)
-    low, high, *halves = pl.pallas_call(
+    low, high, *kept = pl.pallas_call(
         down_kernel,
         in_specs=[whole, whole, pl.BlockSpec(memory_space=pltpu.HBM)],
-        out_specs=(whole,) * 4,
-        out_shape=(shape(width, span),) * 2 + (shape(rows, span),) * 2,
+        out_specs=(whole,) * (2 + parts),
+        out_shape=(shape(width, columns // 2),) * 2 + (shape(rows, span),) * parts,
         scratch_shapes=[pltpu.SemaphoreType.DMA((columns // size,))],
         compiler_params=params(12),
         cost_estimate=cost(8 * rows * columns * width, 4 * rows * columns),
         name="product_down",
     )(first, second, pltpu.with_memory_space_constraint(a, pltpu.HBM))
-    return low, high, tuple(halves)
-
-
-def fix_kernel(low_ref, high_ref, band_ref, top_ref, over_ref, keep_ref, give_ref, *_):
+    return low, high, tuple(kept)
+
+
+def fix_kernel(parts, low_ref, high_ref, band_ref, *refs):
+    tops, keep_ref, give_ref = refs[:parts], refs[parts], refs[parts + 1]
     row = lax.axis_index("row")
     core = lax.rem(row, 2)
     first, second = low_ref[...], high_ref[...]
+    span = tops[0].shape[1]
 
     @pl.when(row == 0)
     def _():
         rh, rl = split(band_ref[...].T)
         left = jnp.concatenate([rh, rl, rh, rl], 1)
-        for value, top, out in ((first, top_ref, keep_ref), (second, over_ref, give_ref)):
+        for at, top in enumerate(tops):
+            half, place = divmod(at, parts // 2)
             ah, al = split(top[...])
-            out[...] = value - fast(left, jnp.concatenate([ah, ah, al, al], 0))
+            value = (first, second)[half][:, place * span : (place + 1) * span]
+            (keep_ref, give_ref)[half][:, place * span : (place + 1) * span] = value - fast(
+                left, jnp.concatenate([ah, ah, al, al], 0)
+            )
 
     @pl.when((row != 0) & (core == 0))
     def _():
@@ -245,22 +259,28 @@
         give_ref[...] = first
 
 
-def fix_down(low, high, band, halves):
-    width, span = low.shape
-    part = pl.BlockSpec((width, span), lambda i: (0, 0))
+def fix_down(low, high, band, kept):
+    width, half = low.shape
+    parts = len(kept)
+    side = pl.BlockSpec((width, half), lambda i: (0, 0))
+    top = pl.BlockSpec((width, kept[0].shape[1]), lambda i: (0, 0))
     anywhere = pl.BlockSpec(memory_space=pl.ANY)
-    keep, give, *halves = pl.pallas_call(
-        fix_kernel,
+
+    def kernel(*refs):
+        fix_kernel(parts, *refs)
+
+    keep, give, *kept = pl.pallas_call(
+        kernel,
         grid=(1,),
-        in_specs=[part, part, pl.BlockSpec((width, width), lambda i: (0, 0)), part, part],
-        out_specs=(part, part, anywhere, anywhere),
-        out_shape=(shape(width, span),) * 2 + tuple(shape(*x.shape) for x in halves),
-        input_output_aliases={3: 2, 4: 3},
+        in_specs=[side, side, pl.BlockSpec((width, width), lambda i: (0, 0))] + [top] * parts,
+        out_specs=(side, side) + (anywhere,) * parts,
+        out_shape=(shape(width, half),) * 2 + tuple(shape(*x.shape) for x in kept),
+        input_output_aliases={3 + k: 2 + k for k in range(parts)},
         compiler_params=params(12),
-        cost_estimate=cost(24 * width * width * span, 32 * width * span),
+        cost_estimate=cost(24 * width * width * half, 32 * width * half),
         name="fix_down",
-    )(low, high, band, *halves)
-    return keep, give, tuple(halves)
+    )(low, high, band, *kept)
+    return keep, give, tuple(kept)
 
 
 def rows_product(right_ref, halves, outs):
@@ -282,7 +302,8 @@
             out_ref[...] = result
 
 
-def across_kernel(held_ref, other_ref, band_ref, low_ref, high_ref, kct_ref, right_ref, *refs):
+def across_kernel(parts, held_ref, other_ref, band_ref, *refs):
+    kct_ref, right_ref = refs[parts : parts + 2]
     width, half = held_ref.shape
     columns = 2 * half
     chunk = block_of(columns, 512)
@@ -308,15 +329,16 @@
         for c in range(0, columns, chunk):
             right_ref[c : c + chunk, :] = jnp.concatenate(split(kct_ref[:, c : c + chunk].T), 1)
 
-    rows_product(right_ref, (low_ref, high_ref), refs[:-2])
-
-
-def more_kernel(right_ref, low_ref, high_ref, *refs):
-    rows_product(right_ref, (low_ref, high_ref), refs[:-2])
-
-
-def across_call(kernel, operands, extra, halves, pieces, start, count, width):
-    rows, span = halves[0].shape
+    rows_product(right_ref, refs[:parts], refs[parts + 2 : -parts])
+
+
+def more_kernel(parts, right_ref, *refs):
+    rows_product(right_ref, refs[:parts], refs[parts:-parts])
+
+
+def across_call(kernel, operands, extra, kept, pieces, start, count, width):
+    rows, span = kept[0].shape
+    parts = len(kept)
     size = rows // pieces
 
     def turn(i):
@@ -325,19 +347,22 @@
     def fixed(array):
         return pl.BlockSpec(array.shape, lambda i: (0, 0))
 
+    def body(*refs):
+        kernel(parts, *refs)
+
     outs = tuple(extra) + (shape(width, size),) * count
     at, to = len(operands), len(outs)
-    *results, low, high = pl.pallas_call(
-        kernel,
+    results = pl.pallas_call(
+        body,
         grid=(count,),
-        in_specs=[fixed(x) for x in operands] + [pl.BlockSpec((size, span), turn)] * 2,
-        out_specs=tuple(fixed(x) for x in outs) + (pl.BlockSpec(memory_space=pl.ANY),) * 2,
-        out_shape=outs + (shape(rows, span),) * 2,
-        input_output_aliases={at: to, at + 1: to + 1},
+        in_specs=[fixed(x) for x in operands] + [pl.BlockSpec((size, span), turn)] * parts,
+        out_specs=tuple(fixed(x) for x in outs) + (pl.BlockSpec(memory_space=pl.ANY),) * parts,
+        out_shape=outs + (shape(rows, span),) * parts,
+        input_output_aliases={at + k: to + k for k in range(parts)},
         compiler_params=params(22),
-        cost_estimate=cost(16 * size * count * span * width, 8 * size * count * span),
-    )(*operands, *halves)
-    return (*results, (low, high))
+        cost_estimate=cost(8 * size * count * span * parts * width, 4 * size * count * span * parts),
+    )(*operands, *kept)
+    return (*results[:to], tuple(results[to:]))
 
 
 def merge_first_kernel(first_ref, second_ref, by_x_ref, by_y_ref, a_ref, b_ref):
@@ -429,68 +454,106 @@
     return jnp.concatenate([high, high, low, low], 0)
 
 
-def near_kernel(left_ref, right_ref, a_ref, _, out_ref, __):
-    rows, span = a_ref.shape
+def near_kernel(count, left_ref, right_ref, *refs):
+    total = (len(refs)) // 2
+    rows, span = refs[0].shape
     deep = block_of(rows, 512)
     chunk = block_of(span, 512)
-
-    @pl.loop(0, span // chunk)
-    def _(i):
-        c = pl.multiple_of(i * chunk, chunk)
-        right = four_parts(right_ref, c, chunk)
-        for r in range(0, rows, deep):
-            out_ref[r : r + deep, pl.ds(c, chunk)] = a_ref[r : r + deep, pl.ds(c, chunk)] - fast(
-                both_parts(left_ref[r : r + deep, :]), right
-            )
-
-
-def subtract_near(left, right, low, high):
-    rows, span = low.shape
+    if (span // 2) % 128 == 0:
+        chunk = span // 2
+    for at in range(count):
+        a_ref, out_ref = refs[at], refs[total + at]
+
+        @pl.loop(0, span // chunk)
+        def _(i):
+            c = pl.multiple_of(i * chunk, chunk)
+            right = four_parts(right_ref, pl.multiple_of(at * span + c, 128), chunk)
+            for r in range(0, rows, deep):
+                out_ref[r : r + deep, pl.ds(c, chunk)] = a_ref[
+                    r : r + deep, pl.ds(c, chunk)
+                ] - fast(both_parts(left_ref[r : r + deep, :]), right)
+
+
+def near_count(parts):
+    return parts - max(1, parts // 4)
+
+
+def subtract_near(left, right, kept):
+    rows, span = kept[0].shape
+    parts = len(kept)
+    count = near_count(parts)
     deep = left.shape[1]
     whole = pl.BlockSpec(memory_space=pltpu.VMEM)
-    anywhere = pl.BlockSpec(memory_space=pl.ANY)
+    places = [whole] * count + [pl.BlockSpec(memory_space=pl.ANY)] * (parts - count)
+
+    def kernel(*refs):
+        near_kernel(count, *refs)
+
     return tuple(
         pl.pallas_call(
-            near_kernel,
-            in_specs=[whole] * 3 + [anywhere],
-            out_specs=(whole, anywhere),
-            out_shape=(shape(rows, span),) * 2,
-            input_output_aliases={2: 0, 3: 1},
+            kernel,
+            in_specs=[whole] * 2 + places,
+            out_specs=tuple(places),
+            out_shape=(shape(rows, span),) * parts,
+            input_output_aliases={2 + k: k for k in range(parts)},
             compiler_params=params(12),
-            cost_estimate=cost(4 * rows * span * deep, 8 * rows * span),
+            cost_estimate=cost(4 * rows * span * count * deep, 8 * rows * span * count),
             name="subtract_near",
-        )(left, right, low, high)
+        )(left, right, *kept)
     )
 
 
+def core_blocks(width):
+    half = width // 2
+    return [(0, 0), (0, half), (half, half)], half
+
+
 def packing(width, size):
+    half = width // 2
     beside = 1
-    while 2 * beside <= min(size // width, 8):
+    while 6 * beside * half <= size and 2 * beside <= half // 8:
         beside *= 2
-    return beside, width // beside
+    return beside, half // beside
 
 
 def line_kernel(*refs):
     *chunks, inner_ref, out_ref = refs
     width, size = chunks[0].shape
     beside, tall = packing(width, size)
+    blocks, half = core_blocks(width)
     total = chunks[0][...]
     for ref in chunks[1:]:
         total = total + ref[...]
     out_ref[:width, :] = total
-    out_ref[width:, :] = jnp.zeros((tall, size), f32)
-    for k in range(beside):
-        out_ref[width:, k * width : (k + 1) * width] = inner_ref[k * tall : (k + 1) * tall, :]
+    below = [
+        inner_ref[r + k * tall : r + (k + 1) * tall, c : c + half]
+        for r, c in blocks
+        for k in range(beside)
+    ]
+    spare = size - half * len(below)
+    if spare:
+        below.append(jnp.zeros((tall, spare), f32))
+    out_ref[width:, :] = jnp.concatenate(below, 1)
 
 
 def core_kernel(st_ref, krt_ref, *refs):
     chunks, out_ref = refs[:-1], refs[-1]
     width = st_ref.shape[0]
     beside, _ = packing(width, chunks[0].shape[1])
+    half = core_blocks(width)[1]
     packed = chunks[0][width:, :]
     for ref in chunks[1:]:
         packed = packed + ref[width:, :]
-    inner = jnp.concatenate([packed[:, k * width : (k + 1) * width] for k in range(beside)], 0)
+    near, cross, far = (
+        jnp.concatenate(
+            [packed[:, (b * beside + k) * half : (b * beside + k + 1) * half] for k in range(beside)],
+            0,
+        )
+        for b in range(3)
+    )
+    inner = jnp.concatenate(
+        [jnp.concatenate([near, cross], 1), jnp.concatenate([cross.T, far], 1)], 0
+    )
     st = st_ref[...]
     cm = dot(dot(st, inner), st.T)
     out_ref[...] = dot(cm, krt_ref[...])
@@ -508,63 +571,66 @@
         left_ref[pl.ds(start, size), :] = jnp.concatenate(split(value.T), 1)
 
 
-def far_kernel(
-    left_ref, right_ref, near_left_ref, near_right_ref, low_ref, high_ref, out_ref, buffer, sems
-):
-    rows, span = low_ref.shape
-    slots, deep, wide = buffer.shape
+def far_kernel(count, left_ref, right_ref, near_left_ref, near_right_ref, *refs):
+    *kept, out_ref, buffer, sems = refs
+    rows, span = kept[0].shape
+    slots, deep, _ = buffer.shape
+    turns = len(kept)
     down = rows // deep
-    pairs = down * (span // wide)
 
     def store(i, slot):
-        turn, pair = lax.rem(i, 2), lax.div(i, 2)
-        r = pl.multiple_of(lax.rem(pair, down) * deep, deep)
-        c = pl.multiple_of(turn * span + lax.div(pair, down) * wide, wide)
+        turn, pair = lax.rem(i, turns), lax.div(i, turns)
+        r = pl.multiple_of(pair * deep, deep)
+        c = pl.multiple_of(turn * span, span)
         return pltpu.make_async_copy(
-            buffer.at[slot], out_ref.at[pl.ds(r, deep), pl.ds(c, wide)], sems.at[slot]
-        )
-
-    @pl.loop(0, pairs)
+            buffer.at[slot], out_ref.at[pl.ds(r, deep), pl.ds(c, span)], sems.at[slot]
+        )
+
+    @pl.loop(0, down)
     def _(pair):
-        r = pl.multiple_of(lax.rem(pair, down) * deep, deep)
-        local = pl.multiple_of(lax.div(pair, down) * wide, wide)
-        for turn, a_ref in enumerate((low_ref, high_ref)):
-            i = pair * 2 + turn
+        r = pl.multiple_of(pair * deep, deep)
+        for turn, a_ref in enumerate(kept):
+            i = pair * turns + turn
             slot = lax.rem(i, slots)
 
             @pl.when(i >= slots)
             def _():
                 store(i - slots, slot).wait()
 
-            c = pl.multiple_of(turn * span + local, wide)
             left = both_parts(left_ref[pl.ds(r, deep), :])
-            right = four_parts(right_ref, c, wide)
-            if turn:
+            right = four_parts(right_ref, turn * span, span)
+            if turn >= count:
                 left = jnp.concatenate([left, both_parts(near_left_ref[pl.ds(r, deep), :])], 1)
-                right = jnp.concatenate([right, four_parts(near_right_ref, c, wide)], 0)
-            buffer[slot] = a_ref[pl.ds(r, deep), pl.ds(local, wide)] - fast(left, right)
+                right = jnp.concatenate([right, four_parts(near_right_ref, turn * span, span)], 0)
+            buffer[slot] = a_ref[pl.ds(r, deep), :] - fast(left, right)
             store(i, slot).start()
 
     for back in range(slots, 0, -1):
-        store(2 * pairs - back, (2 * pairs - back) % slots).wait()
-
-
-def subtract_far(left, right, near_left, near_right, low, high):
-    rows, span = low.shape
+        store(down * turns - back, (down * turns - back) % slots).wait()
+
+
+def subtract_far(left, right, near_left, near_right, kept):
+    rows, span = kept[0].shape
+    parts = len(kept)
     deep = left.shape[1]
     whole = pl.BlockSpec(memory_space=pltpu.VMEM)
-    wide = span if (span // 2) % 128 else span // 2
-    piece = (block_of(rows, 512), wide)
+
+    def kernel(*refs):
+        far_kernel(near_count(parts), *refs)
+
     return pl.pallas_call(
-        far_kernel,
-        in_specs=[whole] * 6,
+        kernel,
+        in_specs=[whole] * (4 + parts),
         out_specs=pl.BlockSpec(memory_space=pltpu.HBM),
-        out_shape=shape(rows, 2 * span),
-        scratch_shapes=[pltpu.VMEM((3,) + piece, f32), pltpu.SemaphoreType.DMA((3,))],
+        out_shape=shape(rows, parts * span),
+        scratch_shapes=[
+            pltpu.VMEM((3, block_of(rows, 512), span), f32),
+            pltpu.SemaphoreType.DMA((3,)),
+        ],
         compiler_params=params(12),
-        cost_estimate=cost(12 * rows * span * deep, 16 * rows * span),
+        cost_estimate=cost(5 * rows * span * parts * deep, 8 * rows * span * parts),
         name="subtract_far",
-    )(left, right, near_left, near_right, low, high)
+    )(left, right, near_left, near_right, *kept)
 
 
 def flip(value, bit, size, axis="row"):
@@ -636,15 +702,15 @@
             eliminate_kernel, (small, small, small, small), *terms, flops=50_000_000, carry=resident
         )
         keep, give, resident = fix_down(low, high, again, resident)
-        quarter = shape(width, columns // 4)
-        a, b, resident = small_call(
-            halve_kernel, (quarter, quarter), keep, flip(give, 1, row_size), carry=resident
-        )
         if row_size == 8:
             held, resident = small_call(
                 join_kernel, shape(width, rows), one, more_y, two, more_x, carry=resident
             )
         other = flip(held, 1, row_size)
+        quarter = shape(width, columns // 4)
+        a, b, resident = small_call(
+            halve_kernel, (quarter, quarter), keep, flip(give, 1, row_size), carry=resident
+        )
         bits = []
         bit = 2
         while bit < row_size:
@@ -722,7 +788,7 @@
             mib=12,
             carry=resident,
         )
-        resident = subtract_near(near_left, xparts, *resident)
+        resident = subtract_near(near_left, xparts, resident)
         core, resident = small_call(
             core_kernel, shape(width, rows), st, krt, *whole, carry=resident
         )
@@ -735,7 +801,7 @@
             mib=12,
             carry=resident,
         )
-        return subtract_far(left, kparts, near_left, xparts, *resident), band
+        return subtract_far(left, kparts, near_left, xparts, resident), band
 
     return body
 

time: 76.8 us -> 76.6 us (level)
  waiting for transfers between devices: 17.5 us -> 15.5 us
  Pallas kernels: 34.9 us -> 36.6 us
    pallas_call x5, Pallas kernels: 18.1 us -> 19.7 us  [the longest x1 8.25 us: subtract_far(): pl.pallas_call(kernel, in_specs=[whole] * (4 + parts), out_specs=pl.Block...]
    ppermute x6, waiting for transfers between devices: 6.42 us -> 4.93 us  [shift(): lax.ppermute(piece, 'col', [(i, (i + by) % size) for i in range(size)])]
  transfers between devices with their start and end apart: 19 -> 19, of which waited for: 10 -> 9; matrix products, arithmetic and copies ran while one was open for 0% -> 0% of each run, Pallas kernels for 27% -> 34%
where the time goes in v7:
time: 76.6 us; the launch traced here: 76.5 us
  Pallas kernels  36.6 us (48%)
  starting transfers between devices  22.3 us (29%)
  waiting for transfers between devices  15.5 us (20%)
  local copies, waits for them, and re-layouts  0.99 us (1%)
  between operations  0.99 us (1%)
    ppermute x13, starting transfers between devices, flip(): return lax.ppermute(value, axis, [(i, i ^ bit) for i in range(size)])  11.7 us
    ppermute x6, starting transfers between devices, shift(): lax.ppermute(piece, 'col', [(i, (i + by) % size) for i in range(size)])  10.6 us
    ppermute x13, waiting for transfers between devices, flip(): return lax.ppermute(value, axis, [(i, i ^ bit) for i in range(size)])  10.6 us
    pallas_call x14, Pallas kernels, small_call(): pl.pallas_call(body, out_shape=out, compiler_params=params(mib), cost_est...  9.82 us
    pallas_call x1, Pallas kernels, subtract_far(): pl.pallas_call(kernel, in_specs=[whole] * (4 + parts), out_specs=pl.Block...  8.25 us
    pallas_call x1, Pallas kernels, product_down(): pl.pallas_call(down_kernel, in_specs=[whole, whole, pl.BlockSpec(memory_s...  7.04 us
    pallas_call x2, Pallas kernels, across_call(): pl.pallas_call(body, grid=(count,), in_specs=[fixed(x) for x in operands]...  6.93 us
    ppermute x6, waiting for transfers between devices, shift(): lax.ppermute(piece, 'col', [(i, (i + by) % size) for i in range(size)])  4.93 us
  transfers between devices with their start and end apart: 19, of which 9 were waited for; matrix products, arithmetic and copies ran while one was open for 0% of the time, Pallas kernels for 34%

profile of v7, /device:TPU:0, one launch (start us, length us, event | category | flops | bytes accessed | tf_op | source)
XLA Modules:
  0.0 76.5 jit_solution(147714074333016734)
XLA Ops:
  0.6 0.0 copy-start
  0.6 1.0 %copy-done = f32[1536,64]{0,1:T(8,128)S(1)} copy-done((f32[1536,64]{0,1:T(8,128)S(1)}, f32[1536,64]{0,1:T(8,128)}, u32[]{:S(2)}) %copy-start) | copy-done | bytes 393240
  1.6 0.5 shard_map.41
  2.1 0.6 collective-permute-start
  2.7 0.9 %collective-permute-done.b_ref = f32[64,128]{1,0:T(8,128)S(1)} collective-permute-done((f32[64,128]{1,0:T(8,128)S(1)}, f32[64,128]{1,0:T(8,128)S(1)}, u32[]{:S(2)}, u32[]{:S(2)}) %collective-permute-start) | collective-permute-done | bytes 32800 | tf_op jit(solution)/shard_map/ppermute | solution.py:637
  3.6 2.9 %collective-permute-start.1 = (f32[64,896]{1,0:T(8,128)S(1)}, f32[64,896]{1,0:T(8,128)S(1)}, u32[]{:S(2)}, u32[]{:S(2)}) collective-permute-start(f32[64,896]{1,0:T(8,128)S(1)} %get-tuple-element.114), channel_id=1, source_target_pairs={{0,8},{4,12},{8,0},{12,4},{16,24},{20,28},{24,16},{28,20},{1,9},{5... | collective-permute-start | bytes 688136 | tf_op jit(solution)/shard_map/ppermute | solution.py:637
  6.4 1.5 %collective-permute-start.2 = (f32[64,896]{1,0:T(8,128)S(1)}, f32[64,896]{1,0:T(8,128)S(1)}, u32[]{:S(2)}, u32[]{:S(2)}) collective-permute-start(f32[64,896]{1,0:T(8,128)S(1)} %get-tuple-element.115), channel_id=1, source_target_pairs={{0,16},{4,20},{8,24},{12,28},{16,0},{20,4},{24,8},{28,12},{1,17},{... | collective-permute-start | bytes 688136 | tf_op jit(solution)/shard_map/ppermute | solution.py:637
  8.0 7.0 %product_down.1 = (f32[64,1536]{1,0:T(8,128)S(1)}, f32[64,1536]{1,0:T(8,128)S(1)}, f32[1536,768]{1,0:T(8,128)S(1)}, f32[1536,768]{1,0:T(8,128)S(1)}, f32[1536,768]{1,0:T(8,128)S(1)}, /*index=5*/f32[1536,768]{1,0:T(8,128)S(1)}) custom-call(f32[64,768]{1,0:T(8,128)S(1)} %get-tuple-element.116.first_ref.refs_0_.refs_3_, ...), custom_call_target="tpu_custom_call" | custom-call | flops 2415919104 | bytes 18874368 | tf_op jit(solution)/shard_map/product_down/pallas_call | solution.py:219
  15.0 0.0 collective-permute-done.1.refs_2_.refs_1_
  15.0 0.0 collective-permute-done.2.refs_3_.refs_2_
  15.0 0.1 shard_map.43
  15.1 0.6 collective-permute-start.4
  15.7 0.3 collective-permute-start.5
  16.0 2.7 %collective-permute-start.3 = (f32[64,128]{1,0:T(8,128)S(1)}, f32[64,128]{1,0:T(8,128)S(1)}, u32[]{:S(2)}, u32[]{:S(2)}) collective-permute-start(f32[64,128]{1,0:T(8,128)S(1)} %get-tuple-element.113.refs_0_), channel_id=1, source_target_pairs={{0,24},{4,28},{8,16},{12,20},{16,8},{20,12},{24,0},{28,4},{1,25},{... | collective-permute-start | bytes 98312 | tf_op jit(solution)/shard_map/ppermute | solution.py:637
  18.7 4.8 %collective-permute-done.3.refs_3_ = f32[64,128]{1,0:T(8,128)S(1)} collective-permute-done((f32[64,128]{1,0:T(8,128)S(1)}, f32[64,128]{1,0:T(8,128)S(1)}, u32[]{:S(2)}, u32[]{:S(2)}) %collective-permute-start.3) | collective-permute-done | bytes 32800 | tf_op jit(solution)/shard_map/ppermute | solution.py:637
  23.5 2.7 %shard_map.44 = (f32[64,64]{1,0:T(8,128)}, f32[64,64]{1,0:T(8,128)S(1)}, f32[64,64]{1,0:T(8,128)S(1)}, f32[64,64]{1,0:T(8,128)S(1)}, f32[1536,768]{1,0:T(8,128)S...) custom-call(f32[64,128]{1,0:T(8,128)S(1)} %get-tuple-element.113.ref, ...), custom_call_target="tpu_custom_call", output_to_operand_aliasing={{4}: (4, {}), {5}: (5, {}), {6}: (6, {}), {7}: (7, {})} | custom-call | flops 50000000 | bytes 1000000 | tf_op jit(solution)/shard_map/pallas_call | solution.py:64
  26.2 0.6 fix_down.1
  26.7 0.1 collective-permute-start.7
  26.8 0.0 collective-permute-done.4.refs_1_
  26.8 0.0 collective-permute-done.5.refs_3_
  26.9 0.5 collective-permute-start.6
  27.4 1.1 %collective-permute-done.7.refs_1_ = f32[64,1536]{1,0:T(8,128)S(1)} collective-permute-done((f32[64,1536]{1,0:T(8,128)S(1)}, f32[64,1536]{1,0:T(8,128)S(1)}, u32[]{:S(2)}, u32[]{:S(2)}) %collective-permute-start.7) | collective-permute-done | bytes 393248 | tf_op jit(solution)/shard_map/ppermute | solution.py:637
  28.6 0.1 collective-permute-start.8
  28.7 0.4 collective-permute-start.9
  29.1 0.0 collective-permute-done.6.refs_1_
  29.1 3.9 %shard_map.47 = (f32[64,3072]{1,0:T(8,128)S(1)}, bf16[3072,128]{1,0:T(8,128)(2,1)S(1)}, f32[64,384]{1,0:T(8,128)S(1)}, f32[64,384]{1,0:T(8,128)S(1)}, f32[1536,7...) custom-call(f32[64,1536]{1,0:T(8,128)S(1)} %get-tuple-element.141.re, ...), custom_call_target="tpu_custom_call", output_to_operand_aliasing={{4}: (3, {}), {5}: (4, {}), {6}: (5, {}), {7}: (6, {})} | custom-call | flops 1207959552 | bytes 9437184 | tf_op jit(solution)/shard_map/pallas_call | solution.py:355
  33.0 2.6 %collective-permute-done.8.refs_1_ = f32[64,768]{1,0:T(8,128)S(1)} collective-permute-done((f32[64,768]{1,0:T(8,128)S(1)}, f32[64,768]{1,0:T(8,128)S(1)}, u32[]{:S(2)}, u32[]{:S(2)}) %collective-permute-start.8) | collective-permute-done | bytes 196640 | tf_op jit(solution)/shard_map/ppermute | solution.py:637
  35.6 0.1 collective-permute-done.9.refs_3_
  35.7 0.4 collective-permute-start.13
  36.0 1.7 %collective-permute-start.14 = (f32[64,768]{1,0:T(8,128)S(1)}, f32[64,768]{1,0:T(8,128)S(1)}, u32[]{:S(2)}, u32[]{:S(2)}) collective-permute-start(f32[64,768]{1,0:T(8,128)S(1)} %get-tuple-element.169.refs_2_), channel_id=1, source_target_pairs={{0,8},{4,12},{8,0},{12,4},{16,24},{20,28},{24,16},{28,20},{1,9},{5... | collective-permute-start | bytes 589832 | tf_op jit(solution)/shard_map/ppermute | solution.py:637
  37.7 3.0 %shard_map.49 = (f32[64,384]{1,0:T(8,128)S(1)}, f32[64,384]{1,0:T(8,128)S(1)}, f32[1536,768]{1,0:T(8,128)S(1)}, f32[1536,768]{1,0:T(8,128)S(1)}, f32[1536,768]{1,0:T(8,128)S(1)}, /*index=5*/f32[1536,768]{1,0:T(8,128)S(1)}) custom-call(bf16[3072,128]{1,0:T(8,128)(2,1)S(1)} %get-tuple-element.1, ...), custom_call_target="tpu_custom_call", output_to_operand_aliasing={{2}: (1, {}), {3}: (2, {}), {4}: (3, {}), {5}: (4, {})} | custom-call | flops 1207959552 | bytes 9437184 | tf_op jit(solution)/shard_map/pallas_call | solution.py:355
  40.7 1.1 %collective-permute-done.13.refs_1_ = f32[64,768]{1,0:T(8,128)S(1)} collective-permute-done((f32[64,768]{1,0:T(8,128)S(1)}, f32[64,768]{1,0:T(8,128)S(1)}, u32[]{:S(2)}, u32[]{:S(2)}) %collective-permute-start.13) | collective-permute-done | bytes 196640 | tf_op jit(solution)/shard_map/ppermute | solution.py:637
  41.8 0.1 collective-permute-done.14.refs_3_
  42.0 0.1 collective-permute-start.15
  42.0 1.6 %collective-permute-start.12 = (f32[64,384]{1,0:T(8,128)S(1)}, f32[64,384]{1,0:T(8,128)S(1)}, u32[]{:S(2)}, u32[]{:S(2)}) collective-permute-start(f32[64,384]{1,0:T(8,128)S(1)} %get-tuple-element.166), channel_id=1, source_target_pairs={{0,1},{1,2},{2,3},{3,0},{4,5},{5,6},{6,7},{7,4},{8,9},{9,10},{10,1... | collective-permute-start | bytes 294920 | tf_op jit(solution)/shard_map/ppermute | solution.py:651
  43.7 2.6 %collective-permute-start.10 = (f32[64,384]{1,0:T(8,128)S(1)}, f32[64,384]{1,0:T(8,128)S(1)}, u32[]{:S(2)}, u32[]{:S(2)}) collective-permute-start(f32[64,384]{1,0:T(8,128)S(1)} %get-tuple-element.164), channel_id=1, source_target_pairs={{0,2},{1,3},{2,0},{3,1},{4,6},{5,7},{6,4},{7,5},{8,10},{9,11},{10,... | collective-permute-start | bytes 294920 | tf_op jit(solution)/shard_map/ppermute | solution.py:651
  46.2 1.4 %collective-permute-start.11 = (f32[64,384]{1,0:T(8,128)S(1)}, f32[64,384]{1,0:T(8,128)S(1)}, u32[]{:S(2)}, u32[]{:S(2)}) collective-permute-start(f32[64,384]{1,0:T(8,128)S(1)} %get-tuple-element.165), channel_id=1, source_target_pairs={{0,3},{1,0},{2,1},{3,2},{4,7},{5,4},{6,5},{7,6},{8,11},{9,8},{10,9... | collective-permute-start | bytes 294920 | tf_op jit(solution)/shard_map/ppermute | solution.py:651
  47.6 0.0 collective-permute-done.15.refs_2_
  47.6 0.8 %shard_map.51 = (f32[64,3072]{1,0:T(8,128)S(1)}, f32[64,64]{1,0:T(8,128)S(1)}, f32[1536,768]{1,0:T(8,128)S(1)}, f32[1536,768]{1,0:T(8,128)S(1)}, f32[1536,768]{1,0:T(8,128)S(1)}, /*index=5*/f32[1536,768]{1,0:T(8,128)S(1)}) custom-call(f32[64,3072]{1,0:T(8,128)S(1)} %get-tuple-element.167.refs, ...), custom_call_target="tpu_custom_call", output_to_operand_aliasing={{2}: (3, {}), {3}: (4, {}), {4}: (5, {}), {5}: (6, {})} | custom-call | flops 1000000 | bytes 1000000 | tf_op jit(solution)/shard_map/pallas_call | solution.py:64
  48.5 1.2 %collective-permute-done.12.refs_3_ = f32[64,384]{1,0:T(8,128)S(1)} collective-permute-done((f32[64,384]{1,0:T(8,128)S(1)}, f32[64,384]{1,0:T(8,128)S(1)}, u32[]{:S(2)}, u32[]{:S(2)}) %collective-permute-start.12) | collective-permute-done | bytes 98336 | tf_op jit(solution)/shard_map/ppermute | solution.py:651
  49.7 3.7 %collective-permute-done.10.refs_1_ = f32[64,384]{1,0:T(8,128)S(1)} collective-permute-done((f32[64,384]{1,0:T(8,128)S(1)}, f32[64,384]{1,0:T(8,128)S(1)}, u32[]{:S(2)}, u32[]{:S(2)}) %collective-permute-start.10) | collective-permute-done | bytes 98336 | tf_op jit(solution)/shard_map/ppermute | solution.py:651
  53.4 0.0 collective-permute-done.11.refs_2_
  53.4 0.1 shard_map.52
  53.5 2.6 %collective-permute-start.16 = (f32[72,384]{1,0:T(8,128)S(1)}, f32[72,384]{1,0:T(8,128)S(1)}, u32[]{:S(2)}, u32[]{:S(2)}) collective-permute-start(f32[72,384]{1,0:T(8,128)S(1)} %get-tuple-element.195.refs_2_), channel_id=1, source_target_pairs={{0,1},{1,2},{2,3},{3,0},{4,5},{5,6},{6,7},{7,4},{8,9},{9,10},{10,1... | collective-permute-start | bytes 331784 | tf_op jit(solution)/shard_map/ppermute | solution.py:651
  56.1 1.6 %collective-permute-start.17 = (f32[72,384]{1,0:T(8,128)S(1)}, f32[72,384]{1,0:T(8,128)S(1)}, u32[]{:S(2)}, u32[]{:S(2)}) collective-permute-start(f32[72,384]{1,0:T(8,128)S(1)} %get-tuple-element.195.refs_2_), channel_id=1, source_target_pairs={{0,2},{1,3},{2,0},{3,1},{4,6},{5,7},{6,4},{7,5},{8,10},{9,11},{10,... | collective-permute-start | bytes 331784 | tf_op jit(solution)/shard_map/ppermute | solution.py:651
  57.7 0.8 %collective-permute-start.18 = (f32[72,384]{1,0:T(8,128)S(1)}, f32[72,384]{1,0:T(8,128)S(1)}, u32[]{:S(2)}, u32[]{:S(2)}) collective-permute-start(f32[72,384]{1,0:T(8,128)S(1)} %get-tuple-element.195.refs_2_), channel_id=1, source_target_pairs={{0,3},{1,0},{2,1},{3,2},{4,7},{5,4},{6,5},{7,6},{8,11},{9,8},{10,9... | collective-permute-start | bytes 331784 | tf_op jit(solution)/shard_map/ppermute | solution.py:651
  58.5 2.3 %shard_map.53 = (f32[64,64]{1,0:T(8,128)S(1)}, f32[1536,768]{1,0:T(8,128)S(1)}, f32[1536,768]{1,0:T(8,128)S(1)}, f32[1536,768]{1,0:T(8,128)S(1)}, f32[1536,768]{1,0:T(8,128)S(1)}) custom-call(f32[64,64]{1,0:T(8,128)S(1)} %get-tuple-element.126.refs_0_, ...), custom_call_target="tpu_custom_call", output_to_operand_aliasing={{1}: (3, {}), {2}: (4, {}), {3}: (5, {}), {4}: (6, {})} | custom-call | flops 50000000 | bytes 1000000 | tf_op jit(solution)/shard_map/pallas_call | solution.py:64
  60.8 1.4 %shard_map.54 = (bf16[128,3072]{1,0:T(8,128)(2,1)S(1)}, bf16[128,3072]{1,0:T(8,128)(2,1)S(1)}, f32[64,1536]{1,0:T(8,128)S(1)}, bf16[1536,128]{1,0:T(8,128)(2,1)S...) custom-call(f32[64,64]{1,0:T(8,128)S(1)} %get-tuple-element.188.refs, ...), custom_call_target="tpu_custom_call", output_to_operand_aliasing={{4}: (6, {}), {5}: (7, {}), {6}: (8, {}), {7}: (9, {})} | custom-call | flops 1000000 | bytes 1000000 | tf_op jit(solution)/shard_map/pallas_call | solution.py:64
  62.2 4.0 %subtract_near.1 = (f32[1536,768]{1,0:T(8,128)S(1)}, f32[1536,768]{1,0:T(8,128)S(1)}, f32[1536,768]{1,0:T(8,128)S(1)}, f32[1536,768]{1,0:T(8,128)S(1)}) custom-call(bf16[1536,128]{1,0:T(8,128)(2,1)S(1)} %get-tuple-element.196.refs_0_.refs_2_, ...), custom_call_target="tpu_custom_call", output_to_operand_aliasing={{0}: (2, {}), {1}: (3, {}), {2}: (4, {}), {3}: (5, {})} | custom-call | flops 1811939328 | bytes 28311552 | tf_op jit(solution)/shard_map/subtract_near/pallas_call | solution.py:493
  66.2 0.0 collective-permute-done.16.refs_3_
  66.2 0.0 collective-permute-done.17.refs_4_
  66.2 0.0 collective-permute-done.18.refs_5_
  66.2 1.0 %shard_map.55 = (f32[64,1536]{1,0:T(8,128)S(1)}, f32[1536,768]{1,0:T(8,128)S(1)}, f32[1536,768]{1,0:T(8,128)S(1)}, f32[1536,768]{1,0:T(8,128)S(1)}, f32[1536,768]{1,0:T(8,128)S(1)}) custom-call(f32[64,64]{1,0:T(8,128)S(1)} %get-tuple-element.188.refs_0_, ...), custom_call_target="tpu_custom_call", output_to_operand_aliasing={{1}: (6, {}), {2}: (7, {}), {3}: (8, {}), {4}: (9, {})} | custom-call | flops 1000000 | bytes 1000000 | tf_op jit(solution)/shard_map/pallas_call | solution.py:64
  67.2 0.8 %shard_map.56 = (bf16[1536,128]{1,0:T(8,128)(2,1)S(1)}, f32[1536,768]{1,0:T(8,128)S(1)}, f32[1536,768]{1,0:T(8,128)S(1)}, f32[1536,768]{1,0:T(8,128)S(1)}, f32[1536,768]{1,0:T(8,128)S(1)}) custom-call(f32[64,64]{1,0:T(8,128)S(1)} %get-tuple-element.188.refs_0_, ...), custom_call_target="tpu_custom_call", output_to_operand_aliasing={{1}: (6, {}), {2}: (7, {}), {3}: (8, {}), {4}: (9, {})} | custom-call | flops 1000000 | bytes 1000000 | tf_op jit(solution)/shard_map/pallas_call | solution.py:64
  68.0 8.3 %subtract_far.1 = f32[1536,3072]{1,0:T(8,128)} custom-call(bf16[1536,128]{1,0:T(8,128)(2,1)S(1)} %get-tuple-element.211.refs_0_, bf16[128,3072]{1,0:T(8,128)(2,1)S(1)} %get-tuple-element.212.refs_1_, bf16[1536,128]{1,0:T(8,128)(2,1)S(1)} %get-tuple-element.196.refs_0_.refs_2_, bf16[128,3072]{1,0:T(8,128)(2,1)S(1)} %get-tuple-element.197.refs_1_.refs_3_, ...), custom_call_target="tpu_custom_call" | custom-call | flops 3019898880 | bytes 37748736 | tf_op jit(solution)/shard_map/subtract_far/pallas_call | solution.py:621
  (5 shorter events, 0.2 us)
Async XLA Ops:
  0.6 1.0 %copy-start = (f32[1536,64]{0,1:T(8,128)S(1)}, f32[1536,64]{0,1:T(8,128)}, u32[]{:S(2)}) copy-start(f32[1536,64]{0,1:T(8,128)} %param.3) | copy-start | bytes 1179652
  2.1 1.4 %collective-permute-start = (f32[64,128]{1,0:T(8,128)S(1)}, f32[64,128]{1,0:T(8,128)S(1)}, u32[]{:S(2)}, u32[]{:S(2)}) collective-permute-start(f32[64,128]{1,0:T(8,128)S(1)} %get-tuple-element.112.a_ref), channel_id=1, source_target_pairs={{0,4},{4,0},{8,12},{12,8},{16,20},{20,16},{24,28},{28,24},{1,5},{5... | collective-permute-start | bytes 98312 | tf_op jit(solution)/shard_map/ppermute | solution.py:637
  3.6 11.5 %collective-permute-start.1 = (f32[64,896]{1,0:T(8,128)S(1)}, f32[64,896]{1,0:T(8,128)S(1)}, u32[]{:S(2)}, u32[]{:S(2)}) collective-permute-start(f32[64,896]{1,0:T(8,128)S(1)} %get-tuple-element.114), channel_id=1, source_target_pairs={{0,8},{4,12},{8,0},{12,4},{16,24},{20,28},{24,16},{28,20},{1,9},{5... | collective-permute-start | bytes 688136 | tf_op jit(solution)/shard_map/ppermute | solution.py:637
  6.4 8.6 %collective-permute-start.2 = (f32[64,896]{1,0:T(8,128)S(1)}, f32[64,896]{1,0:T(8,128)S(1)}, u32[]{:S(2)}, u32[]{:S(2)}) collective-permute-start(f32[64,896]{1,0:T(8,128)S(1)} %get-tuple-element.115), channel_id=1, source_target_pairs={{0,16},{4,20},{8,24},{12,28},{16,0},{20,4},{24,8},{28,12},{1,17},{... | collective-permute-start | bytes 688136 | tf_op jit(solution)/shard_map/ppermute | solution.py:637
  15.1 11.7 %collective-permute-start.4 = (f32[64,768]{1,0:T(8,128)S(1)}, f32[64,768]{1,0:T(8,128)S(1)}, u32[]{:S(2)}, u32[]{:S(2)}) collective-permute-start(f32[64,768]{1,0:T(8,128)S(1)} %get-tuple-element.129.refs_0_), channel_id=1, source_target_pairs={{0,16},{4,20},{8,24},{12,28},{16,0},{20,4},{24,8},{28,12},{1,17},{... | collective-permute-start | bytes 589832 | tf_op jit(solution)/shard_map/ppermute | solution.py:637
  15.7 11.1 %collective-permute-start.5 = (f32[64,768]{1,0:T(8,128)S(1)}, f32[64,768]{1,0:T(8,128)S(1)}, u32[]{:S(2)}, u32[]{:S(2)}) collective-permute-start(f32[64,768]{1,0:T(8,128)S(1)} %get-tuple-element.130.refs_2_), channel_id=1, source_target_pairs={{0,8},{4,12},{8,0},{12,4},{16,24},{20,28},{24,16},{28,20},{1,9},{5... | collective-permute-start | bytes 589832 | tf_op jit(solution)/shard_map/ppermute | solution.py:637
  16.0 7.5 %collective-permute-start.3 = (f32[64,128]{1,0:T(8,128)S(1)}, f32[64,128]{1,0:T(8,128)S(1)}, u32[]{:S(2)}, u32[]{:S(2)}) collective-permute-start(f32[64,128]{1,0:T(8,128)S(1)} %get-tuple-element.113.refs_0_), channel_id=1, source_target_pairs={{0,24},{4,28},{8,16},{12,20},{16,8},{20,12},{24,0},{28,4},{1,25},{... | collective-permute-start | bytes 98312 | tf_op jit(solution)/shard_map/ppermute | solution.py:637
  26.7 1.8 %collective-permute-start.7 = (f32[64,1536]{1,0:T(8,128)S(1)}, f32[64,1536]{1,0:T(8,128)S(1)}, u32[]{:S(2)}, u32[]{:S(2)}) collective-permute-start(f32[64,1536]{1,0:T(8,128)S(1)} %get-tuple-element.143), channel_id=1, source_target_pairs={{0,4},{4,0},{8,12},{12,8},{16,20},{20,16},{24,28},{28,24},{1,5},{5... | collective-permute-start | bytes 1179656 | tf_op jit(solution)/shard_map/ppermute | solution.py:637
  26.9 2.2 %collective-permute-start.6 = (f32[64,1536]{1,0:T(8,128)S(1)}, f32[64,1536]{1,0:T(8,128)S(1)}, u32[]{:S(2)}, u32[]{:S(2)}) collective-permute-start(f32[64,1536]{1,0:T(8,128)S(1)} %get-tuple-element.141.refs_0_), channel_id=1, source_target_pairs={{0,4},{4,0},{8,12},{12,8},{16,20},{20,16},{24,28},{28,24},{1,5},{5... | collective-permute-start | bytes 1179656 | tf_op jit(solution)/shard_map/ppermute | solution.py:637
  28.6 7.0 %collective-permute-start.8 = (f32[64,768]{1,0:T(8,128)S(1)}, f32[64,768]{1,0:T(8,128)S(1)}, u32[]{:S(2)}, u32[]{:S(2)}) collective-permute-start(f32[64,768]{1,0:T(8,128)S(1)} %get-tuple-element.153.refs_0_), channel_id=1, source_target_pairs={{0,8},{4,12},{8,0},{12,4},{16,24},{20,28},{24,16},{28,20},{1,9},{5... | collective-permute-start | bytes 589832 | tf_op jit(solution)/shard_map/ppermute | solution.py:637
  28.7 6.9 %collective-permute-start.9 = (f32[64,768]{1,0:T(8,128)S(1)}, f32[64,768]{1,0:T(8,128)S(1)}, u32[]{:S(2)}, u32[]{:S(2)}) collective-permute-start(f32[64,768]{1,0:T(8,128)S(1)} %get-tuple-element.154.refs_2_), channel_id=1, source_target_pairs={{0,16},{4,20},{8,24},{12,28},{16,0},{20,4},{24,8},{28,12},{1,17},{... | collective-permute-start | bytes 589832 | tf_op jit(solution)/shard_map/ppermute | solution.py:637
  35.7 6.1 %collective-permute-start.13 = (f32[64,768]{1,0:T(8,128)S(1)}, f32[64,768]{1,0:T(8,128)S(1)}, u32[]{:S(2)}, u32[]{:S(2)}) collective-permute-start(f32[64,768]{1,0:T(8,128)S(1)} %get-tuple-element.168.refs_0_), channel_id=1, source_target_pairs={{0,16},{4,20},{8,24},{12,28},{16,0},{20,4},{24,8},{28,12},{1,17},{... | collective-permute-start | bytes 589832 | tf_op jit(solution)/shard_map/ppermute | solution.py:637
  36.0 5.9 %collective-permute-start.14 = (f32[64,768]{1,0:T(8,128)S(1)}, f32[64,768]{1,0:T(8,128)S(1)}, u32[]{:S(2)}, u32[]{:S(2)}) collective-permute-start(f32[64,768]{1,0:T(8,128)S(1)} %get-tuple-element.169.refs_2_), channel_id=1, source_target_pairs={{0,8},{4,12},{8,0},{12,4},{16,24},{20,28},{24,16},{28,20},{1,9},{5... | collective-permute-start | bytes 589832 | tf_op jit(solution)/shard_map/ppermute | solution.py:637
  42.0 5.7 %collective-permute-start.15 = (f32[64,1536]{1,0:T(8,128)S(1)}, f32[64,1536]{1,0:T(8,128)S(1)}, u32[]{:S(2)}, u32[]{:S(2)}) collective-permute-start(f32[64,1536]{1,0:T(8,128)S(1)} %get-tuple-element.174.refs_1_), channel_id=1, source_target_pairs={{0,4},{4,0},{8,12},{12,8},{16,20},{20,16},{24,28},{28,24},{1,5},{5... | collective-permute-start | bytes 1179656 | tf_op jit(solution)/shard_map/ppermute | solution.py:637
  42.0 7.6 %collective-permute-start.12 = (f32[64,384]{1,0:T(8,128)S(1)}, f32[64,384]{1,0:T(8,128)S(1)}, u32[]{:S(2)}, u32[]{:S(2)}) collective-permute-start(f32[64,384]{1,0:T(8,128)S(1)} %get-tuple-element.166), channel_id=1, source_target_pairs={{0,1},{1,2},{2,3},{3,0},{4,5},{5,6},{6,7},{7,4},{8,9},{9,10},{10,1... | collective-permute-start | bytes 294920 | tf_op jit(solution)/shard_map/ppermute | solution.py:651
  43.7 9.7 %collective-permute-start.10 = (f32[64,384]{1,0:T(8,128)S(1)}, f32[64,384]{1,0:T(8,128)S(1)}, u32[]{:S(2)}, u32[]{:S(2)}) collective-permute-start(f32[64,384]{1,0:T(8,128)S(1)} %get-tuple-element.164), channel_id=1, source_target_pairs={{0,2},{1,3},{2,0},{3,1},{4,6},{5,7},{6,4},{7,5},{8,10},{9,11},{10,... | collective-permute-start | bytes 294920 | tf_op jit(solution)/shard_map/ppermute | solution.py:651
  46.2 7.1 %collective-permute-start.11 = (f32[64,384]{1,0:T(8,128)S(1)}, f32[64,384]{1,0:T(8,128)S(1)}, u32[]{:S(2)}, u32[]{:S(2)}) collective-permute-start(f32[64,384]{1,0:T(8,128)S(1)} %get-tuple-element.165), channel_id=1, source_target_pairs={{0,3},{1,0},{2,1},{3,2},{4,7},{5,4},{6,5},{7,6},{8,11},{9,8},{10,9... | collective-permute-start | bytes 294920 | tf_op jit(solution)/shard_map/ppermute | solution.py:651
  53.5 12.8 %collective-permute-start.16 = (f32[72,384]{1,0:T(8,128)S(1)}, f32[72,384]{1,0:T(8,128)S(1)}, u32[]{:S(2)}, u32[]{:S(2)}) collective-permute-start(f32[72,384]{1,0:T(8,128)S(1)} %get-tuple-element.195.refs_2_), channel_id=1, source_target_pairs={{0,1},{1,2},{2,3},{3,0},{4,5},{5,6},{6,7},{7,4},{8,9},{9,10},{10,1... | collective-permute-start | bytes 331784 | tf_op jit(solution)/shard_map/ppermute | solution.py:651
  56.1 10.2 %collective-permute-start.17 = (f32[72,384]{1,0:T(8,128)S(1)}, f32[72,384]{1,0:T(8,128)S(1)}, u32[]{:S(2)}, u32[]{:S(2)}) collective-permute-start(f32[72,384]{1,0:T(8,128)S(1)} %get-tuple-element.195.refs_2_), channel_id=1, source_target_pairs={{0,2},{1,3},{2,0},{3,1},{4,6},{5,7},{6,4},{7,5},{8,10},{9,11},{10,... | collective-permute-start | bytes 331784 | tf_op jit(solution)/shard_map/ppermute | solution.py:651
  57.7 8.5 %collective-permute-start.18 = (f32[72,384]{1,0:T(8,128)S(1)}, f32[72,384]{1,0:T(8,128)S(1)}, u32[]{:S(2)}, u32[]{:S(2)}) collective-permute-start(f32[72,384]{1,0:T(8,128)S(1)} %get-tuple-element.195.refs_2_), channel_id=1, source_target_pairs={{0,3},{1,0},{2,1},{3,2},{4,7},{5,4},{6,5},{7,6},{8,11},{9,8},{10,9... | collective-permute-start | bytes 331784 | tf_op jit(solution)/shard_map/ppermute | solution.py:651

commit v8 on v7

--- a/solution.py
+++ b/solution.py
@@ -394,7 +394,23 @@
     f_ref[...] = c_ref[...] + d_ref[...]
 
 
-def inner_kernel(kct_ref, held_ref, other_ref, xct_ref, inner_ref):
+def half_product(kct_ref, x_ref, core):
+    half = x_ref.shape[1]
+    start = pl.multiple_of(core * half, half)
+    return lax.dot_general(
+        kct_ref[:, pl.ds(start, half)],
+        x_ref[...],
+        (((1,), (1,)), ((), ())),
+        precision=precise,
+        preferred_element_type=f32,
+    )
+
+
+def inner_own_kernel(kct_ref, held_ref, inner_ref):
+    inner_ref[...] = half_product(kct_ref, held_ref, lax.rem(lax.axis_index("row"), 2))
+
+
+def inner_kernel(kct_ref, held_ref, other_ref, own_ref, xct_ref, inner_ref):
     half = held_ref.shape[1]
     core = lax.rem(lax.axis_index("row"), 2)
 
@@ -408,13 +424,7 @@
         xct_ref[:, :half] = other_ref[...]
         xct_ref[:, half:] = held_ref[...]
 
-    inner_ref[...] = lax.dot_general(
-        kct_ref[...],
-        xct_ref[...],
-        (((1,), (1,)), ((), ())),
-        precision=precise,
-        preferred_element_type=f32,
-    )
+    inner_ref[...] = own_ref[...] + half_product(kct_ref, other_ref, 1 - core)
 
 
 def wide_kernel(
@@ -459,8 +469,8 @@
     rows, span = refs[0].shape
     deep = block_of(rows, 512)
     chunk = block_of(span, 512)
-    if (span // 2) % 128 == 0:
-        chunk = span // 2
+    if span % 256 == 0 and span <= 1024:
+        chunk = span
     for at in range(count):
         a_ref, out_ref = refs[at], refs[total + at]
 
@@ -474,14 +484,10 @@
                 ] - fast(both_parts(left_ref[r : r + deep, :]), right)
 
 
-def near_count(parts):
-    return parts - max(1, parts // 4)
-
-
 def subtract_near(left, right, kept):
     rows, span = kept[0].shape
     parts = len(kept)
-    count = near_count(parts)
+    count = parts
     deep = left.shape[1]
     whole = pl.BlockSpec(memory_space=pltpu.VMEM)
     places = [whole] * count + [pl.BlockSpec(memory_space=pl.ANY)] * (parts - count)
@@ -536,10 +542,11 @@
     out_ref[width:, :] = jnp.concatenate(below, 1)
 
 
-def core_kernel(st_ref, krt_ref, *refs):
-    chunks, out_ref = refs[:-1], refs[-1]
-    width = st_ref.shape[0]
-    beside, _ = packing(width, chunks[0].shape[1])
+def left_kernel(st_ref, krt_ref, *refs):
+    chunks, left_ref = refs[:-1], refs[-1]
+    pieces = len(chunks)
+    width, size = st_ref.shape[0], chunks[0].shape[1]
+    beside, _ = packing(width, size)
     half = core_blocks(width)[1]
     packed = chunks[0][width:, :]
     for ref in chunks[1:]:
@@ -555,19 +562,12 @@
         [jnp.concatenate([near, cross], 1), jnp.concatenate([cross.T, far], 1)], 0
     )
     st = st_ref[...]
+    scaled = [dot(st, ref[:width, :]) for ref in chunks]
     cm = dot(dot(st, inner), st.T)
-    out_ref[...] = dot(cm, krt_ref[...])
-
-
-def left_kernel(st_ref, core_ref, *refs):
-    chunks, left_ref = refs[:-1], refs[-1]
-    pieces = len(chunks)
-    size = chunks[0].shape[1]
-    st = st_ref[...]
     col = lax.axis_index("col")
-    for at, ref in enumerate(chunks):
+    for at in range(pieces):
         start = pl.multiple_of(lax.rem(col + pieces - at, pieces) * size, size)
-        value = dot(st, ref[: st.shape[0], :]) - core_ref[:, pl.ds(start, size)]
+        value = scaled[at] - dot(cm, krt_ref[:, pl.ds(start, size)])
         left_ref[pl.ds(start, size), :] = jnp.concatenate(split(value.T), 1)
 
 
@@ -616,7 +616,7 @@
     whole = pl.BlockSpec(memory_space=pltpu.VMEM)
 
     def kernel(*refs):
-        far_kernel(near_count(parts), *refs)
+        far_kernel(parts, *refs)
 
     return pl.pallas_call(
         kernel,
@@ -740,19 +740,26 @@
         received = []
         if late:
             received = [shift(chunks[at], late + at, col_size) for at in range(pieces - late)]
-            *chunks, resident = across_call(
-                more_kernel, (right,), (), resident, pieces, 0, late, width
-            )
-            received += [shift(chunks[by], by, col_size) for by in range(1, late)]
+            chunks = []
+            for at in range(late - 1, -1, -1):
+                piece, resident = across_call(
+                    more_kernel, (right,), (), resident, pieces, at, 1, width
+                )
+                chunks = [piece] + chunks
+                if at:
+                    received += [shift(piece, at, col_size)]
         summed, resident = small_call(
             join_kernel, shape(width, columns // 2), a, ra, b, rb, carry=resident
         )
+        exchanged = flip(summed, 1, row_size)
+        own, resident = small_call(inner_own_kernel, small, kct, summed, carry=resident)
         xct, inner, resident = small_call(
             inner_kernel,
             (shape(width, columns), small),
             kct,
             summed,
-            flip(summed, 1, row_size),
+            exchanged,
+            own,
             carry=resident,
         )
         tall = packing(width, rows // pieces)[1]
@@ -789,17 +796,8 @@
             carry=resident,
         )
         resident = subtract_near(near_left, xparts, resident)
-        core, resident = small_call(
-            core_kernel, shape(width, rows), st, krt, *whole, carry=resident
-        )
         left, resident = small_call(
-            left_kernel,
-            shape(rows, 2 * width, dtype=bf16),
-            st,
-            core,
-            *whole,
-            mib=12,
-            carry=resident,
+            left_kernel, shape(rows, 2 * width, dtype=bf16), st, krt, *whole, mib=12, carry=resident
         )
         return subtract_far(left, kparts, near_left, xparts, resident), band
 

time: 76.6 us -> 75.1 us (0.980)
  Pallas kernels: 36.6 us -> 35.3 us
    pallas_call x1, Pallas kernels: 8.25 us -> 7.35 us  [subtract_far(): pl.pallas_call(kernel, in_specs=[whole] * (4 + parts), out_specs=pl.Block...]
    pallas_call x2 -> x3, Pallas kernels: 6.93 us -> 6.91 us  [across_call(): pl.pallas_call(body, grid=(count,), in_specs=[fixed(x) for x in operands]...]
where the time goes in v8:
time: 75.1 us; the launch traced here: 75 us
  Pallas kernels  35.3 us (47%)
  starting transfers between devices  22.3 us (30%)
  waiting for transfers between devices  15.4 us (21%)
  between operations  1 us (1%)
  local copies, waits for them, and re-layouts  0.99 us (1%)
    ppermute x13, starting transfers between devices, flip(): return lax.ppermute(value, axis, [(i, i ^ bit) for i in range(size)])  11.7 us
    ppermute x13, waiting for transfers between devices, flip(): return lax.ppermute(value, axis, [(i, i ^ bit) for i in range(size)])  10.6 us
    ppermute x6, starting transfers between devices, shift(): lax.ppermute(piece, 'col', [(i, (i + by) % size) for i in range(size)])  10.6 us
    pallas_call x14, Pallas kernels, small_call(): pl.pallas_call(body, out_shape=out, compiler_params=params(mib), cost_est...  9.59 us
    pallas_call x1, Pallas kernels, subtract_far(): pl.pallas_call(kernel, in_specs=[whole] * (4 + parts), out_specs=pl.Block...  7.35 us
    pallas_call x1, Pallas kernels, product_down(): pl.pallas_call(down_kernel, in_specs=[whole, whole, pl.BlockSpec(memory_s...  7.04 us
    pallas_call x3, Pallas kernels, across_call(): pl.pallas_call(body, grid=(count,), in_specs=[fixed(x) for x in operands]...  6.91 us
    ppermute x6, waiting for transfers between devices, shift(): lax.ppermute(piece, 'col', [(i, (i + by) % size) for i in range(size)])  4.73 us
  transfers between devices with their start and end apart: 19, of which 9 were waited for; matrix products, arithmetic and copies ran while one was open for 0% of the time, Pallas kernels for 34%

profile of v8, /device:TPU:0, one launch (start us, length us, event | category | flops | bytes accessed | tf_op | source)
XLA Modules:
  0.0 75.0 jit_solution(13322717165724782142)
XLA Ops:
  0.6 0.0 copy-start
  0.6 1.0 %copy-done = f32[1536,64]{0,1:T(8,128)S(1)} copy-done((f32[1536,64]{0,1:T(8,128)S(1)}, f32[1536,64]{0,1:T(8,128)}, u32[]{:S(2)}) %copy-start) | copy-done | bytes 393240
  1.6 0.5 shard_map.41
  2.1 0.6 collective-permute-start
  2.7 0.9 %collective-permute-done.b_ref = f32[64,128]{1,0:T(8,128)S(1)} collective-permute-done((f32[64,128]{1,0:T(8,128)S(1)}, f32[64,128]{1,0:T(8,128)S(1)}, u32[]{:S(2)}, u32[]{:S(2)}) %collective-permute-start) | collective-permute-done | bytes 32800 | tf_op jit(solution)/shard_map/ppermute | solution.py:637
  3.6 2.9 %collective-permute-start.1 = (f32[64,896]{1,0:T(8,128)S(1)}, f32[64,896]{1,0:T(8,128)S(1)}, u32[]{:S(2)}, u32[]{:S(2)}) collective-permute-start(f32[64,896]{1,0:T(8,128)S(1)} %get-tuple-element.118), channel_id=1, source_target_pairs={{0,8},{4,12},{8,0},{12,4},{16,24},{20,28},{24,16},{28,20},{1,9},{5... | collective-permute-start | bytes 688136 | tf_op jit(solution)/shard_map/ppermute | solution.py:637
  6.4 1.5 %collective-permute-start.2 = (f32[64,896]{1,0:T(8,128)S(1)}, f32[64,896]{1,0:T(8,128)S(1)}, u32[]{:S(2)}, u32[]{:S(2)}) collective-permute-start(f32[64,896]{1,0:T(8,128)S(1)} %get-tuple-element.119), channel_id=1, source_target_pairs={{0,16},{4,20},{8,24},{12,28},{16,0},{20,4},{24,8},{28,12},{1,17},{... | collective-permute-start | bytes 688136 | tf_op jit(solution)/shard_map/ppermute | solution.py:637
  8.0 7.0 %product_down.1 = (f32[64,1536]{1,0:T(8,128)S(1)}, f32[64,1536]{1,0:T(8,128)S(1)}, f32[1536,768]{1,0:T(8,128)S(1)}, f32[1536,768]{1,0:T(8,128)S(1)}, f32[1536,768]{1,0:T(8,128)S(1)}, /*index=5*/f32[1536,768]{1,0:T(8,128)S(1)}) custom-call(f32[64,768]{1,0:T(8,128)S(1)} %get-tuple-element.120.first_ref.refs_0_.refs_3_, ...), custom_call_target="tpu_custom_call" | custom-call | flops 2415919104 | bytes 18874368 | tf_op jit(solution)/shard_map/product_down/pallas_call | solution.py:219
  15.0 0.0 collective-permute-done.1.refs_2_.refs_1_
  15.0 0.0 collective-permute-done.2.refs_3_.refs_2_
  15.0 0.1 shard_map.43
  15.1 0.6 collective-permute-start.4
  15.7 0.3 collective-permute-start.5
  16.0 2.7 %collective-permute-start.3 = (f32[64,128]{1,0:T(8,128)S(1)}, f32[64,128]{1,0:T(8,128)S(1)}, u32[]{:S(2)}, u32[]{:S(2)}) collective-permute-start(f32[64,128]{1,0:T(8,128)S(1)} %get-tuple-element.117.refs_0_), channel_id=1, source_target_pairs={{0,24},{4,28},{8,16},{12,20},{16,8},{20,12},{24,0},{28,4},{1,25},{... | collective-permute-start | bytes 98312 | tf_op jit(solution)/shard_map/ppermute | solution.py:637
  18.7 4.8 %collective-permute-done.3.refs_3_ = f32[64,128]{1,0:T(8,128)S(1)} collective-permute-done((f32[64,128]{1,0:T(8,128)S(1)}, f32[64,128]{1,0:T(8,128)S(1)}, u32[]{:S(2)}, u32[]{:S(2)}) %collective-permute-start.3) | collective-permute-done | bytes 32800 | tf_op jit(solution)/shard_map/ppermute | solution.py:637
  23.5 2.7 %shard_map.44 = (f32[64,64]{1,0:T(8,128)}, f32[64,64]{1,0:T(8,128)S(1)}, f32[64,64]{1,0:T(8,128)S(1)}, f32[64,64]{1,0:T(8,128)S(1)}, f32[1536,768]{1,0:T(8,128)S...) custom-call(f32[64,128]{1,0:T(8,128)S(1)} %get-tuple-element.117.ref, ...), custom_call_target="tpu_custom_call", output_to_operand_aliasing={{4}: (4, {}), {5}: (5, {}), {6}: (6, {}), {7}: (7, {})} | custom-call | flops 50000000 | bytes 1000000 | tf_op jit(solution)/shard_map/pallas_call | solution.py:64
  26.2 0.6 fix_down.1
  26.7 0.1 collective-permute-start.7
  26.8 0.0 collective-permute-done.4.refs_1_
  26.8 0.0 collective-permute-done.5.refs_3_
  26.9 0.5 collective-permute-start.6
  27.4 1.1 %collective-permute-done.7.refs_1_ = f32[64,1536]{1,0:T(8,128)S(1)} collective-permute-done((f32[64,1536]{1,0:T(8,128)S(1)}, f32[64,1536]{1,0:T(8,128)S(1)}, u32[]{:S(2)}, u32[]{:S(2)}) %collective-permute-start.7) | collective-permute-done | bytes 393248 | tf_op jit(solution)/shard_map/ppermute | solution.py:637
  28.6 0.1 collective-permute-start.8
  28.7 0.4 collective-permute-start.9
  29.1 0.0 collective-permute-done.6.refs_1_
  29.1 3.9 %shard_map.47 = (f32[64,3072]{1,0:T(8,128)S(1)}, bf16[3072,128]{1,0:T(8,128)(2,1)S(1)}, f32[64,384]{1,0:T(8,128)S(1)}, f32[64,384]{1,0:T(8,128)S(1)}, f32[1536,7...) custom-call(f32[64,1536]{1,0:T(8,128)S(1)} %get-tuple-element.145.re, ...), custom_call_target="tpu_custom_call", output_to_operand_aliasing={{4}: (3, {}), {5}: (4, {}), {6}: (5, {}), {7}: (6, {})} | custom-call | flops 1207959552 | bytes 9437184 | tf_op jit(solution)/shard_map/pallas_call | solution.py:355
  33.0 2.6 %collective-permute-done.8.refs_1_ = f32[64,768]{1,0:T(8,128)S(1)} collective-permute-done((f32[64,768]{1,0:T(8,128)S(1)}, f32[64,768]{1,0:T(8,128)S(1)}, u32[]{:S(2)}, u32[]{:S(2)}) %collective-permute-start.8) | collective-permute-done | bytes 196640 | tf_op jit(solution)/shard_map/ppermute | solution.py:637
  35.6 0.1 collective-permute-done.9.refs_3_
  35.7 0.4 collective-permute-start.13
  36.0 1.7 %collective-permute-start.14 = (f32[64,768]{1,0:T(8,128)S(1)}, f32[64,768]{1,0:T(8,128)S(1)}, u32[]{:S(2)}, u32[]{:S(2)}) collective-permute-start(f32[64,768]{1,0:T(8,128)S(1)} %get-tuple-element.177.refs_2_), channel_id=1, source_target_pairs={{0,8},{4,12},{8,0},{12,4},{16,24},{20,28},{24,16},{28,20},{1,9},{5... | collective-permute-start | bytes 589832 | tf_op jit(solution)/shard_map/ppermute | solution.py:637
  37.7 1.5 %shard_map.49 = (f32[64,384]{1,0:T(8,128)S(1)}, f32[1536,768]{1,0:T(8,128)S(1)}, f32[1536,768]{1,0:T(8,128)S(1)}, f32[1536,768]{1,0:T(8,128)S(1)}, f32[1536,768]{1,0:T(8,128)S(1)}) custom-call(bf16[3072,128]{1,0:T(8,128)(2,1)S(1)} %get-tuple-element.156.refs_0_, ...), custom_call_target="tpu_custom_call", output_to_operand_aliasing={{1}: (1, {}), {2}: (2, {}), {3}: (3, {}), {4}: (4, {})} | custom-call | flops 603979776 | bytes 4718592 | tf_op jit(solution)/shard_map/pallas_call | solution.py:355
  39.2 1.5 %shard_map.50 = (f32[64,384]{1,0:T(8,128)S(1)}, f32[1536,768]{1,0:T(8,128)S(1)}, f32[1536,768]{1,0:T(8,128)S(1)}, f32[1536,768]{1,0:T(8,128)S(1)}, f32[1536,768]{1,0:T(8,128)S(1)}) custom-call(bf16[3072,128]{1,0:T(8,128)(2,1)S(1)} %get-tuple-element.156.refs_0_, ...), custom_call_target="tpu_custom_call", output_to_operand_aliasing={{1}: (1, {}), {2}: (2, {}), {3}: (3, {}), {4}: (4, {})} | custom-call | flops 603979776 | bytes 4718592 | tf_op jit(solution)/shard_map/pallas_call | solution.py:355
  40.7 1.1 %collective-permute-done.13.refs_1_ = f32[64,768]{1,0:T(8,128)S(1)} collective-permute-done((f32[64,768]{1,0:T(8,128)S(1)}, f32[64,768]{1,0:T(8,128)S(1)}, u32[]{:S(2)}, u32[]{:S(2)}) %collective-permute-start.13) | collective-permute-done | bytes 196640 | tf_op jit(solution)/shard_map/ppermute | solution.py:637
  41.8 0.1 collective-permute-done.14.refs_3_
  42.0 0.1 collective-permute-start.15
  42.0 1.6 %collective-permute-start.12 = (f32[64,384]{1,0:T(8,128)S(1)}, f32[64,384]{1,0:T(8,128)S(1)}, u32[]{:S(2)}, u32[]{:S(2)}) collective-permute-start(f32[64,384]{1,0:T(8,128)S(1)} %get-tuple-element.174), channel_id=1, source_target_pairs={{0,1},{1,2},{2,3},{3,0},{4,5},{5,6},{6,7},{7,4},{8,9},{9,10},{10,1... | collective-permute-start | bytes 294920 | tf_op jit(solution)/shard_map/ppermute | solution.py:651
  43.7 2.6 %collective-permute-start.10 = (f32[64,384]{1,0:T(8,128)S(1)}, f32[64,384]{1,0:T(8,128)S(1)}, u32[]{:S(2)}, u32[]{:S(2)}) collective-permute-start(f32[64,384]{1,0:T(8,128)S(1)} %get-tuple-element.172), channel_id=1, source_target_pairs={{0,2},{1,3},{2,0},{3,1},{4,6},{5,7},{6,4},{7,5},{8,10},{9,11},{10,... | collective-permute-start | bytes 294920 | tf_op jit(solution)/shard_map/ppermute | solution.py:651
  46.2 1.4 %collective-permute-start.11 = (f32[64,384]{1,0:T(8,128)S(1)}, f32[64,384]{1,0:T(8,128)S(1)}, u32[]{:S(2)}, u32[]{:S(2)}) collective-permute-start(f32[64,384]{1,0:T(8,128)S(1)} %get-tuple-element.173), channel_id=1, source_target_pairs={{0,3},{1,0},{2,1},{3,2},{4,7},{5,4},{6,5},{7,6},{8,11},{9,8},{10,9... | collective-permute-start | bytes 294920 | tf_op jit(solution)/shard_map/ppermute | solution.py:651
  47.6 0.5 shard_map.52
  48.1 0.0 collective-permute-done.15.refs_2_
  48.1 0.5 shard_map.53
  48.6 1.0 %collective-permute-done.12.refs_3_ = f32[64,384]{1,0:T(8,128)S(1)} collective-permute-done((f32[64,384]{1,0:T(8,128)S(1)}, f32[64,384]{1,0:T(8,128)S(1)}, u32[]{:S(2)}, u32[]{:S(2)}) %collective-permute-start.12) | collective-permute-done | bytes 98336 | tf_op jit(solution)/shard_map/ppermute | solution.py:651
  49.7 3.7 %collective-permute-done.10.refs_1_ = f32[64,384]{1,0:T(8,128)S(1)} collective-permute-done((f32[64,384]{1,0:T(8,128)S(1)}, f32[64,384]{1,0:T(8,128)S(1)}, u32[]{:S(2)}, u32[]{:S(2)}) %collective-permute-start.10) | collective-permute-done | bytes 98336 | tf_op jit(solution)/shard_map/ppermute | solution.py:651
  53.4 0.0 collective-permute-done.11.refs_2_
  53.4 0.1 shard_map.54
  53.5 2.6 %collective-permute-start.16 = (f32[72,384]{1,0:T(8,128)S(1)}, f32[72,384]{1,0:T(8,128)S(1)}, u32[]{:S(2)}, u32[]{:S(2)}) collective-permute-start(f32[72,384]{1,0:T(8,128)S(1)} %get-tuple-element.208.refs_2_), channel_id=1, source_target_pairs={{0,1},{1,2},{2,3},{3,0},{4,5},{5,6},{6,7},{7,4},{8,9},{9,10},{10,1... | collective-permute-start | bytes 331784 | tf_op jit(solution)/shard_map/ppermute | solution.py:651
  56.1 1.6 %collective-permute-start.17 = (f32[72,384]{1,0:T(8,128)S(1)}, f32[72,384]{1,0:T(8,128)S(1)}, u32[]{:S(2)}, u32[]{:S(2)}) collective-permute-start(f32[72,384]{1,0:T(8,128)S(1)} %get-tuple-element.208.refs_2_), channel_id=1, source_target_pairs={{0,2},{1,3},{2,0},{3,1},{4,6},{5,7},{6,4},{7,5},{8,10},{9,11},{10,... | collective-permute-start | bytes 331784 | tf_op jit(solution)/shard_map/ppermute | solution.py:651
  57.7 0.8 %collective-permute-start.18 = (f32[72,384]{1,0:T(8,128)S(1)}, f32[72,384]{1,0:T(8,128)S(1)}, u32[]{:S(2)}, u32[]{:S(2)}) collective-permute-start(f32[72,384]{1,0:T(8,128)S(1)} %get-tuple-element.208.refs_2_), channel_id=1, source_target_pairs={{0,3},{1,0},{2,1},{3,2},{4,7},{5,4},{6,5},{7,6},{8,11},{9,8},{10,9... | collective-permute-start | bytes 331784 | tf_op jit(solution)/shard_map/ppermute | solution.py:651
  58.5 2.3 %shard_map.55 = (f32[64,64]{1,0:T(8,128)S(1)}, f32[1536,768]{1,0:T(8,128)S(1)}, f32[1536,768]{1,0:T(8,128)S(1)}, f32[1536,768]{1,0:T(8,128)S(1)}, f32[1536,768]{1,0:T(8,128)S(1)}) custom-call(f32[64,64]{1,0:T(8,128)S(1)} %get-tuple-element.130.refs_0_, ...), custom_call_target="tpu_custom_call", output_to_operand_aliasing={{1}: (3, {}), {2}: (4, {}), {3}: (5, {}), {4}: (6, {})} | custom-call | flops 50000000 | bytes 1000000 | tf_op jit(solution)/shard_map/pallas_call | solution.py:64
  60.8 1.3 %shard_map.56 = (bf16[128,3072]{1,0:T(8,128)(2,1)S(1)}, bf16[128,3072]{1,0:T(8,128)(2,1)S(1)}, f32[64,1536]{1,0:T(8,128)S(1)}, bf16[1536,128]{1,0:T(8,128)(2,1)S...) custom-call(f32[64,64]{1,0:T(8,128)S(1)} %get-tuple-element.201.refs, ...), custom_call_target="tpu_custom_call", output_to_operand_aliasing={{4}: (6, {}), {5}: (7, {}), {6}: (8, {}), {7}: (9, {})} | custom-call | flops 1000000 | bytes 1000000 | tf_op jit(solution)/shard_map/pallas_call | solution.py:64
  62.0 3.8 %subtract_near.1 = (f32[1536,768]{1,0:T(8,128)S(1)}, f32[1536,768]{1,0:T(8,128)S(1)}, f32[1536,768]{1,0:T(8,128)S(1)}, f32[1536,768]{1,0:T(8,128)S(1)}) custom-call(bf16[1536,128]{1,0:T(8,128)(2,1)S(1)} %get-tuple-element.209.refs_0_.refs_2_, ...), custom_call_target="tpu_custom_call", output_to_operand_aliasing={{0}: (2, {}), {1}: (3, {}), {2}: (4, {}), {3}: (5, {})} | custom-call | flops 2415919104 | bytes 37748736 | tf_op jit(solution)/shard_map/subtract_near/pallas_call | solution.py:499
  65.9 0.0 collective-permute-done.16.refs_3_
  65.9 0.0 collective-permute-done.17.refs_4_
  65.9 0.0 collective-permute-done.18.refs_5_
  65.9 1.6 %shard_map.57 = (bf16[1536,128]{1,0:T(8,128)(2,1)S(1)}, f32[1536,768]{1,0:T(8,128)S(1)}, f32[1536,768]{1,0:T(8,128)S(1)}, f32[1536,768]{1,0:T(8,128)S(1)}, f32[1536,768]{1,0:T(8,128)S(1)}) custom-call(f32[64,64]{1,0:T(8,128)S(1)} %get-tuple-element.201.refs_0_, ...), custom_call_target="tpu_custom_call", output_to_operand_aliasing={{1}: (6, {}), {2}: (7, {}), {3}: (8, {}), {4}: (9, {})} | custom-call | flops 1000000 | bytes 1000000 | tf_op jit(solution)/shard_map/pallas_call | solution.py:64
  67.4 7.3 %subtract_far.1 = f32[1536,3072]{1,0:T(8,128)} custom-call(bf16[1536,128]{1,0:T(8,128)(2,1)S(1)} %get-tuple-element.219.refs_0_, bf16[128,3072]{1,0:T(8,128)(2,1)S(1)} %get-tuple-element.220.refs_1_, bf16[1536,128]{1,0:T(8,128)(2,1)S(1)} %get-tuple-element.209.refs_0_.refs_2_, bf16[128,3072]{1,0:T(8,128)(2,1)S(1)} %get-tuple-element.210.refs_1_.refs_3_, ...), custom_call_target="tpu_custom_call" | custom-call | flops 3019898880 | bytes 37748736 | tf_op jit(solution)/shard_map/subtract_far/pallas_call | solution.py:621
  (5 shorter events, 0.2 us)
Async XLA Ops:
  0.6 1.0 %copy-start = (f32[1536,64]{0,1:T(8,128)S(1)}, f32[1536,64]{0,1:T(8,128)}, u32[]{:S(2)}) copy-start(f32[1536,64]{0,1:T(8,128)} %param.3) | copy-start | bytes 1179652
  2.1 1.4 %collective-permute-start = (f32[64,128]{1,0:T(8,128)S(1)}, f32[64,128]{1,0:T(8,128)S(1)}, u32[]{:S(2)}, u32[]{:S(2)}) collective-permute-start(f32[64,128]{1,0:T(8,128)S(1)} %get-tuple-element.116.a_ref), channel_id=1, source_target_pairs={{0,4},{4,0},{8,12},{12,8},{16,20},{20,16},{24,28},{28,24},{1,5},{5... | collective-permute-start | bytes 98312 | tf_op jit(solution)/shard_map/ppermute | solution.py:637
  3.6 11.5 %collective-permute-start.1 = (f32[64,896]{1,0:T(8,128)S(1)}, f32[64,896]{1,0:T(8,128)S(1)}, u32[]{:S(2)}, u32[]{:S(2)}) collective-permute-start(f32[64,896]{1,0:T(8,128)S(1)} %get-tuple-element.118), channel_id=1, source_target_pairs={{0,8},{4,12},{8,0},{12,4},{16,24},{20,28},{24,16},{28,20},{1,9},{5... | collective-permute-start | bytes 688136 | tf_op jit(solution)/shard_map/ppermute | solution.py:637
  6.4 8.6 %collective-permute-start.2 = (f32[64,896]{1,0:T(8,128)S(1)}, f32[64,896]{1,0:T(8,128)S(1)}, u32[]{:S(2)}, u32[]{:S(2)}) collective-permute-start(f32[64,896]{1,0:T(8,128)S(1)} %get-tuple-element.119), channel_id=1, source_target_pairs={{0,16},{4,20},{8,24},{12,28},{16,0},{20,4},{24,8},{28,12},{1,17},{... | collective-permute-start | bytes 688136 | tf_op jit(solution)/shard_map/ppermute | solution.py:637
  15.1 11.7 %collective-permute-start.4 = (f32[64,768]{1,0:T(8,128)S(1)}, f32[64,768]{1,0:T(8,128)S(1)}, u32[]{:S(2)}, u32[]{:S(2)}) collective-permute-start(f32[64,768]{1,0:T(8,128)S(1)} %get-tuple-element.133.refs_0_), channel_id=1, source_target_pairs={{0,16},{4,20},{8,24},{12,28},{16,0},{20,4},{24,8},{28,12},{1,17},{... | collective-permute-start | bytes 589832 | tf_op jit(solution)/shard_map/ppermute | solution.py:637
  15.7 11.1 %collective-permute-start.5 = (f32[64,768]{1,0:T(8,128)S(1)}, f32[64,768]{1,0:T(8,128)S(1)}, u32[]{:S(2)}, u32[]{:S(2)}) collective-permute-start(f32[64,768]{1,0:T(8,128)S(1)} %get-tuple-element.134.refs_2_), channel_id=1, source_target_pairs={{0,8},{4,12},{8,0},{12,4},{16,24},{20,28},{24,16},{28,20},{1,9},{5... | collective-permute-start | bytes 589832 | tf_op jit(solution)/shard_map/ppermute | solution.py:637
  16.0 7.5 %collective-permute-start.3 = (f32[64,128]{1,0:T(8,128)S(1)}, f32[64,128]{1,0:T(8,128)S(1)}, u32[]{:S(2)}, u32[]{:S(2)}) collective-permute-start(f32[64,128]{1,0:T(8,128)S(1)} %get-tuple-element.117.refs_0_), channel_id=1, source_target_pairs={{0,24},{4,28},{8,16},{12,20},{16,8},{20,12},{24,0},{28,4},{1,25},{... | collective-permute-start | bytes 98312 | tf_op jit(solution)/shard_map/ppermute | solution.py:637
  26.7 1.8 %collective-permute-start.7 = (f32[64,1536]{1,0:T(8,128)S(1)}, f32[64,1536]{1,0:T(8,128)S(1)}, u32[]{:S(2)}, u32[]{:S(2)}) collective-permute-start(f32[64,1536]{1,0:T(8,128)S(1)} %get-tuple-element.147), channel_id=1, source_target_pairs={{0,4},{4,0},{8,12},{12,8},{16,20},{20,16},{24,28},{28,24},{1,5},{5... | collective-permute-start | bytes 1179656 | tf_op jit(solution)/shard_map/ppermute | solution.py:637
  26.9 2.2 %collective-permute-start.6 = (f32[64,1536]{1,0:T(8,128)S(1)}, f32[64,1536]{1,0:T(8,128)S(1)}, u32[]{:S(2)}, u32[]{:S(2)}) collective-permute-start(f32[64,1536]{1,0:T(8,128)S(1)} %get-tuple-element.145.refs_0_), channel_id=1, source_target_pairs={{0,4},{4,0},{8,12},{12,8},{16,20},{20,16},{24,28},{28,24},{1,5},{5... | collective-permute-start | bytes 1179656 | tf_op jit(solution)/shard_map/ppermute | solution.py:637
  28.6 7.0 %collective-permute-start.8 = (f32[64,768]{1,0:T(8,128)S(1)}, f32[64,768]{1,0:T(8,128)S(1)}, u32[]{:S(2)}, u32[]{:S(2)}) collective-permute-start(f32[64,768]{1,0:T(8,128)S(1)} %get-tuple-element.157.refs_0_), channel_id=1, source_target_pairs={{0,8},{4,12},{8,0},{12,4},{16,24},{20,28},{24,16},{28,20},{1,9},{5... | collective-permute-start | bytes 589832 | tf_op jit(solution)/shard_map/ppermute | solution.py:637
  28.7 6.9 %collective-permute-start.9 = (f32[64,768]{1,0:T(8,128)S(1)}, f32[64,768]{1,0:T(8,128)S(1)}, u32[]{:S(2)}, u32[]{:S(2)}) collective-permute-start(f32[64,768]{1,0:T(8,128)S(1)} %get-tuple-element.158.refs_2_), channel_id=1, source_target_pairs={{0,16},{4,20},{8,24},{12,28},{16,0},{20,4},{24,8},{28,12},{1,17},{... | collective-permute-start | bytes 589832 | tf_op jit(solution)/shard_map/ppermute | solution.py:637
  35.7 6.1 %collective-permute-start.13 = (f32[64,768]{1,0:T(8,128)S(1)}, f32[64,768]{1,0:T(8,128)S(1)}, u32[]{:S(2)}, u32[]{:S(2)}) collective-permute-start(f32[64,768]{1,0:T(8,128)S(1)} %get-tuple-element.176.refs_0_), channel_id=1, source_target_pairs={{0,16},{4,20},{8,24},{12,28},{16,0},{20,4},{24,8},{28,12},{1,17},{... | collective-permute-start | bytes 589832 | tf_op jit(solution)/shard_map/ppermute | solution.py:637
  36.0 5.9 %collective-permute-start.14 = (f32[64,768]{1,0:T(8,128)S(1)}, f32[64,768]{1,0:T(8,128)S(1)}, u32[]{:S(2)}, u32[]{:S(2)}) collective-permute-start(f32[64,768]{1,0:T(8,128)S(1)} %get-tuple-element.177.refs_2_), channel_id=1, source_target_pairs={{0,8},{4,12},{8,0},{12,4},{16,24},{20,28},{24,16},{28,20},{1,9},{5... | collective-permute-start | bytes 589832 | tf_op jit(solution)/shard_map/ppermute | solution.py:637
  42.0 6.1 %collective-permute-start.15 = (f32[64,1536]{1,0:T(8,128)S(1)}, f32[64,1536]{1,0:T(8,128)S(1)}, u32[]{:S(2)}, u32[]{:S(2)}) collective-permute-start(f32[64,1536]{1,0:T(8,128)S(1)} %get-tuple-element.182.refs_1_), channel_id=1, source_target_pairs={{0,4},{4,0},{8,12},{12,8},{16,20},{20,16},{24,28},{28,24},{1,5},{5... | collective-permute-start | bytes 1179656 | tf_op jit(solution)/shard_map/ppermute | solution.py:637
  42.0 7.6 %collective-permute-start.12 = (f32[64,384]{1,0:T(8,128)S(1)}, f32[64,384]{1,0:T(8,128)S(1)}, u32[]{:S(2)}, u32[]{:S(2)}) collective-permute-start(f32[64,384]{1,0:T(8,128)S(1)} %get-tuple-element.174), channel_id=1, source_target_pairs={{0,1},{1,2},{2,3},{3,0},{4,5},{5,6},{6,7},{7,4},{8,9},{9,10},{10,1... | collective-permute-start | bytes 294920 | tf_op jit(solution)/shard_map/ppermute | solution.py:651
  43.7 9.7 %collective-permute-start.10 = (f32[64,384]{1,0:T(8,128)S(1)}, f32[64,384]{1,0:T(8,128)S(1)}, u32[]{:S(2)}, u32[]{:S(2)}) collective-permute-start(f32[64,384]{1,0:T(8,128)S(1)} %get-tuple-element.172), channel_id=1, source_target_pairs={{0,2},{1,3},{2,0},{3,1},{4,6},{5,7},{6,4},{7,5},{8,10},{9,11},{10,... | collective-permute-start | bytes 294920 | tf_op jit(solution)/shard_map/ppermute | solution.py:651
  46.2 7.1 %collective-permute-start.11 = (f32[64,384]{1,0:T(8,128)S(1)}, f32[64,384]{1,0:T(8,128)S(1)}, u32[]{:S(2)}, u32[]{:S(2)}) collective-permute-start(f32[64,384]{1,0:T(8,128)S(1)} %get-tuple-element.173), channel_id=1, source_target_pairs={{0,3},{1,0},{2,1},{3,2},{4,7},{5,4},{6,5},{7,6},{8,11},{9,8},{10,9... | collective-permute-start | bytes 294920 | tf_op jit(solution)/shard_map/ppermute | solution.py:651
  53.5 12.4 %collective-permute-start.16 = (f32[72,384]{1,0:T(8,128)S(1)}, f32[72,384]{1,0:T(8,128)S(1)}, u32[]{:S(2)}, u32[]{:S(2)}) collective-permute-start(f32[72,384]{1,0:T(8,128)S(1)} %get-tuple-element.208.refs_2_), channel_id=1, source_target_pairs={{0,1},{1,2},{2,3},{3,0},{4,5},{5,6},{6,7},{7,4},{8,9},{9,10},{10,1... | collective-permute-start | bytes 331784 | tf_op jit(solution)/shard_map/ppermute | solution.py:651
  56.1 9.8 %collective-permute-start.17 = (f32[72,384]{1,0:T(8,128)S(1)}, f32[72,384]{1,0:T(8,128)S(1)}, u32[]{:S(2)}, u32[]{:S(2)}) collective-permute-start(f32[72,384]{1,0:T(8,128)S(1)} %get-tuple-element.208.refs_2_), channel_id=1, source_target_pairs={{0,2},{1,3},{2,0},{3,1},{4,6},{5,7},{6,4},{7,5},{8,10},{9,11},{10,... | collective-permute-start | bytes 331784 | tf_op jit(solution)/shard_map/ppermute | solution.py:651
  57.7 8.2 %collective-permute-start.18 = (f32[72,384]{1,0:T(8,128)S(1)}, f32[72,384]{1,0:T(8,128)S(1)}, u32[]{:S(2)}, u32[]{:S(2)}) collective-permute-start(f32[72,384]{1,0:T(8,128)S(1)} %get-tuple-element.208.refs_2_), channel_id=1, source_target_pairs={{0,3},{1,0},{2,1},{3,2},{4,7},{5,4},{6,5},{7,6},{8,11},{9,8},{10,9... | collective-permute-start | bytes 331784 | tf_op jit(solution)/shard_map/ppermute | solution.py:651

commit v9 on v8

--- a/solution.py
+++ b/solution.py
@@ -40,6 +40,10 @@
     while size % wanted:
         wanted //= 2
     return wanted
+
+
+def parts_of(columns):
+    return 2 if columns % 512 else 4
 
 
 def small_call(kernel, out, *operands, carry=(), flops=1_000_000, moved=1_000_000, mib=8):
@@ -69,9 +73,17 @@
     return result
 
 
-def open_kernel(turned_ref, first_ref, second_ref, packed_ref):
+def open_kernel(
+    panel_ref, a_ref, first_ref, second_ref, packed_ref, part_ref, turned_ref, sems
+):
     width = turned_ref.shape[0]
     half = first_ref.shape[1]
+    span = part_ref.shape[1]
+    panel_copy = pltpu.make_async_copy(panel_ref, turned_ref, sems.at[0])
+    part_copy = pltpu.make_async_copy(a_ref.at[:, pl.ds(0, span)], part_ref, sems.at[1])
+    panel_copy.start()
+    part_copy.start()
+    panel_copy.wait()
     turned = turned_ref[...]
     first_ref[...] = turned[:, :half]
     second_ref[...] = turned[:, half:]
@@ -80,6 +92,28 @@
     )
     head = jnp.where(lax.axis_index("row") == 0, turned[:, : 2 * width].T[:width], 0.0)
     packed_ref[...] = jnp.concatenate([gram, head], 1)
+    part_copy.wait()
+
+
+def open_panel(turned, a):
+    width, rows = turned.shape
+    whole = pl.BlockSpec(memory_space=pltpu.VMEM)
+    remote = pl.BlockSpec(memory_space=pltpu.HBM)
+    span = a.shape[1] // parts_of(a.shape[1])
+    half = shape(width, rows // 2)
+    return pl.pallas_call(
+        open_kernel,
+        in_specs=[remote, remote],
+        out_specs=(whole,) * 4,
+        out_shape=(half, half, shape(width, 2 * width), shape(rows, span)),
+        scratch_shapes=[pltpu.VMEM((width, rows), f32), pltpu.SemaphoreType.DMA((2,))],
+        compiler_params=params(12),
+        cost_estimate=cost(100_000_000, 4 * rows * span),
+        name="open",
+    )(
+        pltpu.with_memory_space_constraint(turned, pltpu.HBM),
+        pltpu.with_memory_space_constraint(a, pltpu.HBM),
+    )
 
 
 def add_cores_kernel(first_ref, second_ref, a_ref, b_ref, x_ref, y_ref, sum_ref):
@@ -173,20 +207,17 @@
     out_ref[...] = -dot(jnp.concatenate(tiles, 0), inverse_ref[...])
 
 
-def parts_of(columns):
-    return 2 if columns % 512 else 4
-
-
-def down_kernel(first_ref, second_ref, a_ref, low_ref, high_ref, *refs):
-    kept, sems = refs[:-1], refs[-1]
-    width = low_ref.shape[0]
-    span = kept[0].shape[1]
-    count = sems.shape[0] // len(kept)
-    size = span // count
+def down_kernel(begin, first_ref, second_ref, a_ref, given, out_ref, kept, sems):
+    width = out_ref.shape[0]
+    refs = list(given) + list(kept)
+    span = refs[0].shape[1]
+    size = block_of(span, 256)
+    count = span // size
 
     def load(at, i):
         start = pl.multiple_of(i * size, size)
-        source = a_ref.at[:, pl.ds(pl.multiple_of(at * span + start, size), size)]
+        place = (begin + len(given) + at) * span
+        source = a_ref.at[:, pl.ds(pl.multiple_of(place + start, size), size)]
         target = kept[at].at[:, pl.ds(start, size)]
         return pltpu.make_async_copy(source, target, sems.at[at * count + i])
 
@@ -195,38 +226,58 @@
             load(at, i).start()
     kh, kl = split(jnp.concatenate([first_ref[...], second_ref[...]], 1))
     left = jnp.concatenate([kh, kl], 0)
-    for at, ref in enumerate(kept):
-        half, place = divmod(at, len(kept) // 2)
-        out = (low_ref, high_ref)[half]
+    for at, ref in enumerate(refs):
 
         @pl.loop(0, count)
         def _(i):
-            load(at, i).wait()
+            if at >= len(given):
+                load(at - len(given), i).wait()
             start = pl.multiple_of(i * size, size)
             ah, al = split(ref[:, pl.ds(start, size)])
             term = fast(left, ah) + fast(left, al)
-            into = pl.ds(pl.multiple_of(place * span + start, size), size)
-            out[:, into] = term[:width] + term[width:]
-
-
-def product_down(first, second, a):
+            into = pl.ds(pl.multiple_of(at * span + start, size), size)
+            out_ref[:, into] = term[:width] + term[width:]
+
+
+def product_down(first, second, a, given, begin, end, carry=()):
     rows, columns = a.shape
     width = first.shape[0]
-    parts = parts_of(columns)
-    span = columns // parts
-    size = block_of(span, 256)
+    span = columns // parts_of(columns)
+    ready, fresh, more = len(given), end - begin - len(given), len(carry)
     whole = pl.BlockSpec(memory_space=pltpu.VMEM)
-    low, high, *kept = pl.pallas_call(
-        down_kernel,
-        in_specs=[whole, whole, pl.BlockSpec(memory_space=pltpu.HBM)],
-        out_specs=(whole,) * (2 + parts),
-        out_shape=(shape(width, columns // 2),) * 2 + (shape(rows, span),) * parts,
-        scratch_shapes=[pltpu.SemaphoreType.DMA((columns // size,))],
+    anywhere = pl.BlockSpec(memory_space=pl.ANY)
+    copies = max(1, fresh * (span // block_of(span, 256)))
+
+    def kernel(first_ref, second_ref, a_ref, *refs):
+        outs = refs[ready + more : -1]
+        down_kernel(
+            begin,
+            first_ref,
+            second_ref,
+            a_ref,
+            refs[:ready],
+            outs[0],
+            outs[1 : 1 + fresh],
+            refs[-1],
+        )
+
+    out, *kept = pl.pallas_call(
+        kernel,
+        in_specs=[whole, whole, pl.BlockSpec(memory_space=pltpu.HBM)]
+        + [whole] * ready
+        + [anywhere] * more,
+        out_specs=(whole,) * (1 + fresh) + (anywhere,) * more,
+        out_shape=(shape(width, span * (end - begin)),)
+        + (shape(rows, span),) * fresh
+        + tuple(shape(*x.shape) for x in carry),
+        input_output_aliases={3 + ready + k: 1 + fresh + k for k in range(more)},
+        scratch_shapes=[pltpu.SemaphoreType.DMA((copies,))],
         compiler_params=params(12),
-        cost_estimate=cost(8 * rows * columns * width, 4 * rows * columns),
-        name="product_down",
-    )(first, second, pltpu.with_memory_space_constraint(a, pltpu.HBM))
-    return low, high, tuple(kept)
+        cost_estimate=cost(
+            8 * rows * span * (end - begin) * width, 4 * rows * span * (end - begin)
+        ),
+    )(first, second, pltpu.with_memory_space_constraint(a, pltpu.HBM), *given, *carry)
+    return out, tuple(kept[fresh:]) + tuple(given) + tuple(kept[:fresh])
 
 
 def fix_kernel(parts, low_ref, high_ref, band_ref, *refs):
@@ -660,9 +711,8 @@
         small = shape(width, width)
         packed = shape(width, 2 * width)
         half = shape(width, rows // 2)
-        first, second, partial = small_call(
-            open_kernel, (half, half, packed), panel.T, flops=100_000_000, mib=12
-        )
+        first, second, partial, part = open_panel(panel.T, matrix)
+        parts = parts_of(columns)
         apart = flip(partial, 1, row_size)
         if row_size == 8:
             wide_half = shape(width, rows // 2 + 2 * width)
@@ -682,7 +732,7 @@
             zero = jnp.zeros_like(total)
             terms = [total, flip(total, row_size // 2, row_size), zero, zero]
         first, second, partial = lax.optimization_barrier((first, second, partial))
-        low, high, resident = product_down(first, second, matrix)
+        low, resident = product_down(first, second, matrix, (part,), 0, parts // 2)
         if row_size == 8:
             one, two, resident = small_call(
                 merge_first_kernel, (half, half), first, second, by_x, by_y, carry=resident
@@ -698,6 +748,7 @@
                 held = held + from_sources(held, col_size, reached, bit)
                 reached = reached + [r ^ bit for r in reached]
                 bit *= 2
+        high, resident = product_down(first, second, matrix, (), parts // 2, parts, resident)
         band, again, band_inverse, head, resident = small_call(
             eliminate_kernel, (small, small, small, small), *terms, flops=50_000_000, carry=resident
         )

time: 75.1 us -> 74.3 us (0.989)
  Pallas kernels: 35.3 us -> 37.2 us
  starting transfers between devices: 22.3 us -> 21.3 us
  local copies, waits for them, and re-layouts: 0.99 us -> 0 us
  waiting for transfers between devices: 15.4 us -> 14.6 us
    pallas_call x1 -> x3, Pallas kernels: 7.04 us -> 9.51 us  [the longest x2 7.02 us: product_down(): pl.pallas_call(kernel, in_specs=[whole, whole, pl.BlockSpec(memory_space=...]
    unnamed x2 -> x0, local copies, waits for them, and re-layouts: 0.99 us -> none
    ppermute x13, starting transfers between devices: 11.7 us -> 10.7 us  [flip(): return lax.ppermute(value, axis, [(i, i ^ bit) for i in range(size)])]
    ppermute x13, waiting for transfers between devices: 10.6 us -> 9.86 us  [flip(): return lax.ppermute(value, axis, [(i, i ^ bit) for i in range(size)])]
    pallas_call x14 -> x13, Pallas kernels: 9.59 us -> 9.12 us  [small_call(): pl.pallas_call(body, out_shape=out, compiler_params=params(mib), cost_est...]
  transfers between devices with their start and end apart: 19 -> 19, of which waited for: 9 -> 10; matrix products, arithmetic and copies ran while one was open for 0% -> 0% of each run, Pallas kernels for 34% -> 35%
where the time goes in v9:
time: 74.3 us; the launch traced here: 74.2 us
  Pallas kernels  37.2 us (50%)
  starting transfers between devices  21.3 us (29%)
  waiting for transfers between devices  14.6 us (20%)
  between operations  0.98 us (1%)
    ppermute x13, starting transfers between devices, flip(): return lax.ppermute(value, axis, [(i, i ^ bit) for i in range(size)])  10.7 us
    ppermute x6, starting transfers between devices, shift(): lax.ppermute(piece, 'col', [(i, (i + by) % size) for i in range(size)])  10.6 us
    ppermute x13, waiting for transfers between devices, flip(): return lax.ppermute(value, axis, [(i, i ^ bit) for i in range(size)])  9.86 us
    pallas_call x13, Pallas kernels, small_call(): pl.pallas_call(body, out_shape=out, compiler_params=params(mib), cost_est...  9.12 us
    pallas_call x1, Pallas kernels, subtract_far(): pl.pallas_call(kernel, in_specs=[whole] * (4 + parts), out_specs=pl.Block...  7.35 us
    pallas_call x2, Pallas kernels, product_down(): pl.pallas_call(kernel, in_specs=[whole, whole, pl.BlockSpec(memory_space=...  7.02 us
    pallas_call x3, Pallas kernels, across_call(): pl.pallas_call(body, grid=(count,), in_specs=[fixed(x) for x in operands]...  6.91 us
    ppermute x6, waiting for transfers between devices, shift(): lax.ppermute(piece, 'col', [(i, (i + by) % size) for i in range(size)])  4.75 us
  transfers between devices with their start and end apart: 19, of which 10 were waited for; matrix products, arithmetic and copies ran while one was open for 0% of the time, Pallas kernels for 35%

profile of v9, /device:TPU:0, one launch (start us, length us, event | category | flops | bytes accessed | tf_op | source)
XLA Modules:
  0.0 74.2 jit_solution(14370153767398779621)
XLA Ops:
  0.6 2.5 %open.1 = (f32[64,768]{1,0:T(8,128)S(1)}, f32[64,768]{1,0:T(8,128)S(1)}, f32[64,128]{1,0:T(8,128)S(1)}, f32[1536,768]{1,0:T(8,128)S(1)}) custom-call(f32[64,1536]{1,0:T(8,128)} %bitcast.1, f32[1536,3072]{1,0:T(8,128)} %a_ref.5), custom_call_target="tpu_custom_call" | custom-call | flops 100000000 | bytes 4718592 | tf_op jit(solution)/shard_map/open/pallas_call | solution.py:104
  3.1 0.6 collective-permute-start
  3.7 0.9 %collective-permute-done.b_ref = f32[64,128]{1,0:T(8,128)S(1)} collective-permute-done((f32[64,128]{1,0:T(8,128)S(1)}, f32[64,128]{1,0:T(8,128)S(1)}, u32[]{:S(2)}, u32[]{:S(2)}) %collective-permute-start) | collective-permute-done | bytes 32800 | tf_op jit(solution)/shard_map/ppermute | solution.py:688
  4.6 2.9 %collective-permute-start.1 = (f32[64,896]{1,0:T(8,128)S(1)}, f32[64,896]{1,0:T(8,128)S(1)}, u32[]{:S(2)}, u32[]{:S(2)}) collective-permute-start(f32[64,896]{1,0:T(8,128)S(1)} %get-tuple-element.118), channel_id=1, source_target_pairs={{0,8},{4,12},{8,0},{12,4},{16,24},{20,28},{24,16},{28,20},{1,9},{5... | collective-permute-start | bytes 688136 | tf_op jit(solution)/shard_map/ppermute | solution.py:688
  7.5 1.5 %collective-permute-start.2 = (f32[64,896]{1,0:T(8,128)S(1)}, f32[64,896]{1,0:T(8,128)S(1)}, u32[]{:S(2)}, u32[]{:S(2)}) collective-permute-start(f32[64,896]{1,0:T(8,128)S(1)} %get-tuple-element.119), channel_id=1, source_target_pairs={{0,16},{4,20},{8,24},{12,28},{16,0},{20,4},{24,8},{28,12},{1,17},{... | collective-permute-start | bytes 688136 | tf_op jit(solution)/shard_map/ppermute | solution.py:688
  9.0 0.0 collective-permute-start.3
  9.0 2.8 %shard_map.42 = (f32[64,1536]{1,0:T(8,128)S(1)}, f32[1536,768]{1,0:T(8,128)S(1)}) custom-call(f32[64,768]{1,0:T(8,128)S(1)} %get-tuple-element.120.first_ref.refs_0_.refs_3_, f32[64,768]{1,0:T(8,128)S(1)} %get-tuple-element.121.second_ref.refs_1_.refs_4_, f32[1536,3072]{1,0:T(8,128)} %a_ref.5, f32[1536,768]{1,0:T(8,128)S(1)} %get-tuple-element.122.refs_0_.refs_4_), custom_call_target="tpu_custom_call" | custom-call | flops 1207959552 | bytes 9437184 | tf_op jit(solution)/shard_map/pallas_call | solution.py:264
  11.8 1.9 %collective-permute-done.1.refs_2_.refs_1_ = f32[64,896]{1,0:T(8,128)S(1)} collective-permute-done((f32[64,896]{1,0:T(8,128)S(1)}, f32[64,896]{1,0:T(8,128)S(1)}, u32[]{:S(2)}, u32[]{:S(2)}) %collective-permute-start.1) | collective-permute-done | bytes 229408 | tf_op jit(solution)/shard_map/ppermute | solution.py:688
  13.7 1.8 %collective-permute-done.2.refs_3_.refs_2_ = f32[64,896]{1,0:T(8,128)S(1)} collective-permute-done((f32[64,896]{1,0:T(8,128)S(1)}, f32[64,896]{1,0:T(8,128)S(1)}, u32[]{:S(2)}, u32[]{:S(2)}) %collective-permute-start.2) | collective-permute-done | bytes 229408 | tf_op jit(solution)/shard_map/ppermute | solution.py:688
  15.6 0.1 shard_map.43
  15.6 1.6 %collective-permute-start.4 = (f32[64,768]{1,0:T(8,128)S(1)}, f32[64,768]{1,0:T(8,128)S(1)}, u32[]{:S(2)}, u32[]{:S(2)}) collective-permute-start(f32[64,768]{1,0:T(8,128)S(1)} %get-tuple-element.133.refs_0_), channel_id=1, source_target_pairs={{0,16},{4,20},{8,24},{12,28},{16,0},{20,4},{24,8},{28,12},{1,17},{... | collective-permute-start | bytes 589832 | tf_op jit(solution)/shard_map/ppermute | solution.py:688
  17.2 0.5 collective-permute-start.5
  17.7 4.2 %shard_map.44 = (f32[64,1536]{1,0:T(8,128)S(1)}, f32[1536,768]{1,0:T(8,128)S(1)}, f32[1536,768]{1,0:T(8,128)S(1)}, f32[1536,768]{1,0:T(8,128)S(1)}, f32[1536,768]{1,0:T(8,128)S(1)}) custom-call(f32[64,768]{1,0:T(8,128)S(1)} %get-tuple-element.120.first_ref.refs_0_.refs_3_, ...), custom_call_target="tpu_custom_call", output_to_operand_aliasing={{3}: (3, {}), {4}: (4, {})} | custom-call | flops 1207959552 | bytes 9437184 | tf_op jit(solution)/shard_map/pallas_call | solution.py:264
  22.0 0.0 collective-permute-done.3.refs_3_
  22.0 2.7 %shard_map.45 = (f32[64,64]{1,0:T(8,128)}, f32[64,64]{1,0:T(8,128)S(1)}, f32[64,64]{1,0:T(8,128)S(1)}, f32[64,64]{1,0:T(8,128)S(1)}, f32[1536,768]{1,0:T(8,128)S...) custom-call(f32[64,128]{1,0:T(8,128)S(1)} %get-tuple-element.117.ref, ...), custom_call_target="tpu_custom_call", output_to_operand_aliasing={{4}: (4, {}), {5}: (5, {}), {6}: (6, {}), {7}: (7, {})} | custom-call | flops 50000000 | bytes 1000000 | tf_op jit(solution)/shard_map/pallas_call | solution.py:68
  24.7 0.6 fix_down.1
  25.2 0.1 collective-permute-start.7
  25.3 0.0 collective-permute-done.4.refs_1_
  25.3 0.0 collective-permute-done.5.refs_3_
  25.4 0.5 collective-permute-start.6
  25.9 1.1 %collective-permute-done.7.refs_1_ = f32[64,1536]{1,0:T(8,128)S(1)} collective-permute-done((f32[64,1536]{1,0:T(8,128)S(1)}, f32[64,1536]{1,0:T(8,128)S(1)}, u32[]{:S(2)}, u32[]{:S(2)}) %collective-permute-start.7) | collective-permute-done | bytes 393248 | tf_op jit(solution)/shard_map/ppermute | solution.py:688
  27.1 1.1 %collective-permute-start.8 = (f32[64,768]{1,0:T(8,128)S(1)}, f32[64,768]{1,0:T(8,128)S(1)}, u32[]{:S(2)}, u32[]{:S(2)}) collective-permute-start(f32[64,768]{1,0:T(8,128)S(1)} %get-tuple-element.157.refs_0_), channel_id=1, source_target_pairs={{0,8},{4,12},{8,0},{12,4},{16,24},{20,28},{24,16},{28,20},{1,9},{5... | collective-permute-start | bytes 589832 | tf_op jit(solution)/shard_map/ppermute | solution.py:688
  28.2 0.5 collective-permute-start.9
  28.7 0.0 collective-permute-done.6.refs_1_
  28.7 3.9 %shard_map.48 = (f32[64,3072]{1,0:T(8,128)S(1)}, bf16[3072,128]{1,0:T(8,128)(2,1)S(1)}, f32[64,384]{1,0:T(8,128)S(1)}, f32[64,384]{1,0:T(8,128)S(1)}, f32[1536,7...) custom-call(f32[64,1536]{1,0:T(8,128)S(1)} %get-tuple-element.145.re, ...), custom_call_target="tpu_custom_call", output_to_operand_aliasing={{4}: (3, {}), {5}: (4, {}), {6}: (5, {}), {7}: (6, {})} | custom-call | flops 1207959552 | bytes 9437184 | tf_op jit(solution)/shard_map/pallas_call | solution.py:406
  32.6 1.5 %collective-permute-done.8.refs_1_ = f32[64,768]{1,0:T(8,128)S(1)} collective-permute-done((f32[64,768]{1,0:T(8,128)S(1)}, f32[64,768]{1,0:T(8,128)S(1)}, u32[]{:S(2)}, u32[]{:S(2)}) %collective-permute-start.8) | collective-permute-done | bytes 196640 | tf_op jit(solution)/shard_map/ppermute | solution.py:688
  34.1 0.8 %collective-permute-done.9.refs_3_ = f32[64,768]{1,0:T(8,128)S(1)} collective-permute-done((f32[64,768]{1,0:T(8,128)S(1)}, f32[64,768]{1,0:T(8,128)S(1)}, u32[]{:S(2)}, u32[]{:S(2)}) %collective-permute-start.9) | collective-permute-done | bytes 196640 | tf_op jit(solution)/shard_map/ppermute | solution.py:688
  34.9 0.6 collective-permute-start.13
  35.5 0.8 %collective-permute-start.14 = (f32[64,768]{1,0:T(8,128)S(1)}, f32[64,768]{1,0:T(8,128)S(1)}, u32[]{:S(2)}, u32[]{:S(2)}) collective-permute-start(f32[64,768]{1,0:T(8,128)S(1)} %get-tuple-element.177.refs_2_), channel_id=1, source_target_pairs={{0,8},{4,12},{8,0},{12,4},{16,24},{20,28},{24,16},{28,20},{1,9},{5... | collective-permute-start | bytes 589832 | tf_op jit(solution)/shard_map/ppermute | solution.py:688
  36.2 1.5 %shard_map.50 = (f32[64,384]{1,0:T(8,128)S(1)}, f32[1536,768]{1,0:T(8,128)S(1)}, f32[1536,768]{1,0:T(8,128)S(1)}, f32[1536,768]{1,0:T(8,128)S(1)}, f32[1536,768]{1,0:T(8,128)S(1)}) custom-call(bf16[3072,128]{1,0:T(8,128)(2,1)S(1)} %get-tuple-element.156.refs_0_, ...), custom_call_target="tpu_custom_call", output_to_operand_aliasing={{1}: (1, {}), {2}: (2, {}), {3}: (3, {}), {4}: (4, {})} | custom-call | flops 603979776 | bytes 4718592 | tf_op jit(solution)/shard_map/pallas_call | solution.py:406
  37.7 1.5 %shard_map.51 = (f32[64,384]{1,0:T(8,128)S(1)}, f32[1536,768]{1,0:T(8,128)S(1)}, f32[1536,768]{1,0:T(8,128)S(1)}, f32[1536,768]{1,0:T(8,128)S(1)}, f32[1536,768]{1,0:T(8,128)S(1)}) custom-call(bf16[3072,128]{1,0:T(8,128)(2,1)S(1)} %get-tuple-element.156.refs_0_, ...), custom_call_target="tpu_custom_call", output_to_operand_aliasing={{1}: (1, {}), {2}: (2, {}), {3}: (3, {}), {4}: (4, {})} | custom-call | flops 603979776 | bytes 4718592 | tf_op jit(solution)/shard_map/pallas_call | solution.py:406
  39.2 1.5 %collective-permute-done.13.refs_1_ = f32[64,768]{1,0:T(8,128)S(1)} collective-permute-done((f32[64,768]{1,0:T(8,128)S(1)}, f32[64,768]{1,0:T(8,128)S(1)}, u32[]{:S(2)}, u32[]{:S(2)}) %collective-permute-start.13) | collective-permute-done | bytes 196640 | tf_op jit(solution)/shard_map/ppermute | solution.py:688
  40.7 0.4 collective-permute-done.14.refs_3_
  41.2 0.1 collective-permute-start.15
  41.3 1.6 %collective-permute-start.12 = (f32[64,384]{1,0:T(8,128)S(1)}, f32[64,384]{1,0:T(8,128)S(1)}, u32[]{:S(2)}, u32[]{:S(2)}) collective-permute-start(f32[64,384]{1,0:T(8,128)S(1)} %get-tuple-element.174), channel_id=1, source_target_pairs={{0,1},{1,2},{2,3},{3,0},{4,5},{5,6},{6,7},{7,4},{8,9},{9,10},{10,1... | collective-permute-start | bytes 294920 | tf_op jit(solution)/shard_map/ppermute | solution.py:702
  42.9 2.6 %collective-permute-start.10 = (f32[64,384]{1,0:T(8,128)S(1)}, f32[64,384]{1,0:T(8,128)S(1)}, u32[]{:S(2)}, u32[]{:S(2)}) collective-permute-start(f32[64,384]{1,0:T(8,128)S(1)} %get-tuple-element.172), channel_id=1, source_target_pairs={{0,2},{1,3},{2,0},{3,1},{4,6},{5,7},{6,4},{7,5},{8,10},{9,11},{10,... | collective-permute-start | bytes 294920 | tf_op jit(solution)/shard_map/ppermute | solution.py:702
  45.5 1.3 %collective-permute-start.11 = (f32[64,384]{1,0:T(8,128)S(1)}, f32[64,384]{1,0:T(8,128)S(1)}, u32[]{:S(2)}, u32[]{:S(2)}) collective-permute-start(f32[64,384]{1,0:T(8,128)S(1)} %get-tuple-element.173), channel_id=1, source_target_pairs={{0,3},{1,0},{2,1},{3,2},{4,7},{5,4},{6,5},{7,6},{8,11},{9,8},{10,9... | collective-permute-start | bytes 294920 | tf_op jit(solution)/shard_map/ppermute | solution.py:702
  46.8 0.5 shard_map.53
  47.3 0.0 collective-permute-done.15.refs_2_
  47.3 0.5 shard_map.54
  47.9 1.0 %collective-permute-done.12.refs_3_ = f32[64,384]{1,0:T(8,128)S(1)} collective-permute-done((f32[64,384]{1,0:T(8,128)S(1)}, f32[64,384]{1,0:T(8,128)S(1)}, u32[]{:S(2)}, u32[]{:S(2)}) %collective-permute-start.12) | collective-permute-done | bytes 98336 | tf_op jit(solution)/shard_map/ppermute | solution.py:702
  48.9 3.7 %collective-permute-done.10.refs_1_ = f32[64,384]{1,0:T(8,128)S(1)} collective-permute-done((f32[64,384]{1,0:T(8,128)S(1)}, f32[64,384]{1,0:T(8,128)S(1)}, u32[]{:S(2)}, u32[]{:S(2)}) %collective-permute-start.10) | collective-permute-done | bytes 98336 | tf_op jit(solution)/shard_map/ppermute | solution.py:702
  52.6 0.0 collective-permute-done.11.refs_2_
  52.6 0.1 shard_map.55
  52.7 2.6 %collective-permute-start.16 = (f32[72,384]{1,0:T(8,128)S(1)}, f32[72,384]{1,0:T(8,128)S(1)}, u32[]{:S(2)}, u32[]{:S(2)}) collective-permute-start(f32[72,384]{1,0:T(8,128)S(1)} %get-tuple-element.208.refs_2_), channel_id=1, source_target_pairs={{0,1},{1,2},{2,3},{3,0},{4,5},{5,6},{6,7},{7,4},{8,9},{9,10},{10,1... | collective-permute-start | bytes 331784 | tf_op jit(solution)/shard_map/ppermute | solution.py:702
  55.3 1.6 %collective-permute-start.17 = (f32[72,384]{1,0:T(8,128)S(1)}, f32[72,384]{1,0:T(8,128)S(1)}, u32[]{:S(2)}, u32[]{:S(2)}) collective-permute-start(f32[72,384]{1,0:T(8,128)S(1)} %get-tuple-element.208.refs_2_), channel_id=1, source_target_pairs={{0,2},{1,3},{2,0},{3,1},{4,6},{5,7},{6,4},{7,5},{8,10},{9,11},{10,... | collective-permute-start | bytes 331784 | tf_op jit(solution)/shard_map/ppermute | solution.py:702
  56.9 0.8 %collective-permute-start.18 = (f32[72,384]{1,0:T(8,128)S(1)}, f32[72,384]{1,0:T(8,128)S(1)}, u32[]{:S(2)}, u32[]{:S(2)}) collective-permute-start(f32[72,384]{1,0:T(8,128)S(1)} %get-tuple-element.208.refs_2_), channel_id=1, source_target_pairs={{0,3},{1,0},{2,1},{3,2},{4,7},{5,4},{6,5},{7,6},{8,11},{9,8},{10,9... | collective-permute-start | bytes 331784 | tf_op jit(solution)/shard_map/ppermute | solution.py:702
  57.7 2.3 %shard_map.56 = (f32[64,64]{1,0:T(8,128)S(1)}, f32[1536,768]{1,0:T(8,128)S(1)}, f32[1536,768]{1,0:T(8,128)S(1)}, f32[1536,768]{1,0:T(8,128)S(1)}, f32[1536,768]{1,0:T(8,128)S(1)}) custom-call(f32[64,64]{1,0:T(8,128)S(1)} %get-tuple-element.130.refs_0_, ...), custom_call_target="tpu_custom_call", output_to_operand_aliasing={{1}: (3, {}), {2}: (4, {}), {3}: (5, {}), {4}: (6, {})} | custom-call | flops 50000000 | bytes 1000000 | tf_op jit(solution)/shard_map/pallas_call | solution.py:68
  60.0 1.3 %shard_map.57 = (bf16[128,3072]{1,0:T(8,128)(2,1)S(1)}, bf16[128,3072]{1,0:T(8,128)(2,1)S(1)}, f32[64,1536]{1,0:T(8,128)S(1)}, bf16[1536,128]{1,0:T(8,128)(2,1)S...) custom-call(f32[64,64]{1,0:T(8,128)S(1)} %get-tuple-element.201.refs, ...), custom_call_target="tpu_custom_call", output_to_operand_aliasing={{4}: (6, {}), {5}: (7, {}), {6}: (8, {}), {7}: (9, {})} | custom-call | flops 1000000 | bytes 1000000 | tf_op jit(solution)/shard_map/pallas_call | solution.py:68
  61.3 3.8 %subtract_near.1 = (f32[1536,768]{1,0:T(8,128)S(1)}, f32[1536,768]{1,0:T(8,128)S(1)}, f32[1536,768]{1,0:T(8,128)S(1)}, f32[1536,768]{1,0:T(8,128)S(1)}) custom-call(bf16[1536,128]{1,0:T(8,128)(2,1)S(1)} %get-tuple-element.209.refs_0_.refs_2_, ...), custom_call_target="tpu_custom_call", output_to_operand_aliasing={{0}: (2, {}), {1}: (3, {}), {2}: (4, {}), {3}: (5, {})} | custom-call | flops 2415919104 | bytes 37748736 | tf_op jit(solution)/shard_map/subtract_near/pallas_call | solution.py:550
  65.1 0.0 collective-permute-done.16.refs_3_
  65.1 0.0 collective-permute-done.17.refs_4_
  65.1 0.0 collective-permute-done.18.refs_5_
  65.1 1.6 %shard_map.58 = (bf16[1536,128]{1,0:T(8,128)(2,1)S(1)}, f32[1536,768]{1,0:T(8,128)S(1)}, f32[1536,768]{1,0:T(8,128)S(1)}, f32[1536,768]{1,0:T(8,128)S(1)}, f32[1536,768]{1,0:T(8,128)S(1)}) custom-call(f32[64,64]{1,0:T(8,128)S(1)} %get-tuple-element.201.refs_0_, ...), custom_call_target="tpu_custom_call", output_to_operand_aliasing={{1}: (6, {}), {2}: (7, {}), {3}: (8, {}), {4}: (9, {})} | custom-call | flops 1000000 | bytes 1000000 | tf_op jit(solution)/shard_map/pallas_call | solution.py:68
  66.7 7.3 %subtract_far.1 = f32[1536,3072]{1,0:T(8,128)} custom-call(bf16[1536,128]{1,0:T(8,128)(2,1)S(1)} %get-tuple-element.219.refs_0_, bf16[128,3072]{1,0:T(8,128)(2,1)S(1)} %get-tuple-element.220.refs_1_, bf16[1536,128]{1,0:T(8,128)(2,1)S(1)} %get-tuple-element.209.refs_0_.refs_2_, bf16[128,3072]{1,0:T(8,128)(2,1)S(1)} %get-tuple-element.210.refs_1_.refs_3_, ...), custom_call_target="tpu_custom_call" | custom-call | flops 3019898880 | bytes 37748736 | tf_op jit(solution)/shard_map/subtract_far/pallas_call | solution.py:672
  (5 shorter events, 0.2 us)
Async XLA Ops:
  3.1 1.4 %collective-permute-start = (f32[64,128]{1,0:T(8,128)S(1)}, f32[64,128]{1,0:T(8,128)S(1)}, u32[]{:S(2)}, u32[]{:S(2)}) collective-permute-start(f32[64,128]{1,0:T(8,128)S(1)} %get-tuple-element.116.a_ref), channel_id=1, source_target_pairs={{0,4},{4,0},{8,12},{12,8},{16,20},{20,16},{24,28},{28,24},{1,5},{5... | collective-permute-start | bytes 98312 | tf_op jit(solution)/shard_map/ppermute | solution.py:688
  4.6 9.2 %collective-permute-start.1 = (f32[64,896]{1,0:T(8,128)S(1)}, f32[64,896]{1,0:T(8,128)S(1)}, u32[]{:S(2)}, u32[]{:S(2)}) collective-permute-start(f32[64,896]{1,0:T(8,128)S(1)} %get-tuple-element.118), channel_id=1, source_target_pairs={{0,8},{4,12},{8,0},{12,4},{16,24},{20,28},{24,16},{28,20},{1,9},{5... | collective-permute-start | bytes 688136 | tf_op jit(solution)/shard_map/ppermute | solution.py:688
  7.5 8.1 %collective-permute-start.2 = (f32[64,896]{1,0:T(8,128)S(1)}, f32[64,896]{1,0:T(8,128)S(1)}, u32[]{:S(2)}, u32[]{:S(2)}) collective-permute-start(f32[64,896]{1,0:T(8,128)S(1)} %get-tuple-element.119), channel_id=1, source_target_pairs={{0,16},{4,20},{8,24},{12,28},{16,0},{20,4},{24,8},{28,12},{1,17},{... | collective-permute-start | bytes 688136 | tf_op jit(solution)/shard_map/ppermute | solution.py:688
  9.0 13.0 %collective-permute-start.3 = (f32[64,128]{1,0:T(8,128)S(1)}, f32[64,128]{1,0:T(8,128)S(1)}, u32[]{:S(2)}, u32[]{:S(2)}) collective-permute-start(f32[64,128]{1,0:T(8,128)S(1)} %get-tuple-element.117.refs_0_), channel_id=1, source_target_pairs={{0,24},{4,28},{8,16},{12,20},{16,8},{20,12},{24,0},{28,4},{1,25},{... | collective-permute-start | bytes 98312 | tf_op jit(solution)/shard_map/ppermute | solution.py:688
  15.6 9.7 %collective-permute-start.4 = (f32[64,768]{1,0:T(8,128)S(1)}, f32[64,768]{1,0:T(8,128)S(1)}, u32[]{:S(2)}, u32[]{:S(2)}) collective-permute-start(f32[64,768]{1,0:T(8,128)S(1)} %get-tuple-element.133.refs_0_), channel_id=1, source_target_pairs={{0,16},{4,20},{8,24},{12,28},{16,0},{20,4},{24,8},{28,12},{1,17},{... | collective-permute-start | bytes 589832 | tf_op jit(solution)/shard_map/ppermute | solution.py:688
  17.2 8.1 %collective-permute-start.5 = (f32[64,768]{1,0:T(8,128)S(1)}, f32[64,768]{1,0:T(8,128)S(1)}, u32[]{:S(2)}, u32[]{:S(2)}) collective-permute-start(f32[64,768]{1,0:T(8,128)S(1)} %get-tuple-element.134.refs_2_), channel_id=1, source_target_pairs={{0,8},{4,12},{8,0},{12,4},{16,24},{20,28},{24,16},{28,20},{1,9},{5... | collective-permute-start | bytes 589832 | tf_op jit(solution)/shard_map/ppermute | solution.py:688
  25.2 1.8 %collective-permute-start.7 = (f32[64,1536]{1,0:T(8,128)S(1)}, f32[64,1536]{1,0:T(8,128)S(1)}, u32[]{:S(2)}, u32[]{:S(2)}) collective-permute-start(f32[64,1536]{1,0:T(8,128)S(1)} %get-tuple-element.147), channel_id=1, source_target_pairs={{0,4},{4,0},{8,12},{12,8},{16,20},{20,16},{24,28},{28,24},{1,5},{5... | collective-permute-start | bytes 1179656 | tf_op jit(solution)/shard_map/ppermute | solution.py:688
  25.4 3.3 %collective-permute-start.6 = (f32[64,1536]{1,0:T(8,128)S(1)}, f32[64,1536]{1,0:T(8,128)S(1)}, u32[]{:S(2)}, u32[]{:S(2)}) collective-permute-start(f32[64,1536]{1,0:T(8,128)S(1)} %get-tuple-element.145.refs_0_), channel_id=1, source_target_pairs={{0,4},{4,0},{8,12},{12,8},{16,20},{20,16},{24,28},{28,24},{1,5},{5... | collective-permute-start | bytes 1179656 | tf_op jit(solution)/shard_map/ppermute | solution.py:688
  27.1 7.0 %collective-permute-start.8 = (f32[64,768]{1,0:T(8,128)S(1)}, f32[64,768]{1,0:T(8,128)S(1)}, u32[]{:S(2)}, u32[]{:S(2)}) collective-permute-start(f32[64,768]{1,0:T(8,128)S(1)} %get-tuple-element.157.refs_0_), channel_id=1, source_target_pairs={{0,8},{4,12},{8,0},{12,4},{16,24},{20,28},{24,16},{28,20},{1,9},{5... | collective-permute-start | bytes 589832 | tf_op jit(solution)/shard_map/ppermute | solution.py:688
  28.2 6.7 %collective-permute-start.9 = (f32[64,768]{1,0:T(8,128)S(1)}, f32[64,768]{1,0:T(8,128)S(1)}, u32[]{:S(2)}, u32[]{:S(2)}) collective-permute-start(f32[64,768]{1,0:T(8,128)S(1)} %get-tuple-element.158.refs_2_), channel_id=1, source_target_pairs={{0,16},{4,20},{8,24},{12,28},{16,0},{20,4},{24,8},{28,12},{1,17},{... | collective-permute-start | bytes 589832 | tf_op jit(solution)/shard_map/ppermute | solution.py:688
  34.9 5.9 %collective-permute-start.13 = (f32[64,768]{1,0:T(8,128)S(1)}, f32[64,768]{1,0:T(8,128)S(1)}, u32[]{:S(2)}, u32[]{:S(2)}) collective-permute-start(f32[64,768]{1,0:T(8,128)S(1)} %get-tuple-element.176.refs_0_), channel_id=1, source_target_pairs={{0,16},{4,20},{8,24},{12,28},{16,0},{20,4},{24,8},{28,12},{1,17},{... | collective-permute-start | bytes 589832 | tf_op jit(solution)/shard_map/ppermute | solution.py:688
  35.5 5.7 %collective-permute-start.14 = (f32[64,768]{1,0:T(8,128)S(1)}, f32[64,768]{1,0:T(8,128)S(1)}, u32[]{:S(2)}, u32[]{:S(2)}) collective-permute-start(f32[64,768]{1,0:T(8,128)S(1)} %get-tuple-element.177.refs_2_), channel_id=1, source_target_pairs={{0,8},{4,12},{8,0},{12,4},{16,24},{20,28},{24,16},{28,20},{1,9},{5... | collective-permute-start | bytes 589832 | tf_op jit(solution)/shard_map/ppermute | solution.py:688
  41.2 6.1 %collective-permute-start.15 = (f32[64,1536]{1,0:T(8,128)S(1)}, f32[64,1536]{1,0:T(8,128)S(1)}, u32[]{:S(2)}, u32[]{:S(2)}) collective-permute-start(f32[64,1536]{1,0:T(8,128)S(1)} %get-tuple-element.182.refs_1_), channel_id=1, source_target_pairs={{0,4},{4,0},{8,12},{12,8},{16,20},{20,16},{24,28},{28,24},{1,5},{5... | collective-permute-start | bytes 1179656 | tf_op jit(solution)/shard_map/ppermute | solution.py:688
  41.3 7.6 %collective-permute-start.12 = (f32[64,384]{1,0:T(8,128)S(1)}, f32[64,384]{1,0:T(8,128)S(1)}, u32[]{:S(2)}, u32[]{:S(2)}) collective-permute-start(f32[64,384]{1,0:T(8,128)S(1)} %get-tuple-element.174), channel_id=1, source_target_pairs={{0,1},{1,2},{2,3},{3,0},{4,5},{5,6},{6,7},{7,4},{8,9},{9,10},{10,1... | collective-permute-start | bytes 294920 | tf_op jit(solution)/shard_map/ppermute | solution.py:702
  42.9 9.7 %collective-permute-start.10 = (f32[64,384]{1,0:T(8,128)S(1)}, f32[64,384]{1,0:T(8,128)S(1)}, u32[]{:S(2)}, u32[]{:S(2)}) collective-permute-start(f32[64,384]{1,0:T(8,128)S(1)} %get-tuple-element.172), channel_id=1, source_target_pairs={{0,2},{1,3},{2,0},{3,1},{4,6},{5,7},{6,4},{7,5},{8,10},{9,11},{10,... | collective-permute-start | bytes 294920 | tf_op jit(solution)/shard_map/ppermute | solution.py:702
  45.5 7.1 %collective-permute-start.11 = (f32[64,384]{1,0:T(8,128)S(1)}, f32[64,384]{1,0:T(8,128)S(1)}, u32[]{:S(2)}, u32[]{:S(2)}) collective-permute-start(f32[64,384]{1,0:T(8,128)S(1)} %get-tuple-element.173), channel_id=1, source_target_pairs={{0,3},{1,0},{2,1},{3,2},{4,7},{5,4},{6,5},{7,6},{8,11},{9,8},{10,9... | collective-permute-start | bytes 294920 | tf_op jit(solution)/shard_map/ppermute | solution.py:702
  52.7 12.4 %collective-permute-start.16 = (f32[72,384]{1,0:T(8,128)S(1)}, f32[72,384]{1,0:T(8,128)S(1)}, u32[]{:S(2)}, u32[]{:S(2)}) collective-permute-start(f32[72,384]{1,0:T(8,128)S(1)} %get-tuple-element.208.refs_2_), channel_id=1, source_target_pairs={{0,1},{1,2},{2,3},{3,0},{4,5},{5,6},{6,7},{7,4},{8,9},{9,10},{10,1... | collective-permute-start | bytes 331784 | tf_op jit(solution)/shard_map/ppermute | solution.py:702
  55.3 9.8 %collective-permute-start.17 = (f32[72,384]{1,0:T(8,128)S(1)}, f32[72,384]{1,0:T(8,128)S(1)}, u32[]{:S(2)}, u32[]{:S(2)}) collective-permute-start(f32[72,384]{1,0:T(8,128)S(1)} %get-tuple-element.208.refs_2_), channel_id=1, source_target_pairs={{0,2},{1,3},{2,0},{3,1},{4,6},{5,7},{6,4},{7,5},{8,10},{9,11},{10,... | collective-permute-start | bytes 331784 | tf_op jit(solution)/shard_map/ppermute | solution.py:702
  56.9 8.2 %collective-permute-start.18 = (f32[72,384]{1,0:T(8,128)S(1)}, f32[72,384]{1,0:T(8,128)S(1)}, u32[]{:S(2)}, u32[]{:S(2)}) collective-permute-start(f32[72,384]{1,0:T(8,128)S(1)} %get-tuple-element.208.refs_2_), channel_id=1, source_target_pairs={{0,3},{1,0},{2,1},{3,2},{4,7},{5,4},{6,5},{7,6},{8,11},{9,8},{10,9... | collective-permute-start | bytes 331784 | tf_op jit(solution)/shard_map/ppermute | solution.py:702

commit v10 on v8

--- a/solution.py
+++ b/solution.py
@@ -69,9 +69,21 @@
     return result
 
 
-def open_kernel(turned_ref, first_ref, second_ref, packed_ref):
-    width = turned_ref.shape[0]
+def open_kernel(panel_ref, first_ref, second_ref, packed_ref, turned_ref, sems):
+    width, rows = turned_ref.shape
     half = first_ref.shape[1]
+    count = sems.shape[0]
+    size = rows // count
+    copies = [
+        pltpu.make_async_copy(
+            panel_ref.at[:, pl.ds(k * size, size)], turned_ref.at[:, pl.ds(k * size, size)], sems.at[k]
+        )
+        for k in range(count)
+    ]
+    for copy in copies:
+        copy.start()
+    for copy in copies:
+        copy.wait()
     turned = turned_ref[...]
     first_ref[...] = turned[:, :half]
     second_ref[...] = turned[:, half:]
@@ -80,6 +92,23 @@
     )
     head = jnp.where(lax.axis_index("row") == 0, turned[:, : 2 * width].T[:width], 0.0)
     packed_ref[...] = jnp.concatenate([gram, head], 1)
+
+
+def open_panel(turned):
+    width, rows = turned.shape
+    whole = pl.BlockSpec(memory_space=pltpu.VMEM)
+    half = shape(width, rows // 2)
+    count = 1 if (rows // 4) % 128 else 4
+    return pl.pallas_call(
+        open_kernel,
+        in_specs=[pl.BlockSpec(memory_space=pltpu.HBM)],
+        out_specs=(whole,) * 3,
+        out_shape=(half, half, shape(width, 2 * width)),
+        scratch_shapes=[pltpu.VMEM((width, rows), f32), pltpu.SemaphoreType.DMA((count,))],
+        compiler_params=params(12),
+        cost_estimate=cost(100_000_000, 8 * rows * width),
+        name="open",
+    )(pltpu.with_memory_space_constraint(turned, pltpu.HBM))
 
 
 def add_cores_kernel(first_ref, second_ref, a_ref, b_ref, x_ref, y_ref, sum_ref):
@@ -660,9 +689,7 @@
         small = shape(width, width)
         packed = shape(width, 2 * width)
         half = shape(width, rows // 2)
-        first, second, partial = small_call(
-            open_kernel, (half, half, packed), panel.T, flops=100_000_000, mib=12
-        )
+        first, second, partial = open_panel(panel.T)
         apart = flip(partial, 1, row_size)
         if row_size == 8:
             wide_half = shape(width, rows // 2 + 2 * width)

time: 75.1 us -> 75.2 us (level)
  Pallas kernels: 35.3 us -> 36.3 us
  local copies, waits for them, and re-layouts: 0.99 us -> 0 us
    pallas_call x0 -> x1, Pallas kernels: none -> 1.55 us  [open_panel(): pl.pallas_call(open_kernel, in_specs=[pl.BlockSpec(memory_space=pltpu.HBM...]
    unnamed x2 -> x0, local copies, waits for them, and re-layouts: 0.99 us -> none
    pallas_call x14 -> x13, Pallas kernels: 9.59 us -> 9.13 us  [small_call(): pl.pallas_call(body, out_shape=out, compiler_params=params(mib), cost_est...]
where the time goes in v10:
time: 75.2 us; the launch traced here: 75 us
  Pallas kernels  36.3 us (48%)
  starting transfers between devices  22.3 us (30%)
  waiting for transfers between devices  15.4 us (20%)
  between operations  0.99 us (1%)
    ppermute x13, starting transfers between devices, flip(): return lax.ppermute(value, axis, [(i, i ^ bit) for i in range(size)])  11.7 us
    ppermute x13, waiting for transfers between devices, flip(): return lax.ppermute(value, axis, [(i, i ^ bit) for i in range(size)])  10.7 us
    ppermute x6, starting transfers between devices, shift(): lax.ppermute(piece, 'col', [(i, (i + by) % size) for i in range(size)])  10.6 us
    pallas_call x13, Pallas kernels, small_call(): pl.pallas_call(body, out_shape=out, compiler_params=params(mib), cost_est...  9.13 us
    pallas_call x1, Pallas kernels, subtract_far(): pl.pallas_call(kernel, in_specs=[whole] * (4 + parts), out_specs=pl.Block...  7.35 us
    pallas_call x1, Pallas kernels, product_down(): pl.pallas_call(down_kernel, in_specs=[whole, whole, pl.BlockSpec(memory_s...  7.04 us
    pallas_call x3, Pallas kernels, across_call(): pl.pallas_call(body, grid=(count,), in_specs=[fixed(x) for x in operands]...  6.91 us
    ppermute x6, waiting for transfers between devices, shift(): lax.ppermute(piece, 'col', [(i, (i + by) % size) for i in range(size)])  4.77 us
  transfers between devices with their start and end apart: 19, of which 9 were waited for; matrix products, arithmetic and copies ran while one was open for 0% of the time, Pallas kernels for 34%

profile of v10, /device:TPU:0, one launch (start us, length us, event | category | flops | bytes accessed | tf_op | source)
XLA Modules:
  0.0 75.0 jit_solution(5148564517109493834)
XLA Ops:
  0.6 1.5 %open.1 = (f32[64,768]{1,0:T(8,128)S(1)}, f32[64,768]{1,0:T(8,128)S(1)}, f32[64,128]{1,0:T(8,128)S(1)}) custom-call(f32[64,1536]{1,0:T(8,128)} %bitcast.1), custom_call_target="tpu_custom_call" | custom-call | flops 100000000 | bytes 786432 | tf_op jit(solution)/shard_map/open/pallas_call | solution.py:102
  2.2 0.6 collective-permute-start
  2.7 0.9 %collective-permute-done.b_ref = f32[64,128]{1,0:T(8,128)S(1)} collective-permute-done((f32[64,128]{1,0:T(8,128)S(1)}, f32[64,128]{1,0:T(8,128)S(1)}, u32[]{:S(2)}, u32[]{:S(2)}) %collective-permute-start) | collective-permute-done | bytes 32800 | tf_op jit(solution)/shard_map/ppermute | solution.py:666
  3.6 2.9 %collective-permute-start.1 = (f32[64,896]{1,0:T(8,128)S(1)}, f32[64,896]{1,0:T(8,128)S(1)}, u32[]{:S(2)}, u32[]{:S(2)}) collective-permute-start(f32[64,896]{1,0:T(8,128)S(1)} %get-tuple-element.118), channel_id=1, source_target_pairs={{0,8},{4,12},{8,0},{12,4},{16,24},{20,28},{24,16},{28,20},{1,9},{5... | collective-permute-start | bytes 688136 | tf_op jit(solution)/shard_map/ppermute | solution.py:666
  6.5 1.5 %collective-permute-start.2 = (f32[64,896]{1,0:T(8,128)S(1)}, f32[64,896]{1,0:T(8,128)S(1)}, u32[]{:S(2)}, u32[]{:S(2)}) collective-permute-start(f32[64,896]{1,0:T(8,128)S(1)} %get-tuple-element.119), channel_id=1, source_target_pairs={{0,16},{4,20},{8,24},{12,28},{16,0},{20,4},{24,8},{28,12},{1,17},{... | collective-permute-start | bytes 688136 | tf_op jit(solution)/shard_map/ppermute | solution.py:666
  8.0 7.0 %product_down.1 = (f32[64,1536]{1,0:T(8,128)S(1)}, f32[64,1536]{1,0:T(8,128)S(1)}, f32[1536,768]{1,0:T(8,128)S(1)}, f32[1536,768]{1,0:T(8,128)S(1)}, f32[1536,768]{1,0:T(8,128)S(1)}, /*index=5*/f32[1536,768]{1,0:T(8,128)S(1)}) custom-call(f32[64,768]{1,0:T(8,128)S(1)} %get-tuple-element.120.first_ref.refs_0_.refs_3_, ...), custom_call_target="tpu_custom_call" | custom-call | flops 2415919104 | bytes 18874368 | tf_op jit(solution)/shard_map/product_down/pallas_call | solution.py:248
  15.1 0.0 collective-permute-done.1.refs_2_.refs_1_
  15.1 0.0 collective-permute-done.2.refs_3_.refs_2_
  15.1 0.1 shard_map.42
  15.2 0.6 collective-permute-start.4
  15.8 0.3 collective-permute-start.5
  16.1 2.7 %collective-permute-start.3 = (f32[64,128]{1,0:T(8,128)S(1)}, f32[64,128]{1,0:T(8,128)S(1)}, u32[]{:S(2)}, u32[]{:S(2)}) collective-permute-start(f32[64,128]{1,0:T(8,128)S(1)} %get-tuple-element.117.refs_0_), channel_id=1, source_target_pairs={{0,24},{4,28},{8,16},{12,20},{16,8},{20,12},{24,0},{28,4},{1,25},{... | collective-permute-start | bytes 98312 | tf_op jit(solution)/shard_map/ppermute | solution.py:666
  18.7 4.8 %collective-permute-done.3.refs_3_ = f32[64,128]{1,0:T(8,128)S(1)} collective-permute-done((f32[64,128]{1,0:T(8,128)S(1)}, f32[64,128]{1,0:T(8,128)S(1)}, u32[]{:S(2)}, u32[]{:S(2)}) %collective-permute-start.3) | collective-permute-done | bytes 32800 | tf_op jit(solution)/shard_map/ppermute | solution.py:666
  23.6 2.7 %shard_map.43 = (f32[64,64]{1,0:T(8,128)}, f32[64,64]{1,0:T(8,128)S(1)}, f32[64,64]{1,0:T(8,128)S(1)}, f32[64,64]{1,0:T(8,128)S(1)}, f32[1536,768]{1,0:T(8,128)S...) custom-call(f32[64,128]{1,0:T(8,128)S(1)} %get-tuple-element.117.ref, ...), custom_call_target="tpu_custom_call", output_to_operand_aliasing={{4}: (4, {}), {5}: (5, {}), {6}: (6, {}), {7}: (7, {})} | custom-call | flops 50000000 | bytes 1000000 | tf_op jit(solution)/shard_map/pallas_call | solution.py:64
  26.2 0.6 fix_down.1
  26.8 0.1 collective-permute-start.7
  26.9 0.0 collective-permute-done.4.refs_1_
  26.9 0.0 collective-permute-done.5.refs_3_
  27.0 0.5 collective-permute-start.6
  27.5 1.1 %collective-permute-done.7.refs_1_ = f32[64,1536]{1,0:T(8,128)S(1)} collective-permute-done((f32[64,1536]{1,0:T(8,128)S(1)}, f32[64,1536]{1,0:T(8,128)S(1)}, u32[]{:S(2)}, u32[]{:S(2)}) %collective-permute-start.7) | collective-permute-done | bytes 393248 | tf_op jit(solution)/shard_map/ppermute | solution.py:666
  28.6 0.1 collective-permute-start.8
  28.8 0.4 collective-permute-start.9
  29.1 0.0 collective-permute-done.6.refs_1_
  29.2 3.9 %shard_map.46 = (f32[64,3072]{1,0:T(8,128)S(1)}, bf16[3072,128]{1,0:T(8,128)(2,1)S(1)}, f32[64,384]{1,0:T(8,128)S(1)}, f32[64,384]{1,0:T(8,128)S(1)}, f32[1536,7...) custom-call(f32[64,1536]{1,0:T(8,128)S(1)} %get-tuple-element.145.re, ...), custom_call_target="tpu_custom_call", output_to_operand_aliasing={{4}: (3, {}), {5}: (4, {}), {6}: (5, {}), {7}: (6, {})} | custom-call | flops 1207959552 | bytes 9437184 | tf_op jit(solution)/shard_map/pallas_call | solution.py:384
  33.1 2.6 %collective-permute-done.8.refs_1_ = f32[64,768]{1,0:T(8,128)S(1)} collective-permute-done((f32[64,768]{1,0:T(8,128)S(1)}, f32[64,768]{1,0:T(8,128)S(1)}, u32[]{:S(2)}, u32[]{:S(2)}) %collective-permute-start.8) | collective-permute-done | bytes 196640 | tf_op jit(solution)/shard_map/ppermute | solution.py:666
  35.6 0.1 collective-permute-done.9.refs_3_
  35.8 0.4 collective-permute-start.13
  36.1 1.7 %collective-permute-start.14 = (f32[64,768]{1,0:T(8,128)S(1)}, f32[64,768]{1,0:T(8,128)S(1)}, u32[]{:S(2)}, u32[]{:S(2)}) collective-permute-start(f32[64,768]{1,0:T(8,128)S(1)} %get-tuple-element.177.refs_2_), channel_id=1, source_target_pairs={{0,8},{4,12},{8,0},{12,4},{16,24},{20,28},{24,16},{28,20},{1,9},{5... | collective-permute-start | bytes 589832 | tf_op jit(solution)/shard_map/ppermute | solution.py:666
  37.8 1.5 %shard_map.48 = (f32[64,384]{1,0:T(8,128)S(1)}, f32[1536,768]{1,0:T(8,128)S(1)}, f32[1536,768]{1,0:T(8,128)S(1)}, f32[1536,768]{1,0:T(8,128)S(1)}, f32[1536,768]{1,0:T(8,128)S(1)}) custom-call(bf16[3072,128]{1,0:T(8,128)(2,1)S(1)} %get-tuple-element.156.refs_0_, ...), custom_call_target="tpu_custom_call", output_to_operand_aliasing={{1}: (1, {}), {2}: (2, {}), {3}: (3, {}), {4}: (4, {})} | custom-call | flops 603979776 | bytes 4718592 | tf_op jit(solution)/shard_map/pallas_call | solution.py:384
  39.3 1.5 %shard_map.49 = (f32[64,384]{1,0:T(8,128)S(1)}, f32[1536,768]{1,0:T(8,128)S(1)}, f32[1536,768]{1,0:T(8,128)S(1)}, f32[1536,768]{1,0:T(8,128)S(1)}, f32[1536,768]{1,0:T(8,128)S(1)}) custom-call(bf16[3072,128]{1,0:T(8,128)(2,1)S(1)} %get-tuple-element.156.refs_0_, ...), custom_call_target="tpu_custom_call", output_to_operand_aliasing={{1}: (1, {}), {2}: (2, {}), {3}: (3, {}), {4}: (4, {})} | custom-call | flops 603979776 | bytes 4718592 | tf_op jit(solution)/shard_map/pallas_call | solution.py:384
  40.8 1.1 %collective-permute-done.13.refs_1_ = f32[64,768]{1,0:T(8,128)S(1)} collective-permute-done((f32[64,768]{1,0:T(8,128)S(1)}, f32[64,768]{1,0:T(8,128)S(1)}, u32[]{:S(2)}, u32[]{:S(2)}) %collective-permute-start.13) | collective-permute-done | bytes 196640 | tf_op jit(solution)/shard_map/ppermute | solution.py:666
  41.9 0.1 collective-permute-done.14.refs_3_
  42.0 0.1 collective-permute-start.15
  42.1 1.6 %collective-permute-start.12 = (f32[64,384]{1,0:T(8,128)S(1)}, f32[64,384]{1,0:T(8,128)S(1)}, u32[]{:S(2)}, u32[]{:S(2)}) collective-permute-start(f32[64,384]{1,0:T(8,128)S(1)} %get-tuple-element.174), channel_id=1, source_target_pairs={{0,1},{1,2},{2,3},{3,0},{4,5},{5,6},{6,7},{7,4},{8,9},{9,10},{10,1... | collective-permute-start | bytes 294920 | tf_op jit(solution)/shard_map/ppermute | solution.py:680
  43.7 2.6 %collective-permute-start.10 = (f32[64,384]{1,0:T(8,128)S(1)}, f32[64,384]{1,0:T(8,128)S(1)}, u32[]{:S(2)}, u32[]{:S(2)}) collective-permute-start(f32[64,384]{1,0:T(8,128)S(1)} %get-tuple-element.172), channel_id=1, source_target_pairs={{0,2},{1,3},{2,0},{3,1},{4,6},{5,7},{6,4},{7,5},{8,10},{9,11},{10,... | collective-permute-start | bytes 294920 | tf_op jit(solution)/shard_map/ppermute | solution.py:680
  46.3 1.3 %collective-permute-start.11 = (f32[64,384]{1,0:T(8,128)S(1)}, f32[64,384]{1,0:T(8,128)S(1)}, u32[]{:S(2)}, u32[]{:S(2)}) collective-permute-start(f32[64,384]{1,0:T(8,128)S(1)} %get-tuple-element.173), channel_id=1, source_target_pairs={{0,3},{1,0},{2,1},{3,2},{4,7},{5,4},{6,5},{7,6},{8,11},{9,8},{10,9... | collective-permute-start | bytes 294920 | tf_op jit(solution)/shard_map/ppermute | solution.py:680
  47.7 0.5 shard_map.51
  48.2 0.0 collective-permute-done.15.refs_2_
  48.2 0.5 shard_map.52
  48.7 1.0 %collective-permute-done.12.refs_3_ = f32[64,384]{1,0:T(8,128)S(1)} collective-permute-done((f32[64,384]{1,0:T(8,128)S(1)}, f32[64,384]{1,0:T(8,128)S(1)}, u32[]{:S(2)}, u32[]{:S(2)}) %collective-permute-start.12) | collective-permute-done | bytes 98336 | tf_op jit(solution)/shard_map/ppermute | solution.py:680
  49.7 3.7 %collective-permute-done.10.refs_1_ = f32[64,384]{1,0:T(8,128)S(1)} collective-permute-done((f32[64,384]{1,0:T(8,128)S(1)}, f32[64,384]{1,0:T(8,128)S(1)}, u32[]{:S(2)}, u32[]{:S(2)}) %collective-permute-start.10) | collective-permute-done | bytes 98336 | tf_op jit(solution)/shard_map/ppermute | solution.py:680
  53.5 0.0 collective-permute-done.11.refs_2_
  53.5 0.1 shard_map.53
  53.5 2.6 %collective-permute-start.16 = (f32[72,384]{1,0:T(8,128)S(1)}, f32[72,384]{1,0:T(8,128)S(1)}, u32[]{:S(2)}, u32[]{:S(2)}) collective-permute-start(f32[72,384]{1,0:T(8,128)S(1)} %get-tuple-element.208.refs_2_), channel_id=1, source_target_pairs={{0,1},{1,2},{2,3},{3,0},{4,5},{5,6},{6,7},{7,4},{8,9},{9,10},{10,1... | collective-permute-start | bytes 331784 | tf_op jit(solution)/shard_map/ppermute | solution.py:680
  56.2 1.6 %collective-permute-start.17 = (f32[72,384]{1,0:T(8,128)S(1)}, f32[72,384]{1,0:T(8,128)S(1)}, u32[]{:S(2)}, u32[]{:S(2)}) collective-permute-start(f32[72,384]{1,0:T(8,128)S(1)} %get-tuple-element.208.refs_2_), channel_id=1, source_target_pairs={{0,2},{1,3},{2,0},{3,1},{4,6},{5,7},{6,4},{7,5},{8,10},{9,11},{10,... | collective-permute-start | bytes 331784 | tf_op jit(solution)/shard_map/ppermute | solution.py:680
  57.8 0.8 %collective-permute-start.18 = (f32[72,384]{1,0:T(8,128)S(1)}, f32[72,384]{1,0:T(8,128)S(1)}, u32[]{:S(2)}, u32[]{:S(2)}) collective-permute-start(f32[72,384]{1,0:T(8,128)S(1)} %get-tuple-element.208.refs_2_), channel_id=1, source_target_pairs={{0,3},{1,0},{2,1},{3,2},{4,7},{5,4},{6,5},{7,6},{8,11},{9,8},{10,9... | collective-permute-start | bytes 331784 | tf_op jit(solution)/shard_map/ppermute | solution.py:680
  58.6 2.3 %shard_map.54 = (f32[64,64]{1,0:T(8,128)S(1)}, f32[1536,768]{1,0:T(8,128)S(1)}, f32[1536,768]{1,0:T(8,128)S(1)}, f32[1536,768]{1,0:T(8,128)S(1)}, f32[1536,768]{1,0:T(8,128)S(1)}) custom-call(f32[64,64]{1,0:T(8,128)S(1)} %get-tuple-element.130.refs_0_, ...), custom_call_target="tpu_custom_call", output_to_operand_aliasing={{1}: (3, {}), {2}: (4, {}), {3}: (5, {}), {4}: (6, {})} | custom-call | flops 50000000 | bytes 1000000 | tf_op jit(solution)/shard_map/pallas_call | solution.py:64
  60.9 1.3 %shard_map.55 = (bf16[128,3072]{1,0:T(8,128)(2,1)S(1)}, bf16[128,3072]{1,0:T(8,128)(2,1)S(1)}, f32[64,1536]{1,0:T(8,128)S(1)}, bf16[1536,128]{1,0:T(8,128)(2,1)S...) custom-call(f32[64,64]{1,0:T(8,128)S(1)} %get-tuple-element.201.refs, ...), custom_call_target="tpu_custom_call", output_to_operand_aliasing={{4}: (6, {}), {5}: (7, {}), {6}: (8, {}), {7}: (9, {})} | custom-call | flops 1000000 | bytes 1000000 | tf_op jit(solution)/shard_map/pallas_call | solution.py:64
  62.1 3.8 %subtract_near.1 = (f32[1536,768]{1,0:T(8,128)S(1)}, f32[1536,768]{1,0:T(8,128)S(1)}, f32[1536,768]{1,0:T(8,128)S(1)}, f32[1536,768]{1,0:T(8,128)S(1)}) custom-call(bf16[1536,128]{1,0:T(8,128)(2,1)S(1)} %get-tuple-element.209.refs_0_.refs_2_, ...), custom_call_target="tpu_custom_call", output_to_operand_aliasing={{0}: (2, {}), {1}: (3, {}), {2}: (4, {}), {3}: (5, {})} | custom-call | flops 2415919104 | bytes 37748736 | tf_op jit(solution)/shard_map/subtract_near/pallas_call | solution.py:528
  65.9 0.0 collective-permute-done.16.refs_3_
  65.9 0.0 collective-permute-done.17.refs_4_
  66.0 0.0 collective-permute-done.18.refs_5_
  66.0 1.6 %shard_map.56 = (bf16[1536,128]{1,0:T(8,128)(2,1)S(1)}, f32[1536,768]{1,0:T(8,128)S(1)}, f32[1536,768]{1,0:T(8,128)S(1)}, f32[1536,768]{1,0:T(8,128)S(1)}, f32[1536,768]{1,0:T(8,128)S(1)}) custom-call(f32[64,64]{1,0:T(8,128)S(1)} %get-tuple-element.201.refs_0_, ...), custom_call_target="tpu_custom_call", output_to_operand_aliasing={{1}: (6, {}), {2}: (7, {}), {3}: (8, {}), {4}: (9, {})} | custom-call | flops 1000000 | bytes 1000000 | tf_op jit(solution)/shard_map/pallas_call | solution.py:64
  67.5 7.3 %subtract_far.1 = f32[1536,3072]{1,0:T(8,128)} custom-call(bf16[1536,128]{1,0:T(8,128)(2,1)S(1)} %get-tuple-element.219.refs_0_, bf16[128,3072]{1,0:T(8,128)(2,1)S(1)} %get-tuple-element.220.refs_1_, bf16[1536,128]{1,0:T(8,128)(2,1)S(1)} %get-tuple-element.209.refs_0_.refs_2_, bf16[128,3072]{1,0:T(8,128)(2,1)S(1)} %get-tuple-element.210.refs_1_.refs_3_, ...), custom_call_target="tpu_custom_call" | custom-call | flops 3019898880 | bytes 37748736 | tf_op jit(solution)/shard_map/subtract_far/pallas_call | solution.py:650
  (5 shorter events, 0.2 us)
Async XLA Ops:
  2.2 1.4 %collective-permute-start = (f32[64,128]{1,0:T(8,128)S(1)}, f32[64,128]{1,0:T(8,128)S(1)}, u32[]{:S(2)}, u32[]{:S(2)}) collective-permute-start(f32[64,128]{1,0:T(8,128)S(1)} %get-tuple-element.116.a_ref), channel_id=1, source_target_pairs={{0,4},{4,0},{8,12},{12,8},{16,20},{20,16},{24,28},{28,24},{1,5},{5... | collective-permute-start | bytes 98312 | tf_op jit(solution)/shard_map/ppermute | solution.py:666
  3.6 11.5 %collective-permute-start.1 = (f32[64,896]{1,0:T(8,128)S(1)}, f32[64,896]{1,0:T(8,128)S(1)}, u32[]{:S(2)}, u32[]{:S(2)}) collective-permute-start(f32[64,896]{1,0:T(8,128)S(1)} %get-tuple-element.118), channel_id=1, source_target_pairs={{0,8},{4,12},{8,0},{12,4},{16,24},{20,28},{24,16},{28,20},{1,9},{5... | collective-permute-start | bytes 688136 | tf_op jit(solution)/shard_map/ppermute | solution.py:666
  6.5 8.6 %collective-permute-start.2 = (f32[64,896]{1,0:T(8,128)S(1)}, f32[64,896]{1,0:T(8,128)S(1)}, u32[]{:S(2)}, u32[]{:S(2)}) collective-permute-start(f32[64,896]{1,0:T(8,128)S(1)} %get-tuple-element.119), channel_id=1, source_target_pairs={{0,16},{4,20},{8,24},{12,28},{16,0},{20,4},{24,8},{28,12},{1,17},{... | collective-permute-start | bytes 688136 | tf_op jit(solution)/shard_map/ppermute | solution.py:666
  15.2 11.7 %collective-permute-start.4 = (f32[64,768]{1,0:T(8,128)S(1)}, f32[64,768]{1,0:T(8,128)S(1)}, u32[]{:S(2)}, u32[]{:S(2)}) collective-permute-start(f32[64,768]{1,0:T(8,128)S(1)} %get-tuple-element.133.refs_0_), channel_id=1, source_target_pairs={{0,16},{4,20},{8,24},{12,28},{16,0},{20,4},{24,8},{28,12},{1,17},{... | collective-permute-start | bytes 589832 | tf_op jit(solution)/shard_map/ppermute | solution.py:666
  15.8 11.1 %collective-permute-start.5 = (f32[64,768]{1,0:T(8,128)S(1)}, f32[64,768]{1,0:T(8,128)S(1)}, u32[]{:S(2)}, u32[]{:S(2)}) collective-permute-start(f32[64,768]{1,0:T(8,128)S(1)} %get-tuple-element.134.refs_2_), channel_id=1, source_target_pairs={{0,8},{4,12},{8,0},{12,4},{16,24},{20,28},{24,16},{28,20},{1,9},{5... | collective-permute-start | bytes 589832 | tf_op jit(solution)/shard_map/ppermute | solution.py:666
  16.1 7.5 %collective-permute-start.3 = (f32[64,128]{1,0:T(8,128)S(1)}, f32[64,128]{1,0:T(8,128)S(1)}, u32[]{:S(2)}, u32[]{:S(2)}) collective-permute-start(f32[64,128]{1,0:T(8,128)S(1)} %get-tuple-element.117.refs_0_), channel_id=1, source_target_pairs={{0,24},{4,28},{8,16},{12,20},{16,8},{20,12},{24,0},{28,4},{1,25},{... | collective-permute-start | bytes 98312 | tf_op jit(solution)/shard_map/ppermute | solution.py:666
  26.8 1.8 %collective-permute-start.7 = (f32[64,1536]{1,0:T(8,128)S(1)}, f32[64,1536]{1,0:T(8,128)S(1)}, u32[]{:S(2)}, u32[]{:S(2)}) collective-permute-start(f32[64,1536]{1,0:T(8,128)S(1)} %get-tuple-element.147), channel_id=1, source_target_pairs={{0,4},{4,0},{8,12},{12,8},{16,20},{20,16},{24,28},{28,24},{1,5},{5... | collective-permute-start | bytes 1179656 | tf_op jit(solution)/shard_map/ppermute | solution.py:666
  27.0 2.2 %collective-permute-start.6 = (f32[64,1536]{1,0:T(8,128)S(1)}, f32[64,1536]{1,0:T(8,128)S(1)}, u32[]{:S(2)}, u32[]{:S(2)}) collective-permute-start(f32[64,1536]{1,0:T(8,128)S(1)} %get-tuple-element.145.refs_0_), channel_id=1, source_target_pairs={{0,4},{4,0},{8,12},{12,8},{16,20},{20,16},{24,28},{28,24},{1,5},{5... | collective-permute-start | bytes 1179656 | tf_op jit(solution)/shard_map/ppermute | solution.py:666
  28.6 7.0 %collective-permute-start.8 = (f32[64,768]{1,0:T(8,128)S(1)}, f32[64,768]{1,0:T(8,128)S(1)}, u32[]{:S(2)}, u32[]{:S(2)}) collective-permute-start(f32[64,768]{1,0:T(8,128)S(1)} %get-tuple-element.157.refs_0_), channel_id=1, source_target_pairs={{0,8},{4,12},{8,0},{12,4},{16,24},{20,28},{24,16},{28,20},{1,9},{5... | collective-permute-start | bytes 589832 | tf_op jit(solution)/shard_map/ppermute | solution.py:666
  28.8 6.9 %collective-permute-start.9 = (f32[64,768]{1,0:T(8,128)S(1)}, f32[64,768]{1,0:T(8,128)S(1)}, u32[]{:S(2)}, u32[]{:S(2)}) collective-permute-start(f32[64,768]{1,0:T(8,128)S(1)} %get-tuple-element.158.refs_2_), channel_id=1, source_target_pairs={{0,16},{4,20},{8,24},{12,28},{16,0},{20,4},{24,8},{28,12},{1,17},{... | collective-permute-start | bytes 589832 | tf_op jit(solution)/shard_map/ppermute | solution.py:666
  35.8 6.2 %collective-permute-start.13 = (f32[64,768]{1,0:T(8,128)S(1)}, f32[64,768]{1,0:T(8,128)S(1)}, u32[]{:S(2)}, u32[]{:S(2)}) collective-permute-start(f32[64,768]{1,0:T(8,128)S(1)} %get-tuple-element.176.refs_0_), channel_id=1, source_target_pairs={{0,16},{4,20},{8,24},{12,28},{16,0},{20,4},{24,8},{28,12},{1,17},{... | collective-permute-start | bytes 589832 | tf_op jit(solution)/shard_map/ppermute | solution.py:666
  36.1 5.9 %collective-permute-start.14 = (f32[64,768]{1,0:T(8,128)S(1)}, f32[64,768]{1,0:T(8,128)S(1)}, u32[]{:S(2)}, u32[]{:S(2)}) collective-permute-start(f32[64,768]{1,0:T(8,128)S(1)} %get-tuple-element.177.refs_2_), channel_id=1, source_target_pairs={{0,8},{4,12},{8,0},{12,4},{16,24},{20,28},{24,16},{28,20},{1,9},{5... | collective-permute-start | bytes 589832 | tf_op jit(solution)/shard_map/ppermute | solution.py:666
  42.0 6.1 %collective-permute-start.15 = (f32[64,1536]{1,0:T(8,128)S(1)}, f32[64,1536]{1,0:T(8,128)S(1)}, u32[]{:S(2)}, u32[]{:S(2)}) collective-permute-start(f32[64,1536]{1,0:T(8,128)S(1)} %get-tuple-element.182.refs_1_), channel_id=1, source_target_pairs={{0,4},{4,0},{8,12},{12,8},{16,20},{20,16},{24,28},{28,24},{1,5},{5... | collective-permute-start | bytes 1179656 | tf_op jit(solution)/shard_map/ppermute | solution.py:666
  42.1 7.6 %collective-permute-start.12 = (f32[64,384]{1,0:T(8,128)S(1)}, f32[64,384]{1,0:T(8,128)S(1)}, u32[]{:S(2)}, u32[]{:S(2)}) collective-permute-start(f32[64,384]{1,0:T(8,128)S(1)} %get-tuple-element.174), channel_id=1, source_target_pairs={{0,1},{1,2},{2,3},{3,0},{4,5},{5,6},{6,7},{7,4},{8,9},{9,10},{10,1... | collective-permute-start | bytes 294920 | tf_op jit(solution)/shard_map/ppermute | solution.py:680
  43.7 9.7 %collective-permute-start.10 = (f32[64,384]{1,0:T(8,128)S(1)}, f32[64,384]{1,0:T(8,128)S(1)}, u32[]{:S(2)}, u32[]{:S(2)}) collective-permute-start(f32[64,384]{1,0:T(8,128)S(1)} %get-tuple-element.172), channel_id=1, source_target_pairs={{0,2},{1,3},{2,0},{3,1},{4,6},{5,7},{6,4},{7,5},{8,10},{9,11},{10,... | collective-permute-start | bytes 294920 | tf_op jit(solution)/shard_map/ppermute | solution.py:680
  46.3 7.1 %collective-permute-start.11 = (f32[64,384]{1,0:T(8,128)S(1)}, f32[64,384]{1,0:T(8,128)S(1)}, u32[]{:S(2)}, u32[]{:S(2)}) collective-permute-start(f32[64,384]{1,0:T(8,128)S(1)} %get-tuple-element.173), channel_id=1, source_target_pairs={{0,3},{1,0},{2,1},{3,2},{4,7},{5,4},{6,5},{7,6},{8,11},{9,8},{10,9... | collective-permute-start | bytes 294920 | tf_op jit(solution)/shard_map/ppermute | solution.py:680
  53.5 12.4 %collective-permute-start.16 = (f32[72,384]{1,0:T(8,128)S(1)}, f32[72,384]{1,0:T(8,128)S(1)}, u32[]{:S(2)}, u32[]{:S(2)}) collective-permute-start(f32[72,384]{1,0:T(8,128)S(1)} %get-tuple-element.208.refs_2_), channel_id=1, source_target_pairs={{0,1},{1,2},{2,3},{3,0},{4,5},{5,6},{6,7},{7,4},{8,9},{9,10},{10,1... | collective-permute-start | bytes 331784 | tf_op jit(solution)/shard_map/ppermute | solution.py:680
  56.2 9.8 %collective-permute-start.17 = (f32[72,384]{1,0:T(8,128)S(1)}, f32[72,384]{1,0:T(8,128)S(1)}, u32[]{:S(2)}, u32[]{:S(2)}) collective-permute-start(f32[72,384]{1,0:T(8,128)S(1)} %get-tuple-element.208.refs_2_), channel_id=1, source_target_pairs={{0,2},{1,3},{2,0},{3,1},{4,6},{5,7},{6,4},{7,5},{8,10},{9,11},{10,... | collective-permute-start | bytes 331784 | tf_op jit(solution)/shard_map/ppermute | solution.py:680
  57.8 8.2 %collective-permute-start.18 = (f32[72,384]{1,0:T(8,128)S(1)}, f32[72,384]{1,0:T(8,128)S(1)}, u32[]{:S(2)}, u32[]{:S(2)}) collective-permute-start(f32[72,384]{1,0:T(8,128)S(1)} %get-tuple-element.208.refs_2_), channel_id=1, source_target_pairs={{0,3},{1,0},{2,1},{3,2},{4,7},{5,4},{6,5},{7,6},{8,11},{9,8},{10,9... | collective-permute-start | bytes 331784 | tf_op jit(solution)/shard_map/ppermute | solution.py:680

commit v11 on v8

--- a/solution.py
+++ b/solution.py
@@ -484,6 +484,10 @@
                 ] - fast(both_parts(left_ref[r : r + deep, :]), right)
 
 
+def store_slots():
+    return 4
+
+
 def subtract_near(left, right, kept):
     rows, span = kept[0].shape
     parts = len(kept)
@@ -624,8 +628,8 @@
         out_specs=pl.BlockSpec(memory_space=pltpu.HBM),
         out_shape=shape(rows, parts * span),
         scratch_shapes=[
-            pltpu.VMEM((3, block_of(rows, 512), span), f32),
-            pltpu.SemaphoreType.DMA((3,)),
+            pltpu.VMEM((store_slots(), block_of(rows, 512), span), f32),
+            pltpu.SemaphoreType.DMA((store_slots(),)),
         ],
         compiler_params=params(12),
         cost_estimate=cost(5 * rows * span * parts * deep, 8 * rows * span * parts),

time: 75.1 us -> 74.7 us (level)
  no operation moved by 1% of the time
where the time goes in v11:
time: 74.7 us; the launch traced here: 74.6 us
  Pallas kernels  34.8 us (47%)
  starting transfers between devices  22.3 us (30%)
  waiting for transfers between devices  15.4 us (21%)
  between operations  1 us (1%)
  local copies, waits for them, and re-layouts  0.99 us (1%)
    ppermute x13, starting transfers between devices, flip(): return lax.ppermute(value, axis, [(i, i ^ bit) for i in range(size)])  11.7 us
    ppermute x13, waiting for transfers between devices, flip(): return lax.ppermute(value, axis, [(i, i ^ bit) for i in range(size)])  10.6 us
    ppermute x6, starting transfers between devices, shift(): lax.ppermute(piece, 'col', [(i, (i + by) % size) for i in range(size)])  10.6 us
    pallas_call x14, Pallas kernels, small_call(): pl.pallas_call(body, out_shape=out, compiler_params=params(mib), cost_est...  9.59 us
    pallas_call x1, Pallas kernels, product_down(): pl.pallas_call(down_kernel, in_specs=[whole, whole, pl.BlockSpec(memory_s...  7.04 us
    pallas_call x1, Pallas kernels, subtract_far(): pl.pallas_call(kernel, in_specs=[whole] * (4 + parts), out_specs=pl.Block...  6.95 us
    pallas_call x3, Pallas kernels, across_call(): pl.pallas_call(body, grid=(count,), in_specs=[fixed(x) for x in operands]...  6.91 us
    ppermute x6, waiting for transfers between devices, shift(): lax.ppermute(piece, 'col', [(i, (i + by) % size) for i in range(size)])  4.73 us
  transfers between devices with their start and end apart: 19, of which 9 were waited for; matrix products, arithmetic and copies ran while one was open for 0% of the time, Pallas kernels for 34%

profile of v11, /device:TPU:0, one launch (start us, length us, event | category | flops | bytes accessed | tf_op | source)
XLA Modules:
  0.0 74.6 jit_solution(1158166007558297065)
XLA Ops:
  0.6 0.0 copy-start
  0.6 1.0 %copy-done = f32[1536,64]{0,1:T(8,128)S(1)} copy-done((f32[1536,64]{0,1:T(8,128)S(1)}, f32[1536,64]{0,1:T(8,128)}, u32[]{:S(2)}) %copy-start) | copy-done | bytes 393240
  1.6 0.5 shard_map.41
  2.1 0.6 collective-permute-start
  2.7 0.9 %collective-permute-done.b_ref = f32[64,128]{1,0:T(8,128)S(1)} collective-permute-done((f32[64,128]{1,0:T(8,128)S(1)}, f32[64,128]{1,0:T(8,128)S(1)}, u32[]{:S(2)}, u32[]{:S(2)}) %collective-permute-start) | collective-permute-done | bytes 32800 | tf_op jit(solution)/shard_map/ppermute | solution.py:641
  3.6 2.9 %collective-permute-start.1 = (f32[64,896]{1,0:T(8,128)S(1)}, f32[64,896]{1,0:T(8,128)S(1)}, u32[]{:S(2)}, u32[]{:S(2)}) collective-permute-start(f32[64,896]{1,0:T(8,128)S(1)} %get-tuple-element.118), channel_id=1, source_target_pairs={{0,8},{4,12},{8,0},{12,4},{16,24},{20,28},{24,16},{28,20},{1,9},{5... | collective-permute-start | bytes 688136 | tf_op jit(solution)/shard_map/ppermute | solution.py:641
  6.4 1.5 %collective-permute-start.2 = (f32[64,896]{1,0:T(8,128)S(1)}, f32[64,896]{1,0:T(8,128)S(1)}, u32[]{:S(2)}, u32[]{:S(2)}) collective-permute-start(f32[64,896]{1,0:T(8,128)S(1)} %get-tuple-element.119), channel_id=1, source_target_pairs={{0,16},{4,20},{8,24},{12,28},{16,0},{20,4},{24,8},{28,12},{1,17},{... | collective-permute-start | bytes 688136 | tf_op jit(solution)/shard_map/ppermute | solution.py:641
  8.0 7.0 %product_down.1 = (f32[64,1536]{1,0:T(8,128)S(1)}, f32[64,1536]{1,0:T(8,128)S(1)}, f32[1536,768]{1,0:T(8,128)S(1)}, f32[1536,768]{1,0:T(8,128)S(1)}, f32[1536,768]{1,0:T(8,128)S(1)}, /*index=5*/f32[1536,768]{1,0:T(8,128)S(1)}) custom-call(f32[64,768]{1,0:T(8,128)S(1)} %get-tuple-element.120.first_ref.refs_0_.refs_3_, ...), custom_call_target="tpu_custom_call" | custom-call | flops 2415919104 | bytes 18874368 | tf_op jit(solution)/shard_map/product_down/pallas_call | solution.py:219
  15.0 0.0 collective-permute-done.1.refs_2_.refs_1_
  15.0 0.0 collective-permute-done.2.refs_3_.refs_2_
  15.0 0.1 shard_map.43
  15.1 0.6 collective-permute-start.4
  15.7 0.3 collective-permute-start.5
  16.0 2.7 %collective-permute-start.3 = (f32[64,128]{1,0:T(8,128)S(1)}, f32[64,128]{1,0:T(8,128)S(1)}, u32[]{:S(2)}, u32[]{:S(2)}) collective-permute-start(f32[64,128]{1,0:T(8,128)S(1)} %get-tuple-element.117.refs_0_), channel_id=1, source_target_pairs={{0,24},{4,28},{8,16},{12,20},{16,8},{20,12},{24,0},{28,4},{1,25},{... | collective-permute-start | bytes 98312 | tf_op jit(solution)/shard_map/ppermute | solution.py:641
  18.7 4.8 %collective-permute-done.3.refs_3_ = f32[64,128]{1,0:T(8,128)S(1)} collective-permute-done((f32[64,128]{1,0:T(8,128)S(1)}, f32[64,128]{1,0:T(8,128)S(1)}, u32[]{:S(2)}, u32[]{:S(2)}) %collective-permute-start.3) | collective-permute-done | bytes 32800 | tf_op jit(solution)/shard_map/ppermute | solution.py:641
  23.5 2.7 %shard_map.44 = (f32[64,64]{1,0:T(8,128)}, f32[64,64]{1,0:T(8,128)S(1)}, f32[64,64]{1,0:T(8,128)S(1)}, f32[64,64]{1,0:T(8,128)S(1)}, f32[1536,768]{1,0:T(8,128)S...) custom-call(f32[64,128]{1,0:T(8,128)S(1)} %get-tuple-element.117.ref, ...), custom_call_target="tpu_custom_call", output_to_operand_aliasing={{4}: (4, {}), {5}: (5, {}), {6}: (6, {}), {7}: (7, {})} | custom-call | flops 50000000 | bytes 1000000 | tf_op jit(solution)/shard_map/pallas_call | solution.py:64
  26.2 0.6 fix_down.1
  26.7 0.1 collective-permute-start.7
  26.8 0.0 collective-permute-done.4.refs_1_
  26.8 0.0 collective-permute-done.5.refs_3_
  26.9 0.5 collective-permute-start.6
  27.4 1.1 %collective-permute-done.7.refs_1_ = f32[64,1536]{1,0:T(8,128)S(1)} collective-permute-done((f32[64,1536]{1,0:T(8,128)S(1)}, f32[64,1536]{1,0:T(8,128)S(1)}, u32[]{:S(2)}, u32[]{:S(2)}) %collective-permute-start.7) | collective-permute-done | bytes 393248 | tf_op jit(solution)/shard_map/ppermute | solution.py:641
  28.6 0.1 collective-permute-start.8
  28.7 0.4 collective-permute-start.9
  29.1 0.0 collective-permute-done.6.refs_1_
  29.1 3.9 %shard_map.47 = (f32[64,3072]{1,0:T(8,128)S(1)}, bf16[3072,128]{1,0:T(8,128)(2,1)S(1)}, f32[64,384]{1,0:T(8,128)S(1)}, f32[64,384]{1,0:T(8,128)S(1)}, f32[1536,7...) custom-call(f32[64,1536]{1,0:T(8,128)S(1)} %get-tuple-element.145.re, ...), custom_call_target="tpu_custom_call", output_to_operand_aliasing={{4}: (3, {}), {5}: (4, {}), {6}: (5, {}), {7}: (6, {})} | custom-call | flops 1207959552 | bytes 9437184 | tf_op jit(solution)/shard_map/pallas_call | solution.py:355
  33.0 2.6 %collective-permute-done.8.refs_1_ = f32[64,768]{1,0:T(8,128)S(1)} collective-permute-done((f32[64,768]{1,0:T(8,128)S(1)}, f32[64,768]{1,0:T(8,128)S(1)}, u32[]{:S(2)}, u32[]{:S(2)}) %collective-permute-start.8) | collective-permute-done | bytes 196640 | tf_op jit(solution)/shard_map/ppermute | solution.py:641
  35.6 0.1 collective-permute-done.9.refs_3_
  35.7 0.4 collective-permute-start.13
  36.0 1.7 %collective-permute-start.14 = (f32[64,768]{1,0:T(8,128)S(1)}, f32[64,768]{1,0:T(8,128)S(1)}, u32[]{:S(2)}, u32[]{:S(2)}) collective-permute-start(f32[64,768]{1,0:T(8,128)S(1)} %get-tuple-element.177.refs_2_), channel_id=1, source_target_pairs={{0,8},{4,12},{8,0},{12,4},{16,24},{20,28},{24,16},{28,20},{1,9},{5... | collective-permute-start | bytes 589832 | tf_op jit(solution)/shard_map/ppermute | solution.py:641
  37.7 1.5 %shard_map.49 = (f32[64,384]{1,0:T(8,128)S(1)}, f32[1536,768]{1,0:T(8,128)S(1)}, f32[1536,768]{1,0:T(8,128)S(1)}, f32[1536,768]{1,0:T(8,128)S(1)}, f32[1536,768]{1,0:T(8,128)S(1)}) custom-call(bf16[3072,128]{1,0:T(8,128)(2,1)S(1)} %get-tuple-element.156.refs_0_, ...), custom_call_target="tpu_custom_call", output_to_operand_aliasing={{1}: (1, {}), {2}: (2, {}), {3}: (3, {}), {4}: (4, {})} | custom-call | flops 603979776 | bytes 4718592 | tf_op jit(solution)/shard_map/pallas_call | solution.py:355
  39.2 1.5 %shard_map.50 = (f32[64,384]{1,0:T(8,128)S(1)}, f32[1536,768]{1,0:T(8,128)S(1)}, f32[1536,768]{1,0:T(8,128)S(1)}, f32[1536,768]{1,0:T(8,128)S(1)}, f32[1536,768]{1,0:T(8,128)S(1)}) custom-call(bf16[3072,128]{1,0:T(8,128)(2,1)S(1)} %get-tuple-element.156.refs_0_, ...), custom_call_target="tpu_custom_call", output_to_operand_aliasing={{1}: (1, {}), {2}: (2, {}), {3}: (3, {}), {4}: (4, {})} | custom-call | flops 603979776 | bytes 4718592 | tf_op jit(solution)/shard_map/pallas_call | solution.py:355
  40.7 1.1 %collective-permute-done.13.refs_1_ = f32[64,768]{1,0:T(8,128)S(1)} collective-permute-done((f32[64,768]{1,0:T(8,128)S(1)}, f32[64,768]{1,0:T(8,128)S(1)}, u32[]{:S(2)}, u32[]{:S(2)}) %collective-permute-start.13) | collective-permute-done | bytes 196640 | tf_op jit(solution)/shard_map/ppermute | solution.py:641
  41.8 0.1 collective-permute-done.14.refs_3_
  42.0 0.1 collective-permute-start.15
  42.0 1.6 %collective-permute-start.12 = (f32[64,384]{1,0:T(8,128)S(1)}, f32[64,384]{1,0:T(8,128)S(1)}, u32[]{:S(2)}, u32[]{:S(2)}) collective-permute-start(f32[64,384]{1,0:T(8,128)S(1)} %get-tuple-element.174), channel_id=1, source_target_pairs={{0,1},{1,2},{2,3},{3,0},{4,5},{5,6},{6,7},{7,4},{8,9},{9,10},{10,1... | collective-permute-start | bytes 294920 | tf_op jit(solution)/shard_map/ppermute | solution.py:655
  43.7 2.6 %collective-permute-start.10 = (f32[64,384]{1,0:T(8,128)S(1)}, f32[64,384]{1,0:T(8,128)S(1)}, u32[]{:S(2)}, u32[]{:S(2)}) collective-permute-start(f32[64,384]{1,0:T(8,128)S(1)} %get-tuple-element.172), channel_id=1, source_target_pairs={{0,2},{1,3},{2,0},{3,1},{4,6},{5,7},{6,4},{7,5},{8,10},{9,11},{10,... | collective-permute-start | bytes 294920 | tf_op jit(solution)/shard_map/ppermute | solution.py:655
  46.2 1.4 %collective-permute-start.11 = (f32[64,384]{1,0:T(8,128)S(1)}, f32[64,384]{1,0:T(8,128)S(1)}, u32[]{:S(2)}, u32[]{:S(2)}) collective-permute-start(f32[64,384]{1,0:T(8,128)S(1)} %get-tuple-element.173), channel_id=1, source_target_pairs={{0,3},{1,0},{2,1},{3,2},{4,7},{5,4},{6,5},{7,6},{8,11},{9,8},{10,9... | collective-permute-start | bytes 294920 | tf_op jit(solution)/shard_map/ppermute | solution.py:655
  47.6 0.5 shard_map.52
  48.1 0.0 collective-permute-done.15.refs_2_
  48.1 0.5 shard_map.53
  48.6 1.0 %collective-permute-done.12.refs_3_ = f32[64,384]{1,0:T(8,128)S(1)} collective-permute-done((f32[64,384]{1,0:T(8,128)S(1)}, f32[64,384]{1,0:T(8,128)S(1)}, u32[]{:S(2)}, u32[]{:S(2)}) %collective-permute-start.12) | collective-permute-done | bytes 98336 | tf_op jit(solution)/shard_map/ppermute | solution.py:655
  49.7 3.7 %collective-permute-done.10.refs_1_ = f32[64,384]{1,0:T(8,128)S(1)} collective-permute-done((f32[64,384]{1,0:T(8,128)S(1)}, f32[64,384]{1,0:T(8,128)S(1)}, u32[]{:S(2)}, u32[]{:S(2)}) %collective-permute-start.10) | collective-permute-done | bytes 98336 | tf_op jit(solution)/shard_map/ppermute | solution.py:655
  53.4 0.0 collective-permute-done.11.refs_2_
  53.4 0.1 shard_map.54
  53.5 2.6 %collective-permute-start.16 = (f32[72,384]{1,0:T(8,128)S(1)}, f32[72,384]{1,0:T(8,128)S(1)}, u32[]{:S(2)}, u32[]{:S(2)}) collective-permute-start(f32[72,384]{1,0:T(8,128)S(1)} %get-tuple-element.208.refs_2_), channel_id=1, source_target_pairs={{0,1},{1,2},{2,3},{3,0},{4,5},{5,6},{6,7},{7,4},{8,9},{9,10},{10,1... | collective-permute-start | bytes 331784 | tf_op jit(solution)/shard_map/ppermute | solution.py:655
  56.1 1.6 %collective-permute-start.17 = (f32[72,384]{1,0:T(8,128)S(1)}, f32[72,384]{1,0:T(8,128)S(1)}, u32[]{:S(2)}, u32[]{:S(2)}) collective-permute-start(f32[72,384]{1,0:T(8,128)S(1)} %get-tuple-element.208.refs_2_), channel_id=1, source_target_pairs={{0,2},{1,3},{2,0},{3,1},{4,6},{5,7},{6,4},{7,5},{8,10},{9,11},{10,... | collective-permute-start | bytes 331784 | tf_op jit(solution)/shard_map/ppermute | solution.py:655
  57.7 0.8 %collective-permute-start.18 = (f32[72,384]{1,0:T(8,128)S(1)}, f32[72,384]{1,0:T(8,128)S(1)}, u32[]{:S(2)}, u32[]{:S(2)}) collective-permute-start(f32[72,384]{1,0:T(8,128)S(1)} %get-tuple-element.208.refs_2_), channel_id=1, source_target_pairs={{0,3},{1,0},{2,1},{3,2},{4,7},{5,4},{6,5},{7,6},{8,11},{9,8},{10,9... | collective-permute-start | bytes 331784 | tf_op jit(solution)/shard_map/ppermute | solution.py:655
  58.5 2.3 %shard_map.55 = (f32[64,64]{1,0:T(8,128)S(1)}, f32[1536,768]{1,0:T(8,128)S(1)}, f32[1536,768]{1,0:T(8,128)S(1)}, f32[1536,768]{1,0:T(8,128)S(1)}, f32[1536,768]{1,0:T(8,128)S(1)}) custom-call(f32[64,64]{1,0:T(8,128)S(1)} %get-tuple-element.130.refs_0_, ...), custom_call_target="tpu_custom_call", output_to_operand_aliasing={{1}: (3, {}), {2}: (4, {}), {3}: (5, {}), {4}: (6, {})} | custom-call | flops 50000000 | bytes 1000000 | tf_op jit(solution)/shard_map/pallas_call | solution.py:64
  60.8 1.3 %shard_map.56 = (bf16[128,3072]{1,0:T(8,128)(2,1)S(1)}, bf16[128,3072]{1,0:T(8,128)(2,1)S(1)}, f32[64,1536]{1,0:T(8,128)S(1)}, bf16[1536,128]{1,0:T(8,128)(2,1)S...) custom-call(f32[64,64]{1,0:T(8,128)S(1)} %get-tuple-element.201.refs, ...), custom_call_target="tpu_custom_call", output_to_operand_aliasing={{4}: (6, {}), {5}: (7, {}), {6}: (8, {}), {7}: (9, {})} | custom-call | flops 1000000 | bytes 1000000 | tf_op jit(solution)/shard_map/pallas_call | solution.py:64
  62.0 3.8 %subtract_near.1 = (f32[1536,768]{1,0:T(8,128)S(1)}, f32[1536,768]{1,0:T(8,128)S(1)}, f32[1536,768]{1,0:T(8,128)S(1)}, f32[1536,768]{1,0:T(8,128)S(1)}) custom-call(bf16[1536,128]{1,0:T(8,128)(2,1)S(1)} %get-tuple-element.209.refs_0_.refs_2_, ...), custom_call_target="tpu_custom_call", output_to_operand_aliasing={{0}: (2, {}), {1}: (3, {}), {2}: (4, {}), {3}: (5, {})} | custom-call | flops 2415919104 | bytes 37748736 | tf_op jit(solution)/shard_map/subtract_near/pallas_call | solution.py:503
  65.9 0.0 collective-permute-done.16.refs_3_
  65.9 0.0 collective-permute-done.17.refs_4_
  65.9 0.0 collective-permute-done.18.refs_5_
  65.9 1.6 %shard_map.57 = (bf16[1536,128]{1,0:T(8,128)(2,1)S(1)}, f32[1536,768]{1,0:T(8,128)S(1)}, f32[1536,768]{1,0:T(8,128)S(1)}, f32[1536,768]{1,0:T(8,128)S(1)}, f32[1536,768]{1,0:T(8,128)S(1)}) custom-call(f32[64,64]{1,0:T(8,128)S(1)} %get-tuple-element.201.refs_0_, ...), custom_call_target="tpu_custom_call", output_to_operand_aliasing={{1}: (6, {}), {2}: (7, {}), {3}: (8, {}), {4}: (9, {})} | custom-call | flops 1000000 | bytes 1000000 | tf_op jit(solution)/shard_map/pallas_call | solution.py:64
  67.4 6.9 %subtract_far.1 = f32[1536,3072]{1,0:T(8,128)} custom-call(bf16[1536,128]{1,0:T(8,128)(2,1)S(1)} %get-tuple-element.219.refs_0_, bf16[128,3072]{1,0:T(8,128)(2,1)S(1)} %get-tuple-element.220.refs_1_, bf16[1536,128]{1,0:T(8,128)(2,1)S(1)} %get-tuple-element.209.refs_0_.refs_2_, bf16[128,3072]{1,0:T(8,128)(2,1)S(1)} %get-tuple-element.210.refs_1_.refs_3_, ...), custom_call_target="tpu_custom_call" | custom-call | flops 3019898880 | bytes 37748736 | tf_op jit(solution)/shard_map/subtract_far/pallas_call | solution.py:625
  (5 shorter events, 0.2 us)
Async XLA Ops:
  0.6 1.0 %copy-start = (f32[1536,64]{0,1:T(8,128)S(1)}, f32[1536,64]{0,1:T(8,128)}, u32[]{:S(2)}) copy-start(f32[1536,64]{0,1:T(8,128)} %param.3) | copy-start | bytes 1179652
  2.1 1.4 %collective-permute-start = (f32[64,128]{1,0:T(8,128)S(1)}, f32[64,128]{1,0:T(8,128)S(1)}, u32[]{:S(2)}, u32[]{:S(2)}) collective-permute-start(f32[64,128]{1,0:T(8,128)S(1)} %get-tuple-element.116.a_ref), channel_id=1, source_target_pairs={{0,4},{4,0},{8,12},{12,8},{16,20},{20,16},{24,28},{28,24},{1,5},{5... | collective-permute-start | bytes 98312 | tf_op jit(solution)/shard_map/ppermute | solution.py:641
  3.6 11.5 %collective-permute-start.1 = (f32[64,896]{1,0:T(8,128)S(1)}, f32[64,896]{1,0:T(8,128)S(1)}, u32[]{:S(2)}, u32[]{:S(2)}) collective-permute-start(f32[64,896]{1,0:T(8,128)S(1)} %get-tuple-element.118), channel_id=1, source_target_pairs={{0,8},{4,12},{8,0},{12,4},{16,24},{20,28},{24,16},{28,20},{1,9},{5... | collective-permute-start | bytes 688136 | tf_op jit(solution)/shard_map/ppermute | solution.py:641
  6.4 8.6 %collective-permute-start.2 = (f32[64,896]{1,0:T(8,128)S(1)}, f32[64,896]{1,0:T(8,128)S(1)}, u32[]{:S(2)}, u32[]{:S(2)}) collective-permute-start(f32[64,896]{1,0:T(8,128)S(1)} %get-tuple-element.119), channel_id=1, source_target_pairs={{0,16},{4,20},{8,24},{12,28},{16,0},{20,4},{24,8},{28,12},{1,17},{... | collective-permute-start | bytes 688136 | tf_op jit(solution)/shard_map/ppermute | solution.py:641
  15.1 11.7 %collective-permute-start.4 = (f32[64,768]{1,0:T(8,128)S(1)}, f32[64,768]{1,0:T(8,128)S(1)}, u32[]{:S(2)}, u32[]{:S(2)}) collective-permute-start(f32[64,768]{1,0:T(8,128)S(1)} %get-tuple-element.133.refs_0_), channel_id=1, source_target_pairs={{0,16},{4,20},{8,24},{12,28},{16,0},{20,4},{24,8},{28,12},{1,17},{... | collective-permute-start | bytes 589832 | tf_op jit(solution)/shard_map/ppermute | solution.py:641
  15.7 11.1 %collective-permute-start.5 = (f32[64,768]{1,0:T(8,128)S(1)}, f32[64,768]{1,0:T(8,128)S(1)}, u32[]{:S(2)}, u32[]{:S(2)}) collective-permute-start(f32[64,768]{1,0:T(8,128)S(1)} %get-tuple-element.134.refs_2_), channel_id=1, source_target_pairs={{0,8},{4,12},{8,0},{12,4},{16,24},{20,28},{24,16},{28,20},{1,9},{5... | collective-permute-start | bytes 589832 | tf_op jit(solution)/shard_map/ppermute | solution.py:641
  16.0 7.5 %collective-permute-start.3 = (f32[64,128]{1,0:T(8,128)S(1)}, f32[64,128]{1,0:T(8,128)S(1)}, u32[]{:S(2)}, u32[]{:S(2)}) collective-permute-start(f32[64,128]{1,0:T(8,128)S(1)} %get-tuple-element.117.refs_0_), channel_id=1, source_target_pairs={{0,24},{4,28},{8,16},{12,20},{16,8},{20,12},{24,0},{28,4},{1,25},{... | collective-permute-start | bytes 98312 | tf_op jit(solution)/shard_map/ppermute | solution.py:641
  26.7 1.8 %collective-permute-start.7 = (f32[64,1536]{1,0:T(8,128)S(1)}, f32[64,1536]{1,0:T(8,128)S(1)}, u32[]{:S(2)}, u32[]{:S(2)}) collective-permute-start(f32[64,1536]{1,0:T(8,128)S(1)} %get-tuple-element.147), channel_id=1, source_target_pairs={{0,4},{4,0},{8,12},{12,8},{16,20},{20,16},{24,28},{28,24},{1,5},{5... | collective-permute-start | bytes 1179656 | tf_op jit(solution)/shard_map/ppermute | solution.py:641
  26.9 2.2 %collective-permute-start.6 = (f32[64,1536]{1,0:T(8,128)S(1)}, f32[64,1536]{1,0:T(8,128)S(1)}, u32[]{:S(2)}, u32[]{:S(2)}) collective-permute-start(f32[64,1536]{1,0:T(8,128)S(1)} %get-tuple-element.145.refs_0_), channel_id=1, source_target_pairs={{0,4},{4,0},{8,12},{12,8},{16,20},{20,16},{24,28},{28,24},{1,5},{5... | collective-permute-start | bytes 1179656 | tf_op jit(solution)/shard_map/ppermute | solution.py:641
  28.6 7.0 %collective-permute-start.8 = (f32[64,768]{1,0:T(8,128)S(1)}, f32[64,768]{1,0:T(8,128)S(1)}, u32[]{:S(2)}, u32[]{:S(2)}) collective-permute-start(f32[64,768]{1,0:T(8,128)S(1)} %get-tuple-element.157.refs_0_), channel_id=1, source_target_pairs={{0,8},{4,12},{8,0},{12,4},{16,24},{20,28},{24,16},{28,20},{1,9},{5... | collective-permute-start | bytes 589832 | tf_op jit(solution)/shard_map/ppermute | solution.py:641
  28.7 6.9 %collective-permute-start.9 = (f32[64,768]{1,0:T(8,128)S(1)}, f32[64,768]{1,0:T(8,128)S(1)}, u32[]{:S(2)}, u32[]{:S(2)}) collective-permute-start(f32[64,768]{1,0:T(8,128)S(1)} %get-tuple-element.158.refs_2_), channel_id=1, source_target_pairs={{0,16},{4,20},{8,24},{12,28},{16,0},{20,4},{24,8},{28,12},{1,17},{... | collective-permute-start | bytes 589832 | tf_op jit(solution)/shard_map/ppermute | solution.py:641
  35.7 6.1 %collective-permute-start.13 = (f32[64,768]{1,0:T(8,128)S(1)}, f32[64,768]{1,0:T(8,128)S(1)}, u32[]{:S(2)}, u32[]{:S(2)}) collective-permute-start(f32[64,768]{1,0:T(8,128)S(1)} %get-tuple-element.176.refs_0_), channel_id=1, source_target_pairs={{0,16},{4,20},{8,24},{12,28},{16,0},{20,4},{24,8},{28,12},{1,17},{... | collective-permute-start | bytes 589832 | tf_op jit(solution)/shard_map/ppermute | solution.py:641
  36.0 5.9 %collective-permute-start.14 = (f32[64,768]{1,0:T(8,128)S(1)}, f32[64,768]{1,0:T(8,128)S(1)}, u32[]{:S(2)}, u32[]{:S(2)}) collective-permute-start(f32[64,768]{1,0:T(8,128)S(1)} %get-tuple-element.177.refs_2_), channel_id=1, source_target_pairs={{0,8},{4,12},{8,0},{12,4},{16,24},{20,28},{24,16},{28,20},{1,9},{5... | collective-permute-start | bytes 589832 | tf_op jit(solution)/shard_map/ppermute | solution.py:641
  42.0 6.1 %collective-permute-start.15 = (f32[64,1536]{1,0:T(8,128)S(1)}, f32[64,1536]{1,0:T(8,128)S(1)}, u32[]{:S(2)}, u32[]{:S(2)}) collective-permute-start(f32[64,1536]{1,0:T(8,128)S(1)} %get-tuple-element.182.refs_1_), channel_id=1, source_target_pairs={{0,4},{4,0},{8,12},{12,8},{16,20},{20,16},{24,28},{28,24},{1,5},{5... | collective-permute-start | bytes 1179656 | tf_op jit(solution)/shard_map/ppermute | solution.py:641
  42.0 7.6 %collective-permute-start.12 = (f32[64,384]{1,0:T(8,128)S(1)}, f32[64,384]{1,0:T(8,128)S(1)}, u32[]{:S(2)}, u32[]{:S(2)}) collective-permute-start(f32[64,384]{1,0:T(8,128)S(1)} %get-tuple-element.174), channel_id=1, source_target_pairs={{0,1},{1,2},{2,3},{3,0},{4,5},{5,6},{6,7},{7,4},{8,9},{9,10},{10,1... | collective-permute-start | bytes 294920 | tf_op jit(solution)/shard_map/ppermute | solution.py:655
  43.7 9.7 %collective-permute-start.10 = (f32[64,384]{1,0:T(8,128)S(1)}, f32[64,384]{1,0:T(8,128)S(1)}, u32[]{:S(2)}, u32[]{:S(2)}) collective-permute-start(f32[64,384]{1,0:T(8,128)S(1)} %get-tuple-element.172), channel_id=1, source_target_pairs={{0,2},{1,3},{2,0},{3,1},{4,6},{5,7},{6,4},{7,5},{8,10},{9,11},{10,... | collective-permute-start | bytes 294920 | tf_op jit(solution)/shard_map/ppermute | solution.py:655
  46.2 7.1 %collective-permute-start.11 = (f32[64,384]{1,0:T(8,128)S(1)}, f32[64,384]{1,0:T(8,128)S(1)}, u32[]{:S(2)}, u32[]{:S(2)}) collective-permute-start(f32[64,384]{1,0:T(8,128)S(1)} %get-tuple-element.173), channel_id=1, source_target_pairs={{0,3},{1,0},{2,1},{3,2},{4,7},{5,4},{6,5},{7,6},{8,11},{9,8},{10,9... | collective-permute-start | bytes 294920 | tf_op jit(solution)/shard_map/ppermute | solution.py:655
  53.5 12.4 %collective-permute-start.16 = (f32[72,384]{1,0:T(8,128)S(1)}, f32[72,384]{1,0:T(8,128)S(1)}, u32[]{:S(2)}, u32[]{:S(2)}) collective-permute-start(f32[72,384]{1,0:T(8,128)S(1)} %get-tuple-element.208.refs_2_), channel_id=1, source_target_pairs={{0,1},{1,2},{2,3},{3,0},{4,5},{5,6},{6,7},{7,4},{8,9},{9,10},{10,1... | collective-permute-start | bytes 331784 | tf_op jit(solution)/shard_map/ppermute | solution.py:655
  56.1 9.8 %collective-permute-start.17 = (f32[72,384]{1,0:T(8,128)S(1)}, f32[72,384]{1,0:T(8,128)S(1)}, u32[]{:S(2)}, u32[]{:S(2)}) collective-permute-start(f32[72,384]{1,0:T(8,128)S(1)} %get-tuple-element.208.refs_2_), channel_id=1, source_target_pairs={{0,2},{1,3},{2,0},{3,1},{4,6},{5,7},{6,4},{7,5},{8,10},{9,11},{10,... | collective-permute-start | bytes 331784 | tf_op jit(solution)/shard_map/ppermute | solution.py:655
  57.7 8.2 %collective-permute-start.18 = (f32[72,384]{1,0:T(8,128)S(1)}, f32[72,384]{1,0:T(8,128)S(1)}, u32[]{:S(2)}, u32[]{:S(2)}) collective-permute-start(f32[72,384]{1,0:T(8,128)S(1)} %get-tuple-element.208.refs_2_), channel_id=1, source_target_pairs={{0,3},{1,0},{2,1},{3,2},{4,7},{5,4},{6,5},{7,6},{8,11},{9,8},{10,9... | collective-permute-start | bytes 331784 | tf_op jit(solution)/shard_map/ppermute | solution.py:655
